TPU v7x, 128 devices: a whole 4x4x4 slice. The times are simulated.
128 devices in a mesh: fsdp: 32 (over x, z_lo, y), tok: 4 (over z_hi, core).
Axes of the slice: x: 4, y: 4, z: 4 (z_hi: 2, z_lo: 2; z = z_hi * 2 + z_lo), core: 2. Of those that a mesh axis runs over, the one named last changes fastest.
Arguments:
- tokens: bfloat16 [64, 256, 2048], P('fsdp', 'tok'), may hold values from -6 to 6
- cotangent: bfloat16 [64, 256, 2048], P('fsdp', 'tok'), may hold values from -6 to 6
- segments: int32 [64, 256], P('fsdp'), may hold values from 0 to 7, never falling along the last dimension, each value on 1 to 128 neighbouring positions
- adapter_id: int32 [64], P('fsdp'), may hold values from 0 to 7
- w_qkv: bfloat16 [3, 2048, 2048], P(None, 'fsdp', 'tok'), may hold values from -0.125 to 0.125
- w_out: bfloat16 [2048, 2048], P('tok', 'fsdp'), may hold values from -0.125 to 0.125
- w_gateup: bfloat16 [2, 2048, 5632], P(None, 'fsdp', 'tok'), may hold values from -0.125 to 0.125
- w_down: bfloat16 [5632, 2048], P('tok', 'fsdp'), may hold values from -0.078125 to 0.078125
- gain_attn: float32 [2048], replicated, may hold values from 0.5 to 1.5
- gain_ffn: float32 [2048], replicated, may hold values from 0.5 to 1.5
- gain_sub: float32 [256], replicated, may hold values from 0.5 to 1.5
- lambda_head: float32 [8], replicated, may hold values from 0.2 to 0.7
- a_in: bfloat16 [5, 2048, 128], P(None, ('fsdp', 'tok')), may hold values from -0.125 to 0.125
- b_qkv: bfloat16 [3, 128, 2048], P(None, 'fsdp', 'tok'), may hold values from -0.75 to 0.75
- b_gateup: bfloat16 [2, 128, 5632], P(None, 'fsdp', 'tok'), may hold values from -0.75 to 0.75
- a_out: bfloat16 [2048, 128], P('tok', 'fsdp'), may hold values from -0.125 to 0.125
- a_down: bfloat16 [5632, 128], P('tok', 'fsdp'), may hold values from -0.078125 to 0.078125
- b_rows: bfloat16 [2, 128, 2048], P(None, None, ('fsdp', 'tok')), may hold values from -0.75 to 0.75
Outputs:
- output: bfloat16 [64, 256, 2048], P('fsdp', 'tok')
- grad_tokens: float32 [64, 256, 2048], P('fsdp', 'tok')
- grad_a_in: float32 [5, 2048, 128], P(None, ('fsdp', 'tok'))
- grad_b_qkv: float32 [3, 128, 2048], P(None, 'fsdp', 'tok')
- grad_b_gateup: float32 [2, 128, 5632], P(None, 'fsdp', 'tok')
- grad_a_out: float32 [2048, 128], P('tok', 'fsdp')
- grad_a_down: float32 [5632, 128], P('tok', 'fsdp')
- grad_b_rows: float32 [2, 128, 2048], P(None, None, ('fsdp', 'tok'))
Inputs may be any that keep to these rules, and one draw needn't show every extreme that they name: `segments`: segment numbers never fall along a sequence; a document holds at most 128 tokens.
All inputs are finite; a program needn't handle non-finite values.
Results may differ from a plain program's by a relative error of at most 0.02.
The roundings to bfloat16 on the way count: a program that leaves them out, or rounds other values in their place, can miss the bound.
Values may be sent and summed in bfloat16 or wider, within the bound.
No kernel may reach another device: no remote copies, remote signals or barrier semaphores. Data moves between devices by JAX's collectives and lax.ppermute only.
A program may use at most 192 MiB of HBM per device.

v0:
```python
from functools import partial

import jax
import jax.numpy as jnp
from jax import lax
from jax.sharding import PartitionSpec as P

D = 2048
HEAD_DIM = 128
VALUE_DIM = 256
RANK = 16
COLS = 128


highest = lax.Precision.HIGHEST
negative = -1e30
adapter_scale = 2.0
lambda_init = 0.2
rotary_base = 10000.0
row_epsilon = 1e-06
head_epsilon = 1e-05


def rows_norm(values, gain_vector):
    return (
        values
        * lax.rsqrt(jnp.mean(values * values, axis=-1, keepdims=True) + row_epsilon)
        * gain_vector
    )


def head_norm(values, gain_vector):
    scaled = values * lax.rsqrt(jnp.mean(values * values, axis=-1, keepdims=True) + head_epsilon)
    return scaled * gain_vector * (1.0 - lambda_init)


def rotary_heads(values, positions, head_dim):
    length = values.shape[0]
    groups = values.reshape(length, -1, head_dim)
    half_dim = head_dim // 2
    frequency = rotary_base ** (-jnp.arange(half_dim, dtype=jnp.float32) / half_dim)
    angles = positions.astype(jnp.float32)[:, None] * frequency[None, :]
    cosine = jnp.cos(angles)[:, None, :]
    sine_part = jnp.sin(angles)[:, None, :]
    first_half = groups[..., :half_dim]
    second = groups[..., half_dim:]
    turned = jnp.concatenate(
        [first_half * cosine - second * sine_part, second * cosine + first_half * sine_part],
        axis=-1,
    )
    return turned.reshape(length, -1)


def swiglu(gate_rows, up_rows):
    return gate_rows * jax.nn.sigmoid(gate_rows) * up_rows


def contract_last(left, right):
    return lax.dot_general(
        left, right, (((1,), (1,)), ((), ())), preferred_element_type=jnp.float32
    )


def attention_scores(query_in, key_in, allowed):
    raw_scores = jnp.einsum(
        "qhmd,khmd->hmqk", query_in, key_in, preferred_element_type=jnp.float32
    ) * query_in.shape[-1] ** (-0.5)
    return jnp.where(allowed[None, None], raw_scores, negative)


def attend(query_in, key_in, value_in, allowed, lambda_here):
    scores = attention_scores(query_in, key_in, allowed)
    row_max = jnp.max(scores, axis=-1, keepdims=True)
    log_total = row_max + jnp.log(jnp.sum(jnp.exp(scores - row_max), axis=-1, keepdims=True))
    soft_max = jnp.exp(scores - log_total)
    differ = (soft_max[:, 0] - lambda_here[:, None, None] * soft_max[:, 1]).astype(jnp.bfloat16)
    heads_out = jnp.einsum("hqk,khd->qhd", differ, value_in, preferred_element_type=jnp.float32)
    return (heads_out, log_total)


def attend_back(query_in, key_in, value_in, allowed, lambda_here, log_total, grad_heads):
    scale = query_in.shape[-1] ** (-0.5)
    scores = attention_scores(query_in, key_in, allowed)
    soft_max = jnp.exp(scores - log_total)
    differ = (soft_max[:, 0] - lambda_here[:, None, None] * soft_max[:, 1]).astype(jnp.bfloat16)
    grad_values = jnp.einsum("hqk,qhd->khd", differ, grad_heads, preferred_element_type=jnp.float32)
    grad_differ = jnp.einsum(
        "qhd,khd->hqk", grad_heads, value_in, preferred_element_type=jnp.float32
    )
    grad_soft = jnp.stack([grad_differ, -lambda_here[:, None, None] * grad_differ], axis=1)
    grad_scores = (
        soft_max * (grad_soft - jnp.sum(grad_soft * soft_max, axis=-1, keepdims=True))
    ).astype(jnp.bfloat16)
    grad_query = (
        jnp.einsum("hmqk,khmd->qhmd", grad_scores, key_in, preferred_element_type=jnp.float32)
        * scale
    )
    grad_key = (
        jnp.einsum("hmqk,qhmd->khmd", grad_scores, query_in, preferred_element_type=jnp.float32)
        * scale
    )
    return (grad_query, grad_key, grad_values.astype(jnp.bfloat16))


def per_device(
    tokens,
    cotangent,
    segments,
    adapter_id,
    w_qkv,
    w_out,
    w_gateup,
    w_down,
    gain_attn,
    gain_ffn,
    gain_sub,
    lambda_head,
    a_in,
    b_qkv,
    b_gateup,
    a_out,
    a_down,
    b_rows,
):
    tok_count = lax.axis_size("tok")
    micro_count = tokens.shape[0]
    local_len = tokens.shape[1]
    length = local_len * tok_count
    qw_here = w_qkv.shape[2]
    ff_here = w_gateup.shape[2]
    heads_here = qw_here // VALUE_DIM
    lambda_here = lax.dynamic_slice_in_dim(
        lambda_head, lax.axis_index("tok") * heads_here, heads_here
    )
    positions = jnp.arange(length)

    def prepare(offset):
        attn_set = (
            lax.all_gather(w_qkv, "fsdp", axis=1, tiled=True),
            lax.all_gather(w_out, "fsdp", axis=1, tiled=True),
            lax.all_gather(b_qkv, "fsdp", axis=1, tiled=True),
            lax.all_gather(a_out, "fsdp", axis=1, tiled=True),
        )
        feed_set = (
            lax.all_gather(w_gateup, "fsdp", axis=1, tiled=True),
            lax.all_gather(w_down, "fsdp", axis=1, tiled=True),
            lax.all_gather(b_gateup, "fsdp", axis=1, tiled=True),
            lax.all_gather(a_down, "fsdp", axis=1, tiled=True),
        )
        adapt_set = (
            lax.all_gather(a_in, ("fsdp", "tok"), axis=1, tiled=True),
            lax.all_gather(b_rows, ("fsdp", "tok"), axis=2, tiled=True),
        )

        def select_cols(values, axis_num):
            return lax.dynamic_slice_in_dim(values, offset, RANK, axis_num)

        return {
            "w_qkv": attn_set[0],
            "w_out": attn_set[1],
            "w_gateup": feed_set[0],
            "w_down": feed_set[1],
            "b_qkv": select_cols(attn_set[2], 1),
            "a_out": select_cols(attn_set[3], 1),
            "b_gateup": select_cols(feed_set[2], 1),
            "a_down": select_cols(feed_set[3], 1),
            "a_in": select_cols(adapt_set[0], 2),
            "b_rows": select_cols(adapt_set[1], 1),
        }

    def gather_rows(values):
        return lax.all_gather(values, "tok", axis=0, tiled=True)

    def reduce_rows(row_term):
        return lax.psum_scatter(
            row_term(jnp.int32(0), lax.axis_size("tok") * local_len),
            "tok",
            scatter_dimension=0,
            tiled=True,
        )

    def column_forward(normed_full, weight, down_sel, up_sel):
        lowrank = jnp.dot(normed_full, down_sel, preferred_element_type=jnp.float32)
        linear = jnp.dot(normed_full, weight, preferred_element_type=jnp.float32)
        return (
            linear
            + adapter_scale * jnp.dot(lowrank, up_sel.astype(jnp.float32), precision=highest),
            lowrank,
        )

    def row_forward(inputs_here, weight, down_sel, up_sel):
        lowrank = jnp.dot(inputs_here, down_sel, preferred_element_type=jnp.float32)
        up_float = up_sel.astype(jnp.float32)

        def row_term(first_row, row_count):
            main_part = jnp.dot(inputs_here, weight, preferred_element_type=jnp.float32)
            return main_part + adapter_scale * jnp.dot(lowrank, up_float, precision=highest)

        return (reduce_rows(row_term), lowrank)

    def row_backward(grad_full, inputs_here, weight, down_sel, up_sel, lowrank):
        grad_float = grad_full.astype(jnp.float32)
        grad_low = adapter_scale * jnp.dot(
            grad_float, up_sel.astype(jnp.float32).T, precision=highest
        )
        grad_up = adapter_scale * jnp.dot(lowrank.T, grad_float, precision=highest)
        grad_down = jnp.dot(inputs_here.astype(jnp.float32).T, grad_low, precision=highest)
        grad_inputs = contract_last(grad_full, weight) + jnp.dot(
            grad_low, down_sel.astype(jnp.float32).T, precision=highest
        )
        return (grad_inputs, grad_down, grad_up)

    def column_backward(normed_full, entries):
        normed_float = normed_full.astype(jnp.float32)
        grad_lows = []
        grads_down = []
        grads_up = []
        for grad_rows, weight, down_sel, up_sel, lowrank in entries:
            grad_float = grad_rows.astype(jnp.float32)
            grad_low = adapter_scale * jnp.dot(
                grad_float, up_sel.astype(jnp.float32).T, precision=highest
            )
            grads_up.append(adapter_scale * jnp.dot(lowrank.T, grad_float, precision=highest))
            grads_down.append(jnp.dot(normed_float.T, grad_low, precision=highest))
            grad_lows.append(grad_low)

        def row_term(first_row, row_count):
            running = jnp.zeros((row_count, normed_full.shape[1]), jnp.float32)
            for entry, grad_low in zip(entries, grad_lows):
                row_block = entry[0]
                running = running + contract_last(row_block, entry[1])
                running = running + jnp.dot(
                    grad_low, entry[2].astype(jnp.float32).T, precision=highest
                )
            return running

        return (reduce_rows(row_term), grads_down, grads_up)

    outputs = []
    input_grads = []
    totals = (
        jnp.zeros((5, D, COLS), jnp.float32),
        jnp.zeros((3, COLS, qw_here), jnp.float32),
        jnp.zeros((2, COLS, ff_here), jnp.float32),
        jnp.zeros((qw_here, COLS), jnp.float32),
        jnp.zeros((ff_here, COLS), jnp.float32),
        jnp.zeros((2, COLS, D), jnp.float32),
    )
    shards = None
    for micro_idx in range(micro_count):
        offset = adapter_id[micro_idx] * RANK
        inputs_rows = tokens[micro_idx].astype(jnp.float32)
        segment_row = segments[micro_idx]
        allowed = (segment_row[:, None] == segment_row[None, :]) & (
            positions[:, None] >= positions[None, :]
        )
        forward_set = prepare(offset)
        normed_rows, norm_attn_pull = jax.vjp(
            partial(rows_norm, gain_vector=gain_attn), inputs_rows
        )
        normed_full = gather_rows(normed_rows.astype(jnp.bfloat16))
        query_lin, query_low = column_forward(
            normed_full, forward_set["w_qkv"][0], forward_set["a_in"][0], forward_set["b_qkv"][0]
        )
        key_lin, key_low = column_forward(
            normed_full, forward_set["w_qkv"][1], forward_set["a_in"][1], forward_set["b_qkv"][1]
        )
        value_lin, value_low = column_forward(
            normed_full, forward_set["w_qkv"][2], forward_set["a_in"][2], forward_set["b_qkv"][2]
        )
        rotate = partial(rotary_heads, positions=positions, head_dim=HEAD_DIM)
        query_rot, query_pull = jax.vjp(rotate, query_lin)
        key_rot, key_pull = jax.vjp(rotate, key_lin)
        query_in = query_rot.astype(jnp.bfloat16).reshape(length, heads_here, 2, HEAD_DIM)
        key_in = key_rot.astype(jnp.bfloat16).reshape(length, heads_here, 2, HEAD_DIM)
        value_in = value_lin.astype(jnp.bfloat16).reshape(length, heads_here, VALUE_DIM)
        heads_out, log_total = attend(query_in, key_in, value_in, allowed, lambda_here)
        mixed_float, head_pull = jax.vjp(partial(head_norm, gain_vector=gain_sub), heads_out)
        mixed_rows = mixed_float.reshape(length, qw_here).astype(jnp.bfloat16)
        attn_rows, out_low = row_forward(
            mixed_rows, forward_set["w_out"], forward_set["a_out"], forward_set["b_rows"][0]
        )
        hidden = inputs_rows + attn_rows
        normed_ffn, norm_ffn_pull = jax.vjp(partial(rows_norm, gain_vector=gain_ffn), hidden)
        ffn_full = gather_rows(normed_ffn.astype(jnp.bfloat16))
        gate_lin, gate_low = column_forward(
            ffn_full, forward_set["w_gateup"][0], forward_set["a_in"][3], forward_set["b_gateup"][0]
        )
        up_lin, up_low = column_forward(
            ffn_full, forward_set["w_gateup"][1], forward_set["a_in"][4], forward_set["b_gateup"][1]
        )
        product_float, swiglu_pull = jax.vjp(swiglu, gate_lin, up_lin)
        product = product_float.astype(jnp.bfloat16)
        ffn_rows, down_low = row_forward(
            product, forward_set["w_down"], forward_set["a_down"], forward_set["b_rows"][1]
        )
        outputs.append((hidden + ffn_rows).astype(jnp.bfloat16))
        backward_set = prepare(offset)
        tangent = cotangent[micro_idx].astype(jnp.float32)
        grad_ffn_full = gather_rows(tangent.astype(jnp.bfloat16))
        grad_product, grad_a_down, grad_b_down = row_backward(
            grad_ffn_full,
            product,
            backward_set["w_down"],
            backward_set["a_down"],
            backward_set["b_rows"][1],
            down_low,
        )
        grad_gate, grad_up = swiglu_pull(grad_product)
        grad_ffn_rows, ffn_down_grads, ffn_up_grads = column_backward(
            ffn_full,
            (
                (
                    grad_gate.astype(jnp.bfloat16),
                    backward_set["w_gateup"][0],
                    backward_set["a_in"][3],
                    backward_set["b_gateup"][0],
                    gate_low,
                ),
                (
                    grad_up.astype(jnp.bfloat16),
                    backward_set["w_gateup"][1],
                    backward_set["a_in"][4],
                    backward_set["b_gateup"][1],
                    up_low,
                ),
            ),
        )
        grad_hidden = tangent + norm_ffn_pull(grad_ffn_rows)[0]
        grad_attn_full = gather_rows(grad_hidden.astype(jnp.bfloat16))
        grad_mixed, grad_a_out, grad_b_out = row_backward(
            grad_attn_full,
            mixed_rows,
            backward_set["w_out"],
            backward_set["a_out"],
            backward_set["b_rows"][0],
            out_low,
        )
        grad_heads = head_pull(grad_mixed.reshape(length, heads_here, VALUE_DIM))[0].astype(
            jnp.bfloat16
        )
        grad_query_rot, grad_key_rot, grad_values = attend_back(
            query_in, key_in, value_in, allowed, lambda_here, log_total, grad_heads
        )
        grad_query = query_pull(grad_query_rot.reshape(length, qw_here))[0].astype(jnp.bfloat16)
        grad_key = key_pull(grad_key_rot.reshape(length, qw_here))[0].astype(jnp.bfloat16)
        grad_attn_rows, attn_down_grads, attn_up_grads = column_backward(
            normed_full,
            (
                (
                    grad_query,
                    backward_set["w_qkv"][0],
                    backward_set["a_in"][0],
                    backward_set["b_qkv"][0],
                    query_low,
                ),
                (
                    grad_key,
                    backward_set["w_qkv"][1],
                    backward_set["a_in"][1],
                    backward_set["b_qkv"][1],
                    key_low,
                ),
                (
                    grad_values.reshape(length, qw_here),
                    backward_set["w_qkv"][2],
                    backward_set["a_in"][2],
                    backward_set["b_qkv"][2],
                    value_low,
                ),
            ),
        )
        input_grads.append(grad_hidden + norm_attn_pull(grad_attn_rows)[0])
        pieces = (
            jnp.stack(attn_down_grads + ffn_down_grads),
            jnp.stack(attn_up_grads),
            jnp.stack(ffn_up_grads),
            grad_a_out,
            grad_a_down,
            jnp.stack([grad_b_out, grad_b_down]),
        )
        axes_list = (2, 1, 1, 1, 1, 1)
        updated = []
        for add_running, piece, add_axis_num in zip(totals, pieces, axes_list):
            current = lax.dynamic_slice_in_dim(add_running, offset, RANK, add_axis_num)
            updated.append(
                lax.dynamic_update_slice_in_dim(add_running, current + piece, offset, add_axis_num)
            )
        totals = tuple(updated)
    shards = (
        lax.psum_scatter(totals[0], ("fsdp", "tok"), scatter_dimension=1, tiled=True),
        lax.psum_scatter(
            totals[1].astype(jnp.bfloat16), "fsdp", scatter_dimension=1, tiled=True
        ).astype(jnp.float32),
        lax.psum_scatter(
            totals[2].astype(jnp.bfloat16), "fsdp", scatter_dimension=1, tiled=True
        ).astype(jnp.float32),
        lax.psum_scatter(
            totals[3].astype(jnp.bfloat16), "fsdp", scatter_dimension=1, tiled=True
        ).astype(jnp.float32),
        lax.psum_scatter(
            totals[4].astype(jnp.bfloat16), "fsdp", scatter_dimension=1, tiled=True
        ).astype(jnp.float32),
        lax.psum_scatter(totals[5], ("fsdp", "tok"), scatter_dimension=2, tiled=True),
    )
    return (
        jnp.stack(outputs),
        jnp.stack(input_grads),
        shards[0],
        shards[1],
        shards[2],
        shards[3],
        shards[4],
        shards[5],
    )


def solution(mesh):
    return jax.shard_map(
        per_device,
        mesh=mesh,
        in_specs=(
            P("fsdp", "tok", None),
            P("fsdp", "tok", None),
            P("fsdp", None),
            P("fsdp"),
            P(None, "fsdp", "tok"),
            P("tok", "fsdp"),
            P(None, "fsdp", "tok"),
            P("tok", "fsdp"),
            P(),
            P(),
            P(),
            P(),
            P(None, ("fsdp", "tok"), None),
            P(None, "fsdp", "tok"),
            P(None, "fsdp", "tok"),
            P("tok", "fsdp"),
            P("tok", "fsdp"),
            P(None, None, ("fsdp", "tok")),
        ),
        out_specs=(
            P("fsdp", "tok", None),
            P("fsdp", "tok", None),
            P(None, ("fsdp", "tok"), None),
            P(None, "fsdp", "tok"),
            P(None, "fsdp", "tok"),
            P("tok", "fsdp"),
            P("tok", "fsdp"),
            P(None, None, ("fsdp", "tok")),
        ),
        check_vma=False,
    )
```

profile of v0, /device:TPU:1, one launch (start us, length us, event | category | flops | bytes accessed | tf_op | source)
XLA Modules:
  0.0 2756.5 jit_solution(249588392692920390)
XLA Ops:
  16.4 71.8 %all_gather.39 = bf16[3,128,512]{2,0,1:T(4,128)(2,1)S(1)} all-gather(bf16[3,4,512]{2,0,1:T(4,128)(2,1)S(1)} %copy.108), channel_id=1, replica_groups=mesh['fsdp'=32,'tok'=4] {'fsdp'}, dimensions={1}, use_global_device_ids=true | all-gather | bytes 405504 | tf_op jit(solution)/shard_map/all_gather | solution.py:141
  89.7 62.5 %all-gather.2 = bf16[32,4,512]{2,1,0:T(4,128)(2,1)S(1)} all-gather(bf16[1,4,512]{2,1,0:T(4,128)(2,1)S(1)} %bitcast.613), channel_id=1, replica_groups=mesh['fsdp'=32,'tok'=4] {'fsdp'}, dimensions={0}, use_global_device_ids=true | all-gather | bytes 135168 | tf_op jit(solution)/shard_map/all_gather | solution.py:142
  154.3 84.8 %all-gather.23.cloned.1.call-done = bf16[5,2048,128]{2,1,0:T(8,128)(2,1)} async-done(((bf16[5,16,128]{2,1,0:T(8,128)(2,1)}), bf16[5,2048,128]{2,1,0:T(8,128)(2,1)}) %all-gather.23.cloned.1.call-update) | async-done | bytes 2621456 | tf_op jit(solution)/shard_map/all_gather | solution.py:151
  243.0 17.1 all-gather.19.cloned.1.call-done
  272.9 131.6 %all-gather.21.cloned.1.call-done = bf16[3,2048,512]{2,1,0:T(8,128)(2,1)} async-done(((bf16[3,64,512]{2,1,0:T(8,128)(2,1)}), bf16[3,2048,512]{2,1,0:T(8,128)(2,1)}) %all-gather.21.cloned.1.call-update) | async-done | bytes 6291472 | tf_op jit(solution)/shard_map/all_gather | solution.py:139
  404.5 3.4 fusion.62
  409.2 3.5 fusion.59
  414.7 3.5 fusion.60
  420.2 3.5 fusion.61
  425.7 3.6 subtract_convert_fusion.1
  438.5 182.2 %all-gather.27.cloned.1.call-done = bf16[2,128,2048]{1,2,0:T(8,128)(2,1)} async-done(((bf16[2,128,16]{1,2,0:T(8,128)(2,1)}), bf16[2,128,2048]{1,2,0:T(8,128)(2,1)}) %all-gather.27.cloned.1.call-update) | async-done | bytes 1048592 | tf_op jit(solution)/shard_map/all_gather | solution.py:152
  620.7 3.6 convolution_multiply_fusion.7
  624.4 128.2 %all-gather.25.cloned.1.call-done = bf16[512,2048]{0,1:T(8,128)(2,1)} async-done(((bf16[512,64]{0,1:T(8,128)(2,1)}), bf16[512,2048]{0,1:T(8,128)(2,1)}) %all-gather.25.cloned.1.call-update) | async-done | bytes 2097168 | tf_op jit(solution)/shard_map/all_gather | solution.py:140
  752.5 4.3 convolution_add_fusion.9
  765.1 50.9 %reduce-scatter.12.cloned.1.call-done = f32[64,2048]{1,0:T(8,128)} async-done(((f32[256,2048]{1,0:T(8,128)}), f32[64,2048]{1,0:T(8,128)}) %reduce-scatter.12.cloned.1.call-update) | async-done | bytes 524304 | tf_op jit(solution)/shard_map/reduce_scatter | solution.py:175
  816.0 40.5 %reduce-scatter.16.cloned.1.call-done = f32[64,2048]{1,0:T(8,128)} async-done(((f32[256,2048]{1,0:T(8,128)}), f32[64,2048]{1,0:T(8,128)}) %reduce-scatter.16.cloned.1.call-update) | async-done | bytes 524304 | tf_op jit(solution)/shard_map/reduce_scatter | solution.py:175
  862.1 68.9 %all-gather.3 = bf16[32,4,1408]{2,1,0:T(4,128)(2,1)S(1)} all-gather(bf16[1,4,1408]{2,1,0:T(4,128)(2,1)} %bitcast.610), channel_id=1, replica_groups=mesh['fsdp'=32,'tok'=4] {'fsdp'}, dimensions={0}, use_global_device_ids=true | all-gather | bytes 371712 | tf_op jit(solution)/shard_map/all_gather | solution.py:148
  931.9 70.9 %all_gather.45 = bf16[2,128,1408]{2,0,1:T(2,128)(2,1)S(1)} all-gather(bf16[2,4,1408]{2,0,1:T(2,128)(2,1)S(1)} %copy.118), channel_id=1, replica_groups=mesh['fsdp'=32,'tok'=4] {'fsdp'}, dimensions={1}, use_global_device_ids=true | all-gather | bytes 743424 | tf_op jit(solution)/shard_map/all_gather | solution.py:147
  1007.8 38.3 %all-gather.33.cloned.1.call-done = bf16[1408,2048]{0,1:T(8,128)(2,1)} async-done(((bf16[1408,64]{0,1:T(8,128)(2,1)}), bf16[1408,2048]{0,1:T(8,128)(2,1)}) %all-gather.33.cloned.1.call-update) | async-done | bytes 5767184 | tf_op jit(solution)/shard_map/all_gather | solution.py:146
  1046.1 4.9 fusion.80
  1056.8 30.1 %all-gather.29.cloned.1.call-done = bf16[256,2048]{1,0:T(8,128)(2,1)} async-done(((bf16[64,2048]{1,0:T(8,128)(2,1)}), bf16[256,2048]{1,0:T(8,128)(2,1)}) %all-gather.29.cloned.1.call-update) | async-done | bytes 1048592 | tf_op jit(solution)/shard_map/all_gather | solution.py:172
  1090.1 18.6 all-gather.37.cloned.1.call-done
  1112.5 153.7 %all-gather.31.cloned.1.call-done = bf16[2,2048,1408]{2,1,0:T(8,128)(2,1)} async-done(((bf16[2,64,1408]{2,1,0:T(8,128)(2,1)}), bf16[2,2048,1408]{2,1,0:T(8,128)(2,1)}) %all-gather.31.cloned.1.call-update) | async-done | bytes 11534352 | tf_op jit(solution)/shard_map/all_gather | solution.py:145
  1266.2 4.9 fusion.8
  1285.9 4.8 fusion.7
  1292.0 4.6 fusion.3
  1309.3 5.2 fusion.238
  1318.7 4.8 fusion.237
  1326.3 14.3 reduce-scatter.20.cloned.1.call-done
  1340.6 40.4 %reduce-scatter.24.cloned.1.call-done = f32[64,2048]{1,0:T(8,128)} async-done(((f32[256,2048]{1,0:T(8,128)}), f32[64,2048]{1,0:T(8,128)}) %reduce-scatter.24.cloned.1.call-update) | async-done | bytes 524304 | tf_op jit(solution)/shard_map/reduce_scatter | solution.py:175
  1382.9 38.3 %reduce-scatter.18.cloned.1.call-done = f32[64,2048]{1,0:T(8,128)} async-done(((f32[256,2048]{1,0:T(8,128)}), f32[64,2048]{1,0:T(8,128)}) %reduce-scatter.18.cloned.1.call-update) | async-done | bytes 524304 | tf_op jit(solution)/shard_map/reduce_scatter | solution.py:175
  1421.2 40.4 %reduce-scatter.14.cloned.1.call-done = f32[64,2048]{1,0:T(8,128)} async-done(((f32[256,2048]{1,0:T(8,128)}), f32[64,2048]{1,0:T(8,128)}) %reduce-scatter.14.cloned.1.call-update) | async-done | bytes 524304 | tf_op jit(solution)/shard_map/reduce_scatter | solution.py:175
  1461.6 3.6 fusion.224
  1478.5 7.4 all-gather.39.cloned.1.call-done
  1489.2 2.7 convolution_add_fusion.16
  1494.0 13.5 all-gather.41.cloned.1.call-done
  1510.8 2.7 convolution_add_fusion.15
  1550.1 3.2 multiply_add_fusion.7
  1563.6 4.2 copy.152
  1581.9 3.8 fusion.15
  1597.7 3.8 fusion.13
  1605.4 2.9 broadcast_in_dim.59
  1613.9 7.9 copy.151
  1624.6 92.5 %all-reduce.17.cloned.1.call-done = f32[2,128,2048]{1,0,2:T(2,128)} async-done(((f32[2,128,2048]{1,0,2:T(2,128)}), f32[2,128,2048]{1,0,2:T(2,128)}) %all-reduce.17.cloned.1.call-update) | async-done | bytes 2097168
  1718.4 285.3 %all-reduce.19.cloned.1.call-done = (bf16[3,128,512]{2,1,0:T(8,128)(2,1)}, bf16[2,128,1408]{2,1,0:T(8,128)(2,1)}, bf16[512,128]{0,1:T(8,128)(2,1)}, bf16[1408,128]{0,1:T(8,128)(2,1)}) async-done(((bf16[3,128,512]{2,1,0:T(8,128)(2,1)}, bf16[2,128,1408]{2,1,0:T(8,128)(2,1)}, bf16[512,128]{0,1:T(8,128)(2,1)}, bf16[1408,128]{0,1:T(8,128)(2,1)}), (bf16[3,128,512]{2,1,0:T(8,128)(2,1)}, ...) | async-done | bytes 1605648
  2009.2 53.9 %reduce-scatter.22.cloned.1.call-done = f32[64,2048]{1,0:T(8,128)} async-done(((f32[256,2048]{1,0:T(8,128)}), f32[64,2048]{1,0:T(8,128)}) %reduce-scatter.22.cloned.1.call-update) | async-done | bytes 524304 | tf_op jit(solution)/shard_map/reduce_scatter | solution.py:175
  2063.1 40.2 %reduce-scatter.26.cloned.1.call-done = f32[64,2048]{1,0:T(8,128)} async-done(((f32[256,2048]{1,0:T(8,128)}), f32[64,2048]{1,0:T(8,128)}) %reduce-scatter.26.cloned.1.call-update) | async-done | bytes 524304 | tf_op jit(solution)/shard_map/reduce_scatter | solution.py:175
  2107.3 641.0 %reduce-scatter.28.cloned.1.call-done = f32[5,16,128]{2,0,1:T(8,128)} async-done(((f32[5,2048,128]{2,0,1:T(8,128)}), f32[5,16,128]{2,0,1:T(8,128)}) %reduce-scatter.28.cloned.1.call-update) | async-done | bytes 40976 | tf_op jit(solution)/shard_map/reduce_scatter | solution.py:391
  (642 shorter events, 230.8 us)
Async XLA Ops:
  7.2 145.6 %copy-start.178 = (f32[8]{0:T(128)S(1)}, f32[8]{0:T(128)}, u32[]{:S(2)}) copy-start(f32[8]{0:T(128)} %param.29) | copy-start | bytes 100
  7.2 147.1 %all-gather.35.cloned.1.call-start = ((), (), s32[]{:S(2)}) async-start(), calls=%async_computation.19 | async-start | bytes 1310720 | tf_op jit(solution)/shard_map/all_gather | solution.py:172
  11.1 227.9 %all-gather.23.cloned.1.call-start = ((), (), s32[]{:S(2)}) async-start(), calls=%async_computation.11 | async-start | bytes 2641920 | tf_op jit(solution)/shard_map/all_gather | solution.py:151
  11.9 248.2 %all-gather.19.cloned.1.call-start = ((), (), s32[]{:S(2)}) async-start(), calls=%async_computation.9 | async-start | bytes 1310720 | tf_op jit(solution)/shard_map/all_gather | solution.py:172
  12.6 391.9 %all-gather.21.cloned.1.call-start = ((), (), s32[]{:S(2)}) async-start(), calls=%async_computation.10 | async-start | bytes 6488064 | tf_op jit(solution)/shard_map/all_gather | solution.py:139
  13.2 607.5 %all-gather.27.cloned.1.call-start = ((), (), s32[]{:S(2)}) async-start(), calls=%async_computation.13 | async-start | bytes 1056768 | tf_op jit(solution)/shard_map/all_gather | solution.py:152
  13.8 738.7 %all-gather.25.cloned.1.call-start = ((), (), s32[]{:S(2)}) async-start(), calls=%async_computation.12 | async-start | bytes 2162688 | tf_op jit(solution)/shard_map/all_gather | solution.py:140
  14.4 801.6 %reduce-scatter.12.cloned.1.call-start = ((), (), s32[]{:S(2)}) async-start(), calls=%async_computation.14 | async-start | bytes 2621440 | tf_op jit(solution)/shard_map/reduce_scatter | solution.py:175
  152.2 604.7 %copy-start.85 = (bf16[128,512]{1,0:T(8,128)(2,1)}, bf16[128,512]{1,0:T(8,128)(2,1)S(1)}, u32[]{:S(2)}) copy-start(bf16[128,512]{1,0:T(8,128)(2,1)S(1)} %reshape.369) | copy-start | bytes 393220
  152.8 272.9 %copy-start.65 = (f32[256,64]{1,0:T(8,128)}, f32[256,64]{1,0:T(8,128)S(1)}, u32[]{:S(2)}) copy-start(f32[256,64]{1,0:T(8,128)S(1)} %get-tuple-element.118) | copy-start | bytes 196612
  152.8 272.9 %copy-start.67 = (f32[256,64]{1,0:T(8,128)}, f32[256,64]{1,0:T(8,128)S(1)}, u32[]{:S(2)}) copy-start(f32[256,64]{1,0:T(8,128)S(1)} %get-tuple-element.119) | copy-start | bytes 196612
  437.5 186.8 %copy-start.153 = (f32[256,2]{0,1:T(2,128)}, f32[256,2]{0,1:T(2,128)S(1)}, u32[]{:S(2)}) copy-start(f32[256,2]{0,1:T(2,128)S(1)} %get-tuple-element.136) | copy-start | bytes 6148
  437.6 186.8 %copy-start.149 = (f32[256,2]{0,1:T(2,128)}, f32[256,2]{0,1:T(2,128)S(1)}, u32[]{:S(2)}) copy-start(f32[256,2]{0,1:T(2,128)S(1)} %fusion.216) | copy-start | bytes 6148
  438.3 318.5 %copy-start.38 = (bf16[256,2,256]{0,2,1:T(8,128)(2,1)}, bf16[256,2,256]{0,2,1:T(8,128)(2,1)S(1)}, u32[]{:S(2)}) copy-start(bf16[256,2,256]{0,2,1:T(8,128)(2,1)S(1)} %get-tuple-element.123) | copy-start | bytes 786436
  438.3 321.2 %copy-start.36 = (bf16[256,2,256]{0,2,1:T(8,128)(2,1)}, bf16[256,2,256]{0,2,1:T(8,128)(2,1)S(1)}, u32[]{:S(2)}) copy-start(bf16[256,2,256]{0,2,1:T(8,128)(2,1)S(1)} %get-tuple-element.122) | copy-start | bytes 786436
  756.9 99.6 %reduce-scatter.16.cloned.1.call-start = ((), (), s32[]{:S(2)}) async-start(), calls=%async_computation.20 | async-start | bytes 2621440 | tf_op jit(solution)/shard_map/reduce_scatter | solution.py:175
  761.7 94.8 %copy-start.10 = (bf16[2,64,2048]{2,1,0:T(8,128)(2,1)S(1)}, bf16[2,64,2048]{2,1,0:T(8,128)(2,1)}, u32[]{:S(2)}) copy-start(bf16[2,64,2048]{2,1,0:T(8,128)(2,1)} %param.18) | copy-start | bytes 1572868
  761.7 96.8 %copy-start.128 = (f32[2048]{0:T(1024)S(1)}, f32[2048]{0:T(1024)}, u32[]{:S(2)}) copy-start(f32[2048]{0:T(1024)} %param.27) | copy-start | bytes 24580
  761.7 242.1 %all-gather.43.cloned.1.call-start = ((), (), s32[]{:S(2)}) async-start(), calls=%async_computation.30 | async-start | bytes 1310720 | tf_op jit(solution)/shard_map/all_gather | solution.py:172
  763.7 242.1 %all-gather.45.cloned.1.call-start = ((), (), s32[]{:S(2)}) async-start(), calls=%async_computation.31 | async-start | bytes 1310720 | tf_op jit(solution)/shard_map/all_gather | solution.py:172
  764.3 281.8 %all-gather.33.cloned.1.call-start = ((), (), s32[]{:S(2)}) async-start(), calls=%async_computation.17 | async-start | bytes 5947392 | tf_op jit(solution)/shard_map/all_gather | solution.py:146
  765.0 321.9 %all-gather.29.cloned.1.call-start = ((), (), s32[]{:S(2)}) async-start(), calls=%async_computation.15 | async-start | bytes 1310720 | tf_op jit(solution)/shard_map/all_gather | solution.py:172
  858.5 144.3 %copy-start.170 = (f32[64]{0:T(128)}, f32[64]{0:T(128)S(1)}, u32[]{:S(2)}) copy-start(f32[64]{0:T(128)S(1)} %fusion.219) | copy-start | bytes 772
  858.5 144.3 %copy-start.172 = (f32[64]{0:T(128)}, f32[64]{0:T(128)S(1)}, u32[]{:S(2)}) copy-start(f32[64]{0:T(128)S(1)} %fusion.221) | copy-start | bytes 772
  860.8 248.0 %all-gather.37.cloned.1.call-start = ((), (), s32[]{:S(2)}) async-start(), calls=%async_computation.21 | async-start | bytes 1310720 | tf_op jit(solution)/shard_map/all_gather | solution.py:172
  861.5 404.7 %all-gather.31.cloned.1.call-start = ((), (), s32[]{:S(2)}) async-start(), calls=%async_computation.16 | async-start | bytes 11894784 | tf_op jit(solution)/shard_map/all_gather | solution.py:145
  862.1 478.5 %reduce-scatter.20.cloned.1.call-start = ((), (), s32[]{:S(2)}) async-start(), calls=%async_computation.23 | async-start | bytes 2621440 | tf_op jit(solution)/shard_map/reduce_scatter | solution.py:175
  1088.8 182.3 %copy-start.97 = (f32[256,16]{0,1:T(8,128)}, f32[256,16]{0,1:T(8,128)S(1)}, u32[]{:S(2)}) copy-start(f32[256,16]{0,1:T(8,128)S(1)} %fusion.116) | copy-start | bytes 49156
  1285.9 95.1 %reduce-scatter.24.cloned.1.call-start = ((), (), s32[]{:S(2)}) async-start(), calls=%async_computation.26 | async-start | bytes 2621440 | tf_op jit(solution)/shard_map/reduce_scatter | solution.py:175
  1307.6 113.6 %reduce-scatter.18.cloned.1.call-start = ((), (), s32[]{:S(2)}) async-start(), calls=%async_computation.22 | async-start | bytes 2621440 | tf_op jit(solution)/shard_map/reduce_scatter | solution.py:175
  1317.2 144.4 %reduce-scatter.14.cloned.1.call-start = ((), (), s32[]{:S(2)}) async-start(), calls=%async_computation.18 | async-start | bytes 2621440 | tf_op jit(solution)/shard_map/reduce_scatter | solution.py:175
  1326.2 135.4 %copy-start.171 = (f32[64]{0:T(128)S(1)}, f32[64]{0:T(128)}, u32[]{:S(2)}) copy-start(f32[64]{0:T(128)} %copy-done.170) | copy-start | bytes 772
  1326.2 135.4 %copy-start.173 = (f32[64]{0:T(128)S(1)}, f32[64]{0:T(128)}, u32[]{:S(2)}) copy-start(f32[64]{0:T(128)} %copy-done.172) | copy-start | bytes 772
  1326.2 159.7 %all-gather.39.cloned.1.call-start = ((), (), s32[]{:S(2)}) async-start(), calls=%async_computation.24 | async-start | bytes 1310720 | tf_op jit(solution)/shard_map/all_gather | solution.py:172
  1382.9 85.5 %copy-start.100 = (f32[256,16]{0,1:T(8,128)S(1)}, f32[256,16]{0,1:T(8,128)}, u32[]{:S(2)}) copy-start(f32[256,16]{0,1:T(8,128)} %fusion.122) | copy-start | bytes 49156
  1465.2 42.3 %all-gather.41.cloned.1.call-start = ((), (), s32[]{:S(2)}) async-start(), calls=%async_computation.27 | async-start | bytes 1310720 | tf_op jit(solution)/shard_map/all_gather | solution.py:172
  1471.5 245.6 %all-reduce.17.cloned.1.call-start = ((), (), s32[]{:S(2)}) async-start(), calls=%async_computation.32 | async-start | bytes 4194304
  1567.8 436.0 %all-reduce.19.cloned.1.call-start = ((), (), s32[]{:S(2)}) async-start(), calls=%async_computation.33 | async-start | bytes 3211264
  1573.1 490.0 %reduce-scatter.22.cloned.1.call-start = ((), (), s32[]{:S(2)}) async-start(), calls=%async_computation.25 | async-start | bytes 2621440 | tf_op jit(solution)/shard_map/reduce_scatter | solution.py:175
  1585.8 517.5 %reduce-scatter.26.cloned.1.call-start = ((), (), s32[]{:S(2)}) async-start(), calls=%async_computation.28 | async-start | bytes 2621440 | tf_op jit(solution)/shard_map/reduce_scatter | solution.py:175
  1601.6 1146.8 %reduce-scatter.28.cloned.1.call-start = ((), (), s32[]{:S(2)}) async-start(), calls=%async_computation.29 | async-start | bytes 8454144 | tf_op jit(solution)/shard_map/reduce_scatter | solution.py:391
  1621.8 481.4 %copy-start.130 = (f32[2048]{0:T(1024)S(1)}, f32[2048]{0:T(1024)}, u32[]{:S(2)}) copy-start(f32[2048]{0:T(1024)} %param.26) | copy-start | bytes 24580
  1621.9 482.8 %copy-start.167 = (f32[64]{0:T(128)S(1)}, f32[64]{0:T(128)}, u32[]{:S(2)}) copy-start(f32[64]{0:T(128)} %copy-done.166) | copy-start | bytes 772
  1621.9 482.8 %copy-start.169 = (f32[64]{0:T(128)S(1)}, f32[64]{0:T(128)}, u32[]{:S(2)}) copy-start(f32[64]{0:T(128)} %copy-done.168) | copy-start | bytes 772
  1621.9 482.9 %copy-start.61 = (f32[64,2048]{1,0:T(8,128)S(1)}, f32[64,2048]{1,0:T(8,128)}, u32[]{:S(2)}) copy-start(f32[64,2048]{1,0:T(8,128)} %get-tuple-element.49) | copy-start | bytes 1572868
  1621.9 482.9 %copy-start.62 = (f32[64,2048]{1,0:T(8,128)S(1)}, f32[64,2048]{1,0:T(8,128)}, u32[]{:S(2)}) copy-start(f32[64,2048]{1,0:T(8,128)} %get-tuple-element.67) | copy-start | bytes 1572868
  1621.9 482.9 %copy-start.160 = (f32[64]{0:T(128)S(1)}, f32[64]{0:T(128)}, u32[]{:S(2)}) copy-start(f32[64]{0:T(128)} %copy-done.159) | copy-start | bytes 772
  1621.9 482.9 %copy-start.162 = (f32[64]{0:T(128)S(1)}, f32[64]{0:T(128)}, u32[]{:S(2)}) copy-start(f32[64]{0:T(128)} %copy-done.161) | copy-start | bytes 772
  (164 other events, 1221.1 us)
Sparse Core Ops, SparseCore 0:
  11.3 25.0 all-gather.34
  38.0 201.0 all-gather.22
  241.3 18.7 all-gather.18
  261.6 142.8 all-gather.20
  406.0 214.6 all-gather.26
  622.2 130.2 all-gather.24
  757.0 58.9 reduce-scatter.11
  818.8 37.6 reduce-scatter.15
  858.2 20.8 all-gather.42
  880.6 19.9 all-gather.44
  902.2 143.8 all-gather.32
  1047.6 39.2 all-gather.28
  1088.6 20.1 all-gather.36
  1110.2 155.9 all-gather.30
  1286.0 54.5 reduce-scatter.19
  1343.3 37.6 reduce-scatter.23
  1383.5 37.6 reduce-scatter.17
  1423.9 37.6 reduce-scatter.13
  1465.4 20.5 all-gather.38
  1487.4 20.0 all-gather.40
  1567.9 149.1 all-reduce.16
  1720.4 283.2 all-reduce.18
  2006.6 56.4 reduce-scatter.21
  2065.6 37.6 reduce-scatter.25
  2105.7 642.5 reduce-scatter.27
where the time goes:
time: 2770 us; the launch traced here: 2760 us
  waiting for transfers between devices  2150 us (78%)
  blocking collectives  274 us (10%)
  matrix products  191 us (7%)
  local copies, waits for them, and re-layouts  73.6 us (3%)
  other arithmetic  48.2 us (2%)
    reduce_scatter x1, waiting for transfers between devices, per_device(): lax.psum_scatter(totals[0], ('fsdp', 'tok'), scatter_dimension=1, tiled=T...  641 us
    unnamed x27, waiting for transfers between devices  384 us
    reduce_scatter x8, waiting for transfers between devices, reduce_rows(): lax.psum_scatter(row_term(jnp.int32(0), lax.axis_size('tok') * local_len)...  319 us
    all_gather x1, waiting for transfers between devices, prepare(): lax.all_gather(b_rows, ('fsdp', 'tok'), axis=2, tiled=True)  182 us
    all_gather x1, waiting for transfers between devices, prepare(): lax.all_gather(w_gateup, 'fsdp', axis=1, tiled=True)  154 us
    all_gather x1, waiting for transfers between devices, prepare(): lax.all_gather(w_qkv, 'fsdp', axis=1, tiled=True)  132 us
    all_gather x1, waiting for transfers between devices, prepare(): lax.all_gather(w_out, 'fsdp', axis=1, tiled=True)  128 us
    all_gather x8, waiting for transfers between devices, gather_rows(): return lax.all_gather(values, 'tok', axis=0, tiled=True)  86.9 us
  transfers between devices with their start and end apart: 25, of which 22 were waited for; matrix products, arithmetic and copies ran while one was open for 8% of the time, Pallas kernels for 0%

commit v1 on v0

v1 whole, which is shorter than its diff:
```python
from functools import partial

import jax
import jax.numpy as jnp
from jax import lax
from jax.sharding import PartitionSpec as P

D = 2048
HEAD_DIM = 128
VALUE_DIM = 256
RANK = 16
COLS = 128


highest = lax.Precision.HIGHEST
negative = -1e30
adapter_scale = 2.0
lambda_init = 0.2
rotary_base = 10000.0
row_epsilon = 1e-06
head_epsilon = 1e-05


def rows_norm(values, gain_vector):
    return (
        values
        * lax.rsqrt(jnp.mean(values * values, axis=-1, keepdims=True) + row_epsilon)
        * gain_vector
    )


def head_norm(values, gain_vector):
    scaled = values * lax.rsqrt(jnp.mean(values * values, axis=-1, keepdims=True) + head_epsilon)
    return scaled * gain_vector * (1.0 - lambda_init)


def rotary_heads(values, positions, head_dim):
    lead = values.shape[:-1]
    groups = values.reshape(lead + (-1, head_dim))
    half_dim = head_dim // 2
    frequency = rotary_base ** (-jnp.arange(half_dim, dtype=jnp.float32) / half_dim)
    angles = positions.astype(jnp.float32)[:, None] * frequency[None, :]
    cosine = jnp.cos(angles)[:, None, :]
    sine_part = jnp.sin(angles)[:, None, :]
    first_half = groups[..., :half_dim]
    second = groups[..., half_dim:]
    turned = jnp.concatenate(
        [first_half * cosine - second * sine_part, second * cosine + first_half * sine_part],
        axis=-1,
    )
    return turned.reshape(values.shape)


def swiglu(gate_rows, up_rows):
    return gate_rows * jax.nn.sigmoid(gate_rows) * up_rows


def attention_scores(query_in, key_in, allowed):
    raw_scores = jnp.einsum(
        "qhmd,khmd->hmqk", query_in, key_in, preferred_element_type=jnp.float32
    ) * query_in.shape[-1] ** (-0.5)
    return jnp.where(allowed[None, None], raw_scores, negative)


def attend(query_in, key_in, value_in, allowed, lambda_here):
    scores = attention_scores(query_in, key_in, allowed)
    row_max = jnp.max(scores, axis=-1, keepdims=True)
    log_total = row_max + jnp.log(jnp.sum(jnp.exp(scores - row_max), axis=-1, keepdims=True))
    soft_max = jnp.exp(scores - log_total)
    differ = (soft_max[:, 0] - lambda_here[:, None, None] * soft_max[:, 1]).astype(jnp.bfloat16)
    heads_out = jnp.einsum("hqk,khd->qhd", differ, value_in, preferred_element_type=jnp.float32)
    return (heads_out, log_total)


def attend_back(query_in, key_in, value_in, allowed, lambda_here, log_total, grad_heads):
    scale = query_in.shape[-1] ** (-0.5)
    scores = attention_scores(query_in, key_in, allowed)
    soft_max = jnp.exp(scores - log_total)
    differ = (soft_max[:, 0] - lambda_here[:, None, None] * soft_max[:, 1]).astype(jnp.bfloat16)
    grad_values = jnp.einsum("hqk,qhd->khd", differ, grad_heads, preferred_element_type=jnp.float32)
    grad_differ = jnp.einsum(
        "qhd,khd->hqk", grad_heads, value_in, preferred_element_type=jnp.float32
    )
    grad_soft = jnp.stack([grad_differ, -lambda_here[:, None, None] * grad_differ], axis=1)
    grad_scores = (
        soft_max * (grad_soft - jnp.sum(grad_soft * soft_max, axis=-1, keepdims=True))
    ).astype(jnp.bfloat16)
    grad_query = (
        jnp.einsum("hmqk,khmd->qhmd", grad_scores, key_in, preferred_element_type=jnp.float32)
        * scale
    )
    grad_key = (
        jnp.einsum("hmqk,qhmd->khmd", grad_scores, query_in, preferred_element_type=jnp.float32)
        * scale
    )
    return (grad_query, grad_key, grad_values.astype(jnp.bfloat16))


def xor_pairs(count, bit):
    return [(i, i ^ bit) for i in range(count)]


def tok_gather(values):
    count = lax.axis_size("tok")
    me = lax.axis_index("tok")
    far = lax.ppermute(values, "tok", xor_pairs(count, 2))
    pair = jnp.where((me & 2) == 0, jnp.stack([values, far]), jnp.stack([far, values]))
    near = lax.ppermute(pair, "tok", xor_pairs(count, 1))
    full = jnp.where((me & 1) == 0, jnp.stack([pair, near], 1), jnp.stack([near, pair], 1))
    return full.reshape((count,) + values.shape)


def tok_scatter(blocks):
    count = lax.axis_size("tok")
    me = lax.axis_index("tok")
    core = me & 1
    half = (me >> 1) & 1
    split = blocks.reshape((2, 2) + blocks.shape[1:])
    mine = lax.dynamic_index_in_dim(split, core, 1, keepdims=False)
    theirs = lax.dynamic_index_in_dim(split, 1 - core, 1, keepdims=False)
    chip_sum = mine + lax.ppermute(theirs, "tok", xor_pairs(count, 1))
    keep = lax.dynamic_index_in_dim(chip_sum, half, 0, keepdims=False)
    send = lax.dynamic_index_in_dim(chip_sum, 1 - half, 0, keepdims=False)
    return keep + lax.ppermute(send, "tok", xor_pairs(count, 2))


def tok_sum(values):
    count = lax.axis_size("tok")
    chip_sum = values + lax.ppermute(values, "tok", xor_pairs(count, 1))
    return chip_sum + lax.ppermute(chip_sum, "tok", xor_pairs(count, 2))


def hp_dot(left, right, spec):
    return jnp.einsum(spec, left, right, precision=highest, preferred_element_type=jnp.float32)


def per_device(
    tokens,
    cotangent,
    segments,
    adapter_id,
    w_qkv,
    w_out,
    w_gateup,
    w_down,
    gain_attn,
    gain_ffn,
    gain_sub,
    lambda_head,
    a_in,
    b_qkv,
    b_gateup,
    a_out,
    a_down,
    b_rows,
):
    tok_count = lax.axis_size("tok")
    fsdp_count = lax.axis_size("fsdp")
    me_tok = lax.axis_index("tok")
    seqs, local_len, _ = tokens.shape
    length = local_len * tok_count
    qw_here = w_qkv.shape[2]
    ff_here = w_gateup.shape[2]
    heads_here = qw_here // VALUE_DIM
    lambda_here = lax.dynamic_slice_in_dim(lambda_head, me_tok * heads_here, heads_here)
    positions = jnp.arange(length)
    offsets = adapter_id * RANK
    fsdp_rows = w_qkv.shape[1]
    groups_per_adapter = RANK // b_qkv.shape[1]

    a_in_tok = tok_gather(a_in)
    b_rows_tok = tok_gather(b_rows)
    pieces = [w_qkv, w_out, w_gateup, w_down, b_qkv, b_gateup, a_out, a_down, a_in_tok, b_rows_tok]
    flat = jnp.concatenate([p.reshape(-1) for p in pieces])
    gathered = lax.all_gather(flat, "fsdp", axis=0, tiled=False)
    unpacked = []
    start = 0
    for p in pieces:
        size = p.size
        unpacked.append(gathered[:, start : start + size].reshape((fsdp_count,) + p.shape))
        start += size
    (g_qkv, g_out, g_gateup, g_down, g_bqkv, g_bgateup, g_aout, g_adown, g_ain, g_brows) = unpacked
    w_qkv_full = jnp.moveaxis(g_qkv, 0, 1).reshape(3, fsdp_count * fsdp_rows, qw_here)
    w_out_full = jnp.moveaxis(g_out, 0, 1).reshape(qw_here, fsdp_count * fsdp_rows)
    w_gateup_full = jnp.moveaxis(g_gateup, 0, 1).reshape(2, fsdp_count * fsdp_rows, ff_here)
    w_down_full = jnp.moveaxis(g_down, 0, 1).reshape(ff_here, fsdp_count * fsdp_rows)
    a_in_full = jnp.transpose(g_ain, (2, 0, 1, 3, 4)).reshape(5, D, COLS)
    b_rows_full = jnp.transpose(g_brows, (2, 3, 0, 1, 4)).reshape(2, COLS, D)

    def pick_cols(values, axis):
        return jnp.stack(
            [lax.dynamic_slice_in_dim(values, offsets[s], RANK, axis) for s in range(seqs)]
        )

    def pick_groups(values):
        return jnp.stack(
            [
                lax.dynamic_slice_in_dim(values, adapter_id[s] * groups_per_adapter, groups_per_adapter, 0)
                for s in range(seqs)
            ]
        )

    a_in_sel = pick_cols(a_in_full, 2)
    b_rows_sel = pick_cols(b_rows_full, 1)
    b_qkv_sel = jnp.moveaxis(pick_groups(g_bqkv), 1, 2).reshape(seqs, 3, RANK, qw_here)
    b_gateup_sel = jnp.moveaxis(pick_groups(g_bgateup), 1, 2).reshape(seqs, 2, RANK, ff_here)
    a_out_sel = jnp.moveaxis(pick_groups(g_aout), 1, 2).reshape(seqs, qw_here, RANK)
    a_down_sel = jnp.moveaxis(pick_groups(g_adown), 1, 2).reshape(seqs, ff_here, RANK)

    def gather_rows(values):
        full = tok_gather(values)
        return jnp.moveaxis(full, 0, 1).reshape(seqs, length, values.shape[-1])

    def scatter_rows(values):
        blocks = jnp.moveaxis(values.reshape(seqs, tok_count, local_len, values.shape[-1]), 1, 0)
        return tok_scatter(blocks)

    def column_forward(rows_full, weight, down_sel, up_sel):
        lowrank = jnp.einsum("std,sdr->str", rows_full, down_sel, preferred_element_type=jnp.float32)
        linear = jnp.einsum("std,de->ste", rows_full, weight, preferred_element_type=jnp.float32)
        return linear + adapter_scale * hp_dot(lowrank, up_sel.astype(jnp.float32), "str,sre->ste"), lowrank

    def row_forward(rows_here, weight, down_sel, up_sel):
        lowrank = jnp.einsum("std,sdr->str", rows_here, down_sel, preferred_element_type=jnp.float32)
        main_part = jnp.einsum("std,de->ste", rows_here, weight, preferred_element_type=jnp.float32)
        total = main_part + adapter_scale * hp_dot(lowrank, up_sel.astype(jnp.float32), "str,sre->ste")
        return scatter_rows(total), lowrank

    inputs_rows = tokens.astype(jnp.float32)
    allowed = (segments[:, :, None] == segments[:, None, :]) & (
        positions[:, None] >= positions[None, :]
    )[None]
    grad_ffn_full = gather_rows(cotangent)
    normed_rows, norm_attn_pull = jax.vjp(partial(rows_norm, gain_vector=gain_attn), inputs_rows)
    normed_full = gather_rows(normed_rows.astype(jnp.bfloat16))
    proj_lin = []
    proj_low = []
    for p in range(3):
        lin, lowr = column_forward(normed_full, w_qkv_full[p], a_in_sel[:, p], b_qkv_sel[:, p])
        proj_lin.append(lin)
        proj_low.append(lowr)
    rotate = partial(rotary_heads, positions=positions, head_dim=HEAD_DIM)
    query_rot, query_pull = jax.vjp(rotate, proj_lin[0])
    key_rot, key_pull = jax.vjp(rotate, proj_lin[1])
    query_in = query_rot.astype(jnp.bfloat16).reshape(seqs, length, heads_here, 2, HEAD_DIM)
    key_in = key_rot.astype(jnp.bfloat16).reshape(seqs, length, heads_here, 2, HEAD_DIM)
    value_in = proj_lin[2].astype(jnp.bfloat16).reshape(seqs, length, heads_here, VALUE_DIM)
    heads_out, log_total = jax.vmap(attend, in_axes=(0, 0, 0, 0, None))(
        query_in, key_in, value_in, allowed, lambda_here
    )
    mixed_float, head_pull = jax.vjp(partial(head_norm, gain_vector=gain_sub), heads_out)
    mixed_rows = mixed_float.reshape(seqs, length, qw_here).astype(jnp.bfloat16)
    attn_rows, out_low = row_forward(mixed_rows, w_out_full, a_out_sel, b_rows_sel[:, 0])
    hidden = inputs_rows + attn_rows
    normed_ffn, norm_ffn_pull = jax.vjp(partial(rows_norm, gain_vector=gain_ffn), hidden)
    ffn_full = gather_rows(normed_ffn.astype(jnp.bfloat16))
    gate_lin, gate_low = column_forward(ffn_full, w_gateup_full[0], a_in_sel[:, 3], b_gateup_sel[:, 0])
    up_lin, up_low = column_forward(ffn_full, w_gateup_full[1], a_in_sel[:, 4], b_gateup_sel[:, 1])
    product_float, swiglu_pull = jax.vjp(swiglu, gate_lin, up_lin)
    product = product_float.astype(jnp.bfloat16)
    ffn_rows, down_low = row_forward(product, w_down_full, a_down_sel, b_rows_sel[:, 1])
    output = (hidden + ffn_rows).astype(jnp.bfloat16)
    row_lows = tok_sum(jnp.stack([out_low, down_low]))

    tangent = cotangent.astype(jnp.float32)

    def row_backward(grad_full, rows_here, weight, down_sel, up_sel):
        grad_float = grad_full.astype(jnp.float32)
        grad_low = adapter_scale * hp_dot(grad_float, up_sel.astype(jnp.float32), "ste,sre->str")
        grad_down = hp_dot(rows_here.astype(jnp.float32), grad_low, "std,str->sdr")
        grad_inputs = jnp.einsum(
            "ste,de->std", grad_full, weight, preferred_element_type=jnp.float32
        ) + hp_dot(grad_low, down_sel.astype(jnp.float32), "str,sdr->std")
        return grad_inputs, grad_down

    def column_backward(rows_full, entries):
        running = None
        grad_lows = []
        grads_up = []
        for grad_rows, weight, down_sel, up_sel, lowrank in entries:
            grad_float = grad_rows.astype(jnp.float32)
            grad_low = adapter_scale * hp_dot(grad_float, up_sel.astype(jnp.float32), "ste,sre->str")
            grads_up.append(adapter_scale * hp_dot(lowrank, grad_float, "str,ste->sre"))
            grad_lows.append(grad_low)
            term = jnp.einsum(
                "ste,de->std", grad_rows, weight, preferred_element_type=jnp.float32
            ) + hp_dot(grad_low, down_sel.astype(jnp.float32), "str,sdr->std")
            running = term if running is None else running + term
        return scatter_rows(running), grad_lows, grads_up

    def rows_of_mine(rows_full):
        split = rows_full.reshape(seqs, length, fsdp_count, tok_count, D // (fsdp_count * tok_count))
        return lax.dynamic_index_in_dim(split, me_tok, 3, keepdims=False)

    grad_product, grad_a_down = row_backward(
        grad_ffn_full, product, w_down_full, a_down_sel, b_rows_sel[:, 1]
    )
    grad_gate, grad_up = swiglu_pull(grad_product)
    grad_ffn_rows, ffn_grad_lows, ffn_grads_up = column_backward(
        ffn_full,
        (
            (grad_gate.astype(jnp.bfloat16), w_gateup_full[0], a_in_sel[:, 3], b_gateup_sel[:, 0], gate_low),
            (grad_up.astype(jnp.bfloat16), w_gateup_full[1], a_in_sel[:, 4], b_gateup_sel[:, 1], up_low),
        ),
    )
    grad_hidden = tangent + norm_ffn_pull(grad_ffn_rows)[0]
    grad_attn_full = gather_rows(grad_hidden.astype(jnp.bfloat16))
    grad_mixed, grad_a_out = row_backward(
        grad_attn_full, mixed_rows, w_out_full, a_out_sel, b_rows_sel[:, 0]
    )
    grad_heads = head_pull(grad_mixed.reshape(seqs, length, heads_here, VALUE_DIM))[0].astype(
        jnp.bfloat16
    )
    grad_query_rot, grad_key_rot, grad_values = jax.vmap(
        attend_back, in_axes=(0, 0, 0, 0, None, 0, 0)
    )(query_in, key_in, value_in, allowed, lambda_here, log_total, grad_heads)
    grad_query = query_pull(grad_query_rot.reshape(seqs, length, qw_here))[0].astype(jnp.bfloat16)
    grad_key = key_pull(grad_key_rot.reshape(seqs, length, qw_here))[0].astype(jnp.bfloat16)
    grad_attn_rows, attn_grad_lows, attn_grads_up = column_backward(
        normed_full,
        (
            (grad_query, w_qkv_full[0], a_in_sel[:, 0], b_qkv_sel[:, 0], proj_low[0]),
            (grad_key, w_qkv_full[1], a_in_sel[:, 1], b_qkv_sel[:, 1], proj_low[1]),
            (grad_values.reshape(seqs, length, qw_here), w_qkv_full[2], a_in_sel[:, 2], b_qkv_sel[:, 2], proj_low[2]),
        ),
    )
    grad_tokens = grad_hidden + norm_attn_pull(grad_attn_rows)[0]

    grad_lows = tok_sum(jnp.stack(attn_grad_lows + ffn_grad_lows))
    attn_mine = rows_of_mine(normed_full)
    ffn_mine = rows_of_mine(ffn_full)
    grad_a_in_part = jnp.concatenate(
        [
            hp_dot(attn_mine.astype(jnp.float32), grad_lows[:3], "stfi,pstr->psfir"),
            hp_dot(ffn_mine.astype(jnp.float32), grad_lows[3:], "stfi,pstr->psfir"),
        ]
    )
    e_attn_mine = rows_of_mine(grad_attn_full).astype(jnp.float32)
    e_ffn_mine = rows_of_mine(grad_ffn_full).astype(jnp.float32)
    grad_b_rows_part = adapter_scale * jnp.stack(
        [
            hp_dot(row_lows[0], e_attn_mine, "str,stfj->srfj"),
            hp_dot(row_lows[1], e_ffn_mine, "str,stfj->srfj"),
        ]
    )

    def place(part, axis, total):
        shape = list(part.shape[1:])
        shape[axis] = total
        dense = jnp.zeros(shape, jnp.float32)
        for s in range(seqs):
            current = lax.dynamic_slice_in_dim(dense, offsets[s], RANK, axis)
            dense = lax.dynamic_update_slice_in_dim(dense, current + part[s], offsets[s], axis)
        return dense

    dense_a_in = place(jnp.moveaxis(grad_a_in_part, 1, 0), 3, COLS)
    dense_b_rows = place(jnp.moveaxis(grad_b_rows_part, 1, 0), 1, COLS)
    wide = jnp.concatenate(
        [
            jnp.moveaxis(dense_a_in, 1, 0).reshape(fsdp_count, -1),
            jnp.moveaxis(dense_b_rows, 2, 0).reshape(fsdp_count, -1),
        ],
        axis=1,
    )
    wide_sum = lax.all_to_all(wide, "fsdp", 0, 0, tiled=False).sum(0)
    a_in_block = wide_sum[: 5 * 16 * COLS].reshape(5, 16, COLS)
    b_rows_block = wide_sum[5 * 16 * COLS :].reshape(2, COLS, 16)

    dense_b_qkv = place(jnp.stack(attn_grads_up, 1), 1, COLS)
    dense_b_gateup = place(jnp.stack(ffn_grads_up, 1), 1, COLS)
    dense_a_out = place(grad_a_out, 1, COLS)
    dense_a_down = place(grad_a_down, 1, COLS)
    per = COLS // fsdp_count
    narrow = jnp.concatenate(
        [
            jnp.moveaxis(dense_b_qkv.reshape(3, fsdp_count, per, qw_here), 1, 0).reshape(fsdp_count, -1),
            jnp.moveaxis(dense_b_gateup.reshape(2, fsdp_count, per, ff_here), 1, 0).reshape(fsdp_count, -1),
            jnp.moveaxis(dense_a_out.reshape(qw_here, fsdp_count, per), 1, 0).reshape(fsdp_count, -1),
            jnp.moveaxis(dense_a_down.reshape(ff_here, fsdp_count, per), 1, 0).reshape(fsdp_count, -1),
        ],
        axis=1,
    ).astype(jnp.bfloat16)
    narrow_sum = lax.all_to_all(narrow, "fsdp", 0, 0, tiled=False).astype(jnp.float32).sum(0)
    sizes = [3 * per * qw_here, 2 * per * ff_here, qw_here * per, ff_here * per]
    cuts = [0]
    for size in sizes:
        cuts.append(cuts[-1] + size)
    b_qkv_block = narrow_sum[cuts[0] : cuts[1]].reshape(3, per, qw_here)
    b_gateup_block = narrow_sum[cuts[1] : cuts[2]].reshape(2, per, ff_here)
    a_out_block = narrow_sum[cuts[2] : cuts[3]].reshape(qw_here, per)
    a_down_block = narrow_sum[cuts[3] : cuts[4]].reshape(ff_here, per)

    return (
        output,
        grad_tokens,
        a_in_block,
        b_qkv_block,
        b_gateup_block,
        a_out_block,
        a_down_block,
        b_rows_block,
    )


def solution(mesh):
    return jax.shard_map(
        per_device,
        mesh=mesh,
        in_specs=(
            P("fsdp", "tok", None),
            P("fsdp", "tok", None),
            P("fsdp", None),
            P("fsdp"),
            P(None, "fsdp", "tok"),
            P("tok", "fsdp"),
            P(None, "fsdp", "tok"),
            P("tok", "fsdp"),
            P(),
            P(),
            P(),
            P(),
            P(None, ("fsdp", "tok"), None),
            P(None, "fsdp", "tok"),
            P(None, "fsdp", "tok"),
            P("tok", "fsdp"),
            P("tok", "fsdp"),
            P(None, None, ("fsdp", "tok")),
        ),
        out_specs=(
            P("fsdp", "tok", None),
            P("fsdp", "tok", None),
            P(None, ("fsdp", "tok"), None),
            P(None, "fsdp", "tok"),
            P(None, "fsdp", "tok"),
            P("tok", "fsdp"),
            P("tok", "fsdp"),
            P(None, None, ("fsdp", "tok")),
        ),
        check_vma=False,
    )
```

time: 2770 us -> 1380 us (0.50)
  waiting for transfers between devices: 2150 us -> 743 us
  local copies, waits for them, and re-layouts: 73.6 us -> 356 us
  blocking collectives: 274 us -> 0 us
  matrix products: 191 us -> 113 us
  starting transfers between devices: 1.69 us -> 57.4 us
    reduce_scatter x9 -> x0, waiting for transfers between devices: 960 us -> none  [the longest x1 641 us: per_device(): lax.psum_scatter(totals[0], ('fsdp', 'tok'), scatter_dimension=1, tiled=T...]
    all_gather x14 -> x1, waiting for transfers between devices: 806 us -> 0.02 us  [per_device(): gathered = lax.all_gather(flat, 'fsdp', axis=0, tiled=False)]
    ppermute x0 -> x24, waiting for transfers between devices: none -> 742 us  [the longest x6 667 us: tok_gather(): far = lax.ppermute(values, 'tok', xor_pairs(count, 2))]
    unnamed x27 -> x1, waiting for transfers between devices: 384 us -> 0.02 us
    all_gather x4 -> x0, blocking collectives: 274 us -> none  [the longest x1 71.8 us: prepare(): lax.all_gather(b_qkv, 'fsdp', axis=1, tiled=True)]
    dot_general x112 -> x53, matrix products: 185 us -> 110 us  [the longest x32 55 us: hp_dot(): jnp.einsum(spec, left, right, precision=highest, preferred_element_type=j...]
    unnamed x390 -> x303, local copies, waits for them, and re-layouts: 33.6 us -> 97 us
    transpose x0 -> x15, local copies, waits for them, and re-layouts: none -> 52.5 us  [the longest x8 26 us: gather_rows(): return jnp.moveaxis(full, 0, 1).reshape(seqs, length, values.shape[-1])]
  transfers between devices with their start and end apart: 25 -> 27, of which waited for: 22 -> 13; matrix products, arithmetic and copies ran while one was open for 8% -> 29% of each run, Pallas kernels for 0% -> 0%
where the time goes in v1:
time: 1380 us; the launch traced here: 1360 us
  waiting for transfers between devices  743 us (54%)
  local copies, waits for them, and re-layouts  356 us (26%)
  matrix products  113 us (8%)
  other arithmetic  69.2 us (5%)
  starting transfers between devices  57.4 us (4%)
  between operations  21.8 us (2%)
    ppermute x6, waiting for transfers between devices, tok_gather(): far = lax.ppermute(values, 'tok', xor_pairs(count, 2))  667 us
    unnamed x303, local copies, waits for them, and re-layouts  97 us
    ppermute x4, waiting for transfers between devices, tok_scatter(): return keep + lax.ppermute(send, 'tok', xor_pairs(count, 2))  71.5 us
    dot_general x32, matrix products, hp_dot(): jnp.einsum(spec, left, right, precision=highest, preferred_element_type=j...  55 us
    slice x12, local copies, waits for them, and re-layouts, per_device(): gathered[:, start:start + size].reshape((fsdp_count,) + p.shape)  32.4 us
  transfers between devices with their start and end apart: 27, of which 13 were waited for; matrix products, arithmetic and copies ran while one was open for 29% of the time, Pallas kernels for 0%

profile of v1, /device:TPU:1, one launch (start us, length us, event | category | flops | bytes accessed | tf_op | source)
XLA Modules:
  0.0 1359.6 jit_solution(2276348433503699046)
XLA Ops:
  7.2 4.5 collective-permute-start.2
  22.3 11.8 reshape.892
  46.6 645.1 %collective-permute-done = bf16[2,64,2048]{2,1,0:T(8,128)(2,1)S(1)} collective-permute-done((bf16[2,64,2048]{2,1,0:T(8,128)(2,1)S(1)}, bf16[2,64,2048]{2,1,0:T(8,128)(2,1)S(1)}, u32[]{:S(2)}, u32[]{:S(2)}) %collective-permute-start) | collective-permute-done | bytes 524320 | tf_op jit(solution)/shard_map/ppermute | solution.py:106
  694.8 9.1 collective-permute-done.12
  709.5 31.1 %copy.423 = bf16[32,1,483840]{2,0,1:T(8,128)(2,1)} copy(bf16[32,1,483840]{2,1,0:T(2,128)(2,1)} %all-gather.4.cloned.1.call-done) | data formatting | bytes 61931520
  744.3 5.8 slice.330
  751.5 3.8 constant_dynamic-slice_fusion.18
  775.5 5.2 copy.379
  812.0 6.5 reshape.857
  818.5 4.9 copy.255
  826.5 5.7 copy.263
  839.8 4.2 multiply_add_fusion.1
  851.4 6.0 slice.356
  859.5 5.5 slice.364
  865.1 5.8 copy.381
  875.9 3.5 copy.274
  881.7 13.5 reshape.869
  895.2 11.8 copy.271
  910.7 7.7 fusion.111
  924.8 9.4 fusion.95
  934.2 13.5 collective-permute-done.7
  954.2 9.8 collective-permute-done.8
  981.4 3.6 fusion.4
  985.5 3.5 fusion.112
  989.5 3.5 fusion.113
  993.0 3.4 fusion.109
  1010.6 7.0 copy.304
  1017.6 7.0 copy.312
  1024.6 7.0 reshape_reshape.22
  1031.6 7.0 reshape_reshape.25
  1056.4 18.3 %collective-permute-done.15 = f32[2,64,2048]{2,1,0:T(8,128)S(1)} collective-permute-done((f32[2,64,2048]{2,1,0:T(8,128)S(1)}, f32[2,64,2048]{2,1,0:T(8,128)S(1)}, u32[]{:S(2)}, u32[]{:S(2)}) %collective-permute-start.15) | collective-permute-done | bytes 1048608 | tf_op jit(solution)/shard_map/ppermute | solution.py:124
  1074.9 22.2 %collective-permute-done.11 = f32[2,64,2048]{2,1,0:T(8,128)S(1)} collective-permute-done((f32[2,64,2048]{2,1,0:T(8,128)S(1)}, f32[2,64,2048]{2,1,0:T(8,128)S(1)}, u32[]{:S(2)}, u32[]{:S(2)}) %collective-permute-start.11) | collective-permute-done | bytes 1048608 | tf_op jit(solution)/shard_map/ppermute | solution.py:124
  1119.1 4.7 copy.307
  1134.9 6.0 reshape_reshape.23
  1183.8 4.6 multiply_add_fusion.5
  1195.2 5.2 copy.310
  1200.3 5.2 fusion.115
  1210.4 4.5 fusion.116
  1228.4 8.1 all-to-all-start.1
  1239.5 6.1 reshape_reshape.24
  1250.9 5.3 add_add_fusion
  1276.2 4.6 dynamic_update_slice.36
  1282.1 5.3 dynamic_update_slice.37
  1287.4 4.1 copy.316
  1294.2 8.2 all-to-all-start
  1307.1 9.5 reshape.911
  1316.6 5.3 convert_reduce_fusion
  1330.8 17.6 %collective-permute-done.19 = f32[2,64,2048]{2,1,0:T(8,128)} collective-permute-done((f32[2,64,2048]{2,1,0:T(8,128)}, f32[2,64,2048]{2,1,0:T(8,128)}, u32[]{:S(2)}, u32[]{:S(2)}) %collective-permute-start.19) | collective-permute-done | bytes 1048608 | tf_op jit(solution)/shard_map/ppermute | solution.py:124
  (609 shorter events, 327.0 us)
Async XLA Ops:
  7.2 702.3 %all-gather.4.cloned.1.call-start = ((), (), s32[]{:S(2)}) async-start(), calls=%async_computation.2 | async-start | bytes 63866880 | tf_op jit(solution)/shard_map/all_gather | solution.py:175
  7.2 12.3 collective-permute-start.2
  11.7 6.8 collective-permute-start.4
  18.5 1.9 collective-permute-start.5
  19.6 1.3 collective-permute-start.3
  34.4 657.6 %copy-start.119 = (f32[2,64]{1,0:T(2,128)}, f32[2,64]{1,0:T(2,128)S(1)}, u32[]{:S(2)}) copy-start(f32[2,64]{1,0:T(2,128)S(1)} %fusion.18) | copy-start | bytes 1540
  34.4 657.6 %copy-start.114 = (f32[2,64]{1,0:T(2,128)}, f32[2,64]{1,0:T(2,128)S(1)}, u32[]{:S(2)}) copy-start(f32[2,64]{1,0:T(2,128)S(1)} %fusion.70) | copy-start | bytes 1540
  34.6 657.2 %collective-permute-start = (bf16[2,64,2048]{2,1,0:T(8,128)(2,1)S(1)}, bf16[2,64,2048]{2,1,0:T(8,128)(2,1)S(1)}, u32[]{:S(2)}, u32[]{:S(2)}) collective-permute-start(bf16[2,64,2048]{2,1,0:T(8,128)(2,1)S(1)} %fusion.20), channel_id=1, source_target_pairs={{0,2},{1,3},{2,0},{3,1},{4,6},{5,7},{6,4},{7,5},{8,10},{9,11},{10,... | collective-permute-start | bytes 1572872 | tf_op jit(solution)/shard_map/ppermute | solution.py:106
  37.8 666.1 %collective-permute-start.12 = (bf16[2,64,2048]{2,1,0:T(8,128)(2,1)S(1)}, bf16[2,64,2048]{2,1,0:T(8,128)(2,1)S(1)}, u32[]{:S(2)}, u32[]{:S(2)}) collective-permute-start(bf16[2,64,2048]{2,1,0:T(8,128)(2,1)S(1)} %copy-done.43), channel_id=1, source_target_pairs={{0,2},{1,3},{2,0},{3,1},{4,6},{5,7},{6,4},{7,5},{8,10},{9,11},{10,... | collective-permute-start | bytes 1572872 | tf_op jit(solution)/shard_map/ppermute | solution.py:106
  691.9 15.5 %collective-permute-start.1 = (bf16[2,2,64,2048]{3,2,1,0:T(8,128)(2,1)S(1)}, bf16[2,2,64,2048]{3,2,1,0:T(8,128)(2,1)S(1)}, u32[]{:S(2)}, u32[]{:S(2)}) collective-permute-start(bf16[2,2,64,2048]{3,2,1,0:T(8,128)(2,1)S(1)} %maximum_select_fusion.4), channel_id=1, source_target_pairs={{0,1},{1,0},{2,3},{3,2},{4,5},{5,4},{6,7},{7,6},{8,9},{9,8},{10,11... | collective-permute-start | bytes 3145736 | tf_op jit(solution)/shard_map/ppermute | solution.py:108
  694.8 103.4 %copy-start.59 = (f32[256,64]{1,0:T(8,128)}, f32[256,64]{1,0:T(8,128)S(1)}, u32[]{:S(2)}) copy-start(f32[256,64]{1,0:T(8,128)S(1)} %get-tuple-element.83) | copy-start | bytes 196612
  694.8 103.4 %copy-start.61 = (f32[256,64]{1,0:T(8,128)}, f32[256,64]{1,0:T(8,128)S(1)}, u32[]{:S(2)}) copy-start(f32[256,64]{1,0:T(8,128)S(1)} %get-tuple-element.84) | copy-start | bytes 196612
  705.1 142.1 %collective-permute-start.13 = (bf16[2,2,64,2048]{3,2,1,0:T(8,128)(2,1)}, bf16[2,2,64,2048]{3,2,1,0:T(8,128)(2,1)}, u32[]{:S(2)}, u32[]{:S(2)}) collective-permute-start(bf16[2,2,64,2048]{3,2,1,0:T(8,128)(2,1)} %maximum_select_fusion.7), channel_id=1, source_target_pairs={{0,1},{1,0},{2,3},{3,2},{4,5},{5,4},{6,7},{7,6},{8,9},{9,8},{10,11... | collective-permute-start | bytes 3145736 | tf_op jit(solution)/shard_map/ppermute | solution.py:108
  806.7 27.5 %copy-start.10 = (f32[2,256,2,256]{1,3,2,0:T(8,128)}, f32[2,256,2,256]{1,3,2,0:T(8,128)S(1)}, u32[]{:S(2)}) copy-start(f32[2,256,2,256]{1,3,2,0:T(8,128)S(1)} %get-tuple-element.92) | copy-start | bytes 3145732
  807.3 26.9 %copy-start.109 = (f32[2,256,2]{1,2,0:T(2,128)}, f32[2,256,2]{1,2,0:T(2,128)S(1)}, u32[]{:S(2)}) copy-start(f32[2,256,2]{1,2,0:T(2,128)S(1)} %fusion.69) | copy-start | bytes 12292
  847.2 71.2 %collective-permute-start.6 = (f32[2,2,64,2048]{3,2,1,0:T(8,128)}, f32[2,2,64,2048]{3,2,1,0:T(8,128)}, u32[]{:S(2)}, u32[]{:S(2)}) collective-permute-start(f32[2,2,64,2048]{3,2,1,0:T(8,128)} %bitcast.556), channel_id=1, source_target_pairs={{0,1},{1,0},{2,3},{3,2},{4,5},{5,4},{6,7},{7,6},{8,9},{9,8},{10,11... | collective-permute-start | bytes 6291464 | tf_op jit(solution)/shard_map/ppermute | solution.py:121
  921.8 25.9 %collective-permute-start.7 = (f32[2,64,2048]{2,1,0:T(8,128)S(1)}, f32[2,64,2048]{2,1,0:T(8,128)S(1)}, u32[]{:S(2)}, u32[]{:S(2)}) collective-permute-start(f32[2,64,2048]{2,1,0:T(8,128)S(1)} %dynamic-slice_bitcast_fusion.3), channel_id=1, source_target_pairs={{0,2},{1,3},{2,0},{3,1},{4,6},{5,7},{6,4},{7,5},{8,10},{9,11},{10,... | collective-permute-start | bytes 3145736 | tf_op jit(solution)/shard_map/ppermute | solution.py:124
  934.2 18.9 %copy-start.101 = (bf16[4,1408,4]{1,2,0:T(4,128)(2,1)S(1)}, bf16[4,1408,4]{1,2,0:T(4,128)(2,1)}, u32[]{:S(2)}) copy-start(bf16[4,1408,4]{1,2,0:T(4,128)(2,1)} %copy.274) | copy-start | bytes 135172
  934.2 18.9 %copy-start.102 = (bf16[4,1408,4]{1,2,0:T(4,128)(2,1)S(1)}, bf16[4,1408,4]{1,2,0:T(4,128)(2,1)}, u32[]{:S(2)}) copy-start(bf16[4,1408,4]{1,2,0:T(4,128)(2,1)} %copy.275) | copy-start | bytes 135172
  934.2 19.0 %copy-start.74 = (bf16[2,2,4,4,1408]{4,3,1,2,0:T(4,128)(2,1)S(1)}, bf16[2,2,4,4,1408]{4,3,1,2,0:T(4,128)(2,1)}, u32[]{:S(2)}) copy-start(bf16[2,2,4,4,1408]{4,3,1,2,0:T(4,128)(2,1)} %maximum_bitcast_fusion.3) | copy-start | bytes 540676
  950.1 13.9 %collective-permute-start.8 = (bf16[2,64,2048]{2,1,0:T(8,128)(2,1)}, bf16[2,64,2048]{2,1,0:T(8,128)(2,1)S(1)}, u32[]{:S(2)}, u32[]{:S(2)}) collective-permute-start(bf16[2,64,2048]{2,1,0:T(8,128)(2,1)} %multiply_convert_fusion.3), channel_id=1, source_target_pairs={{0,2},{1,3},{2,0},{3,1},{4,6},{5,7},{6,4},{7,5},{8,10},{9,11},{10,... | collective-permute-start | bytes 1572872 | tf_op jit(solution)/shard_map/ppermute | solution.py:106
  964.2 4.7 collective-permute-start.9
  985.0 19.6 %copy-start.31 = (bf16[2,256,1408]{2,1,0:T(8,128)(2,1)}, bf16[2,256,1408]{2,1,0:T(8,128)(2,1)S(1)}, u32[]{:S(2)}) copy-start(bf16[2,256,1408]{2,1,0:T(8,128)(2,1)S(1)} %get-tuple-element.45) | copy-start | bytes 4325380
  1004.1 42.2 %collective-permute-start.14 = (f32[2,2,64,2048]{3,2,1,0:T(8,128)}, f32[2,2,64,2048]{3,2,1,0:T(8,128)}, u32[]{:S(2)}, u32[]{:S(2)}) collective-permute-start(f32[2,2,64,2048]{3,2,1,0:T(8,128)} %bitcast.554), channel_id=1, source_target_pairs={{0,1},{1,0},{2,3},{3,2},{4,5},{5,4},{6,7},{7,6},{8,9},{9,8},{10,11... | collective-permute-start | bytes 6291464 | tf_op jit(solution)/shard_map/ppermute | solution.py:121
  1005.1 37.5 %copy-start.70 = (f32[2,256,16]{1,2,0:T(8,128)}, f32[2,256,16]{1,2,0:T(8,128)S(1)}, u32[]{:S(2)}) copy-start(f32[2,256,16]{1,2,0:T(8,128)S(1)} %fusion.110) | copy-start | bytes 98308
  1010.5 41.0 %collective-permute-start.10 = (f32[2,2,64,2048]{3,2,1,0:T(8,128)}, f32[2,2,64,2048]{3,2,1,0:T(8,128)}, u32[]{:S(2)}, u32[]{:S(2)}) collective-permute-start(f32[2,2,64,2048]{3,2,1,0:T(8,128)} %bitcast.555), channel_id=1, source_target_pairs={{0,1},{1,0},{2,3},{3,2},{4,5},{5,4},{6,7},{7,6},{8,9},{9,8},{10,11... | collective-permute-start | bytes 6291464 | tf_op jit(solution)/shard_map/ppermute | solution.py:121
  1043.3 97.6 %collective-permute-start.22 = (f32[2,2,256,16]{2,3,1,0:T(8,128)}, f32[2,2,256,16]{2,3,1,0:T(8,128)}, u32[]{:S(2)}, u32[]{:S(2)}) collective-permute-start(f32[2,2,256,16]{2,3,1,0:T(8,128)} %pad_maximum_fusion.9), channel_id=1, source_target_pairs={{0,1},{1,0},{2,3},{3,2},{4,5},{5,4},{6,7},{7,6},{8,9},{9,8},{10,11... | collective-permute-start | bytes 196616 | tf_op jit(solution)/shard_map/ppermute | solution.py:129
  1045.7 56.2 %copy-start.55 = (f32[2,1,16,1408]{3,2,0,1:T(8,128)}, f32[2,1,16,1408]{3,2,0,1:T(8,128)S(1)}, u32[]{:S(2)}) copy-start(f32[2,1,16,1408]{3,2,0,1:T(8,128)S(1)} %fusion.7) | copy-start | bytes 540676
  1048.4 26.2 %collective-permute-start.15 = (f32[2,64,2048]{2,1,0:T(8,128)S(1)}, f32[2,64,2048]{2,1,0:T(8,128)S(1)}, u32[]{:S(2)}, u32[]{:S(2)}) collective-permute-start(f32[2,64,2048]{2,1,0:T(8,128)S(1)} %dynamic-slice_bitcast_fusion.1), channel_id=1, source_target_pairs={{0,2},{1,3},{2,0},{3,1},{4,6},{5,7},{6,4},{7,5},{8,10},{9,11},{10,... | collective-permute-start | bytes 3145736 | tf_op jit(solution)/shard_map/ppermute | solution.py:124
  1053.5 21.4 %copy-start.122 = (f32[2,64]{1,0:T(2,128)S(1)}, f32[2,64]{1,0:T(2,128)}, u32[]{:S(2)}) copy-start(f32[2,64]{1,0:T(2,128)} %copy-done.121) | copy-start | bytes 1540
  1053.5 43.6 %copy-start.44 = (bf16[2,64,2048]{2,1,0:T(8,128)(2,1)S(1)}, bf16[2,64,2048]{2,1,0:T(8,128)(2,1)}, u32[]{:S(2)}) copy-start(bf16[2,64,2048]{2,1,0:T(8,128)(2,1)} %param.19) | copy-start | bytes 1572868
  1053.5 43.6 %collective-permute-start.11 = (f32[2,64,2048]{2,1,0:T(8,128)S(1)}, f32[2,64,2048]{2,1,0:T(8,128)S(1)}, u32[]{:S(2)}, u32[]{:S(2)}) collective-permute-start(f32[2,64,2048]{2,1,0:T(8,128)S(1)} %dynamic-slice_bitcast_fusion.2), channel_id=1, source_target_pairs={{0,2},{1,3},{2,0},{3,1},{4,6},{5,7},{6,4},{7,5},{8,10},{9,11},{10,... | collective-permute-start | bytes 3145736 | tf_op jit(solution)/shard_map/ppermute | solution.py:124
  1055.7 46.2 %copy-start.57 = (f32[2,1,16,1408]{3,2,0,1:T(8,128)}, f32[2,1,16,1408]{3,2,0,1:T(8,128)S(1)}, u32[]{:S(2)}) copy-start(f32[2,1,16,1408]{3,2,0,1:T(8,128)S(1)} %fusion.6) | copy-start | bytes 540676
  1098.9 14.1 %collective-permute-start.16 = (bf16[2,64,2048]{2,1,0:T(8,128)(2,1)S(1)}, bf16[2,64,2048]{2,1,0:T(8,128)(2,1)}, u32[]{:S(2)}, u32[]{:S(2)}) collective-permute-start(bf16[2,64,2048]{2,1,0:T(8,128)(2,1)S(1)} %get-tuple-element.34), channel_id=1, source_target_pairs={{0,2},{1,3},{2,0},{3,1},{4,6},{5,7},{6,4},{7,5},{8,10},{9,11},{10,... | collective-permute-start | bytes 1572872 | tf_op jit(solution)/shard_map/ppermute | solution.py:106
  1103.8 15.3 %copy-start.7 = (bf16[2,2,2,64,2048]{4,3,2,1,0:T(8,128)(2,1)S(1)}, bf16[2,2,2,64,2048]{4,3,2,1,0:T(8,128)(2,1)}, u32[]{:S(2)}) copy-start(bf16[2,2,2,64,2048]{4,3,2,1,0:T(8,128)(2,1)} %copy-done.6) | copy-start | bytes 6291460
  1115.4 36.8 %collective-permute-start.17 = (bf16[2,2,64,2048]{3,2,1,0:T(8,128)(2,1)}, bf16[2,2,64,2048]{3,2,1,0:T(8,128)(2,1)}, u32[]{:S(2)}, u32[]{:S(2)}) collective-permute-start(bf16[2,2,64,2048]{3,2,1,0:T(8,128)(2,1)} %maximum_select_fusion.9), channel_id=1, source_target_pairs={{0,1},{1,0},{2,3},{3,2},{4,5},{5,4},{6,7},{7,6},{8,9},{9,8},{10,11... | collective-permute-start | bytes 3145736 | tf_op jit(solution)/shard_map/ppermute | solution.py:108
  1141.7 5.3 collective-permute-start.23
  1228.4 65.8 %all-to-all-start.1 = ((bf16[32,2,12544]{2,1,0:T(2,128)(2,1)}), bf16[32,2,12544]{2,1,0:T(2,128)(2,1)}, u32[]{:S(2)}, u32[]{:S(2)}) async-start(bf16[32,2,12544]{2,1,0:T(2,128)(2,1)} %reshape.910), calls=%async_computation.1 | async-start | bytes 3211264 | tf_op jit(solution)/shard_map/all_to_all | solution.py:383
  1238.3 21.2 %collective-permute-start.20 = (f32[5,2,256,16]{2,3,1,0:T(8,128)S(1)}, f32[5,2,256,16]{2,3,1,0:T(8,128)S(1)}, u32[]{:S(2)}, u32[]{:S(2)}) collective-permute-start(f32[5,2,256,16]{2,3,1,0:T(8,128)S(1)} %bitcast_dynamic-update-slice_fusion), channel_id=1, source_target_pairs={{0,1},{1,0},{2,3},{3,2},{4,5},{5,4},{6,7},{7,6},{8,9},{9,8},{10,11... | collective-permute-start | bytes 491528 | tf_op jit(solution)/shard_map/ppermute | solution.py:129
  1259.5 10.8 collective-permute-start.21
  1269.8 32.6 %collective-permute-start.18 = (f32[2,2,64,2048]{3,2,1,0:T(8,128)}, f32[2,2,64,2048]{3,2,1,0:T(8,128)}, u32[]{:S(2)}, u32[]{:S(2)}) collective-permute-start(f32[2,2,64,2048]{3,2,1,0:T(8,128)} %bitcast.553), channel_id=1, source_target_pairs={{0,1},{1,0},{2,3},{3,2},{4,5},{5,4},{6,7},{7,6},{8,9},{9,8},{10,11... | collective-permute-start | bytes 6291464 | tf_op jit(solution)/shard_map/ppermute | solution.py:121
  1294.2 32.7 %all-to-all-start = ((f32[32,1,14336]{2,1,0:T(1,128)}), f32[32,1,14336]{2,1,0:T(1,128)}, u32[]{:S(2)}, u32[]{:S(2)}) async-start(f32[32,1,14336]{2,1,0:T(1,128)} %all_to_all.10), calls=%async_computation | async-start | bytes 3670016 | tf_op jit(solution)/shard_map/all_to_all | solution.py:365
  1306.0 42.4 %collective-permute-start.19 = (f32[2,64,2048]{2,1,0:T(8,128)}, f32[2,64,2048]{2,1,0:T(8,128)}, u32[]{:S(2)}, u32[]{:S(2)}) collective-permute-start(f32[2,64,2048]{2,1,0:T(8,128)} %dynamic-slice_bitcast_fusion), channel_id=1, source_target_pairs={{0,2},{1,3},{2,0},{3,1},{4,6},{5,7},{6,4},{7,5},{8,10},{9,11},{10,... | collective-permute-start | bytes 3145736 | tf_op jit(solution)/shard_map/ppermute | solution.py:124
  1321.9 26.5 %copy-start.3 = (bf16[2,64,2048]{2,1,0:T(8,128)(2,1)S(1)}, bf16[2,64,2048]{2,1,0:T(8,128)(2,1)}, u32[]{:S(2)}) copy-start(bf16[2,64,2048]{2,1,0:T(8,128)(2,1)} %param.18) | copy-start | bytes 1572868
  1321.9 26.5 %copy-start.99 = (f32[2048]{0:T(1024)S(1)}, f32[2048]{0:T(1024)}, u32[]{:S(2)}) copy-start(f32[2048]{0:T(1024)} %param.26) | copy-start | bytes 24580
  1325.8 24.1 %copy-start.120 = (f32[2,64]{1,0:T(2,128)S(1)}, f32[2,64]{1,0:T(2,128)}, u32[]{:S(2)}) copy-start(f32[2,64]{1,0:T(2,128)} %copy-done.119) | copy-start | bytes 1540
  1325.8 24.1 %copy-start.115 = (f32[2,64]{1,0:T(2,128)S(1)}, f32[2,64]{1,0:T(2,128)}, u32[]{:S(2)}) copy-start(f32[2,64]{1,0:T(2,128)} %copy-done.114) | copy-start | bytes 1540
  1330.8 19.1 %copy-start.50 = (f32[2,64,2048]{2,1,0:T(8,128)S(1)}, f32[2,64,2048]{2,1,0:T(8,128)}, u32[]{:S(2)}) copy-start(f32[2,64,2048]{2,1,0:T(8,128)} %get-tuple-element.35) | copy-start | bytes 3145732
  (115 other events, 520.5 us)
Sparse Core Ops, SparseCore 0:
  34.3 660.7 all-gather.3

commit v2 on v1

--- a/solution.py
+++ b/solution.py
@@ -168,22 +168,25 @@
     fsdp_rows = w_qkv.shape[1]
     groups_per_adapter = RANK // b_qkv.shape[1]
 
+    def fsdp_gather(values, axis):
+        tiled_in = jnp.concatenate([values] * fsdp_count, axis=0)
+        return lax.all_to_all(tiled_in, "fsdp", 0, axis, tiled=True)
+
     a_in_tok = tok_gather(a_in)
     b_rows_tok = tok_gather(b_rows)
-    pieces = [w_qkv, w_out, w_gateup, w_down, b_qkv, b_gateup, a_out, a_down, a_in_tok, b_rows_tok]
-    flat = jnp.concatenate([p.reshape(-1) for p in pieces])
-    gathered = lax.all_gather(flat, "fsdp", axis=0, tiled=False)
+    small = [b_qkv, b_gateup, a_out, a_down, a_in_tok, b_rows_tok]
+    small_flat = jnp.concatenate([p.reshape(1, -1) for p in small], axis=1)
+    small_all = fsdp_gather(small_flat, 0)
     unpacked = []
     start = 0
-    for p in pieces:
-        size = p.size
-        unpacked.append(gathered[:, start : start + size].reshape((fsdp_count,) + p.shape))
-        start += size
-    (g_qkv, g_out, g_gateup, g_down, g_bqkv, g_bgateup, g_aout, g_adown, g_ain, g_brows) = unpacked
-    w_qkv_full = jnp.moveaxis(g_qkv, 0, 1).reshape(3, fsdp_count * fsdp_rows, qw_here)
-    w_out_full = jnp.moveaxis(g_out, 0, 1).reshape(qw_here, fsdp_count * fsdp_rows)
-    w_gateup_full = jnp.moveaxis(g_gateup, 0, 1).reshape(2, fsdp_count * fsdp_rows, ff_here)
-    w_down_full = jnp.moveaxis(g_down, 0, 1).reshape(ff_here, fsdp_count * fsdp_rows)
+    for p in small:
+        unpacked.append(small_all[:, start : start + p.size].reshape((fsdp_count,) + p.shape))
+        start += p.size
+    (g_bqkv, g_bgateup, g_aout, g_adown, g_ain, g_brows) = unpacked
+    w_qkv_full = fsdp_gather(w_qkv, 1)
+    w_out_full = fsdp_gather(w_out, 1)
+    w_gateup_full = fsdp_gather(w_gateup, 1)
+    w_down_full = fsdp_gather(w_down, 1)
     a_in_full = jnp.transpose(g_ain, (2, 0, 1, 3, 4)).reshape(5, D, COLS)
     b_rows_full = jnp.transpose(g_brows, (2, 3, 0, 1, 4)).reshape(2, COLS, D)
 

time: 1380 us -> 1130 us (0.82)
  waiting for transfers between devices: 743 us -> 288 us
  other arithmetic: 69.2 us -> 182 us
  starting transfers between devices: 57.4 us -> 125 us
  local copies, waits for them, and re-layouts: 356 us -> 404 us
    ppermute x6, waiting for transfers between devices: 667 us -> 41.7 us  [tok_gather(): far = lax.ppermute(values, 'tok', xor_pairs(count, 2))]
    all_to_all x0 -> x5, waiting for transfers between devices: none -> 129 us  [fsdp_gather(): return lax.all_to_all(tiled_in, 'fsdp', 0, axis, tiled=True)]
    concatenate x0 -> x2, other arithmetic: none -> 99.4 us  [the longest x1 97.5 us: fsdp_gather(): tiled_in = jnp.concatenate([values] * fsdp_count, axis=0)]
    unnamed x303 -> x416, local copies, waits for them, and re-layouts: 97 us -> 148 us
    all_to_all x0 -> x5, starting transfers between devices: none -> 50.1 us  [fsdp_gather(): return lax.all_to_all(tiled_in, 'fsdp', 0, axis, tiled=True)]
    ppermute x4, waiting for transfers between devices: 71.5 us -> 114 us  [tok_scatter(): return keep + lax.ppermute(send, 'tok', xor_pairs(count, 2))]
    reshape x10 -> x6, local copies, waits for them, and re-layouts: 25.9 us -> 3.6 us  [the longest x2 2.88 us: per_device(): small_all[:, start:start + p.size].reshape((fsdp_count,) + p.shape)]
    all_to_all x0 -> x4, local copies, waits for them, and re-layouts: none -> 21.2 us  [fsdp_gather(): return lax.all_to_all(tiled_in, 'fsdp', 0, axis, tiled=True)]
  transfers between devices with their start and end apart: 27 -> 31, of which waited for: 13 -> 13; matrix products, arithmetic and copies ran while one was open for 29% -> 50% of each run, Pallas kernels for 0% -> 0%
where the time goes in v2:
time: 1130 us; the launch traced here: 1120 us
  local copies, waits for them, and re-layouts  404 us (36%)
  waiting for transfers between devices  288 us (25%)
  other arithmetic  182 us (16%)
  starting transfers between devices  125 us (11%)
  matrix products  108 us (10%)
    unnamed x416, local copies, waits for them, and re-layouts  148 us
    all_to_all x5, waiting for transfers between devices, fsdp_gather(): return lax.all_to_all(tiled_in, 'fsdp', 0, axis, tiled=True)  129 us
    ppermute x4, waiting for transfers between devices, tok_scatter(): return keep + lax.ppermute(send, 'tok', xor_pairs(count, 2))  114 us
    concatenate x1, other arithmetic, fsdp_gather(): tiled_in = jnp.concatenate([values] * fsdp_count, axis=0)  97.5 us
    dot_general x32, matrix products, hp_dot(): jnp.einsum(spec, left, right, precision=highest, preferred_element_type=j...  51.4 us
    all_to_all x5, starting transfers between devices, fsdp_gather(): return lax.all_to_all(tiled_in, 'fsdp', 0, axis, tiled=True)  50.1 us
    ppermute x6, waiting for transfers between devices, tok_gather(): far = lax.ppermute(values, 'tok', xor_pairs(count, 2))  41.7 us
    transpose x8, local copies, waits for them, and re-layouts, gather_rows(): return jnp.moveaxis(full, 0, 1).reshape(seqs, length, values.shape[-1])  28.5 us
  transfers between devices with their start and end apart: 31, of which 13 were waited for; matrix products, arithmetic and copies ran while one was open for 50% of the time, Pallas kernels for 0%

profile of v2, /device:TPU:1, one launch (start us, length us, event | category | flops | bytes accessed | tf_op | source)
XLA Modules:
  0.0 1115.4 jit_solution(16627367412113520688)
XLA Ops:
  21.8 7.6 all-to-all-start.2
  85.4 10.3 concatenate.140
  96.2 97.5 %reduce.3 = bf16[32,82432]{1,0:T(8,128)(2,1)} reduce(bf16[32,1,82432]{2,1,0:T(2,128)(2,1)} %concatenate.140, bf16[]{:T(256)} %broadcast.349), dimensions={1}, to_apply=%concatenate.140.reduce_sub_computation | reduce | bytes 10551298 | tf_op jit(solution)/shard_map/concatenate | solution.py:172
  193.7 5.8 reshape.908
  200.7 7.5 all-to-all-start.1
  225.5 71.5 %all-to-all-done.1 = bf16[32,2,41216]{2,1,0:T(2,128)(2,1)} async-done(((bf16[32,2,41216]{2,1,0:T(2,128)(2,1)}), bf16[32,2,41216]{2,1,0:T(2,128)(2,1)}, u32[]{:S(2)}, u32[]{:S(2)}) %all-to-all-start.1) | async-done | bytes 5275680 | tf_op jit(solution)/shard_map/all_to_all | solution.py:173
  296.9 9.1 all-to-all-start
  321.4 5.9 copy.429
  335.3 23.2 %reshape.909 = bf16[32,1,82432]{2,1,0:T(2,128)(2,1)} reshape(bf16[32,2,41216]{2,1,0:T(2,128)(2,1)} %all-to-all-done.1) | data formatting | bytes 10551296
  358.5 4.6 copy.430
  367.7 32.2 %all-to-all-done = bf16[96,64,512]{2,1,0:T(8,128)(2,1)} async-done(((bf16[96,64,512]{2,1,0:T(8,128)(2,1)}), bf16[96,64,512]{2,1,0:T(8,128)(2,1)}, u32[]{:S(2)}, u32[]{:S(2)}) %all-to-all-start) | async-done | bytes 6291488 | tf_op jit(solution)/shard_map/all_to_all | solution.py:173
  399.9 13.4 %all-to-all-start.4 = ((bf16[32,1408,64]{1,2,0:T(8,128)(2,1)}), bf16[32,1408,64]{1,2,0:T(8,128)(2,1)}, u32[]{:S(2)}, u32[]{:S(2)}) async-start(bf16[32,1408,64]{1,2,0:T(8,128)(2,1)} %bitcast.592), calls=%async_computation.4 | async-start | bytes 11534336 | tf_op jit(solution)/shard_map/all_to_all | solution.py:173
  413.3 6.4 constant_dynamic-slice_fusion.18
  435.0 4.6 copy.263
  439.6 6.6 copy.264
  482.2 8.6 all-to-all-done.4
  490.8 12.4 %all-to-all-start.3 = ((bf16[64,64,1408]{2,1,0:T(8,128)(2,1)}), bf16[64,64,1408]{2,1,0:T(8,128)(2,1)}, u32[]{:S(2)}, u32[]{:S(2)}) async-start(bf16[64,64,1408]{2,1,0:T(8,128)(2,1)} %constant_dynamic-update-slice_fusion.70), calls=%async_computation.3 | async-start | bytes 23068672 | tf_op jit(solution)/shard_map/all_to_all | solution.py:173
  547.3 4.6 constant_dynamic-slice_fusion.11
  560.7 55.2 %collective-permute-done.7 = f32[2,64,2048]{2,1,0:T(8,128)} collective-permute-done((f32[2,64,2048]{2,1,0:T(8,128)}, f32[2,64,2048]{2,1,0:T(8,128)}, u32[]{:S(2)}, u32[]{:S(2)}) %collective-permute-start.7) | collective-permute-done | bytes 1048608 | tf_op jit(solution)/shard_map/ppermute | solution.py:124
  617.8 5.8 fusion.111
  623.8 35.7 %collective-permute-done.8 = bf16[2,64,2048]{2,1,0:T(8,128)(2,1)S(1)} collective-permute-done((bf16[2,64,2048]{2,1,0:T(8,128)(2,1)S(1)}, bf16[2,64,2048]{2,1,0:T(8,128)(2,1)S(1)}, u32[]{:S(2)}, u32[]{:S(2)}) %collective-permute-start.8) | collective-permute-done | bytes 524320 | tf_op jit(solution)/shard_map/ppermute | solution.py:106
  659.7 10.1 collective-permute-start.9
  676.7 16.9 %all-to-all-done.3 = bf16[64,64,1408]{2,1,0:T(8,128)(2,1)} async-done(((bf16[64,64,1408]{2,1,0:T(8,128)(2,1)}), bf16[64,64,1408]{2,1,0:T(8,128)(2,1)}, u32[]{:S(2)}, u32[]{:S(2)}) %all-to-all-start.3) | async-done | bytes 11534368 | tf_op jit(solution)/shard_map/all_to_all | solution.py:173
  693.6 10.1 copy.427
  703.7 9.5 fusion.95
  713.2 6.5 fusion.107
  736.2 5.7 fusion.109
  749.6 6.4 collective-permute-start.14
  763.1 7.4 copy.306
  770.5 7.0 copy.314
  777.5 7.0 reshape_reshape.22
  784.4 7.0 reshape_reshape.25
  795.2 7.0 copy.309
  802.2 7.0 reshape_reshape.23
  825.7 19.9 %collective-permute-done.15 = f32[2,64,2048]{2,1,0:T(8,128)S(1)} collective-permute-done((f32[2,64,2048]{2,1,0:T(8,128)S(1)}, f32[2,64,2048]{2,1,0:T(8,128)S(1)}, u32[]{:S(2)}, u32[]{:S(2)}) %collective-permute-start.15) | collective-permute-done | bytes 1048608 | tf_op jit(solution)/shard_map/ppermute | solution.py:124
  845.9 22.2 %collective-permute-done.11 = f32[2,64,2048]{2,1,0:T(8,128)S(1)} collective-permute-done((f32[2,64,2048]{2,1,0:T(8,128)S(1)}, f32[2,64,2048]{2,1,0:T(8,128)S(1)}, u32[]{:S(2)}, u32[]{:S(2)}) %collective-permute-start.11) | collective-permute-done | bytes 1048608 | tf_op jit(solution)/shard_map/ppermute | solution.py:124
  879.7 5.9 collective-permute-done.16
  952.7 5.0 copy.312
  957.7 5.0 fusion.115
  983.0 14.7 %all-to-all-start.6 = ((bf16[32,2,12544]{2,1,0:T(2,128)(2,1)}), bf16[32,2,12544]{2,1,0:T(2,128)(2,1)}, u32[]{:S(2)}, u32[]{:S(2)}) async-start(bf16[32,2,12544]{2,1,0:T(2,128)(2,1)} %reshape.910), calls=%async_computation.6 | async-start | bytes 3211264 | tf_op jit(solution)/shard_map/all_to_all | solution.py:386
  1001.2 6.3 reshape_reshape.24
  1012.9 5.3 add_add_fusion
  1035.9 5.3 dynamic_update_slice.36
  1042.5 5.3 dynamic_update_slice.37
  1054.7 7.8 all-to-all-start.5
  1069.8 9.4 reshape.911
  1079.3 5.3 convert_reduce_fusion
  1094.5 16.6 %collective-permute-done.19 = f32[2,64,2048]{2,1,0:T(8,128)} collective-permute-done((f32[2,64,2048]{2,1,0:T(8,128)}, f32[2,64,2048]{2,1,0:T(8,128)}, u32[]{:S(2)}, u32[]{:S(2)}) %collective-permute-start.19) | collective-permute-done | bytes 1048608 | tf_op jit(solution)/shard_map/ppermute | solution.py:124
  (729 shorter events, 436.8 us)
Async XLA Ops:
  0.6 79.0 %collective-permute-start.2 = (bf16[5,16,128]{2,1,0:T(8,128)(2,1)}, bf16[5,16,128]{2,1,0:T(8,128)(2,1)S(1)}, u32[]{:S(2)}, u32[]{:S(2)}) collective-permute-start(bf16[5,16,128]{2,1,0:T(8,128)(2,1)} %param.30), channel_id=1, source_target_pairs={{0,2},{1,3},{2,0},{3,1},{4,6},{5,7},{6,4},{7,5},{8,10},{9,11},{10,... | collective-permute-start | bytes 61448 | tf_op jit(solution)/shard_map/ppermute | solution.py:106
  5.1 72.3 %collective-permute-start.4 = (bf16[2,128,16]{1,2,0:T(8,128)(2,1)}, bf16[2,128,16]{1,2,0:T(8,128)(2,1)S(1)}, u32[]{:S(2)}, u32[]{:S(2)}) collective-permute-start(bf16[2,128,16]{1,2,0:T(8,128)(2,1)} %param.35), channel_id=1, source_target_pairs={{0,2},{1,3},{2,0},{3,1},{4,6},{5,7},{6,4},{7,5},{8,10},{9,11},{10,... | collective-permute-start | bytes 24584 | tf_op jit(solution)/shard_map/ppermute | solution.py:106
  6.5 325.9 %copy-start.115 = (f32[2,64]{1,0:T(2,128)}, f32[2,64]{1,0:T(2,128)S(1)}, u32[]{:S(2)}) copy-start(f32[2,64]{1,0:T(2,128)S(1)} %fusion.70) | copy-start | bytes 1540
  8.5 320.3 %collective-permute-start = (bf16[2,64,2048]{2,1,0:T(8,128)(2,1)}, bf16[2,64,2048]{2,1,0:T(8,128)(2,1)S(1)}, u32[]{:S(2)}, u32[]{:S(2)}) collective-permute-start(bf16[2,64,2048]{2,1,0:T(8,128)(2,1)} %fusion.20), channel_id=1, source_target_pairs={{0,2},{1,3},{2,0},{3,1},{4,6},{5,7},{6,4},{7,5},{8,10},{9,11},{10,... | collective-permute-start | bytes 1572872 | tf_op jit(solution)/shard_map/ppermute | solution.py:106
  21.8 177.6 %all-to-all-start.2 = ((bf16[32,512,64]{1,2,0:T(8,128)(2,1)}), bf16[32,512,64]{1,2,0:T(8,128)(2,1)S(1)}, u32[]{:S(2)}, u32[]{:S(2)}) async-start(bf16[32,512,64]{1,2,0:T(8,128)(2,1)} %bitcast.626), calls=%async_computation.2 | async-start | bytes 4194304 | tf_op jit(solution)/shard_map/all_to_all | solution.py:173
  29.4 488.4 %collective-permute-start.12 = (bf16[2,64,2048]{2,1,0:T(8,128)(2,1)}, bf16[2,64,2048]{2,1,0:T(8,128)(2,1)}, u32[]{:S(2)}, u32[]{:S(2)}) collective-permute-start(bf16[2,64,2048]{2,1,0:T(8,128)(2,1)} %param.19), channel_id=1, source_target_pairs={{0,2},{1,3},{2,0},{3,1},{4,6},{5,7},{6,4},{7,5},{8,10},{9,11},{10,... | collective-permute-start | bytes 1572872 | tf_op jit(solution)/shard_map/ppermute | solution.py:106
  77.4 3.0 collective-permute-start.5
  80.3 1.6 collective-permute-start.3
  200.7 96.2 %all-to-all-start.1 = ((bf16[32,2,41216]{2,1,0:T(2,128)(2,1)}), bf16[32,2,41216]{2,1,0:T(2,128)(2,1)}, u32[]{:S(2)}, u32[]{:S(2)}) async-start(bf16[32,2,41216]{2,1,0:T(2,128)(2,1)} %reshape.908), calls=%async_computation.1 | async-start | bytes 10551296 | tf_op jit(solution)/shard_map/all_to_all | solution.py:173
  296.9 103.0 %all-to-all-start = ((bf16[96,64,512]{2,1,0:T(8,128)(2,1)}), bf16[96,64,512]{2,1,0:T(8,128)(2,1)}, u32[]{:S(2)}, u32[]{:S(2)}) async-start(bf16[96,64,512]{2,1,0:T(8,128)(2,1)} %constant_dynamic-update-slice_fusion), calls=%async_computation | async-start | bytes 12582912 | tf_op jit(solution)/shard_map/all_to_all | solution.py:173
  329.0 4.3 collective-permute-start.1
  335.3 131.5 %copy-start.4 = (bf16[2,4,64,2048]{3,2,1,0:T(8,128)(2,1)}, bf16[2,4,64,2048]{3,2,1,0:T(8,128)(2,1)S(1)}, u32[]{:S(2)}) copy-start(bf16[2,4,64,2048]{3,2,1,0:T(8,128)(2,1)S(1)} %copy.242) | copy-start | bytes 6291460
  399.9 90.9 %all-to-all-start.4 = ((bf16[32,1408,64]{1,2,0:T(8,128)(2,1)}), bf16[32,1408,64]{1,2,0:T(8,128)(2,1)}, u32[]{:S(2)}, u32[]{:S(2)}) async-start(bf16[32,1408,64]{1,2,0:T(8,128)(2,1)} %bitcast.592), calls=%async_computation.4 | async-start | bytes 11534336 | tf_op jit(solution)/shard_map/all_to_all | solution.py:173
  428.7 129.5 %copy-start.6 = (bf16[5,2048,16]{1,2,0:T(8,128)(2,1)}, bf16[5,2048,16]{1,2,0:T(8,128)(2,1)S(1)}, u32[]{:S(2)}) copy-start(bf16[5,2048,16]{1,2,0:T(8,128)(2,1)S(1)} %copy.249) | copy-start | bytes 983044
  429.2 75.8 %copy-start.77 = (bf16[2,3,16,512]{3,2,0,1:T(8,128)(2,1)}, bf16[2,3,16,512]{3,2,0,1:T(8,128)(2,1)S(1)}, u32[]{:S(2)}) copy-start(bf16[2,3,16,512]{3,2,0,1:T(8,128)(2,1)S(1)} %reshape.859) | copy-start | bytes 294916
  435.0 72.3 %copy-start.94 = (bf16[2,512,16]{1,2,0:T(8,128)(2,1)}, bf16[2,512,16]{1,2,0:T(8,128)(2,1)S(1)}, u32[]{:S(2)}) copy-start(bf16[2,512,16]{1,2,0:T(8,128)(2,1)S(1)} %reshape.864) | copy-start | bytes 98308
  451.4 106.8 %copy-start.56 = (bf16[2,16,2048]{2,1,0:T(8,128)(2,1)}, bf16[2,16,2048]{2,1,0:T(8,128)(2,1)S(1)}, u32[]{:S(2)}) copy-start(bf16[2,16,2048]{2,1,0:T(8,128)(2,1)S(1)} %copy.265) | copy-start | bytes 393220
  453.0 105.2 %copy-start.59 = (bf16[2,16,2048]{2,1,0:T(8,128)(2,1)}, bf16[2,16,2048]{2,1,0:T(8,128)(2,1)S(1)}, u32[]{:S(2)}) copy-start(bf16[2,16,2048]{2,1,0:T(8,128)(2,1)S(1)} %copy.266) | copy-start | bytes 393220
  453.7 51.4 %copy-start.92 = (f32[2,256,16]{1,2,0:T(8,128)}, f32[2,256,16]{1,2,0:T(8,128)S(1)}, u32[]{:S(2)}) copy-start(f32[2,256,16]{1,2,0:T(8,128)S(1)} %fusion.86) | copy-start | bytes 98308
  490.8 202.8 %all-to-all-start.3 = ((bf16[64,64,1408]{2,1,0:T(8,128)(2,1)}), bf16[64,64,1408]{2,1,0:T(8,128)(2,1)}, u32[]{:S(2)}, u32[]{:S(2)}) async-start(bf16[64,64,1408]{2,1,0:T(8,128)(2,1)} %constant_dynamic-update-slice_fusion.70), calls=%async_computation.3 | async-start | bytes 23068672 | tf_op jit(solution)/shard_map/all_to_all | solution.py:173
  514.2 20.9 %collective-permute-start.6 = (f32[2,2,64,2048]{3,2,1,0:T(8,128)}, f32[2,2,64,2048]{3,2,1,0:T(8,128)}, u32[]{:S(2)}, u32[]{:S(2)}) collective-permute-start(f32[2,2,64,2048]{3,2,1,0:T(8,128)} %bitcast.561), channel_id=1, source_target_pairs={{0,1},{1,0},{2,3},{3,2},{4,5},{5,4},{6,7},{7,6},{8,9},{9,8},{10,11... | collective-permute-start | bytes 6291464 | tf_op jit(solution)/shard_map/ppermute | solution.py:121
  520.5 3.0 collective-permute-start.13
  540.0 75.9 %collective-permute-start.7 = (f32[2,64,2048]{2,1,0:T(8,128)}, f32[2,64,2048]{2,1,0:T(8,128)}, u32[]{:S(2)}, u32[]{:S(2)}) collective-permute-start(f32[2,64,2048]{2,1,0:T(8,128)} %dynamic-slice_bitcast_fusion.3), channel_id=1, source_target_pairs={{0,2},{1,3},{2,0},{3,1},{4,6},{5,7},{6,4},{7,5},{8,10},{9,11},{10,... | collective-permute-start | bytes 3145736 | tf_op jit(solution)/shard_map/ppermute | solution.py:124
  558.2 57.7 %copy-start.28 = (f32[2,2,64,2048]{3,2,1,0:T(8,128)S(1)}, f32[2,2,64,2048]{3,2,1,0:T(8,128)}, u32[]{:S(2)}) copy-start(f32[2,2,64,2048]{3,2,1,0:T(8,128)} %copy-done.27) | copy-start | bytes 6291460
  558.2 117.9 %copy-start.72 = (bf16[2,2048,16]{1,2,0:T(8,128)(2,1)}, bf16[2,2048,16]{1,2,0:T(8,128)(2,1)S(1)}, u32[]{:S(2)}) copy-start(bf16[2,2048,16]{1,2,0:T(8,128)(2,1)S(1)} %fusion.61) | copy-start | bytes 393220
  558.3 59.3 %copy-start.106 = (f32[2048]{0:T(1024)S(1)}, f32[2048]{0:T(1024)}, u32[]{:S(2)}) copy-start(f32[2048]{0:T(1024)} %param.27) | copy-start | bytes 24580
  560.6 109.1 %copy-start.90 = (f32[2,256,16]{1,2,0:T(8,128)}, f32[2,256,16]{1,2,0:T(8,128)S(1)}, u32[]{:S(2)}) copy-start(f32[2,256,16]{1,2,0:T(8,128)S(1)} %convolution_multiply_fusion.15) | copy-start | bytes 98308
  560.6 57.2 %copy-start.33 = (bf16[2,4,64,2048]{3,2,1,0:T(8,128)(2,1)S(1)}, bf16[2,4,64,2048]{3,2,1,0:T(8,128)(2,1)}, u32[]{:S(2)}) copy-start(bf16[2,4,64,2048]{3,2,1,0:T(8,128)(2,1)} %copy.283) | copy-start | bytes 6291460
  617.5 55.2 %copy-start.117 = (f32[2,64]{1,0:T(2,128)}, f32[2,64]{1,0:T(2,128)S(1)}, u32[]{:S(2)}) copy-start(f32[2,64]{1,0:T(2,128)S(1)} %fusion.71) | copy-start | bytes 1540
  617.7 41.8 %collective-permute-start.8 = (bf16[2,64,2048]{2,1,0:T(8,128)(2,1)S(1)}, bf16[2,64,2048]{2,1,0:T(8,128)(2,1)S(1)}, u32[]{:S(2)}, u32[]{:S(2)}) collective-permute-start(bf16[2,64,2048]{2,1,0:T(8,128)(2,1)S(1)} %multiply_convert_fusion.3), channel_id=1, source_target_pairs={{0,2},{1,3},{2,0},{3,1},{4,6},{5,7},{6,4},{7,5},{8,10},{9,11},{10,... | collective-permute-start | bytes 1572872 | tf_op jit(solution)/shard_map/ppermute | solution.py:106
  659.7 13.4 %collective-permute-start.9 = (bf16[2,2,64,2048]{3,2,1,0:T(8,128)(2,1)S(1)}, bf16[2,2,64,2048]{3,2,1,0:T(8,128)(2,1)S(1)}, u32[]{:S(2)}, u32[]{:S(2)}) collective-permute-start(bf16[2,2,64,2048]{3,2,1,0:T(8,128)(2,1)S(1)} %maximum_select_fusion.6), channel_id=1, source_target_pairs={{0,1},{1,0},{2,3},{3,2},{4,5},{5,4},{6,7},{7,6},{8,9},{9,8},{10,11... | collective-permute-start | bytes 3145736 | tf_op jit(solution)/shard_map/ppermute | solution.py:108
  749.6 66.9 %collective-permute-start.14 = (f32[2,2,64,2048]{3,2,1,0:T(8,128)}, f32[2,2,64,2048]{3,2,1,0:T(8,128)}, u32[]{:S(2)}, u32[]{:S(2)}) collective-permute-start(f32[2,2,64,2048]{3,2,1,0:T(8,128)} %bitcast.559), channel_id=1, source_target_pairs={{0,1},{1,0},{2,3},{3,2},{4,5},{5,4},{6,7},{7,6},{8,9},{9,8},{10,11... | collective-permute-start | bytes 6291464 | tf_op jit(solution)/shard_map/ppermute | solution.py:121
  756.5 54.7 %copy-start.79 = (f32[2,256,16]{1,2,0:T(8,128)}, f32[2,256,16]{1,2,0:T(8,128)S(1)}, u32[]{:S(2)}) copy-start(f32[2,256,16]{1,2,0:T(8,128)S(1)} %fusion.110) | copy-start | bytes 98308
  761.9 60.2 %collective-permute-start.10 = (f32[2,2,64,2048]{3,2,1,0:T(8,128)}, f32[2,2,64,2048]{3,2,1,0:T(8,128)}, u32[]{:S(2)}, u32[]{:S(2)}) collective-permute-start(f32[2,2,64,2048]{3,2,1,0:T(8,128)} %bitcast.560), channel_id=1, source_target_pairs={{0,1},{1,0},{2,3},{3,2},{4,5},{5,4},{6,7},{7,6},{8,9},{9,8},{10,11... | collective-permute-start | bytes 6291464 | tf_op jit(solution)/shard_map/ppermute | solution.py:121
  811.8 77.9 %collective-permute-start.22 = (f32[2,2,256,16]{2,3,1,0:T(8,128)}, f32[2,2,256,16]{2,3,1,0:T(8,128)}, u32[]{:S(2)}, u32[]{:S(2)}) collective-permute-start(f32[2,2,256,16]{2,3,1,0:T(8,128)} %pad_maximum_fusion.9), channel_id=1, source_target_pairs={{0,1},{1,0},{2,3},{3,2},{4,5},{5,4},{6,7},{7,6},{8,9},{9,8},{10,11... | collective-permute-start | bytes 196616 | tf_op jit(solution)/shard_map/ppermute | solution.py:129
  814.4 59.2 %copy-start.66 = (f32[2,1,16,1408]{3,2,0,1:T(8,128)}, f32[2,1,16,1408]{3,2,0,1:T(8,128)S(1)}, u32[]{:S(2)}) copy-start(f32[2,1,16,1408]{3,2,0,1:T(8,128)S(1)} %fusion.7) | copy-start | bytes 540676
  818.7 26.9 %collective-permute-start.15 = (f32[2,64,2048]{2,1,0:T(8,128)S(1)}, f32[2,64,2048]{2,1,0:T(8,128)S(1)}, u32[]{:S(2)}, u32[]{:S(2)}) collective-permute-start(f32[2,64,2048]{2,1,0:T(8,128)S(1)} %dynamic-slice_bitcast_fusion.1), channel_id=1, source_target_pairs={{0,2},{1,3},{2,0},{3,1},{4,6},{5,7},{6,4},{7,5},{8,10},{9,11},{10,... | collective-permute-start | bytes 3145736 | tf_op jit(solution)/shard_map/ppermute | solution.py:124
  824.2 43.9 %collective-permute-start.11 = (f32[2,64,2048]{2,1,0:T(8,128)S(1)}, f32[2,64,2048]{2,1,0:T(8,128)S(1)}, u32[]{:S(2)}, u32[]{:S(2)}) collective-permute-start(f32[2,64,2048]{2,1,0:T(8,128)S(1)} %dynamic-slice_bitcast_fusion.2), channel_id=1, source_target_pairs={{0,2},{1,3},{2,0},{3,1},{4,6},{5,7},{6,4},{7,5},{8,10},{9,11},{10,... | collective-permute-start | bytes 3145736 | tf_op jit(solution)/shard_map/ppermute | solution.py:124
  825.0 48.6 %copy-start.68 = (f32[2,1,16,1408]{3,2,0,1:T(8,128)}, f32[2,1,16,1408]{3,2,0,1:T(8,128)S(1)}, u32[]{:S(2)}) copy-start(f32[2,1,16,1408]{3,2,0,1:T(8,128)S(1)} %fusion.6) | copy-start | bytes 540676
  870.9 14.7 %collective-permute-start.16 = (bf16[2,64,2048]{2,1,0:T(8,128)(2,1)}, bf16[2,64,2048]{2,1,0:T(8,128)(2,1)}, u32[]{:S(2)}, u32[]{:S(2)}) collective-permute-start(bf16[2,64,2048]{2,1,0:T(8,128)(2,1)} %get-tuple-element.34), channel_id=1, source_target_pairs={{0,2},{1,3},{2,0},{3,1},{4,6},{5,7},{6,4},{7,5},{8,10},{9,11},{10,... | collective-permute-start | bytes 1572872 | tf_op jit(solution)/shard_map/ppermute | solution.py:106
  888.3 30.3 %collective-permute-start.17 = (bf16[2,2,64,2048]{3,2,1,0:T(8,128)(2,1)}, bf16[2,2,64,2048]{3,2,1,0:T(8,128)(2,1)}, u32[]{:S(2)}, u32[]{:S(2)}) collective-permute-start(bf16[2,2,64,2048]{3,2,1,0:T(8,128)(2,1)} %maximum_select_fusion.9), channel_id=1, source_target_pairs={{0,1},{1,0},{2,3},{3,2},{4,5},{5,4},{6,7},{7,6},{8,9},{9,8},{10,11... | collective-permute-start | bytes 3145736 | tf_op jit(solution)/shard_map/ppermute | solution.py:108
  891.2 22.9 %collective-permute-start.23 = (f32[2,2,256,16]{2,3,1,0:T(8,128)}, f32[2,2,256,16]{2,3,1,0:T(8,128)}, u32[]{:S(2)}, u32[]{:S(2)}) collective-permute-start(f32[2,2,256,16]{2,3,1,0:T(8,128)} %fusion.74), channel_id=1, source_target_pairs={{0,2},{1,3},{2,0},{3,1},{4,6},{5,7},{6,4},{7,5},{8,10},{9,11},{10,... | collective-permute-start | bytes 196616 | tf_op jit(solution)/shard_map/ppermute | solution.py:130
  983.0 71.6 %all-to-all-start.6 = ((bf16[32,2,12544]{2,1,0:T(2,128)(2,1)}), bf16[32,2,12544]{2,1,0:T(2,128)(2,1)}, u32[]{:S(2)}, u32[]{:S(2)}) async-start(bf16[32,2,12544]{2,1,0:T(2,128)(2,1)} %reshape.910), calls=%async_computation.6 | async-start | bytes 3211264 | tf_op jit(solution)/shard_map/all_to_all | solution.py:386
  1000.6 20.9 %collective-permute-start.20 = (f32[5,2,256,16]{2,3,1,0:T(8,128)}, f32[5,2,256,16]{2,3,1,0:T(8,128)S(1)}, u32[]{:S(2)}, u32[]{:S(2)}) collective-permute-start(f32[5,2,256,16]{2,3,1,0:T(8,128)} %constant_dynamic-update-slice_fusion.134), channel_id=1, source_target_pairs={{0,1},{1,0},{2,3},{3,2},{4,5},{5,4},{6,7},{7,6},{8,9},{9,8},{10,11... | collective-permute-start | bytes 491528 | tf_op jit(solution)/shard_map/ppermute | solution.py:129
  1022.4 7.6 collective-permute-start.21
  1029.6 32.9 %collective-permute-start.18 = (f32[2,2,64,2048]{3,2,1,0:T(8,128)}, f32[2,2,64,2048]{3,2,1,0:T(8,128)}, u32[]{:S(2)}, u32[]{:S(2)}) collective-permute-start(f32[2,2,64,2048]{3,2,1,0:T(8,128)} %bitcast.558), channel_id=1, source_target_pairs={{0,1},{1,0},{2,3},{3,2},{4,5},{5,4},{6,7},{7,6},{8,9},{9,8},{10,11... | collective-permute-start | bytes 6291464 | tf_op jit(solution)/shard_map/ppermute | solution.py:121
  1054.7 35.9 %all-to-all-start.5 = ((f32[32,1,14336]{2,1,0:T(1,128)}), f32[32,1,14336]{2,1,0:T(1,128)}, u32[]{:S(2)}, u32[]{:S(2)}) async-start(f32[32,1,14336]{2,1,0:T(1,128)} %all_to_all.82), calls=%async_computation.5 | async-start | bytes 3670016 | tf_op jit(solution)/shard_map/all_to_all | solution.py:368
  1066.0 45.1 %collective-permute-start.19 = (f32[2,64,2048]{2,1,0:T(8,128)}, f32[2,64,2048]{2,1,0:T(8,128)}, u32[]{:S(2)}, u32[]{:S(2)}) collective-permute-start(f32[2,64,2048]{2,1,0:T(8,128)} %dynamic-slice_bitcast_fusion), channel_id=1, source_target_pairs={{0,2},{1,3},{2,0},{3,1},{4,6},{5,7},{6,4},{7,5},{8,10},{9,11},{10,... | collective-permute-start | bytes 3145736 | tf_op jit(solution)/shard_map/ppermute | solution.py:124
  (118 other events, 905.3 us)

commit v3 on v2

--- a/solution.py
+++ b/solution.py
@@ -172,23 +172,29 @@
         tiled_in = jnp.concatenate([values] * fsdp_count, axis=0)
         return lax.all_to_all(tiled_in, "fsdp", 0, axis, tiled=True)
 
-    a_in_tok = tok_gather(a_in)
-    b_rows_tok = tok_gather(b_rows)
-    small = [b_qkv, b_gateup, a_out, a_down, a_in_tok, b_rows_tok]
-    small_flat = jnp.concatenate([p.reshape(1, -1) for p in small], axis=1)
-    small_all = fsdp_gather(small_flat, 0)
-    unpacked = []
-    start = 0
-    for p in small:
-        unpacked.append(small_all[:, start : start + p.size].reshape((fsdp_count,) + p.shape))
-        start += p.size
-    (g_bqkv, g_bgateup, g_aout, g_adown, g_ain, g_brows) = unpacked
+    def packed_gather(small, axes):
+        count = 1
+        for name in axes:
+            count *= lax.axis_size(name)
+        flat = jnp.concatenate([p.reshape(-1, COLS) for p in small], axis=0)
+        tiled_in = jnp.broadcast_to(flat[None], (count,) + flat.shape).reshape(-1, COLS)
+        got = lax.all_to_all(tiled_in, axes, 0, 0, tiled=True).reshape((count,) + flat.shape)
+        out = []
+        start = 0
+        for p in small:
+            rows = p.size // COLS
+            out.append(got[:, start : start + rows].reshape((count,) + p.shape))
+            start += rows
+        return out
+
     w_qkv_full = fsdp_gather(w_qkv, 1)
+    g_ain, g_brows = packed_gather([a_in, b_rows], ("fsdp", "tok"))
+    g_bqkv, g_bgateup, g_aout, g_adown = packed_gather([b_qkv, b_gateup, a_out, a_down], ("fsdp",))
     w_out_full = fsdp_gather(w_out, 1)
     w_gateup_full = fsdp_gather(w_gateup, 1)
     w_down_full = fsdp_gather(w_down, 1)
-    a_in_full = jnp.transpose(g_ain, (2, 0, 1, 3, 4)).reshape(5, D, COLS)
-    b_rows_full = jnp.transpose(g_brows, (2, 3, 0, 1, 4)).reshape(2, COLS, D)
+    a_in_full = jnp.moveaxis(g_ain, 0, 1).reshape(5, D, COLS)
+    b_rows_full = jnp.moveaxis(g_brows, 0, 2).reshape(2, COLS, D)
 
     def pick_cols(values, axis):
         return jnp.stack(

time: 1130 us -> 1010 us (0.89)
  other arithmetic: 182 us -> 87.9 us
  local copies, waits for them, and re-layouts: 404 us -> 328 us
  waiting for transfers between devices: 288 us -> 339 us
    concatenate x2, other arithmetic: 99.4 us -> 0.01 us  [packed_gather(): flat = jnp.concatenate([p.reshape(-1, COLS) for p in small], axis=0)]
    unnamed x416 -> x405, local copies, waits for them, and re-layouts: 148 us -> 99.8 us
    all_to_all x0 -> x2, waiting for transfers between devices: none -> 34.3 us  [packed_gather(): lax.all_to_all(tiled_in, axes, 0, 0, tiled=True)]
    all_to_all x5 -> x4, waiting for transfers between devices: 129 us -> 106 us  [fsdp_gather(): return lax.all_to_all(tiled_in, 'fsdp', 0, axis, tiled=True)]
    ppermute x6 -> x4, waiting for transfers between devices: 41.7 us -> 64.5 us  [tok_gather(): far = lax.ppermute(values, 'tok', xor_pairs(count, 2))]
    ppermute x4, waiting for transfers between devices: 114 us -> 135 us  [tok_scatter(): return keep + lax.ppermute(send, 'tok', xor_pairs(count, 2))]
    all_to_all x0 -> x2, starting transfers between devices: none -> 15.4 us  [packed_gather(): lax.all_to_all(tiled_in, axes, 0, 0, tiled=True)]
    all_to_all x5 -> x4, starting transfers between devices: 50.1 us -> 35.7 us  [fsdp_gather(): return lax.all_to_all(tiled_in, 'fsdp', 0, axis, tiled=True)]
  transfers between devices with their start and end apart: 31 -> 28, of which waited for: 13 -> 11; matrix products, arithmetic and copies ran while one was open for 50% -> 38% of each run, Pallas kernels for 0% -> 0%
where the time goes in v3:
time: 1010 us; the launch traced here: 998 us
  waiting for transfers between devices  339 us (34%)
  local copies, waits for them, and re-layouts  328 us (32%)
  starting transfers between devices  128 us (13%)
  matrix products  107 us (11%)
  other arithmetic  87.9 us (9%)
    ppermute x4, waiting for transfers between devices, tok_scatter(): return keep + lax.ppermute(send, 'tok', xor_pairs(count, 2))  135 us
    all_to_all x4, waiting for transfers between devices, fsdp_gather(): return lax.all_to_all(tiled_in, 'fsdp', 0, axis, tiled=True)  106 us
    unnamed x405, local copies, waits for them, and re-layouts  99.8 us
    ppermute x4, waiting for transfers between devices, tok_gather(): far = lax.ppermute(values, 'tok', xor_pairs(count, 2))  64.5 us
    dot_general x32, matrix products, hp_dot(): jnp.einsum(spec, left, right, precision=highest, preferred_element_type=j...  49.7 us
    all_to_all x4, starting transfers between devices, fsdp_gather(): return lax.all_to_all(tiled_in, 'fsdp', 0, axis, tiled=True)  35.7 us
    all_to_all x2, waiting for transfers between devices, packed_gather(): lax.all_to_all(tiled_in, axes, 0, 0, tiled=True)  34.3 us
    transpose x8, local copies, waits for them, and re-layouts, gather_rows(): return jnp.moveaxis(full, 0, 1).reshape(seqs, length, values.shape[-1])  27.2 us
  transfers between devices with their start and end apart: 28, of which 11 were waited for; matrix products, arithmetic and copies ran while one was open for 38% of the time, Pallas kernels for 0%

profile of v3, /device:TPU:1, one launch (start us, length us, event | category | flops | bytes accessed | tf_op | source)
XLA Modules:
  0.0 998.4 jit_solution(11815561919948838286)
XLA Ops:
  4.4 4.4 collective-permute-start
  14.3 7.5 all-to-all-start.2
  65.3 7.7 all-to-all-start.3
  78.4 21.1 %all-to-all-done.3 = bf16[32,512,64]{1,2,0:T(8,128)(2,1)S(1)} async-done(((bf16[32,512,64]{1,2,0:T(8,128)(2,1)}), bf16[32,512,64]{1,2,0:T(8,128)(2,1)S(1)}, u32[]{:S(2)}, u32[]{:S(2)}) %all-to-all-start.3) | async-done | bytes 2097184 | tf_op jit(solution)/shard_map/all_to_all | solution.py:173
  103.1 7.9 all-to-all-start.1
  123.2 34.3 %all-to-all-done.1 = bf16[128,112,128]{2,1,0:T(8,128)(2,1)} async-done(((bf16[128,112,128]{2,1,0:T(8,128)(2,1)}), bf16[128,112,128]{2,1,0:T(8,128)(2,1)}, u32[]{:S(2)}, u32[]{:S(2)}) %all-to-all-start.1) | async-done | bytes 3670048 | tf_op jit(solution)/shard_map/all_to_all | solution.py:181
  157.5 5.2 all-to-all-start
  180.3 6.0 copy.426
  197.8 64.4 %all-to-all-done = bf16[96,64,512]{2,1,0:T(8,128)(2,1)} async-done(((bf16[96,64,512]{2,1,0:T(8,128)(2,1)}), bf16[96,64,512]{2,1,0:T(8,128)(2,1)}, u32[]{:S(2)}, u32[]{:S(2)}) %all-to-all-start) | async-done | bytes 6291488 | tf_op jit(solution)/shard_map/all_to_all | solution.py:173
  262.3 8.1 all-to-all-start.5
  276.3 3.8 constant_dynamic-slice_fusion.18
  292.6 3.5 constant_dynamic-slice_fusion.14
  301.2 3.6 copy.425
  328.7 20.5 %all-to-all-done.5 = bf16[32,1408,64]{1,2,0:T(8,128)(2,1)} async-done(((bf16[32,1408,64]{1,2,0:T(8,128)(2,1)}), bf16[32,1408,64]{1,2,0:T(8,128)(2,1)}, u32[]{:S(2)}, u32[]{:S(2)}) %all-to-all-start.5) | async-done | bytes 5767200 | tf_op jit(solution)/shard_map/all_to_all | solution.py:173
  349.2 14.7 %all-to-all-start.4 = ((bf16[64,64,1408]{2,1,0:T(8,128)(2,1)}), bf16[64,64,1408]{2,1,0:T(8,128)(2,1)}, u32[]{:S(2)}, u32[]{:S(2)}) async-start(bf16[64,64,1408]{2,1,0:T(8,128)(2,1)} %constant_dynamic-update-slice_fusion.64), calls=%async_computation.4 | async-start | bytes 23068672 | tf_op jit(solution)/shard_map/all_to_all | solution.py:173
  378.0 10.6 %collective-permute-start.8 = (bf16[2,64,2048]{2,1,0:T(8,128)(2,1)}, bf16[2,64,2048]{2,1,0:T(8,128)(2,1)}, u32[]{:S(2)}, u32[]{:S(2)}) collective-permute-start(bf16[2,64,2048]{2,1,0:T(8,128)(2,1)} %param.19), channel_id=1, source_target_pairs={{0,2},{1,3},{2,0},{3,1},{4,6},{5,7},{6,4},{7,5},{8,10},{9,11},{10,... | collective-permute-start | bytes 1572872 | tf_op jit(solution)/shard_map/ppermute | solution.py:106
  388.6 49.7 %collective-permute-done.8 = bf16[2,64,2048]{2,1,0:T(8,128)(2,1)} collective-permute-done((bf16[2,64,2048]{2,1,0:T(8,128)(2,1)}, bf16[2,64,2048]{2,1,0:T(8,128)(2,1)}, u32[]{:S(2)}, u32[]{:S(2)}) %collective-permute-start.8) | collective-permute-done | bytes 524320 | tf_op jit(solution)/shard_map/ppermute | solution.py:106
  470.4 74.0 %collective-permute-done.3 = f32[2,64,2048]{2,1,0:T(8,128)} collective-permute-done((f32[2,64,2048]{2,1,0:T(8,128)}, f32[2,64,2048]{2,1,0:T(8,128)}, u32[]{:S(2)}, u32[]{:S(2)}) %collective-permute-start.3) | collective-permute-done | bytes 1048608 | tf_op jit(solution)/shard_map/ppermute | solution.py:124
  546.7 5.8 fusion.111
  552.7 8.6 collective-permute-done.4
  569.8 10.2 %copy.424 = bf16[32,2,64,1408]{3,2,0,1:T(8,128)(2,1)} copy(bf16[32,2,64,1408]{3,2,1,0:T(8,128)(2,1)} %bitcast.72) | data formatting | bytes 23068672 | tf_op jit(solution)/shard_map/all_to_all | solution.py:173
  580.0 9.3 fusion.95
  589.3 6.5 fusion.107
  612.3 5.9 fusion.109
  633.6 7.1 copy.306
  640.8 7.0 copy.314
  647.7 7.0 reshape_reshape.20
  654.7 7.0 reshape_reshape.23
  665.5 7.0 copy.309
  672.4 7.0 reshape_reshape.21
  688.5 16.3 %collective-permute-start.11 = (f32[2,64,2048]{2,1,0:T(8,128)S(1)}, f32[2,64,2048]{2,1,0:T(8,128)S(1)}, u32[]{:S(2)}, u32[]{:S(2)}) collective-permute-start(f32[2,64,2048]{2,1,0:T(8,128)S(1)} %dynamic-slice_bitcast_fusion.1), channel_id=1, source_target_pairs={{0,2},{1,3},{2,0},{3,1},{4,6},{5,7},{6,4},{7,5},{8,10},{9,11},{10,... | collective-permute-start | bytes 3145736 | tf_op jit(solution)/shard_map/ppermute | solution.py:124
  708.4 19.9 %collective-permute-done.11 = f32[2,64,2048]{2,1,0:T(8,128)S(1)} collective-permute-done((f32[2,64,2048]{2,1,0:T(8,128)S(1)}, f32[2,64,2048]{2,1,0:T(8,128)S(1)}, u32[]{:S(2)}, u32[]{:S(2)}) %collective-permute-start.11) | collective-permute-done | bytes 1048608 | tf_op jit(solution)/shard_map/ppermute | solution.py:124
  728.6 22.2 %collective-permute-done.7 = f32[2,64,2048]{2,1,0:T(8,128)S(1)} collective-permute-done((f32[2,64,2048]{2,1,0:T(8,128)S(1)}, f32[2,64,2048]{2,1,0:T(8,128)S(1)}, u32[]{:S(2)}, u32[]{:S(2)}) %collective-permute-start.7) | collective-permute-done | bytes 1048608 | tf_op jit(solution)/shard_map/ppermute | solution.py:124
  762.1 6.2 collective-permute-done.12
  826.3 3.9 multiply_add_fusion.5
  835.4 5.2 copy.312
  840.5 5.1 fusion.115
  866.2 14.5 %all-to-all-start.7 = ((bf16[32,2,12544]{2,1,0:T(2,128)(2,1)}), bf16[32,2,12544]{2,1,0:T(2,128)(2,1)}, u32[]{:S(2)}, u32[]{:S(2)}) async-start(bf16[32,2,12544]{2,1,0:T(2,128)(2,1)} %reshape.766), calls=%async_computation.7 | async-start | bytes 3211264 | tf_op jit(solution)/shard_map/all_to_all | solution.py:392
  884.2 6.1 reshape_reshape.22
  895.7 5.3 add_add_fusion
  918.7 4.6 dynamic_update_slice.36
  924.6 5.3 dynamic_update_slice.37
  930.0 4.1 copy.318
  936.7 8.5 all-to-all-start.6
  948.9 3.9 collective-permute-start.15
  952.7 9.5 reshape.767
  962.2 5.3 convert_reduce_fusion
  975.4 18.5 %collective-permute-done.15 = f32[2,64,2048]{2,1,0:T(8,128)} collective-permute-done((f32[2,64,2048]{2,1,0:T(8,128)}, f32[2,64,2048]{2,1,0:T(8,128)}, u32[]{:S(2)}, u32[]{:S(2)}) %collective-permute-start.15) | collective-permute-done | bytes 1048608 | tf_op jit(solution)/shard_map/ppermute | solution.py:124
  (708 shorter events, 389.7 us)
Async XLA Ops:
  2.4 185.2 %copy-start.116 = (f32[2,64]{1,0:T(2,128)}, f32[2,64]{1,0:T(2,128)S(1)}, u32[]{:S(2)}) copy-start(f32[2,64]{1,0:T(2,128)S(1)} %fusion.70) | copy-start | bytes 1540
  4.4 183.4 %collective-permute-start = (bf16[2,64,2048]{2,1,0:T(8,128)(2,1)}, bf16[2,64,2048]{2,1,0:T(8,128)(2,1)}, u32[]{:S(2)}, u32[]{:S(2)}) collective-permute-start(bf16[2,64,2048]{2,1,0:T(8,128)(2,1)} %fusion.20), channel_id=1, source_target_pairs={{0,2},{1,3},{2,0},{3,1},{4,6},{5,7},{6,4},{7,5},{8,10},{9,11},{10,... | collective-permute-start | bytes 1572872 | tf_op jit(solution)/shard_map/ppermute | solution.py:106
  14.3 49.8 %all-to-all-start.2 = ((bf16[32,196,128]{2,1,0:T(8,128)(2,1)}), bf16[32,196,128]{2,1,0:T(8,128)(2,1)S(1)}, u32[]{:S(2)}, u32[]{:S(2)}) async-start(bf16[32,196,128]{2,1,0:T(8,128)(2,1)} %broadcast_in_dim.35), calls=%async_computation.2 | async-start | bytes 3276800 | tf_op jit(solution)/shard_map/all_to_all | solution.py:181
  65.3 34.2 %all-to-all-start.3 = ((bf16[32,512,64]{1,2,0:T(8,128)(2,1)}), bf16[32,512,64]{1,2,0:T(8,128)(2,1)S(1)}, u32[]{:S(2)}, u32[]{:S(2)}) async-start(bf16[32,512,64]{1,2,0:T(8,128)(2,1)} %bitcast.600), calls=%async_computation.3 | async-start | bytes 4194304 | tf_op jit(solution)/shard_map/all_to_all | solution.py:173
  78.4 240.6 %copy-start.73 = (f32[256,64]{1,0:T(8,128)}, f32[256,64]{1,0:T(8,128)S(1)}, u32[]{:S(2)}) copy-start(f32[256,64]{1,0:T(8,128)S(1)} %get-tuple-element.83) | copy-start | bytes 196612
  78.4 240.6 %copy-start.74 = (f32[256,64]{1,0:T(8,128)}, f32[256,64]{1,0:T(8,128)S(1)}, u32[]{:S(2)}) copy-start(f32[256,64]{1,0:T(8,128)S(1)} %get-tuple-element.84) | copy-start | bytes 196612
  103.1 54.4 %all-to-all-start.1 = ((bf16[128,112,128]{2,1,0:T(8,128)(2,1)}), bf16[128,112,128]{2,1,0:T(8,128)(2,1)}, u32[]{:S(2)}, u32[]{:S(2)}) async-start(bf16[128,112,128]{2,1,0:T(8,128)(2,1)} %broadcast_in_dim.34), calls=%async_computation.1 | async-start | bytes 7340032 | tf_op jit(solution)/shard_map/all_to_all | solution.py:181
  157.5 104.8 %all-to-all-start = ((bf16[96,64,512]{2,1,0:T(8,128)(2,1)}), bf16[96,64,512]{2,1,0:T(8,128)(2,1)}, u32[]{:S(2)}, u32[]{:S(2)}) async-start(bf16[96,64,512]{2,1,0:T(8,128)(2,1)} %constant_dynamic-update-slice_fusion), calls=%async_computation | async-start | bytes 12582912 | tf_op jit(solution)/shard_map/all_to_all | solution.py:173
  190.2 80.3 %collective-permute-start.1 = (bf16[2,2,64,2048]{3,2,1,0:T(8,128)(2,1)}, bf16[2,2,64,2048]{3,2,1,0:T(8,128)(2,1)}, u32[]{:S(2)}, u32[]{:S(2)}) collective-permute-start(bf16[2,2,64,2048]{3,2,1,0:T(8,128)(2,1)} %maximum_select_fusion.4), channel_id=1, source_target_pairs={{0,1},{1,0},{2,3},{3,2},{4,5},{5,4},{6,7},{7,6},{8,9},{9,8},{10,11... | collective-permute-start | bytes 3145736 | tf_op jit(solution)/shard_map/ppermute | solution.py:108
  262.3 86.9 %all-to-all-start.5 = ((bf16[32,1408,64]{1,2,0:T(8,128)(2,1)}), bf16[32,1408,64]{1,2,0:T(8,128)(2,1)}, u32[]{:S(2)}, u32[]{:S(2)}) async-start(bf16[32,1408,64]{1,2,0:T(8,128)(2,1)} %bitcast.573), calls=%async_computation.5 | async-start | bytes 11534336 | tf_op jit(solution)/shard_map/all_to_all | solution.py:173
  270.5 95.3 %copy-start.80 = (bf16[2,3,16,512]{3,2,0,1:T(8,128)(2,1)}, bf16[2,3,16,512]{3,2,0,1:T(8,128)(2,1)S(1)}, u32[]{:S(2)}) copy-start(bf16[2,3,16,512]{3,2,0,1:T(8,128)(2,1)S(1)} %reshape.718) | copy-start | bytes 294916
  270.5 97.5 %copy-start.97 = (bf16[2,512,16]{1,2,0:T(8,128)(2,1)}, bf16[2,512,16]{1,2,0:T(8,128)(2,1)S(1)}, u32[]{:S(2)}) copy-start(bf16[2,512,16]{1,2,0:T(8,128)(2,1)S(1)} %reshape.723) | copy-start | bytes 98308
  272.7 40.3 %copy-start.4 = (bf16[2,4,64,2048]{3,2,1,0:T(8,128)(2,1)}, bf16[2,4,64,2048]{3,2,1,0:T(8,128)(2,1)S(1)}, u32[]{:S(2)}) copy-start(bf16[2,4,64,2048]{3,2,1,0:T(8,128)(2,1)S(1)} %copy.242) | copy-start | bytes 6291460
  284.4 184.4 %copy-start.6 = (bf16[5,2048,16]{1,2,0:T(8,128)(2,1)}, bf16[5,2048,16]{1,2,0:T(8,128)(2,1)S(1)}, u32[]{:S(2)}) copy-start(bf16[5,2048,16]{1,2,0:T(8,128)(2,1)S(1)} %copy.247) | copy-start | bytes 983044
  297.6 71.9 %copy-start.57 = (bf16[2,16,2048]{2,1,0:T(8,128)(2,1)}, bf16[2,16,2048]{2,1,0:T(8,128)(2,1)S(1)}, u32[]{:S(2)}) copy-start(bf16[2,16,2048]{2,1,0:T(8,128)(2,1)S(1)} %copy.265) | copy-start | bytes 393220
  299.2 70.3 %copy-start.61 = (bf16[2,16,2048]{2,1,0:T(8,128)(2,1)}, bf16[2,16,2048]{2,1,0:T(8,128)(2,1)S(1)}, u32[]{:S(2)}) copy-start(bf16[2,16,2048]{2,1,0:T(8,128)(2,1)S(1)} %copy.266) | copy-start | bytes 393220
  301.2 64.6 %copy-start.95 = (f32[2,256,16]{1,2,0:T(8,128)}, f32[2,256,16]{1,2,0:T(8,128)S(1)}, u32[]{:S(2)}) copy-start(f32[2,256,16]{1,2,0:T(8,128)S(1)} %fusion.86) | copy-start | bytes 98308
  349.2 220.6 %all-to-all-start.4 = ((bf16[64,64,1408]{2,1,0:T(8,128)(2,1)}), bf16[64,64,1408]{2,1,0:T(8,128)(2,1)}, u32[]{:S(2)}, u32[]{:S(2)}) async-start(bf16[64,64,1408]{2,1,0:T(8,128)(2,1)} %constant_dynamic-update-slice_fusion.64), calls=%async_computation.4 | async-start | bytes 23068672 | tf_op jit(solution)/shard_map/all_to_all | solution.py:173
  374.9 72.2 %slice-start.2 = ((bf16[32,196,128]{2,1,0:T(8,128)(2,1)}), bf16[32,88,128]{2,1,0:T(8,128)(2,1)S(1)}, s32[]{:S(2)}) async-start(bf16[32,196,128]{2,1,0:T(8,128)(2,1)} %copy-done.40), calls=%async_computation.10 | async-start | bytes 1441792 | tf_op jit(solution)/shard_map/slice | solution.py:186
  374.9 77.0 %collective-permute-start.2 = (f32[2,2,64,2048]{3,2,1,0:T(8,128)}, f32[2,2,64,2048]{3,2,1,0:T(8,128)}, u32[]{:S(2)}, u32[]{:S(2)}) collective-permute-start(f32[2,2,64,2048]{3,2,1,0:T(8,128)} %bitcast.542), channel_id=1, source_target_pairs={{0,1},{1,0},{2,3},{3,2},{4,5},{5,4},{6,7},{7,6},{8,9},{9,8},{10,11... | collective-permute-start | bytes 6291464 | tf_op jit(solution)/shard_map/ppermute | solution.py:121
  378.0 60.3 %collective-permute-start.8 = (bf16[2,64,2048]{2,1,0:T(8,128)(2,1)}, bf16[2,64,2048]{2,1,0:T(8,128)(2,1)}, u32[]{:S(2)}, u32[]{:S(2)}) collective-permute-start(bf16[2,64,2048]{2,1,0:T(8,128)(2,1)} %param.19), channel_id=1, source_target_pairs={{0,2},{1,3},{2,0},{3,1},{4,6},{5,7},{6,4},{7,5},{8,10},{9,11},{10,... | collective-permute-start | bytes 1572872 | tf_op jit(solution)/shard_map/ppermute | solution.py:106
  441.0 24.8 %collective-permute-start.9 = (bf16[2,2,64,2048]{3,2,1,0:T(8,128)(2,1)}, bf16[2,2,64,2048]{3,2,1,0:T(8,128)(2,1)}, u32[]{:S(2)}, u32[]{:S(2)}) collective-permute-start(bf16[2,2,64,2048]{3,2,1,0:T(8,128)(2,1)} %maximum_select_fusion.7), channel_id=1, source_target_pairs={{0,1},{1,0},{2,3},{3,2},{4,5},{5,4},{6,7},{7,6},{8,9},{9,8},{10,11... | collective-permute-start | bytes 3145736 | tf_op jit(solution)/shard_map/ppermute | solution.py:108
  455.6 88.8 %collective-permute-start.3 = (f32[2,64,2048]{2,1,0:T(8,128)}, f32[2,64,2048]{2,1,0:T(8,128)}, u32[]{:S(2)}, u32[]{:S(2)}) collective-permute-start(f32[2,64,2048]{2,1,0:T(8,128)} %dynamic-slice_bitcast_fusion.3), channel_id=1, source_target_pairs={{0,2},{1,3},{2,0},{3,1},{4,6},{5,7},{6,4},{7,5},{8,10},{9,11},{10,... | collective-permute-start | bytes 3145736 | tf_op jit(solution)/shard_map/ppermute | solution.py:124
  468.5 75.9 %copy-start.11 = (bf16[2,64,2048]{2,1,0:T(8,128)(2,1)S(1)}, bf16[2,64,2048]{2,1,0:T(8,128)(2,1)}, u32[]{:S(2)}) copy-start(bf16[2,64,2048]{2,1,0:T(8,128)(2,1)} %param.18) | copy-start | bytes 1572868
  468.5 75.9 %copy-start.29 = (f32[2,2,64,2048]{3,2,1,0:T(8,128)S(1)}, f32[2,2,64,2048]{3,2,1,0:T(8,128)}, u32[]{:S(2)}) copy-start(f32[2,2,64,2048]{3,2,1,0:T(8,128)} %copy-done.28) | copy-start | bytes 6291460
  468.8 100.4 %copy-start.75 = (bf16[2,2048,16]{1,2,0:T(8,128)(2,1)}, bf16[2,2048,16]{1,2,0:T(8,128)(2,1)S(1)}, u32[]{:S(2)}) copy-start(bf16[2,2048,16]{1,2,0:T(8,128)(2,1)S(1)} %fusion.61) | copy-start | bytes 393220
  469.7 76.8 %copy-start.109 = (f32[2048]{0:T(1024)S(1)}, f32[2048]{0:T(1024)}, u32[]{:S(2)}) copy-start(f32[2048]{0:T(1024)} %param.27) | copy-start | bytes 24580
  470.3 92.5 %copy-start.93 = (f32[2,256,16]{1,2,0:T(8,128)}, f32[2,256,16]{1,2,0:T(8,128)S(1)}, u32[]{:S(2)}) copy-start(f32[2,256,16]{1,2,0:T(8,128)S(1)} %convolution_multiply_fusion.15) | copy-start | bytes 98308
  546.7 14.7 %collective-permute-start.4 = (bf16[2,64,2048]{2,1,0:T(8,128)(2,1)S(1)}, bf16[2,64,2048]{2,1,0:T(8,128)(2,1)S(1)}, u32[]{:S(2)}, u32[]{:S(2)}) collective-permute-start(bf16[2,64,2048]{2,1,0:T(8,128)(2,1)S(1)} %multiply_convert_fusion.3), channel_id=1, source_target_pairs={{0,2},{1,3},{2,0},{3,1},{4,6},{5,7},{6,4},{7,5},{8,10},{9,11},{10,... | collective-permute-start | bytes 1572872 | tf_op jit(solution)/shard_map/ppermute | solution.py:106
  561.5 4.6 collective-permute-start.5
  625.9 60.4 %collective-permute-start.10 = (f32[2,2,64,2048]{3,2,1,0:T(8,128)}, f32[2,2,64,2048]{3,2,1,0:T(8,128)}, u32[]{:S(2)}, u32[]{:S(2)}) collective-permute-start(f32[2,2,64,2048]{3,2,1,0:T(8,128)} %bitcast.540), channel_id=1, source_target_pairs={{0,1},{1,0},{2,3},{3,2},{4,5},{5,4},{6,7},{7,6},{8,9},{9,8},{10,11... | collective-permute-start | bytes 6291464 | tf_op jit(solution)/shard_map/ppermute | solution.py:121
  626.4 55.0 %copy-start.82 = (f32[2,256,16]{1,2,0:T(8,128)}, f32[2,256,16]{1,2,0:T(8,128)S(1)}, u32[]{:S(2)}) copy-start(f32[2,256,16]{1,2,0:T(8,128)S(1)} %fusion.110) | copy-start | bytes 98308
  631.9 72.9 %collective-permute-start.6 = (f32[2,2,64,2048]{3,2,1,0:T(8,128)}, f32[2,2,64,2048]{3,2,1,0:T(8,128)}, u32[]{:S(2)}, u32[]{:S(2)}) collective-permute-start(f32[2,2,64,2048]{3,2,1,0:T(8,128)} %bitcast.541), channel_id=1, source_target_pairs={{0,1},{1,0},{2,3},{3,2},{4,5},{5,4},{6,7},{7,6},{8,9},{9,8},{10,11... | collective-permute-start | bytes 6291464 | tf_op jit(solution)/shard_map/ppermute | solution.py:121
  682.1 90.3 %collective-permute-start.18 = (f32[2,2,256,16]{2,3,1,0:T(8,128)}, f32[2,2,256,16]{2,3,1,0:T(8,128)}, u32[]{:S(2)}, u32[]{:S(2)}) collective-permute-start(f32[2,2,256,16]{2,3,1,0:T(8,128)} %pad_maximum_fusion.9), channel_id=1, source_target_pairs={{0,1},{1,0},{2,3},{3,2},{4,5},{5,4},{6,7},{7,6},{8,9},{9,8},{10,11... | collective-permute-start | bytes 196616 | tf_op jit(solution)/shard_map/ppermute | solution.py:129
  684.2 72.1 %copy-start.69 = (f32[2,1,16,1408]{3,2,0,1:T(8,128)}, f32[2,1,16,1408]{3,2,0,1:T(8,128)S(1)}, u32[]{:S(2)}) copy-start(f32[2,1,16,1408]{3,2,0,1:T(8,128)S(1)} %fusion.7) | copy-start | bytes 540676
  688.5 39.8 %collective-permute-start.11 = (f32[2,64,2048]{2,1,0:T(8,128)S(1)}, f32[2,64,2048]{2,1,0:T(8,128)S(1)}, u32[]{:S(2)}, u32[]{:S(2)}) collective-permute-start(f32[2,64,2048]{2,1,0:T(8,128)S(1)} %dynamic-slice_bitcast_fusion.1), channel_id=1, source_target_pairs={{0,2},{1,3},{2,0},{3,1},{4,6},{5,7},{6,4},{7,5},{8,10},{9,11},{10,... | collective-permute-start | bytes 3145736 | tf_op jit(solution)/shard_map/ppermute | solution.py:124
  706.9 43.9 %copy-start.119 = (f32[2,64]{1,0:T(2,128)S(1)}, f32[2,64]{1,0:T(2,128)}, u32[]{:S(2)}) copy-start(f32[2,64]{1,0:T(2,128)} %copy-done.118) | copy-start | bytes 1540
  706.9 43.9 %collective-permute-start.7 = (f32[2,64,2048]{2,1,0:T(8,128)S(1)}, f32[2,64,2048]{2,1,0:T(8,128)S(1)}, u32[]{:S(2)}, u32[]{:S(2)}) collective-permute-start(f32[2,64,2048]{2,1,0:T(8,128)S(1)} %dynamic-slice_bitcast_fusion.2), channel_id=1, source_target_pairs={{0,2},{1,3},{2,0},{3,1},{4,6},{5,7},{6,4},{7,5},{8,10},{9,11},{10,... | collective-permute-start | bytes 3145736 | tf_op jit(solution)/shard_map/ppermute | solution.py:124
  707.7 48.6 %copy-start.71 = (f32[2,1,16,1408]{3,2,0,1:T(8,128)}, f32[2,1,16,1408]{3,2,0,1:T(8,128)S(1)}, u32[]{:S(2)}) copy-start(f32[2,1,16,1408]{3,2,0,1:T(8,128)S(1)} %fusion.6) | copy-start | bytes 540676
  753.6 14.7 %collective-permute-start.12 = (bf16[2,64,2048]{2,1,0:T(8,128)(2,1)}, bf16[2,64,2048]{2,1,0:T(8,128)(2,1)}, u32[]{:S(2)}, u32[]{:S(2)}) collective-permute-start(bf16[2,64,2048]{2,1,0:T(8,128)(2,1)} %get-tuple-element.34), channel_id=1, source_target_pairs={{0,2},{1,3},{2,0},{3,1},{4,6},{5,7},{6,4},{7,5},{8,10},{9,11},{10,... | collective-permute-start | bytes 1572872 | tf_op jit(solution)/shard_map/ppermute | solution.py:106
  771.0 30.3 %collective-permute-start.13 = (bf16[2,2,64,2048]{3,2,1,0:T(8,128)(2,1)}, bf16[2,2,64,2048]{3,2,1,0:T(8,128)(2,1)}, u32[]{:S(2)}, u32[]{:S(2)}) collective-permute-start(bf16[2,2,64,2048]{3,2,1,0:T(8,128)(2,1)} %maximum_select_fusion.9), channel_id=1, source_target_pairs={{0,1},{1,0},{2,3},{3,2},{4,5},{5,4},{6,7},{7,6},{8,9},{9,8},{10,11... | collective-permute-start | bytes 3145736 | tf_op jit(solution)/shard_map/ppermute | solution.py:108
  773.9 22.9 %collective-permute-start.19 = (f32[2,2,256,16]{2,3,1,0:T(8,128)}, f32[2,2,256,16]{2,3,1,0:T(8,128)}, u32[]{:S(2)}, u32[]{:S(2)}) collective-permute-start(f32[2,2,256,16]{2,3,1,0:T(8,128)} %fusion.74), channel_id=1, source_target_pairs={{0,2},{1,3},{2,0},{3,1},{4,6},{5,7},{6,4},{7,5},{8,10},{9,11},{10,... | collective-permute-start | bytes 196616 | tf_op jit(solution)/shard_map/ppermute | solution.py:130
  866.2 70.5 %all-to-all-start.7 = ((bf16[32,2,12544]{2,1,0:T(2,128)(2,1)}), bf16[32,2,12544]{2,1,0:T(2,128)(2,1)}, u32[]{:S(2)}, u32[]{:S(2)}) async-start(bf16[32,2,12544]{2,1,0:T(2,128)(2,1)} %reshape.766), calls=%async_computation.7 | async-start | bytes 3211264 | tf_op jit(solution)/shard_map/all_to_all | solution.py:392
  883.6 20.6 %collective-permute-start.16 = (f32[5,2,256,16]{2,3,1,0:T(8,128)}, f32[5,2,256,16]{2,3,1,0:T(8,128)S(1)}, u32[]{:S(2)}, u32[]{:S(2)}) collective-permute-start(f32[5,2,256,16]{2,3,1,0:T(8,128)} %constant_dynamic-update-slice_fusion.128), channel_id=1, source_target_pairs={{0,1},{1,0},{2,3},{3,2},{4,5},{5,4},{6,7},{7,6},{8,9},{9,8},{10,11... | collective-permute-start | bytes 491528 | tf_op jit(solution)/shard_map/ppermute | solution.py:129
  905.2 7.7 collective-permute-start.17
  912.3 33.0 %collective-permute-start.14 = (f32[2,2,64,2048]{3,2,1,0:T(8,128)}, f32[2,2,64,2048]{3,2,1,0:T(8,128)}, u32[]{:S(2)}, u32[]{:S(2)}) collective-permute-start(f32[2,2,64,2048]{3,2,1,0:T(8,128)} %bitcast.539), channel_id=1, source_target_pairs={{0,1},{1,0},{2,3},{3,2},{4,5},{5,4},{6,7},{7,6},{8,9},{9,8},{10,11... | collective-permute-start | bytes 6291464 | tf_op jit(solution)/shard_map/ppermute | solution.py:121
  936.7 34.7 %all-to-all-start.6 = ((f32[32,1,14336]{2,1,0:T(1,128)}), f32[32,1,14336]{2,1,0:T(1,128)}, u32[]{:S(2)}, u32[]{:S(2)}) async-start(f32[32,1,14336]{2,1,0:T(1,128)} %all_to_all.84), calls=%async_computation.6 | async-start | bytes 3670016 | tf_op jit(solution)/shard_map/all_to_all | solution.py:374
  948.9 45.0 %collective-permute-start.15 = (f32[2,64,2048]{2,1,0:T(8,128)}, f32[2,64,2048]{2,1,0:T(8,128)}, u32[]{:S(2)}, u32[]{:S(2)}) collective-permute-start(f32[2,64,2048]{2,1,0:T(8,128)} %dynamic-slice_bitcast_fusion), channel_id=1, source_target_pairs={{0,2},{1,3},{2,0},{3,1},{4,6},{5,7},{6,4},{7,5},{8,10},{9,11},{10,... | collective-permute-start | bytes 3145736 | tf_op jit(solution)/shard_map/ppermute | solution.py:124
  (117 other events, 770.2 us)

commit v4 on v3

--- a/solution.py
+++ b/solution.py
@@ -100,27 +100,31 @@
     return [(i, i ^ bit) for i in range(count)]
 
 
-def tok_gather(values):
+def tok_gather(values, axis=0):
     count = lax.axis_size("tok")
     me = lax.axis_index("tok")
     far = lax.ppermute(values, "tok", xor_pairs(count, 2))
-    pair = jnp.where((me & 2) == 0, jnp.stack([values, far]), jnp.stack([far, values]))
+    pair = jnp.where(
+        (me & 2) == 0, jnp.stack([values, far], axis), jnp.stack([far, values], axis)
+    )
     near = lax.ppermute(pair, "tok", xor_pairs(count, 1))
-    full = jnp.where((me & 1) == 0, jnp.stack([pair, near], 1), jnp.stack([near, pair], 1))
-    return full.reshape((count,) + values.shape)
-
-
-def tok_scatter(blocks):
+    full = jnp.where(
+        (me & 1) == 0, jnp.stack([pair, near], axis + 1), jnp.stack([near, pair], axis + 1)
+    )
+    return full.reshape(values.shape[:axis] + (count,) + values.shape[axis:])
+
+
+def tok_scatter(blocks, axis=0):
     count = lax.axis_size("tok")
     me = lax.axis_index("tok")
     core = me & 1
     half = (me >> 1) & 1
-    split = blocks.reshape((2, 2) + blocks.shape[1:])
-    mine = lax.dynamic_index_in_dim(split, core, 1, keepdims=False)
-    theirs = lax.dynamic_index_in_dim(split, 1 - core, 1, keepdims=False)
+    split = blocks.reshape(blocks.shape[:axis] + (2, 2) + blocks.shape[axis + 1 :])
+    mine = lax.dynamic_index_in_dim(split, core, axis + 1, keepdims=False)
+    theirs = lax.dynamic_index_in_dim(split, 1 - core, axis + 1, keepdims=False)
     chip_sum = mine + lax.ppermute(theirs, "tok", xor_pairs(count, 1))
-    keep = lax.dynamic_index_in_dim(chip_sum, half, 0, keepdims=False)
-    send = lax.dynamic_index_in_dim(chip_sum, 1 - half, 0, keepdims=False)
+    keep = lax.dynamic_index_in_dim(chip_sum, half, axis, keepdims=False)
+    send = lax.dynamic_index_in_dim(chip_sum, 1 - half, axis, keepdims=False)
     return keep + lax.ppermute(send, "tok", xor_pairs(count, 2))
 
 
@@ -169,7 +173,8 @@
     groups_per_adapter = RANK // b_qkv.shape[1]
 
     def fsdp_gather(values, axis):
-        tiled_in = jnp.concatenate([values] * fsdp_count, axis=0)
+        tiled_in = jnp.broadcast_to(values[None], (fsdp_count,) + values.shape)
+        tiled_in = tiled_in.reshape((fsdp_count * values.shape[0],) + values.shape[1:])
         return lax.all_to_all(tiled_in, "fsdp", 0, axis, tiled=True)
 
     def packed_gather(small, axes):
@@ -217,12 +222,11 @@
     a_down_sel = jnp.moveaxis(pick_groups(g_adown), 1, 2).reshape(seqs, ff_here, RANK)
 
     def gather_rows(values):
-        full = tok_gather(values)
-        return jnp.moveaxis(full, 0, 1).reshape(seqs, length, values.shape[-1])
+        full = tok_gather(values, 1)
+        return full.reshape(seqs, length, values.shape[-1])
 
     def scatter_rows(values):
-        blocks = jnp.moveaxis(values.reshape(seqs, tok_count, local_len, values.shape[-1]), 1, 0)
-        return tok_scatter(blocks)
+        return tok_scatter(values.reshape(seqs, tok_count, local_len, values.shape[-1]), 1)
 
     def column_forward(rows_full, weight, down_sel, up_sel):
         lowrank = jnp.einsum("std,sdr->str", rows_full, down_sel, preferred_element_type=jnp.float32)
@@ -297,9 +301,12 @@
             running = term if running is None else running + term
         return scatter_rows(running), grad_lows, grads_up
 
-    def rows_of_mine(rows_full):
-        split = rows_full.reshape(seqs, length, fsdp_count, tok_count, D // (fsdp_count * tok_count))
-        return lax.dynamic_index_in_dim(split, me_tok, 3, keepdims=False)
+    def mine_of(values, axis):
+        shape = values.shape
+        split = values.reshape(
+            shape[:axis] + (fsdp_count, tok_count, D // (fsdp_count * tok_count)) + shape[axis + 1 :]
+        )
+        return lax.dynamic_index_in_dim(split, me_tok, axis + 1, keepdims=False)
 
     grad_product, grad_a_down = row_backward(
         grad_ffn_full, product, w_down_full, a_down_sel, b_rows_sel[:, 1]
@@ -336,22 +343,20 @@
     grad_tokens = grad_hidden + norm_attn_pull(grad_attn_rows)[0]
 
     grad_lows = tok_sum(jnp.stack(attn_grad_lows + ffn_grad_lows))
-    attn_mine = rows_of_mine(normed_full)
-    ffn_mine = rows_of_mine(ffn_full)
-    grad_a_in_part = jnp.concatenate(
+    grad_a_in_all = jnp.concatenate(
         [
-            hp_dot(attn_mine.astype(jnp.float32), grad_lows[:3], "stfi,pstr->psfir"),
-            hp_dot(ffn_mine.astype(jnp.float32), grad_lows[3:], "stfi,pstr->psfir"),
+            hp_dot(normed_full.astype(jnp.float32), grad_lows[:3], "std,pstr->psdr"),
+            hp_dot(ffn_full.astype(jnp.float32), grad_lows[3:], "std,pstr->psdr"),
         ]
     )
-    e_attn_mine = rows_of_mine(grad_attn_full).astype(jnp.float32)
-    e_ffn_mine = rows_of_mine(grad_ffn_full).astype(jnp.float32)
-    grad_b_rows_part = adapter_scale * jnp.stack(
+    grad_a_in_part = mine_of(grad_a_in_all, 2)
+    grad_b_rows_all = adapter_scale * jnp.stack(
         [
-            hp_dot(row_lows[0], e_attn_mine, "str,stfj->srfj"),
-            hp_dot(row_lows[1], e_ffn_mine, "str,stfj->srfj"),
+            hp_dot(row_lows[0], grad_attn_full.astype(jnp.float32), "str,std->srd"),
+            hp_dot(row_lows[1], grad_ffn_full.astype(jnp.float32), "str,std->srd"),
         ]
     )
+    grad_b_rows_part = mine_of(grad_b_rows_all, 3)
 
     def place(part, axis, total):
         shape = list(part.shape[1:])

time: 1010 us -> 984 us (0.974)
  local copies, waits for them, and re-layouts: 328 us -> 237 us
  blocking collectives: 0 us -> 87.4 us
  starting transfers between devices: 128 us -> 111 us
  waiting for transfers between devices: 339 us -> 325 us
    all_to_all x0 -> x2, blocking collectives: none -> 87.4 us  [packed_gather(): lax.all_to_all(tiled_in, axes, 0, 0, tiled=True)]
    unnamed x405 -> x283, local copies, waits for them, and re-layouts: 99.8 us -> 41.4 us
    all_to_all x2 -> x0, waiting for transfers between devices: 34.3 us -> none  [packed_gather(): lax.all_to_all(tiled_in, axes, 0, 0, tiled=True)]
    ppermute x4, waiting for transfers between devices: 64.5 us -> 95.1 us  [tok_gather(): far = lax.ppermute(values, 'tok', xor_pairs(count, 2))]
    transpose x9 -> x2, local copies, waits for them, and re-layouts: 29.8 us -> 5.92 us  [the longest x1 4.17 us: per_device(): dense_a_in = place(jnp.moveaxis(grad_a_in_part, 1, 0), 3, COLS)]
    all_to_all x4 -> x0, local copies, waits for them, and re-layouts: 21.3 us -> none  [fsdp_gather(): return lax.all_to_all(tiled_in, 'fsdp', 0, axis, tiled=True)]
    another operation x4 -> x2, local copies, waits for them, and re-layouts: 27 us -> 6.07 us  [per_device(): jnp.stack([hp_dot(row_lows[0], grad_attn_full.astype(jnp.float32), 'str,s...]
    all_to_all x2 -> x0, starting transfers between devices: 15.4 us -> none  [packed_gather(): lax.all_to_all(tiled_in, axes, 0, 0, tiled=True)]
  transfers between devices with their start and end apart: 28 -> 26, of which waited for: 11 -> 12; matrix products, arithmetic and copies ran while one was open for 38% -> 28% of each run, Pallas kernels for 0% -> 0%
where the time goes in v4:
time: 984 us; the launch traced here: 972 us
  waiting for transfers between devices  325 us (33%)
  local copies, waits for them, and re-layouts  237 us (24%)
  matrix products  114 us (12%)
  starting transfers between devices  111 us (11%)
  other arithmetic  89.2 us (9%)
  blocking collectives  87.4 us (9%)
    ppermute x4, waiting for transfers between devices, tok_scatter(): return keep + lax.ppermute(send, 'tok', xor_pairs(count, 2))  135 us
    ppermute x4, waiting for transfers between devices, tok_gather(): far = lax.ppermute(values, 'tok', xor_pairs(count, 2))  95.1 us
    all_to_all x4, waiting for transfers between devices, fsdp_gather(): return lax.all_to_all(tiled_in, 'fsdp', 0, axis, tiled=True)  91.5 us
    all_to_all x2, blocking collectives, packed_gather(): lax.all_to_all(tiled_in, axes, 0, 0, tiled=True)  87.4 us
    dot_general x32, matrix products, hp_dot(): jnp.einsum(spec, left, right, precision=highest, preferred_element_type=j...  51.1 us
    unnamed x283, local copies, waits for them, and re-layouts  41.4 us
    all_to_all x4, starting transfers between devices, fsdp_gather(): return lax.all_to_all(tiled_in, 'fsdp', 0, axis, tiled=True)  33.5 us
    dynamic_update_slice x11, local copies, waits for them, and re-layouts, place(): lax.dynamic_update_slice_in_dim(dense, current + part[s], offsets[s], axis)  21 us
  transfers between devices with their start and end apart: 26, of which 12 were waited for; matrix products, arithmetic and copies ran while one was open for 28% of the time, Pallas kernels for 0%

profile of v4, /device:TPU:1, one launch (start us, length us, event | category | flops | bytes accessed | tf_op | source)
XLA Modules:
  0.0 972.5 jit_solution(16708284985216514691)
XLA Ops:
  4.9 30.9 %all_to_all.89 = bf16[32,196,128]{2,1,0:T(8,128)(2,1)} all-to-all(bf16[32,196,128]{2,1,0:T(8,128)(2,1)S(1)} %broadcast_in_dim.44), channel_id=1, replica_groups=mesh['fsdp'=32,'tok'=4] {'fsdp'}, dimensions={0} | all-to-all | bytes 3211264 | tf_op jit(solution)/shard_map/all_to_all | solution.py:186
  37.4 5.3 all-to-all-start.3
  43.0 26.4 %all-to-all-done.3 = bf16[32,512,64]{1,2,0:T(8,128)(2,1)S(1)} async-done(((bf16[32,512,64]{1,2,0:T(8,128)(2,1)}), bf16[32,512,64]{1,2,0:T(8,128)(2,1)S(1)}, u32[]{:S(2)}, u32[]{:S(2)}) %all-to-all-start.3) | async-done | bytes 2097184 | tf_op jit(solution)/shard_map/all_to_all | solution.py:178
  69.9 56.4 %all_to_all.90 = bf16[128,112,128]{2,1,0:T(8,128)(2,1)} all-to-all(bf16[128,112,128]{2,1,0:T(8,128)(2,1)S(1)} %broadcast_in_dim.43), channel_id=1, replica_groups=mesh['fsdp'=32,'tok'=4] {'fsdp','tok'}, dimensions={0} | all-to-all | bytes 7340032 | tf_op jit(solution)/shard_map/all_to_all | solution.py:186
  126.3 3.5 broadcast_in_dim.42
  129.8 5.3 all-to-all-start
  146.7 31.2 %collective-permute-done = bf16[2,64,2048]{2,1,0:T(8,128)(2,1)S(1)} collective-permute-done((bf16[2,64,2048]{2,1,0:T(8,128)(2,1)S(1)}, bf16[2,64,2048]{2,1,0:T(8,128)(2,1)S(1)}, u32[]{:S(2)}, u32[]{:S(2)}) %collective-permute-start) | collective-permute-done | bytes 524320 | tf_op jit(solution)/shard_map/ppermute | solution.py:106
  186.7 47.6 %all-to-all-done = bf16[96,64,512]{2,1,0:T(8,128)(2,1)} async-done(((bf16[96,64,512]{2,1,0:T(8,128)(2,1)}), bf16[96,64,512]{2,1,0:T(8,128)(2,1)}, u32[]{:S(2)}, u32[]{:S(2)}) %all-to-all-start) | async-done | bytes 6291488 | tf_op jit(solution)/shard_map/all_to_all | solution.py:178
  237.5 9.4 all-to-all-start.5
  252.5 3.7 constant_dynamic-slice_fusion.7
  268.7 3.5 constant_dynamic-slice_fusion.3
  282.3 5.6 fusion.90
  294.0 4.1 convolution_add_fusion.2
  308.8 17.5 %all-to-all-done.5 = bf16[32,1408,64]{1,2,0:T(8,128)(2,1)} async-done(((bf16[32,1408,64]{1,2,0:T(8,128)(2,1)}), bf16[32,1408,64]{1,2,0:T(8,128)(2,1)}, u32[]{:S(2)}, u32[]{:S(2)}) %all-to-all-start.5) | async-done | bytes 5767200 | tf_op jit(solution)/shard_map/all_to_all | solution.py:178
  326.3 6.7 broadcast_in_dim.48
  333.0 13.4 %all-to-all-start.4 = ((bf16[64,64,1408]{2,1,0:T(8,128)(2,1)}), bf16[64,64,1408]{2,1,0:T(8,128)(2,1)}, u32[]{:S(2)}, u32[]{:S(2)}) async-start(bf16[64,64,1408]{2,1,0:T(8,128)(2,1)} %bitcast.507), calls=%async_computation.4 | async-start | bytes 23068672 | tf_op jit(solution)/shard_map/all_to_all | solution.py:178
  361.2 12.9 %collective-permute-start.8 = (bf16[2,64,2048]{2,1,0:T(8,128)(2,1)S(1)}, bf16[2,64,2048]{2,1,0:T(8,128)(2,1)S(1)}, u32[]{:S(2)}, u32[]{:S(2)}) collective-permute-start(bf16[2,64,2048]{2,1,0:T(8,128)(2,1)S(1)} %copy-done.47), channel_id=1, source_target_pairs={{0,2},{1,3},{2,0},{3,1},{4,6},{5,7},{6,4},{7,5},{8,10},{9,11},{10,... | collective-permute-start | bytes 1572872 | tf_op jit(solution)/shard_map/ppermute | solution.py:106
  374.1 49.3 %collective-permute-done.8 = bf16[2,64,2048]{2,1,0:T(8,128)(2,1)S(1)} collective-permute-done((bf16[2,64,2048]{2,1,0:T(8,128)(2,1)S(1)}, bf16[2,64,2048]{2,1,0:T(8,128)(2,1)S(1)}, u32[]{:S(2)}, u32[]{:S(2)}) %collective-permute-start.8) | collective-permute-done | bytes 524320 | tf_op jit(solution)/shard_map/ppermute | solution.py:106
  451.9 77.3 %collective-permute-done.3 = f32[2,64,2048]{2,1,0:T(8,128)} collective-permute-done((f32[2,64,2048]{2,1,0:T(8,128)}, f32[2,64,2048]{2,1,0:T(8,128)}, u32[]{:S(2)}, u32[]{:S(2)}) %collective-permute-start.3) | collective-permute-done | bytes 1048608 | tf_op jit(solution)/shard_map/ppermute | solution.py:128
  531.0 5.8 fusion.102
  537.0 8.6 collective-permute-done.4
  553.0 9.4 fusion.89
  562.5 6.0 fusion.98
  577.5 3.5 fusion.103
  581.5 3.4 fusion.104
  585.0 5.9 fusion.100
  612.7 18.8 %collective-permute-start.11 = (f32[2,64,2048]{2,1,0:T(8,128)S(1)}, f32[2,64,2048]{2,1,0:T(8,128)S(1)}, u32[]{:S(2)}, u32[]{:S(2)}) collective-permute-start(f32[2,64,2048]{2,1,0:T(8,128)S(1)} %dynamic-slice_bitcast_fusion.5), channel_id=1, source_target_pairs={{0,2},{1,3},{2,0},{3,1},{4,6},{5,7},{6,4},{7,5},{8,10},{9,11},{10,... | collective-permute-start | bytes 3145736 | tf_op jit(solution)/shard_map/ppermute | solution.py:128
  636.1 18.9 %collective-permute-done.11 = f32[2,64,2048]{2,1,0:T(8,128)S(1)} collective-permute-done((f32[2,64,2048]{2,1,0:T(8,128)S(1)}, f32[2,64,2048]{2,1,0:T(8,128)S(1)}, u32[]{:S(2)}, u32[]{:S(2)}) %collective-permute-start.11) | collective-permute-done | bytes 1048608 | tf_op jit(solution)/shard_map/ppermute | solution.py:128
  655.2 22.2 %collective-permute-done.7 = f32[2,64,2048]{2,1,0:T(8,128)S(1)} collective-permute-done((f32[2,64,2048]{2,1,0:T(8,128)S(1)}, f32[2,64,2048]{2,1,0:T(8,128)S(1)}, u32[]{:S(2)}, u32[]{:S(2)}) %collective-permute-start.7) | collective-permute-done | bytes 1048608 | tf_op jit(solution)/shard_map/ppermute | solution.py:128
  688.0 5.9 collective-permute-done.12
  759.6 4.4 multiply_add_fusion.5
  773.2 3.8 fusion.28
  780.5 5.2 fusion.106
  787.6 5.3 fusion.107
  816.0 4.0 reduce.2
  822.4 15.1 %all-to-all-start.7 = ((bf16[32,2,12544]{2,1,0:T(2,128)(2,1)}), bf16[32,2,12544]{2,1,0:T(2,128)(2,1)}, u32[]{:S(2)}, u32[]{:S(2)}) async-start(bf16[32,2,12544]{2,1,0:T(2,128)(2,1)} %reshape.787), calls=%async_computation.7 | async-start | bytes 3211264 | tf_op jit(solution)/shard_map/all_to_all | solution.py:397
  847.9 5.0 add_add_fusion
  866.9 8.7 reshape.767
  875.6 6.8 constant_dynamic-slice_fusion
  882.4 4.2 copy.329
  886.6 4.2 copy.281
  894.8 5.3 dynamic_update_slice.36
  901.4 5.3 dynamic_update_slice.37
  906.7 4.1 copy.330
  914.2 8.1 all-to-all-start.6
  926.8 9.4 reshape.788
  936.3 5.3 convert_reduce_fusion
  951.5 16.7 %collective-permute-done.15 = f32[2,64,2048]{2,1,0:T(8,128)} collective-permute-done((f32[2,64,2048]{2,1,0:T(8,128)}, f32[2,64,2048]{2,1,0:T(8,128)}, u32[]{:S(2)}, u32[]{:S(2)}) %collective-permute-start.15) | collective-permute-done | bytes 1048608 | tf_op jit(solution)/shard_map/ppermute | solution.py:128
  (568 shorter events, 324.8 us)
Async XLA Ops:
  4.7 31.2 %copy-start.111 = (bf16[512,64]{0,1:T(8,128)(2,1)S(1)}, bf16[512,64]{0,1:T(8,128)(2,1)}, u32[]{:S(2)}) copy-start(bf16[512,64]{0,1:T(8,128)(2,1)} %param.23) | copy-start | bytes 196612
  37.4 32.0 %all-to-all-start.3 = ((bf16[32,512,64]{1,2,0:T(8,128)(2,1)}), bf16[32,512,64]{1,2,0:T(8,128)(2,1)S(1)}, u32[]{:S(2)}, u32[]{:S(2)}) async-start(bf16[32,512,64]{1,2,0:T(8,128)(2,1)} %broadcast_in_dim.47), calls=%async_computation.3 | async-start | bytes 4194304 | tf_op jit(solution)/shard_map/all_to_all | solution.py:178
  69.4 56.9 %copy-start.24 = (bf16[32,512,64]{1,2,0:T(8,128)(2,1)}, bf16[32,512,64]{1,2,0:T(8,128)(2,1)S(1)}, u32[]{:S(2)}) copy-start(bf16[32,512,64]{1,2,0:T(8,128)(2,1)S(1)} %all-to-all-done.3) | copy-start | bytes 6291460
  69.9 56.5 %copy-start.108 = (bf16[3,64,512]{2,1,0:T(8,128)(2,1)S(1)}, bf16[3,64,512]{2,1,0:T(8,128)(2,1)}, u32[]{:S(2)}) copy-start(bf16[3,64,512]{2,1,0:T(8,128)(2,1)} %param.22) | copy-start | bytes 589828
  129.8 104.5 %all-to-all-start = ((bf16[96,64,512]{2,1,0:T(8,128)(2,1)}), bf16[96,64,512]{2,1,0:T(8,128)(2,1)}, u32[]{:S(2)}, u32[]{:S(2)}) async-start(bf16[96,64,512]{2,1,0:T(8,128)(2,1)} %bitcast.531), calls=%async_computation | async-start | bytes 12582912 | tf_op jit(solution)/shard_map/all_to_all | solution.py:178
  135.4 43.6 %copy-start.116 = (f32[2,64]{1,0:T(2,128)}, f32[2,64]{1,0:T(2,128)S(1)}, u32[]{:S(2)}) copy-start(f32[2,64]{1,0:T(2,128)S(1)} %fusion.64) | copy-start | bytes 1540
  135.6 42.2 %collective-permute-start = (bf16[2,64,2048]{2,1,0:T(8,128)(2,1)S(1)}, bf16[2,64,2048]{2,1,0:T(8,128)(2,1)S(1)}, u32[]{:S(2)}, u32[]{:S(2)}) collective-permute-start(bf16[2,64,2048]{2,1,0:T(8,128)(2,1)S(1)} %fusion.17), channel_id=1, source_target_pairs={{0,2},{1,3},{2,0},{3,1},{4,6},{5,7},{6,4},{7,5},{8,10},{9,11},{10,... | collective-permute-start | bytes 1572872 | tf_op jit(solution)/shard_map/ppermute | solution.py:106
  179.0 67.9 %collective-permute-start.1 = (bf16[2,2,64,2048]{3,2,1,0:T(8,128)(2,1)}, bf16[2,2,64,2048]{3,2,1,0:T(8,128)(2,1)}, u32[]{:S(2)}, u32[]{:S(2)}) collective-permute-start(bf16[2,2,64,2048]{3,2,1,0:T(8,128)(2,1)} %maximum_select_fusion.4), channel_id=1, source_target_pairs={{0,1},{1,0},{2,3},{3,2},{4,5},{5,4},{6,7},{7,6},{8,9},{9,8},{10,11... | collective-permute-start | bytes 3145736 | tf_op jit(solution)/shard_map/ppermute | solution.py:110
  184.4 49.9 %copy-start.109 = (bf16[1408,64]{0,1:T(8,128)(2,1)S(1)}, bf16[1408,64]{0,1:T(8,128)(2,1)}, u32[]{:S(2)}) copy-start(bf16[1408,64]{0,1:T(8,128)(2,1)} %param.25) | copy-start | bytes 540676
  237.5 88.7 %all-to-all-start.5 = ((bf16[32,1408,64]{1,2,0:T(8,128)(2,1)}), bf16[32,1408,64]{1,2,0:T(8,128)(2,1)}, u32[]{:S(2)}, u32[]{:S(2)}) async-start(bf16[32,1408,64]{1,2,0:T(8,128)(2,1)} %broadcast_in_dim.49), calls=%async_computation.5 | async-start | bytes 11534336 | tf_op jit(solution)/shard_map/all_to_all | solution.py:178
  249.6 96.9 %copy-start = (bf16[2,2,2,64,2048]{4,3,2,1,0:T(8,128)(2,1)}, bf16[2,2,2,64,2048]{4,3,2,1,0:T(8,128)(2,1)S(1)}, u32[]{:S(2)}) copy-start(bf16[2,2,2,64,2048]{4,3,2,1,0:T(8,128)(2,1)S(1)} %maximum_select_fusion) | copy-start | bytes 6291460
  260.4 190.1 %copy-start.4 = (bf16[5,2048,16]{1,2,0:T(8,128)(2,1)}, bf16[5,2048,16]{1,2,0:T(8,128)(2,1)S(1)}, u32[]{:S(2)}) copy-start(bf16[5,2048,16]{1,2,0:T(8,128)(2,1)S(1)} %copy.225) | copy-start | bytes 983044
  273.7 79.5 %copy-start.52 = (bf16[2,16,2048]{2,1,0:T(8,128)(2,1)}, bf16[2,16,2048]{2,1,0:T(8,128)(2,1)S(1)}, u32[]{:S(2)}) copy-start(bf16[2,16,2048]{2,1,0:T(8,128)(2,1)S(1)} %copy.242) | copy-start | bytes 393220
  275.2 77.9 %copy-start.56 = (bf16[2,16,2048]{2,1,0:T(8,128)(2,1)}, bf16[2,16,2048]{2,1,0:T(8,128)(2,1)S(1)}, u32[]{:S(2)}) copy-start(bf16[2,16,2048]{2,1,0:T(8,128)(2,1)S(1)} %copy.243) | copy-start | bytes 393220
  333.0 220.1 %all-to-all-start.4 = ((bf16[64,64,1408]{2,1,0:T(8,128)(2,1)}), bf16[64,64,1408]{2,1,0:T(8,128)(2,1)}, u32[]{:S(2)}, u32[]{:S(2)}) async-start(bf16[64,64,1408]{2,1,0:T(8,128)(2,1)} %bitcast.507), calls=%async_computation.4 | async-start | bytes 23068672 | tf_op jit(solution)/shard_map/all_to_all | solution.py:178
  357.9 77.6 %collective-permute-start.2 = (f32[2,2,64,2048]{3,2,1,0:T(8,128)}, f32[2,2,64,2048]{3,2,1,0:T(8,128)}, u32[]{:S(2)}, u32[]{:S(2)}) collective-permute-start(f32[2,2,64,2048]{3,2,1,0:T(8,128)} %dynamic-slice_bitcast_fusion.3), channel_id=1, source_target_pairs={{0,1},{1,0},{2,3},{3,2},{4,5},{5,4},{6,7},{7,6},{8,9},{9,8},{10,11... | collective-permute-start | bytes 6291464 | tf_op jit(solution)/shard_map/ppermute | solution.py:125
  361.2 62.2 %collective-permute-start.8 = (bf16[2,64,2048]{2,1,0:T(8,128)(2,1)S(1)}, bf16[2,64,2048]{2,1,0:T(8,128)(2,1)S(1)}, u32[]{:S(2)}, u32[]{:S(2)}) collective-permute-start(bf16[2,64,2048]{2,1,0:T(8,128)(2,1)S(1)} %copy-done.47), channel_id=1, source_target_pairs={{0,2},{1,3},{2,0},{3,1},{4,6},{5,7},{6,4},{7,5},{8,10},{9,11},{10,... | collective-permute-start | bytes 1572872 | tf_op jit(solution)/shard_map/ppermute | solution.py:106
  424.5 23.1 %collective-permute-start.9 = (bf16[2,2,64,2048]{3,2,0,1:T(8,128)(2,1)}, bf16[2,2,64,2048]{3,2,0,1:T(8,128)(2,1)}, u32[]{:S(2)}, u32[]{:S(2)}) collective-permute-start(bf16[2,2,64,2048]{3,2,0,1:T(8,128)(2,1)} %maximum_select_fusion.7), channel_id=1, source_target_pairs={{0,1},{1,0},{2,3},{3,2},{4,5},{5,4},{6,7},{7,6},{8,9},{9,8},{10,11... | collective-permute-start | bytes 3145736 | tf_op jit(solution)/shard_map/ppermute | solution.py:110
  439.2 90.1 %collective-permute-start.3 = (f32[2,64,2048]{2,1,0:T(8,128)}, f32[2,64,2048]{2,1,0:T(8,128)}, u32[]{:S(2)}, u32[]{:S(2)}) collective-permute-start(f32[2,64,2048]{2,1,0:T(8,128)} %dynamic-slice_bitcast_fusion.7), channel_id=1, source_target_pairs={{0,2},{1,3},{2,0},{3,1},{4,6},{5,7},{6,4},{7,5},{8,10},{9,11},{10,... | collective-permute-start | bytes 3145736 | tf_op jit(solution)/shard_map/ppermute | solution.py:128
  447.6 99.5 %copy-start.81 = (bf16[2,1408,16]{1,2,0:T(8,128)(2,1)}, bf16[2,1408,16]{1,2,0:T(8,128)(2,1)S(1)}, u32[]{:S(2)}) copy-start(bf16[2,1408,16]{1,2,0:T(8,128)(2,1)S(1)} %reshape.764) | copy-start | bytes 270340
  450.6 80.5 %copy-start.10 = (bf16[2,2,2,64,2048]{4,3,2,1,0:T(8,128)(2,1)}, bf16[2,2,2,64,2048]{4,3,2,1,0:T(8,128)(2,1)S(1)}, u32[]{:S(2)}) copy-start(bf16[2,2,2,64,2048]{4,3,2,1,0:T(8,128)(2,1)S(1)} %copy.256) | copy-start | bytes 6291460
  450.6 78.7 %copy-start.23 = (f32[2,2,64,2048]{3,2,1,0:T(8,128)S(1)}, f32[2,2,64,2048]{3,2,1,0:T(8,128)}, u32[]{:S(2)}) copy-start(f32[2,2,64,2048]{3,2,1,0:T(8,128)} %copy-done.22) | copy-start | bytes 6291460
  450.6 101.8 %copy-start.69 = (bf16[2,2048,16]{1,2,0:T(8,128)(2,1)}, bf16[2,2048,16]{1,2,0:T(8,128)(2,1)S(1)}, u32[]{:S(2)}) copy-start(bf16[2,2048,16]{1,2,0:T(8,128)(2,1)S(1)} %fusion.53) | copy-start | bytes 393220
  451.9 95.2 %copy-start.86 = (f32[2,256,16]{1,2,0:T(8,128)}, f32[2,256,16]{1,2,0:T(8,128)S(1)}, u32[]{:S(2)}) copy-start(f32[2,256,16]{1,2,0:T(8,128)S(1)} %convolution_multiply_fusion.15) | copy-start | bytes 98308
  451.9 78.9 %copy-start.107 = (f32[2048]{0:T(1024)S(1)}, f32[2048]{0:T(1024)}, u32[]{:S(2)}) copy-start(f32[2048]{0:T(1024)} %param.27) | copy-start | bytes 24580
  530.9 14.7 %collective-permute-start.4 = (bf16[2,64,2048]{2,1,0:T(8,128)(2,1)S(1)}, bf16[2,64,2048]{2,1,0:T(8,128)(2,1)S(1)}, u32[]{:S(2)}, u32[]{:S(2)}) collective-permute-start(bf16[2,64,2048]{2,1,0:T(8,128)(2,1)S(1)} %multiply_convert_fusion.3), channel_id=1, source_target_pairs={{0,2},{1,3},{2,0},{3,1},{4,6},{5,7},{6,4},{7,5},{8,10},{9,11},{10,... | collective-permute-start | bytes 1572872 | tf_op jit(solution)/shard_map/ppermute | solution.py:106
  545.8 4.6 collective-permute-start.5
  598.0 11.9 %collective-permute-start.10 = (f32[2,2,64,2048]{3,2,1,0:T(8,128)}, f32[2,2,64,2048]{3,2,1,0:T(8,128)}, u32[]{:S(2)}, u32[]{:S(2)}) collective-permute-start(f32[2,2,64,2048]{3,2,1,0:T(8,128)} %dynamic-slice_bitcast_fusion.1), channel_id=1, source_target_pairs={{0,1},{1,0},{2,3},{3,2},{4,5},{5,4},{6,7},{7,6},{8,9},{9,8},{10,11... | collective-permute-start | bytes 6291464 | tf_op jit(solution)/shard_map/ppermute | solution.py:125
  603.4 28.0 %collective-permute-start.6 = (f32[2,2,64,2048]{3,2,1,0:T(8,128)}, f32[2,2,64,2048]{3,2,1,0:T(8,128)}, u32[]{:S(2)}, u32[]{:S(2)}) collective-permute-start(f32[2,2,64,2048]{3,2,1,0:T(8,128)} %dynamic-slice_bitcast_fusion.2), channel_id=1, source_target_pairs={{0,1},{1,0},{2,3},{3,2},{4,5},{5,4},{6,7},{7,6},{8,9},{9,8},{10,11... | collective-permute-start | bytes 6291464 | tf_op jit(solution)/shard_map/ppermute | solution.py:125
  605.7 92.3 %collective-permute-start.18 = (f32[2,2,256,16]{2,3,1,0:T(8,128)}, f32[2,2,256,16]{2,3,1,0:T(8,128)}, u32[]{:S(2)}, u32[]{:S(2)}) collective-permute-start(f32[2,2,256,16]{2,3,1,0:T(8,128)} %pad_maximum_fusion.11), channel_id=1, source_target_pairs={{0,1},{1,0},{2,3},{3,2},{4,5},{5,4},{6,7},{7,6},{8,9},{9,8},{10,11... | collective-permute-start | bytes 196616 | tf_op jit(solution)/shard_map/ppermute | solution.py:133
  607.8 74.2 %copy-start.65 = (f32[2,1,16,1408]{3,2,0,1:T(8,128)}, f32[2,1,16,1408]{3,2,0,1:T(8,128)S(1)}, u32[]{:S(2)}) copy-start(f32[2,1,16,1408]{3,2,0,1:T(8,128)S(1)} %fusion.6) | copy-start | bytes 540676
  609.9 25.5 %copy-start.83 = (f32[2,1408,16]{1,2,0:T(8,128)}, f32[2,1408,16]{1,2,0:T(8,128)S(1)}, u32[]{:S(2)}) copy-start(f32[2,1408,16]{1,2,0:T(8,128)S(1)} %fusion.110) | copy-start | bytes 540676
  612.7 42.3 %collective-permute-start.11 = (f32[2,64,2048]{2,1,0:T(8,128)S(1)}, f32[2,64,2048]{2,1,0:T(8,128)S(1)}, u32[]{:S(2)}, u32[]{:S(2)}) collective-permute-start(f32[2,64,2048]{2,1,0:T(8,128)S(1)} %dynamic-slice_bitcast_fusion.5), channel_id=1, source_target_pairs={{0,2},{1,3},{2,0},{3,1},{4,6},{5,7},{6,4},{7,5},{8,10},{9,11},{10,... | collective-permute-start | bytes 3145736 | tf_op jit(solution)/shard_map/ppermute | solution.py:128
  633.5 44.0 %copy-start.48 = (bf16[2,64,2048]{2,1,0:T(8,128)(2,1)S(1)}, bf16[2,64,2048]{2,1,0:T(8,128)(2,1)}, u32[]{:S(2)}) copy-start(bf16[2,64,2048]{2,1,0:T(8,128)(2,1)} %param.19) | copy-start | bytes 1572868
  633.5 44.0 %copy-start.119 = (f32[2,64]{1,0:T(2,128)S(1)}, f32[2,64]{1,0:T(2,128)}, u32[]{:S(2)}) copy-start(f32[2,64]{1,0:T(2,128)} %copy-done.118) | copy-start | bytes 1540
  633.5 44.0 %collective-permute-start.7 = (f32[2,64,2048]{2,1,0:T(8,128)S(1)}, f32[2,64,2048]{2,1,0:T(8,128)S(1)}, u32[]{:S(2)}, u32[]{:S(2)}) collective-permute-start(f32[2,64,2048]{2,1,0:T(8,128)S(1)} %dynamic-slice_bitcast_fusion.6), channel_id=1, source_target_pairs={{0,2},{1,3},{2,0},{3,1},{4,6},{5,7},{6,4},{7,5},{8,10},{9,11},{10,... | collective-permute-start | bytes 3145736 | tf_op jit(solution)/shard_map/ppermute | solution.py:128
  635.4 46.6 %copy-start.67 = (f32[2,1,16,1408]{3,2,0,1:T(8,128)}, f32[2,1,16,1408]{3,2,0,1:T(8,128)S(1)}, u32[]{:S(2)}) copy-start(f32[2,1,16,1408]{3,2,0,1:T(8,128)S(1)} %fusion.7) | copy-start | bytes 540676
  679.2 14.7 %collective-permute-start.12 = (bf16[2,64,2048]{2,1,0:T(8,128)(2,1)}, bf16[2,64,2048]{2,1,0:T(8,128)(2,1)}, u32[]{:S(2)}, u32[]{:S(2)}) collective-permute-start(bf16[2,64,2048]{2,1,0:T(8,128)(2,1)} %get-tuple-element.34), channel_id=1, source_target_pairs={{0,2},{1,3},{2,0},{3,1},{4,6},{5,7},{6,4},{7,5},{8,10},{9,11},{10,... | collective-permute-start | bytes 1572872 | tf_op jit(solution)/shard_map/ppermute | solution.py:106
  696.6 32.0 %collective-permute-start.13 = (bf16[2,2,64,2048]{3,2,0,1:T(8,128)(2,1)}, bf16[2,2,64,2048]{3,2,0,1:T(8,128)(2,1)}, u32[]{:S(2)}, u32[]{:S(2)}) collective-permute-start(bf16[2,2,64,2048]{3,2,0,1:T(8,128)(2,1)} %maximum_select_fusion.9), channel_id=1, source_target_pairs={{0,1},{1,0},{2,3},{3,2},{4,5},{5,4},{6,7},{7,6},{8,9},{9,8},{10,11... | collective-permute-start | bytes 3145736 | tf_op jit(solution)/shard_map/ppermute | solution.py:110
  699.5 21.1 %collective-permute-start.19 = (f32[2,2,256,16]{2,3,1,0:T(8,128)}, f32[2,2,256,16]{2,3,1,0:T(8,128)}, u32[]{:S(2)}, u32[]{:S(2)}) collective-permute-start(f32[2,2,256,16]{2,3,1,0:T(8,128)} %fusion.68), channel_id=1, source_target_pairs={{0,2},{1,3},{2,0},{3,1},{4,6},{5,7},{6,4},{7,5},{8,10},{9,11},{10,... | collective-permute-start | bytes 196616 | tf_op jit(solution)/shard_map/ppermute | solution.py:134
  822.4 91.7 %all-to-all-start.7 = ((bf16[32,2,12544]{2,1,0:T(2,128)(2,1)}), bf16[32,2,12544]{2,1,0:T(2,128)(2,1)}, u32[]{:S(2)}, u32[]{:S(2)}) async-start(bf16[32,2,12544]{2,1,0:T(2,128)(2,1)} %reshape.787), calls=%async_computation.7 | async-start | bytes 3211264 | tf_op jit(solution)/shard_map/all_to_all | solution.py:397
  841.4 15.4 %collective-permute-start.16 = (f32[5,2,256,16]{2,3,1,0:T(8,128)}, f32[5,2,256,16]{2,3,1,0:T(8,128)S(1)}, u32[]{:S(2)}, u32[]{:S(2)}) collective-permute-start(f32[5,2,256,16]{2,3,1,0:T(8,128)} %bitcast_dynamic-update-slice_fusion), channel_id=1, source_target_pairs={{0,1},{1,0},{2,3},{3,2},{4,5},{5,4},{6,7},{7,6},{8,9},{9,8},{10,11... | collective-permute-start | bytes 491528 | tf_op jit(solution)/shard_map/ppermute | solution.py:133
  856.9 7.4 collective-permute-start.17
  860.5 61.8 %collective-permute-start.14 = (f32[2,2,64,2048]{3,2,1,0:T(8,128)}, f32[2,2,64,2048]{3,2,1,0:T(8,128)}, u32[]{:S(2)}, u32[]{:S(2)}) collective-permute-start(f32[2,2,64,2048]{3,2,1,0:T(8,128)} %dynamic-slice_bitcast_fusion), channel_id=1, source_target_pairs={{0,1},{1,0},{2,3},{3,2},{4,5},{5,4},{6,7},{7,6},{8,9},{9,8},{10,11... | collective-permute-start | bytes 6291464 | tf_op jit(solution)/shard_map/ppermute | solution.py:125
  914.2 33.3 %all-to-all-start.6 = ((f32[32,1,14336]{2,1,0:T(1,128)}), f32[32,1,14336]{2,1,0:T(1,128)}, u32[]{:S(2)}, u32[]{:S(2)}) async-start(f32[32,1,14336]{2,1,0:T(1,128)} %copy.287), calls=%async_computation.6 | async-start | bytes 3670016 | tf_op jit(solution)/shard_map/all_to_all | solution.py:379
  925.8 42.3 %collective-permute-start.15 = (f32[2,64,2048]{2,1,0:T(8,128)}, f32[2,64,2048]{2,1,0:T(8,128)}, u32[]{:S(2)}, u32[]{:S(2)}) collective-permute-start(f32[2,64,2048]{2,1,0:T(8,128)} %dynamic-slice_bitcast_fusion.4), channel_id=1, source_target_pairs={{0,2},{1,3},{2,0},{3,1},{4,6},{5,7},{6,4},{7,5},{8,10},{9,11},{10,... | collective-permute-start | bytes 3145736 | tf_op jit(solution)/shard_map/ppermute | solution.py:128
  941.7 26.5 %copy-start.9 = (bf16[2,64,2048]{2,1,0:T(8,128)(2,1)S(1)}, bf16[2,64,2048]{2,1,0:T(8,128)(2,1)}, u32[]{:S(2)}) copy-start(bf16[2,64,2048]{2,1,0:T(8,128)(2,1)} %param.18) | copy-start | bytes 1572868
  941.7 26.5 %copy-start.106 = (f32[2048]{0:T(1024)S(1)}, f32[2048]{0:T(1024)}, u32[]{:S(2)}) copy-start(f32[2048]{0:T(1024)} %param.26) | copy-start | bytes 24580
  (117 other events, 672.9 us)

commit v5 on v4

--- a/solution.py
+++ b/solution.py
@@ -193,10 +193,15 @@
         return out
 
     w_qkv_full = fsdp_gather(w_qkv, 1)
+    w_qkv_full, a_in, b_rows = lax.optimization_barrier((w_qkv_full, a_in, b_rows))
     g_ain, g_brows = packed_gather([a_in, b_rows], ("fsdp", "tok"))
+    g_ain, b_qkv, b_gateup, a_out, a_down = lax.optimization_barrier((g_ain, b_qkv, b_gateup, a_out, a_down))
     g_bqkv, g_bgateup, g_aout, g_adown = packed_gather([b_qkv, b_gateup, a_out, a_down], ("fsdp",))
+    g_bqkv, w_out = lax.optimization_barrier((g_bqkv, w_out))
     w_out_full = fsdp_gather(w_out, 1)
+    w_out_full, w_gateup = lax.optimization_barrier((w_out_full, w_gateup))
     w_gateup_full = fsdp_gather(w_gateup, 1)
+    w_gateup_full, w_down = lax.optimization_barrier((w_gateup_full, w_down))
     w_down_full = fsdp_gather(w_down, 1)
     a_in_full = jnp.moveaxis(g_ain, 0, 1).reshape(5, D, COLS)
     b_rows_full = jnp.moveaxis(g_brows, 0, 2).reshape(2, COLS, D)

time: 984 us -> 955 us (0.971)
  starting transfers between devices: 111 us -> 94.6 us
    all_to_all x0 -> x2, waiting for transfers between devices: none -> 50.4 us  [packed_gather(): lax.all_to_all(tiled_in, axes, 0, 0, tiled=True)]
    all_to_all x4 -> x3, waiting for transfers between devices: 91.5 us -> 46.2 us  [fsdp_gather(): return lax.all_to_all(tiled_in, 'fsdp', 0, axis, tiled=True)]
    slice x2 -> x0, local copies, waits for them, and re-layouts: 15 us -> none  [the longest x1 9.4 us: per_device(): w_gateup_full[0]]
    ppermute x4, waiting for transfers between devices: 95.1 us -> 80.4 us  [tok_gather(): far = lax.ppermute(values, 'tok', xor_pairs(count, 2))]
    all_to_all x0 -> x2, starting transfers between devices: none -> 14.4 us  [packed_gather(): lax.all_to_all(tiled_in, axes, 0, 0, tiled=True)]
    ppermute x4, starting transfers between devices: 20.5 us -> 6.84 us  [tok_scatter(): return keep + lax.ppermute(send, 'tok', xor_pairs(count, 2))]
    all_to_all x0 -> x2, local copies, waits for them, and re-layouts: none -> 13.4 us  [fsdp_gather(): return lax.all_to_all(tiled_in, 'fsdp', 0, axis, tiled=True)]
    all_to_all x2 -> x1, blocking collectives: 87.4 us -> 80 us  [fsdp_gather(): return lax.all_to_all(tiled_in, 'fsdp', 0, axis, tiled=True)]
  transfers between devices with their start and end apart: 26 -> 27, of which waited for: 12 -> 10; matrix products, arithmetic and copies ran while one was open for 28% -> 32% of each run, Pallas kernels for 0% -> 0%
where the time goes in v5:
time: 955 us; the launch traced here: 945 us
  waiting for transfers between devices  319 us (33%)
  local copies, waits for them, and re-layouts  234 us (25%)
  matrix products  120 us (13%)
  starting transfers between devices  94.6 us (10%)
  other arithmetic  89 us (9%)
  blocking collectives  80 us (8%)
    ppermute x4, waiting for transfers between devices, tok_scatter(): return keep + lax.ppermute(send, 'tok', xor_pairs(count, 2))  142 us
    ppermute x4, waiting for transfers between devices, tok_gather(): far = lax.ppermute(values, 'tok', xor_pairs(count, 2))  80.4 us
    all_to_all x1, blocking collectives, fsdp_gather(): return lax.all_to_all(tiled_in, 'fsdp', 0, axis, tiled=True)  80 us
    all_to_all x2, waiting for transfers between devices, packed_gather(): lax.all_to_all(tiled_in, axes, 0, 0, tiled=True)  50.4 us
    dot_general x32, matrix products, hp_dot(): jnp.einsum(spec, left, right, precision=highest, preferred_element_type=j...  48.6 us
    all_to_all x3, waiting for transfers between devices, fsdp_gather(): return lax.all_to_all(tiled_in, 'fsdp', 0, axis, tiled=True)  46.2 us
    unnamed x284, local copies, waits for them, and re-layouts  35.9 us
    all_to_all x3, starting transfers between devices, fsdp_gather(): return lax.all_to_all(tiled_in, 'fsdp', 0, axis, tiled=True)  33.1 us
  transfers between devices with their start and end apart: 27, of which 10 were waited for; matrix products, arithmetic and copies ran while one was open for 32% of the time, Pallas kernels for 0%

profile of v5, /device:TPU:1, one launch (start us, length us, event | category | flops | bytes accessed | tf_op | source)
XLA Modules:
  0.0 944.7 jit_solution(5375670721579515820)
XLA Ops:
  2.3 80.0 %all_to_all.95 = bf16[96,64,512]{2,1,0:T(8,128)(2,1)S(1)} all-to-all(bf16[96,64,512]{2,1,0:T(8,128)(2,1)S(1)} %bitcast.555), channel_id=1, replica_groups=mesh['fsdp'=32,'tok'=4] {'fsdp'}, dimensions={0} | all-to-all | bytes 12582912 | tf_op jit(solution)/shard_map/all_to_all | solution.py:178
  88.4 9.8 %all-to-all-start.1 = ((bf16[128,112,128]{2,1,0:T(8,128)(2,1)}), bf16[128,112,128]{2,1,0:T(8,128)(2,1)}, u32[]{:S(2)}, u32[]{:S(2)}) async-start(bf16[128,112,128]{2,1,0:T(8,128)(2,1)} %broadcast_in_dim.43), calls=%async_computation.1 | async-start | bytes 7340032 | tf_op jit(solution)/shard_map/all_to_all | solution.py:186
  104.7 40.6 %all-to-all-done.1 = bf16[128,112,128]{2,1,0:T(8,128)(2,1)} async-done(((bf16[128,112,128]{2,1,0:T(8,128)(2,1)}), bf16[128,112,128]{2,1,0:T(8,128)(2,1)}, u32[]{:S(2)}, u32[]{:S(2)}) %all-to-all-start.1) | async-done | bytes 3670048 | tf_op jit(solution)/shard_map/all_to_all | solution.py:186
  151.3 4.7 all-to-all-start.2
  166.7 9.8 %all-to-all-done.2 = bf16[32,196,128]{2,1,0:T(8,128)(2,1)S(1)} async-done(((bf16[32,196,128]{2,1,0:T(8,128)(2,1)}), bf16[32,196,128]{2,1,0:T(8,128)(2,1)S(1)}, u32[]{:S(2)}, u32[]{:S(2)}) %all-to-all-start.2) | async-done | bytes 1605664 | tf_op jit(solution)/shard_map/all_to_all | solution.py:186
  179.1 7.5 all-to-all-start.3
  189.8 4.0 constant_dynamic-slice_fusion.7
  206.2 3.6 constant_dynamic-slice_fusion.3
  215.5 6.8 broadcast_in_dim.48
  222.2 8.0 all-to-all-start.4
  235.4 3.8 fusion.48
  242.4 3.8 fusion.45
  248.8 3.5 subtract_convert_fusion
  286.7 13.2 %collective-permute-done.8 = bf16[2,64,2048]{2,1,0:T(8,128)(2,1)S(1)} collective-permute-done((bf16[2,64,2048]{2,1,0:T(8,128)(2,1)S(1)}, bf16[2,64,2048]{2,1,0:T(8,128)(2,1)S(1)}, u32[]{:S(2)}, u32[]{:S(2)}) %collective-permute-start.8) | collective-permute-done | bytes 524320 | tf_op jit(solution)/shard_map/ppermute | solution.py:106
  313.8 83.7 %collective-permute-done.3 = f32[2,64,2048]{2,1,0:T(8,128)} collective-permute-done((f32[2,64,2048]{2,1,0:T(8,128)}, f32[2,64,2048]{2,1,0:T(8,128)}, u32[]{:S(2)}, u32[]{:S(2)}) %collective-permute-start.3) | collective-permute-done | bytes 1048608 | tf_op jit(solution)/shard_map/ppermute | solution.py:128
  399.3 46.2 %all-to-all-done.4 = bf16[64,64,1408]{2,1,0:T(8,128)(2,1)} async-done(((bf16[64,64,1408]{2,1,0:T(8,128)(2,1)}), bf16[64,64,1408]{2,1,0:T(8,128)(2,1)}, u32[]{:S(2)}, u32[]{:S(2)}) %all-to-all-start.4) | async-done | bytes 11534368 | tf_op jit(solution)/shard_map/all_to_all | solution.py:178
  445.5 10.0 %copy.252 = bf16[2,32,64,1408]{3,2,1,0:T(8,128)(2,1)} copy(bf16[2,32,64,1408]{3,2,0,1:T(8,128)(2,1)} %bitcast.67) | data formatting | bytes 23068672 | tf_op jit(solution)/shard_map/all_to_all | solution.py:178
  458.7 17.6 %all-to-all-start.5 = ((bf16[32,1408,64]{1,2,0:T(8,128)(2,1)}), bf16[32,1408,64]{1,2,0:T(8,128)(2,1)}, u32[]{:S(2)}, u32[]{:S(2)}) async-start(bf16[32,1408,64]{1,2,0:T(8,128)(2,1)} %broadcast_in_dim.49), calls=%async_computation.5 | async-start | bytes 11534336 | tf_op jit(solution)/shard_map/all_to_all | solution.py:178
  488.0 61.4 %collective-permute-done.4 = bf16[2,64,2048]{2,1,0:T(8,128)(2,1)} collective-permute-done((bf16[2,64,2048]{2,1,0:T(8,128)(2,1)}, bf16[2,64,2048]{2,1,0:T(8,128)(2,1)}, u32[]{:S(2)}, u32[]{:S(2)}) %collective-permute-start.4) | collective-permute-done | bytes 524320 | tf_op jit(solution)/shard_map/ppermute | solution.py:106
  550.8 4.3 collective-permute-start.5
  565.0 6.1 fusion.2
  574.2 5.0 fusion.6
  579.2 6.5 fusion.145
  587.2 3.5 fusion.16
  590.8 3.4 fusion.4
  594.7 3.5 fusion
  605.8 5.5 fusion.143
  632.5 19.3 %collective-permute-done.11 = f32[2,64,2048]{2,1,0:T(8,128)S(1)} collective-permute-done((f32[2,64,2048]{2,1,0:T(8,128)S(1)}, f32[2,64,2048]{2,1,0:T(8,128)S(1)}, u32[]{:S(2)}, u32[]{:S(2)}) %collective-permute-start.11) | collective-permute-done | bytes 1048608 | tf_op jit(solution)/shard_map/ppermute | solution.py:128
  652.0 22.2 %collective-permute-done.7 = f32[2,64,2048]{2,1,0:T(8,128)S(1)} collective-permute-done((f32[2,64,2048]{2,1,0:T(8,128)S(1)}, f32[2,64,2048]{2,1,0:T(8,128)S(1)}, u32[]{:S(2)}, u32[]{:S(2)}) %collective-permute-start.7) | collective-permute-done | bytes 1048608 | tf_op jit(solution)/shard_map/ppermute | solution.py:128
  684.1 5.7 collective-permute-done.12
  725.3 3.9 fusion.51
  752.5 4.3 multiply_add_fusion.5
  759.3 5.4 fusion.28
  768.5 3.8 fusion.76
  778.0 5.2 fusion.32
  821.7 4.0 reduce.2
  828.3 7.5 all-to-all-start.7
  838.7 8.7 reshape.746
  847.5 6.8 constant_dynamic-slice_fusion
  854.3 4.2 copy.335
  858.5 4.2 copy.287
  866.7 4.6 dynamic_update_slice.36
  872.7 5.3 dynamic_update_slice.37
  878.0 4.1 copy.336
  885.4 8.5 all-to-all-start.6
  899.1 9.6 %reshape.767 = bf16[32,1,25088]{2,1,0:T(2,128)(2,1)} reshape(bf16[32,2,12544]{2,1,0:T(2,128)(2,1)} %all-to-all-done.7) | data formatting | bytes 3211264
  908.7 5.3 convert_reduce_fusion
  923.9 16.5 %collective-permute-done.15 = f32[2,64,2048]{2,1,0:T(8,128)} collective-permute-done((f32[2,64,2048]{2,1,0:T(8,128)}, f32[2,64,2048]{2,1,0:T(8,128)}, u32[]{:S(2)}, u32[]{:S(2)}) %collective-permute-start.15) | collective-permute-done | bytes 1048608 | tf_op jit(solution)/shard_map/ppermute | solution.py:128
  (573 shorter events, 321.4 us)
Async XLA Ops:
  88.4 56.9 %all-to-all-start.1 = ((bf16[128,112,128]{2,1,0:T(8,128)(2,1)}), bf16[128,112,128]{2,1,0:T(8,128)(2,1)}, u32[]{:S(2)}, u32[]{:S(2)}) async-start(bf16[128,112,128]{2,1,0:T(8,128)(2,1)} %broadcast_in_dim.43), calls=%async_computation.1 | async-start | bytes 7340032 | tf_op jit(solution)/shard_map/all_to_all | solution.py:186
  98.3 58.5 %copy-start.109 = (f32[2,64]{1,0:T(2,128)}, f32[2,64]{1,0:T(2,128)S(1)}, u32[]{:S(2)}) copy-start(f32[2,64]{1,0:T(2,128)S(1)} %fusion.112) | copy-start | bytes 1540
  99.3 58.5 %collective-permute-start = (bf16[2,64,2048]{2,1,0:T(8,128)(2,1)}, bf16[2,64,2048]{2,1,0:T(8,128)(2,1)S(1)}, u32[]{:S(2)}, u32[]{:S(2)}) collective-permute-start(bf16[2,64,2048]{2,1,0:T(8,128)(2,1)} %fusion.65), channel_id=1, source_target_pairs={{0,2},{1,3},{2,0},{3,1},{4,6},{5,7},{6,4},{7,5},{8,10},{9,11},{10,... | collective-permute-start | bytes 1572872 | tf_op jit(solution)/shard_map/ppermute | solution.py:106
  104.6 44.0 %copy-start.116 = (bf16[1408,4]{0,1:T(4,128)(2,1)S(1)}, bf16[1408,4]{0,1:T(4,128)(2,1)}, u32[]{:S(2)}) copy-start(bf16[1408,4]{0,1:T(4,128)(2,1)} %param.34) | copy-start | bytes 33796
  104.6 44.8 %copy-start.124 = (bf16[512,4]{0,1:T(4,128)(2,1)S(1)}, bf16[512,4]{0,1:T(4,128)(2,1)}, u32[]{:S(2)}) copy-start(bf16[512,4]{0,1:T(4,128)(2,1)} %param.33) | copy-start | bytes 12292
  104.6 45.2 %copy-start.113 = (bf16[2,4,1408]{2,1,0:T(4,128)(2,1)S(1)}, bf16[2,4,1408]{2,1,0:T(4,128)(2,1)}, u32[]{:S(2)}) copy-start(bf16[2,4,1408]{2,1,0:T(4,128)(2,1)} %param.32) | copy-start | bytes 67588
  104.7 45.2 %copy-start.115 = (bf16[3,4,512]{2,1,0:T(4,128)(2,1)S(1)}, bf16[3,4,512]{2,1,0:T(4,128)(2,1)}, u32[]{:S(2)}) copy-start(bf16[3,4,512]{2,1,0:T(4,128)(2,1)} %param.31) | copy-start | bytes 36868
  151.3 25.2 %all-to-all-start.2 = ((bf16[32,196,128]{2,1,0:T(8,128)(2,1)}), bf16[32,196,128]{2,1,0:T(8,128)(2,1)S(1)}, u32[]{:S(2)}, u32[]{:S(2)}) async-start(bf16[32,196,128]{2,1,0:T(8,128)(2,1)} %broadcast_in_dim.44), calls=%async_computation.2 | async-start | bytes 3276800 | tf_op jit(solution)/shard_map/all_to_all | solution.py:186
  158.9 28.0 %collective-permute-start.1 = (bf16[2,2,64,2048]{3,2,1,0:T(8,128)(2,1)}, bf16[2,2,64,2048]{3,2,1,0:T(8,128)(2,1)}, u32[]{:S(2)}, u32[]{:S(2)}) collective-permute-start(bf16[2,2,64,2048]{3,2,1,0:T(8,128)(2,1)} %maximum_select_fusion.4), channel_id=1, source_target_pairs={{0,1},{1,0},{2,3},{3,2},{4,5},{5,4},{6,7},{7,6},{8,9},{9,8},{10,11... | collective-permute-start | bytes 3145736 | tf_op jit(solution)/shard_map/ppermute | solution.py:110
  179.1 36.3 %all-to-all-start.3 = ((bf16[32,512,64]{1,2,0:T(8,128)(2,1)}), bf16[32,512,64]{1,2,0:T(8,128)(2,1)}, u32[]{:S(2)}, u32[]{:S(2)}) async-start(bf16[32,512,64]{1,2,0:T(8,128)(2,1)} %broadcast_in_dim.47), calls=%async_computation.3 | async-start | bytes 4194304 | tf_op jit(solution)/shard_map/all_to_all | solution.py:178
  189.0 81.1 %copy-start = (bf16[2,2,2,64,2048]{4,3,2,1,0:T(8,128)(2,1)}, bf16[2,2,2,64,2048]{4,3,2,1,0:T(8,128)(2,1)S(1)}, u32[]{:S(2)}) copy-start(bf16[2,2,2,64,2048]{4,3,2,1,0:T(8,128)(2,1)S(1)} %maximum_select_fusion) | copy-start | bytes 6291460
  197.9 109.3 %copy-start.4 = (bf16[5,2048,16]{1,2,0:T(8,128)(2,1)}, bf16[5,2048,16]{1,2,0:T(8,128)(2,1)S(1)}, u32[]{:S(2)}) copy-start(bf16[5,2048,16]{1,2,0:T(8,128)(2,1)S(1)} %copy.230) | copy-start | bytes 983044
  211.3 96.7 %copy-start.44 = (bf16[2,16,2048]{2,1,0:T(8,128)(2,1)}, bf16[2,16,2048]{2,1,0:T(8,128)(2,1)S(1)}, u32[]{:S(2)}) copy-start(bf16[2,16,2048]{2,1,0:T(8,128)(2,1)S(1)} %copy.247) | copy-start | bytes 393220
  215.4 26.3 %copy-start.81 = (f32[2,256,16]{1,2,0:T(8,128)}, f32[2,256,16]{1,2,0:T(8,128)S(1)}, u32[]{:S(2)}) copy-start(f32[2,256,16]{1,2,0:T(8,128)S(1)} %fusion.125) | copy-start | bytes 98308
  222.2 223.3 %all-to-all-start.4 = ((bf16[64,64,1408]{2,1,0:T(8,128)(2,1)}), bf16[64,64,1408]{2,1,0:T(8,128)(2,1)}, u32[]{:S(2)}, u32[]{:S(2)}) async-start(bf16[64,64,1408]{2,1,0:T(8,128)(2,1)} %bitcast.524), calls=%async_computation.4 | async-start | bytes 23068672 | tf_op jit(solution)/shard_map/all_to_all | solution.py:178
  282.6 18.3 %collective-permute-start.2 = (f32[2,2,64,2048]{3,2,1,0:T(8,128)}, f32[2,2,64,2048]{3,2,1,0:T(8,128)}, u32[]{:S(2)}, u32[]{:S(2)}) collective-permute-start(f32[2,2,64,2048]{3,2,1,0:T(8,128)} %dynamic-slice_bitcast_fusion.3), channel_id=1, source_target_pairs={{0,1},{1,0},{2,3},{3,2},{4,5},{5,4},{6,7},{7,6},{8,9},{9,8},{10,11... | collective-permute-start | bytes 6291464 | tf_op jit(solution)/shard_map/ppermute | solution.py:125
  284.8 15.2 %collective-permute-start.8 = (bf16[2,64,2048]{2,1,0:T(8,128)(2,1)S(1)}, bf16[2,64,2048]{2,1,0:T(8,128)(2,1)S(1)}, u32[]{:S(2)}, u32[]{:S(2)}) collective-permute-start(bf16[2,64,2048]{2,1,0:T(8,128)(2,1)S(1)} %copy-done.39), channel_id=1, source_target_pairs={{0,2},{1,3},{2,0},{3,1},{4,6},{5,7},{6,4},{7,5},{8,10},{9,11},{10,... | collective-permute-start | bytes 1572872 | tf_op jit(solution)/shard_map/ppermute | solution.py:106
  300.1 6.7 collective-permute-start.9
  304.5 93.0 %collective-permute-start.3 = (f32[2,64,2048]{2,1,0:T(8,128)}, f32[2,64,2048]{2,1,0:T(8,128)}, u32[]{:S(2)}, u32[]{:S(2)}) collective-permute-start(f32[2,64,2048]{2,1,0:T(8,128)} %dynamic-slice_bitcast_fusion.7), channel_id=1, source_target_pairs={{0,2},{1,3},{2,0},{3,1},{4,6},{5,7},{6,4},{7,5},{8,10},{9,11},{10,... | collective-permute-start | bytes 3145736 | tf_op jit(solution)/shard_map/ppermute | solution.py:128
  399.3 77.0 %copy-start.120 = (f32[2,64]{1,0:T(2,128)}, f32[2,64]{1,0:T(2,128)S(1)}, u32[]{:S(2)}) copy-start(f32[2,64]{1,0:T(2,128)S(1)} %get-tuple-element.64) | copy-start | bytes 1540
  458.7 120.4 %all-to-all-start.5 = ((bf16[32,1408,64]{1,2,0:T(8,128)(2,1)}), bf16[32,1408,64]{1,2,0:T(8,128)(2,1)}, u32[]{:S(2)}, u32[]{:S(2)}) async-start(bf16[32,1408,64]{1,2,0:T(8,128)(2,1)} %broadcast_in_dim.49), calls=%async_computation.5 | async-start | bytes 11534336 | tf_op jit(solution)/shard_map/all_to_all | solution.py:178
  476.4 84.4 %copy-start.111 = (f32[2,64]{1,0:T(2,128)}, f32[2,64]{1,0:T(2,128)S(1)}, u32[]{:S(2)}) copy-start(f32[2,64]{1,0:T(2,128)S(1)} %fusion.113) | copy-start | bytes 1540
  477.4 72.1 %collective-permute-start.4 = (bf16[2,64,2048]{2,1,0:T(8,128)(2,1)}, bf16[2,64,2048]{2,1,0:T(8,128)(2,1)}, u32[]{:S(2)}, u32[]{:S(2)}) collective-permute-start(bf16[2,64,2048]{2,1,0:T(8,128)(2,1)} %multiply_convert_fusion.3), channel_id=1, source_target_pairs={{0,2},{1,3},{2,0},{3,1},{4,6},{5,7},{6,4},{7,5},{8,10},{9,11},{10,... | collective-permute-start | bytes 1572872 | tf_op jit(solution)/shard_map/ppermute | solution.py:106
  487.9 67.2 %copy-start.101 = (bf16[4,1408,4]{1,2,0:T(4,128)(2,1)S(1)}, bf16[4,1408,4]{1,2,0:T(4,128)(2,1)}, u32[]{:S(2)}) copy-start(bf16[4,1408,4]{1,2,0:T(4,128)(2,1)} %copy.256) | copy-start | bytes 135172
  550.8 11.5 %collective-permute-start.5 = (bf16[2,2,64,2048]{3,2,0,1:T(8,128)(2,1)S(1)}, bf16[2,2,64,2048]{3,2,0,1:T(8,128)(2,1)S(1)}, u32[]{:S(2)}, u32[]{:S(2)}) collective-permute-start(bf16[2,2,64,2048]{3,2,0,1:T(8,128)(2,1)S(1)} %maximum_select_fusion.6), channel_id=1, source_target_pairs={{0,1},{1,0},{2,3},{3,2},{4,5},{5,4},{6,7},{7,6},{8,9},{9,8},{10,11... | collective-permute-start | bytes 3145736 | tf_op jit(solution)/shard_map/ppermute | solution.py:110
  564.3 22.9 %copy-start.102 = (f32[2,256,16]{1,2,0:T(8,128)}, f32[2,256,16]{1,2,0:T(8,128)S(1)}, u32[]{:S(2)}) copy-start(f32[2,256,16]{1,2,0:T(8,128)S(1)} %fusion.132) | copy-start | bytes 98308
  605.8 17.4 %collective-permute-start.10 = (f32[2,2,64,2048]{3,2,1,0:T(8,128)}, f32[2,2,64,2048]{3,2,1,0:T(8,128)}, u32[]{:S(2)}, u32[]{:S(2)}) collective-permute-start(f32[2,2,64,2048]{3,2,1,0:T(8,128)} %dynamic-slice_bitcast_fusion.1), channel_id=1, source_target_pairs={{0,1},{1,0},{2,3},{3,2},{4,5},{5,4},{6,7},{7,6},{8,9},{9,8},{10,11... | collective-permute-start | bytes 6291464 | tf_op jit(solution)/shard_map/ppermute | solution.py:125
  616.7 11.0 %collective-permute-start.6 = (f32[2,2,64,2048]{3,2,1,0:T(8,128)}, f32[2,2,64,2048]{3,2,1,0:T(8,128)}, u32[]{:S(2)}, u32[]{:S(2)}) collective-permute-start(f32[2,2,64,2048]{3,2,1,0:T(8,128)} %dynamic-slice_bitcast_fusion.2), channel_id=1, source_target_pairs={{0,1},{1,0},{2,3},{3,2},{4,5},{5,4},{6,7},{7,6},{8,9},{9,8},{10,11... | collective-permute-start | bytes 6291464 | tf_op jit(solution)/shard_map/ppermute | solution.py:125
  619.0 75.9 %collective-permute-start.18 = (f32[2,2,256,16]{2,3,1,0:T(8,128)}, f32[2,2,256,16]{2,3,1,0:T(8,128)}, u32[]{:S(2)}, u32[]{:S(2)}) collective-permute-start(f32[2,2,256,16]{2,3,1,0:T(8,128)} %pad_maximum_fusion.11), channel_id=1, source_target_pairs={{0,1},{1,0},{2,3},{3,2},{4,5},{5,4},{6,7},{7,6},{8,9},{9,8},{10,11... | collective-permute-start | bytes 196616 | tf_op jit(solution)/shard_map/ppermute | solution.py:133
  621.1 56.6 %copy-start.56 = (f32[2,1,16,1408]{3,2,0,1:T(8,128)}, f32[2,1,16,1408]{3,2,0,1:T(8,128)S(1)}, u32[]{:S(2)}) copy-start(f32[2,1,16,1408]{3,2,0,1:T(8,128)S(1)} %fusion.18) | copy-start | bytes 540676
  626.0 25.8 %collective-permute-start.11 = (f32[2,64,2048]{2,1,0:T(8,128)S(1)}, f32[2,64,2048]{2,1,0:T(8,128)S(1)}, u32[]{:S(2)}, u32[]{:S(2)}) collective-permute-start(f32[2,64,2048]{2,1,0:T(8,128)S(1)} %dynamic-slice_bitcast_fusion.5), channel_id=1, source_target_pairs={{0,2},{1,3},{2,0},{3,1},{4,6},{5,7},{6,4},{7,5},{8,10},{9,11},{10,... | collective-permute-start | bytes 3145736 | tf_op jit(solution)/shard_map/ppermute | solution.py:128
  629.7 22.3 %copy-start.121 = (f32[2,64]{1,0:T(2,128)S(1)}, f32[2,64]{1,0:T(2,128)}, u32[]{:S(2)}) copy-start(f32[2,64]{1,0:T(2,128)} %copy-done.120) | copy-start | bytes 1540
  629.7 44.5 %copy-start.40 = (bf16[2,64,2048]{2,1,0:T(8,128)(2,1)S(1)}, bf16[2,64,2048]{2,1,0:T(8,128)(2,1)}, u32[]{:S(2)}) copy-start(bf16[2,64,2048]{2,1,0:T(8,128)(2,1)} %param.19) | copy-start | bytes 1572868
  629.7 44.5 %copy-start.112 = (f32[2,64]{1,0:T(2,128)S(1)}, f32[2,64]{1,0:T(2,128)}, u32[]{:S(2)}) copy-start(f32[2,64]{1,0:T(2,128)} %copy-done.111) | copy-start | bytes 1540
  629.7 44.5 %collective-permute-start.7 = (f32[2,64,2048]{2,1,0:T(8,128)S(1)}, f32[2,64,2048]{2,1,0:T(8,128)S(1)}, u32[]{:S(2)}, u32[]{:S(2)}) collective-permute-start(f32[2,64,2048]{2,1,0:T(8,128)S(1)} %dynamic-slice_bitcast_fusion.6), channel_id=1, source_target_pairs={{0,2},{1,3},{2,0},{3,1},{4,6},{5,7},{6,4},{7,5},{8,10},{9,11},{10,... | collective-permute-start | bytes 3145736 | tf_op jit(solution)/shard_map/ppermute | solution.py:128
  631.8 45.9 %copy-start.58 = (f32[2,1,16,1408]{3,2,0,1:T(8,128)}, f32[2,1,16,1408]{3,2,0,1:T(8,128)S(1)}, u32[]{:S(2)}) copy-start(f32[2,1,16,1408]{3,2,0,1:T(8,128)S(1)} %fusion.19) | copy-start | bytes 540676
  676.0 13.9 %collective-permute-start.12 = (bf16[2,64,2048]{2,1,0:T(8,128)(2,1)}, bf16[2,64,2048]{2,1,0:T(8,128)(2,1)}, u32[]{:S(2)}, u32[]{:S(2)}) collective-permute-start(bf16[2,64,2048]{2,1,0:T(8,128)(2,1)} %get-tuple-element.62), channel_id=1, source_target_pairs={{0,2},{1,3},{2,0},{3,1},{4,6},{5,7},{6,4},{7,5},{8,10},{9,11},{10,... | collective-permute-start | bytes 1572872 | tf_op jit(solution)/shard_map/ppermute | solution.py:106
  692.7 28.3 %collective-permute-start.13 = (bf16[2,2,64,2048]{3,2,0,1:T(8,128)(2,1)}, bf16[2,2,64,2048]{3,2,0,1:T(8,128)(2,1)}, u32[]{:S(2)}, u32[]{:S(2)}) collective-permute-start(bf16[2,2,64,2048]{3,2,0,1:T(8,128)(2,1)} %maximum_select_fusion.9), channel_id=1, source_target_pairs={{0,1},{1,0},{2,3},{3,2},{4,5},{5,4},{6,7},{7,6},{8,9},{9,8},{10,11... | collective-permute-start | bytes 3145736 | tf_op jit(solution)/shard_map/ppermute | solution.py:110
  696.4 16.5 %collective-permute-start.19 = (f32[2,2,256,16]{2,3,1,0:T(8,128)}, f32[2,2,256,16]{2,3,1,0:T(8,128)}, u32[]{:S(2)}, u32[]{:S(2)}) collective-permute-start(f32[2,2,256,16]{2,3,1,0:T(8,128)} %fusion.116), channel_id=1, source_target_pairs={{0,2},{1,3},{2,0},{3,1},{4,6},{5,7},{6,4},{7,5},{8,10},{9,11},{10,... | collective-permute-start | bytes 196616 | tf_op jit(solution)/shard_map/ppermute | solution.py:134
  802.2 91.7 %collective-permute-start.14 = (f32[2,2,64,2048]{3,2,1,0:T(8,128)}, f32[2,2,64,2048]{3,2,1,0:T(8,128)}, u32[]{:S(2)}, u32[]{:S(2)}) collective-permute-start(f32[2,2,64,2048]{3,2,1,0:T(8,128)} %dynamic-slice_bitcast_fusion), channel_id=1, source_target_pairs={{0,1},{1,0},{2,3},{3,2},{4,5},{5,4},{6,7},{7,6},{8,9},{9,8},{10,11... | collective-permute-start | bytes 6291464 | tf_op jit(solution)/shard_map/ppermute | solution.py:125
  803.7 11.3 %collective-permute-start.16 = (f32[5,2,256,16]{2,3,1,0:T(8,128)}, f32[5,2,256,16]{2,3,1,0:T(8,128)}, u32[]{:S(2)}, u32[]{:S(2)}) collective-permute-start(f32[5,2,256,16]{2,3,1,0:T(8,128)} %bitcast_dynamic-update-slice_fusion), channel_id=1, source_target_pairs={{0,1},{1,0},{2,3},{3,2},{4,5},{5,4},{6,7},{7,6},{8,9},{9,8},{10,11... | collective-permute-start | bytes 491528 | tf_op jit(solution)/shard_map/ppermute | solution.py:133
  816.0 19.8 %collective-permute-start.17 = (f32[5,2,256,16]{2,3,1,0:T(8,128)S(1)}, f32[5,2,256,16]{2,3,1,0:T(8,128)S(1)}, u32[]{:S(2)}, u32[]{:S(2)}) collective-permute-start(f32[5,2,256,16]{2,3,1,0:T(8,128)S(1)} %add.296), channel_id=1, source_target_pairs={{0,2},{1,3},{2,0},{3,1},{4,6},{5,7},{6,4},{7,5},{8,10},{9,11},{10,... | collective-permute-start | bytes 491528 | tf_op jit(solution)/shard_map/ppermute | solution.py:134
  828.3 57.2 %all-to-all-start.7 = ((bf16[32,2,12544]{2,1,0:T(2,128)(2,1)}), bf16[32,2,12544]{2,1,0:T(2,128)(2,1)}, u32[]{:S(2)}, u32[]{:S(2)}) async-start(bf16[32,2,12544]{2,1,0:T(2,128)(2,1)} %reshape.766), calls=%async_computation.7 | async-start | bytes 3211264 | tf_op jit(solution)/shard_map/all_to_all | solution.py:402
  885.4 34.5 %all-to-all-start.6 = ((f32[32,1,14336]{2,1,0:T(1,128)}), f32[32,1,14336]{2,1,0:T(1,128)}, u32[]{:S(2)}, u32[]{:S(2)}) async-start(f32[32,1,14336]{2,1,0:T(1,128)} %copy.293), calls=%async_computation.6 | async-start | bytes 3670016 | tf_op jit(solution)/shard_map/all_to_all | solution.py:384
  897.4 43.0 %collective-permute-start.15 = (f32[2,64,2048]{2,1,0:T(8,128)}, f32[2,64,2048]{2,1,0:T(8,128)}, u32[]{:S(2)}, u32[]{:S(2)}) collective-permute-start(f32[2,64,2048]{2,1,0:T(8,128)} %dynamic-slice_bitcast_fusion.4), channel_id=1, source_target_pairs={{0,2},{1,3},{2,0},{3,1},{4,6},{5,7},{6,4},{7,5},{8,10},{9,11},{10,... | collective-permute-start | bytes 3145736 | tf_op jit(solution)/shard_map/ppermute | solution.py:128
  915.6 24.8 %copy-start.9 = (bf16[2,64,2048]{2,1,0:T(8,128)(2,1)S(1)}, bf16[2,64,2048]{2,1,0:T(8,128)(2,1)}, u32[]{:S(2)}) copy-start(bf16[2,64,2048]{2,1,0:T(8,128)(2,1)} %param.18) | copy-start | bytes 1572868
  915.6 24.8 %copy-start.98 = (f32[2048]{0:T(1024)S(1)}, f32[2048]{0:T(1024)}, u32[]{:S(2)}) copy-start(f32[2048]{0:T(1024)} %param.26) | copy-start | bytes 24580
  919.9 22.0 %copy-start.110 = (f32[2,64]{1,0:T(2,128)S(1)}, f32[2,64]{1,0:T(2,128)}, u32[]{:S(2)}) copy-start(f32[2,64]{1,0:T(2,128)} %copy-done.109) | copy-start | bytes 1540
  (119 other events, 616.3 us)

commit v6 on v5

--- a/solution.py
+++ b/solution.py
@@ -3,6 +3,8 @@
 import jax
 import jax.numpy as jnp
 from jax import lax
+from jax.experimental import pallas as pl
+from jax.experimental.pallas import tpu as pltpu
 from jax.sharding import PartitionSpec as P
 
 D = 2048
@@ -94,6 +96,52 @@
         * scale
     )
     return (grad_query, grad_key, grad_values.astype(jnp.bfloat16))
+
+
+def _colgrad_kernel(e_ref, w_ref, el_ref, at_ref, o_ref, acc_ref):
+    p = pl.program_id(2)
+
+    @pl.when(p == 0)
+    def _():
+        acc_ref[...] = jnp.zeros_like(acc_ref)
+
+    acc_ref[...] += lax.dot_general(
+        e_ref[...], w_ref[...], (((1,), (1,)), ((), ())), preferred_element_type=jnp.float32
+    )
+    acc_ref[...] += jnp.dot(
+        el_ref[...], at_ref[...].astype(jnp.float32),
+        precision=lax.Precision.HIGHEST, preferred_element_type=jnp.float32,
+    )
+
+    @pl.when(p == pl.num_programs(2) - 1)
+    def _():
+        o_ref[...] = acc_ref[...]
+
+def column_input_grad(e_all, w_all, el_all, at_all, tile=512):
+    projs, seqs, length, width = e_all.shape
+    model = w_all.shape[1]
+    rank = el_all.shape[-1]
+    return pl.pallas_call(
+        _colgrad_kernel,
+        out_shape=jax.ShapeDtypeStruct((seqs, length, model), jnp.float32),
+        grid=(seqs, model // tile, projs),
+        in_specs=[
+            pl.BlockSpec((None, None, length, width), lambda s, j, p: (p, s, 0, 0)),
+            pl.BlockSpec((None, tile, width), lambda s, j, p: (p, j, 0)),
+            pl.BlockSpec((None, None, length, rank), lambda s, j, p: (p, s, 0, 0)),
+            pl.BlockSpec((None, None, rank, tile), lambda s, j, p: (p, s, 0, j)),
+        ],
+        out_specs=pl.BlockSpec((None, length, tile), lambda s, j, p: (s, 0, j)),
+        scratch_shapes=[pltpu.VMEM((length, tile), jnp.float32)],
+        compiler_params=pltpu.CompilerParams(
+            dimension_semantics=("parallel", "parallel", "arbitrary")
+        ),
+        cost_estimate=pl.CostEstimate(
+            flops=2 * projs * seqs * length * model * (width + rank),
+            transcendentals=0,
+            bytes_accessed=2 * (e_all.size + seqs * w_all.size) + 4 * seqs * length * model,
+        ),
+    )(e_all, w_all, el_all, at_all)
 
 
 def xor_pairs(count, bit):
@@ -291,19 +339,18 @@
         ) + hp_dot(grad_low, down_sel.astype(jnp.float32), "str,sdr->std")
         return grad_inputs, grad_down
 
-    def column_backward(rows_full, entries):
-        running = None
+    def column_backward(weights, downs_t, entries):
         grad_lows = []
         grads_up = []
-        for grad_rows, weight, down_sel, up_sel, lowrank in entries:
+        for grad_rows, up_sel, lowrank in entries:
             grad_float = grad_rows.astype(jnp.float32)
-            grad_low = adapter_scale * hp_dot(grad_float, up_sel.astype(jnp.float32), "ste,sre->str")
+            grad_lows.append(
+                adapter_scale * hp_dot(grad_float, up_sel.astype(jnp.float32), "ste,sre->str")
+            )
             grads_up.append(adapter_scale * hp_dot(lowrank, grad_float, "str,ste->sre"))
-            grad_lows.append(grad_low)
-            term = jnp.einsum(
-                "ste,de->std", grad_rows, weight, preferred_element_type=jnp.float32
-            ) + hp_dot(grad_low, down_sel.astype(jnp.float32), "str,sdr->std")
-            running = term if running is None else running + term
+        running = column_input_grad(
+            jnp.stack([entry[0] for entry in entries]), weights, jnp.stack(grad_lows), downs_t
+        )
         return scatter_rows(running), grad_lows, grads_up
 
     def mine_of(values, axis):
@@ -318,10 +365,11 @@
     )
     grad_gate, grad_up = swiglu_pull(grad_product)
     grad_ffn_rows, ffn_grad_lows, ffn_grads_up = column_backward(
-        ffn_full,
+        w_gateup_full,
+        jnp.transpose(a_in_sel[:, 3:5], (1, 0, 3, 2)),
         (
-            (grad_gate.astype(jnp.bfloat16), w_gateup_full[0], a_in_sel[:, 3], b_gateup_sel[:, 0], gate_low),
-            (grad_up.astype(jnp.bfloat16), w_gateup_full[1], a_in_sel[:, 4], b_gateup_sel[:, 1], up_low),
+            (grad_gate.astype(jnp.bfloat16), b_gateup_sel[:, 0], gate_low),
+            (grad_up.astype(jnp.bfloat16), b_gateup_sel[:, 1], up_low),
         ),
     )
     grad_hidden = tangent + norm_ffn_pull(grad_ffn_rows)[0]
@@ -338,11 +386,12 @@
     grad_query = query_pull(grad_query_rot.reshape(seqs, length, qw_here))[0].astype(jnp.bfloat16)
     grad_key = key_pull(grad_key_rot.reshape(seqs, length, qw_here))[0].astype(jnp.bfloat16)
     grad_attn_rows, attn_grad_lows, attn_grads_up = column_backward(
-        normed_full,
+        w_qkv_full,
+        jnp.transpose(a_in_sel[:, 0:3], (1, 0, 3, 2)),
         (
-            (grad_query, w_qkv_full[0], a_in_sel[:, 0], b_qkv_sel[:, 0], proj_low[0]),
-            (grad_key, w_qkv_full[1], a_in_sel[:, 1], b_qkv_sel[:, 1], proj_low[1]),
-            (grad_values.reshape(seqs, length, qw_here), w_qkv_full[2], a_in_sel[:, 2], b_qkv_sel[:, 2], proj_low[2]),
+            (grad_query, b_qkv_sel[:, 0], proj_low[0]),
+            (grad_key, b_qkv_sel[:, 1], proj_low[1]),
+            (grad_values.reshape(seqs, length, qw_here), b_qkv_sel[:, 2], proj_low[2]),
         ),
     )
     grad_tokens = grad_hidden + norm_attn_pull(grad_attn_rows)[0]

time: 955 us -> 1030 us (1.079)
  Pallas kernels: 0 us -> 50.5 us
  matrix products: 120 us -> 89.6 us
  local copies, waits for them, and re-layouts: 234 us -> 264 us
  other arithmetic: 89 us -> 109 us
    pallas_call x0 -> x2, Pallas kernels: none -> 50.5 us  [column_input_grad(): pl.pallas_call(_colgrad_kernel, out_shape=jax.ShapeDtypeStruct((seqs, len...]
    dot_general x5 -> x0, matrix products: 20.5 us -> none  [column_backward(): jnp.einsum('ste,de->std', grad_rows, weight, preferred_element_type=jnp.f...]
    dot_general x32 -> x27, matrix products: 48.6 us -> 34.6 us  [hp_dot(): jnp.einsum(spec, left, right, precision=highest, preferred_element_type=j...]
    unnamed x284 -> x264, local copies, waits for them, and re-layouts: 35.9 us -> 34.1 us
  transfers between devices with their start and end apart: 27 -> 27, of which waited for: 10 -> 11; matrix products, arithmetic and copies ran while one was open for 32% -> 29% of each run, Pallas kernels for 0% -> 3%
where the time goes in v6:
time: 1030 us; the launch traced here: 1020 us
  waiting for transfers between devices  324 us (31%)
  local copies, waits for them, and re-layouts  264 us (26%)
  other arithmetic  109 us (11%)
  starting transfers between devices  96.2 us (9%)
  matrix products  89.6 us (9%)
  blocking collectives  80 us (8%)
  Pallas kernels  50.5 us (5%)
    ppermute x4, waiting for transfers between devices, tok_scatter(): return keep + lax.ppermute(send, 'tok', xor_pairs(count, 2))  144 us
    ppermute x4, waiting for transfers between devices, tok_gather(): far = lax.ppermute(values, 'tok', xor_pairs(count, 2))  84.7 us
    all_to_all x1, blocking collectives, fsdp_gather(): return lax.all_to_all(tiled_in, 'fsdp', 0, axis, tiled=True)  80 us
    all_to_all x2, waiting for transfers between devices, packed_gather(): lax.all_to_all(tiled_in, axes, 0, 0, tiled=True)  51.4 us
    pallas_call x2, Pallas kernels, column_input_grad(): pl.pallas_call(_colgrad_kernel, out_shape=jax.ShapeDtypeStruct((seqs, len...  50.5 us
    all_to_all x3, waiting for transfers between devices, fsdp_gather(): return lax.all_to_all(tiled_in, 'fsdp', 0, axis, tiled=True)  43.9 us
    dot_general x27, matrix products, hp_dot(): jnp.einsum(spec, left, right, precision=highest, preferred_element_type=j...  34.6 us
    unnamed x264, local copies, waits for them, and re-layouts  34.1 us
  transfers between devices with their start and end apart: 27, of which 11 were waited for; matrix products, arithmetic and copies ran while one was open for 29% of the time, Pallas kernels for 3%

profile of v6, /device:TPU:1, one launch (start us, length us, event | category | flops | bytes accessed | tf_op | source)
XLA Modules:
  0.0 1021.0 jit_solution(17002093755695798050)
XLA Ops:
  2.3 80.0 %all_to_all.95 = bf16[96,64,512]{2,1,0:T(8,128)(2,1)S(1)} all-to-all(bf16[96,64,512]{2,1,0:T(8,128)(2,1)S(1)} %bitcast.518), channel_id=1, replica_groups=mesh['fsdp'=32,'tok'=4] {'fsdp'}, dimensions={0} | all-to-all | bytes 12582912 | tf_op jit(solution)/shard_map/all_to_all | solution.py:226
  88.3 9.8 all-to-all-start.1
  103.9 41.3 %all-to-all-done.1 = bf16[128,112,128]{2,1,0:T(8,128)(2,1)} async-done(((bf16[128,112,128]{2,1,0:T(8,128)(2,1)}), bf16[128,112,128]{2,1,0:T(8,128)(2,1)}, u32[]{:S(2)}, u32[]{:S(2)}) %all-to-all-start.1) | async-done | bytes 3670048 | tf_op jit(solution)/shard_map/all_to_all | solution.py:234
  145.1 3.5 slice.307
  151.2 4.8 all-to-all-start.2
  166.2 10.1 all-to-all-done.2
  179.9 7.6 all-to-all-start.3
  190.6 3.8 constant_dynamic-slice_fusion.7
  206.8 3.6 constant_dynamic-slice_fusion.3
  215.5 5.7 broadcast_in_dim.48
  221.2 8.0 all-to-all-start.4
  231.5 3.8 fusion.30
  238.5 3.8 fusion.33
  244.8 3.6 subtract_convert_fusion
  280.7 14.6 %collective-permute-done.8 = bf16[2,64,2048]{2,1,0:T(8,128)(2,1)} collective-permute-done((bf16[2,64,2048]{2,1,0:T(8,128)(2,1)S(1)}, bf16[2,64,2048]{2,1,0:T(8,128)(2,1)}, u32[]{:S(2)}, u32[]{:S(2)}) %collective-permute-start.8) | collective-permute-done | bytes 524320 | tf_op jit(solution)/shard_map/ppermute | solution.py:154
  312.4 84.0 %collective-permute-done.3 = f32[2,64,2048]{2,1,0:T(8,128)} collective-permute-done((f32[2,64,2048]{2,1,0:T(8,128)}, f32[2,64,2048]{2,1,0:T(8,128)}, u32[]{:S(2)}, u32[]{:S(2)}) %collective-permute-start.3) | collective-permute-done | bytes 1048608 | tf_op jit(solution)/shard_map/ppermute | solution.py:176
  398.9 43.9 %all-to-all-done.4 = bf16[64,64,1408]{2,1,0:T(8,128)(2,1)} async-done(((bf16[64,64,1408]{2,1,0:T(8,128)(2,1)}), bf16[64,64,1408]{2,1,0:T(8,128)(2,1)}, u32[]{:S(2)}, u32[]{:S(2)}) %all-to-all-start.4) | async-done | bytes 11534368 | tf_op jit(solution)/shard_map/all_to_all | solution.py:226
  442.8 9.9 copy.285
  455.9 17.6 %all-to-all-start.5 = ((bf16[32,1408,64]{1,2,0:T(8,128)(2,1)}), bf16[32,1408,64]{1,2,0:T(8,128)(2,1)}, u32[]{:S(2)}, u32[]{:S(2)}) async-start(bf16[32,1408,64]{1,2,0:T(8,128)(2,1)} %broadcast_in_dim.49), calls=%async_computation.5 | async-start | bytes 11534336 | tf_op jit(solution)/shard_map/all_to_all | solution.py:226
  485.8 63.2 %collective-permute-done.4 = bf16[2,64,2048]{2,1,0:T(8,128)(2,1)} collective-permute-done((bf16[2,64,2048]{2,1,0:T(8,128)(2,1)}, bf16[2,64,2048]{2,1,0:T(8,128)(2,1)}, u32[]{:S(2)}, u32[]{:S(2)}) %collective-permute-start.4) | collective-permute-done | bytes 524320 | tf_op jit(solution)/shard_map/ppermute | solution.py:154
  559.5 3.4 copy.289
  576.6 6.1 fusion
  585.7 4.9 fusion.2
  590.6 6.5 fusion.136
  599.0 3.6 fusion.10
  602.6 9.2 fusion.134
  616.0 3.7 pad_maximum_fusion.e_ref
  619.7 24.4 %shard_map.233 = f32[2,256,2048]{2,1,0:T(8,128)} custom-call(bf16[2,2,256,1408]{3,2,1,0:T(8,128)(2,1)} %pad_maximum_fusion.e_ref, bf16[2,2048,1408]{2,1,0:T(8,128)(2,1)} %bitcast.553, f32[2,2,256,16]{3,2,1,0:T(8,128)} %copy.297.el_ref, bf16[2,2,16,2048]{3,2,1,0:T(8,128)(2,1)} %fusion.75.at_ref), custom_call_target="tpu_custom_call" | custom-call | flops 5972688896 | bytes 30146560 | tf_op jit(solution)/shard_map/pallas_call | solution.py:124
  670.7 19.3 %collective-permute-done.11 = f32[2,64,2048]{2,1,0:T(8,128)S(1)} collective-permute-done((f32[2,64,2048]{2,1,0:T(8,128)S(1)}, f32[2,64,2048]{2,1,0:T(8,128)S(1)}, u32[]{:S(2)}, u32[]{:S(2)}) %collective-permute-start.11) | collective-permute-done | bytes 1048608 | tf_op jit(solution)/shard_map/ppermute | solution.py:176
  690.2 22.2 %collective-permute-done.7 = f32[2,64,2048]{2,1,0:T(8,128)S(1)} collective-permute-done((f32[2,64,2048]{2,1,0:T(8,128)S(1)}, f32[2,64,2048]{2,1,0:T(8,128)S(1)}, u32[]{:S(2)}, u32[]{:S(2)}) %collective-permute-start.7) | collective-permute-done | bytes 1048608 | tf_op jit(solution)/shard_map/ppermute | solution.py:176
  721.3 6.9 collective-permute-done.12
  763.1 3.9 fusion.36
  791.3 4.2 multiply_add_fusion.5
  803.0 3.8 fusion.66
  845.0 4.0 reduce.2
  851.5 6.7 all-to-all-start.7
  871.6 26.1 %shard_map.234 = f32[2,256,2048]{2,1,0:T(8,128)} custom-call(bf16[3,2,256,512]{3,2,1,0:T(8,128)(2,1)} %pad_maximum_fusion.3.e_ref, bf16[3,2048,512]{2,1,0:T(8,128)(2,1)} %bitcast.516, f32[3,2,256,16]{3,2,1,0:T(8,128)} %copy.316.el_ref, bf16[3,2,16,2048]{3,2,1,0:T(8,128)(2,1)} %fusion.73.at_ref), custom_call_target="tpu_custom_call" | custom-call | flops 3321888768 | bytes 18350080 | tf_op jit(solution)/shard_map/pallas_call | solution.py:124
  909.0 8.7 reshape.766
  917.7 8.4 constant_dynamic-slice_fusion
  926.1 5.7 copy.372
  931.8 5.7 copy.324
  940.5 5.3 dynamic_update_slice.36
  947.1 5.4 dynamic_update_slice.37
  952.5 4.1 copy.373
  961.0 7.7 all-to-all-start.6
  975.9 9.4 reshape.787
  985.3 5.3 convert_reduce_fusion
  998.6 18.1 %collective-permute-done.15 = f32[2,64,2048]{2,1,0:T(8,128)S(1)} collective-permute-done((f32[2,64,2048]{2,1,0:T(8,128)}, f32[2,64,2048]{2,1,0:T(8,128)S(1)}, u32[]{:S(2)}, u32[]{:S(2)}) %collective-permute-start.15) | collective-permute-done | bytes 1048608 | tf_op jit(solution)/shard_map/ppermute | solution.py:176
  (551 shorter events, 347.9 us)
Async XLA Ops:
  88.3 56.9 %all-to-all-start.1 = ((bf16[128,112,128]{2,1,0:T(8,128)(2,1)}), bf16[128,112,128]{2,1,0:T(8,128)(2,1)}, u32[]{:S(2)}, u32[]{:S(2)}) async-start(bf16[128,112,128]{2,1,0:T(8,128)(2,1)} %broadcast_in_dim.43), calls=%async_computation.1 | async-start | bytes 7340032 | tf_op jit(solution)/shard_map/all_to_all | solution.py:234
  98.2 58.7 %copy-start.104 = (f32[2,64]{1,0:T(2,128)}, f32[2,64]{1,0:T(2,128)S(1)}, u32[]{:S(2)}) copy-start(f32[2,64]{1,0:T(2,128)S(1)} %fusion.114) | copy-start | bytes 1540
  98.4 58.7 %collective-permute-start = (bf16[2,64,2048]{2,1,0:T(8,128)(2,1)S(1)}, bf16[2,64,2048]{2,1,0:T(8,128)(2,1)S(1)}, u32[]{:S(2)}, u32[]{:S(2)}) collective-permute-start(bf16[2,64,2048]{2,1,0:T(8,128)(2,1)S(1)} %fusion.55), channel_id=1, source_target_pairs={{0,2},{1,3},{2,0},{3,1},{4,6},{5,7},{6,4},{7,5},{8,10},{9,11},{10,... | collective-permute-start | bytes 1572872 | tf_op jit(solution)/shard_map/ppermute | solution.py:154
  103.8 44.7 %copy-start.111 = (bf16[1408,4]{0,1:T(4,128)(2,1)S(1)}, bf16[1408,4]{0,1:T(4,128)(2,1)}, u32[]{:S(2)}) copy-start(bf16[1408,4]{0,1:T(4,128)(2,1)} %param.34) | copy-start | bytes 33796
  103.8 45.5 %copy-start.118 = (bf16[512,4]{0,1:T(4,128)(2,1)S(1)}, bf16[512,4]{0,1:T(4,128)(2,1)}, u32[]{:S(2)}) copy-start(bf16[512,4]{0,1:T(4,128)(2,1)} %param.33) | copy-start | bytes 12292
  103.8 45.9 %copy-start.108 = (bf16[2,4,1408]{2,1,0:T(4,128)(2,1)S(1)}, bf16[2,4,1408]{2,1,0:T(4,128)(2,1)}, u32[]{:S(2)}) copy-start(bf16[2,4,1408]{2,1,0:T(4,128)(2,1)} %param.32) | copy-start | bytes 67588
  103.8 45.9 %copy-start.110 = (bf16[3,4,512]{2,1,0:T(4,128)(2,1)S(1)}, bf16[3,4,512]{2,1,0:T(4,128)(2,1)}, u32[]{:S(2)}) copy-start(bf16[3,4,512]{2,1,0:T(4,128)(2,1)} %param.31) | copy-start | bytes 36868
  151.2 25.1 %all-to-all-start.2 = ((bf16[32,196,128]{2,1,0:T(8,128)(2,1)}), bf16[32,196,128]{2,1,0:T(8,128)(2,1)}, u32[]{:S(2)}, u32[]{:S(2)}) async-start(bf16[32,196,128]{2,1,0:T(8,128)(2,1)} %broadcast_in_dim.44), calls=%async_computation.2 | async-start | bytes 3276800 | tf_op jit(solution)/shard_map/all_to_all | solution.py:234
  158.3 29.4 %collective-permute-start.1 = (bf16[2,2,64,2048]{3,2,1,0:T(8,128)(2,1)}, bf16[2,2,64,2048]{3,2,1,0:T(8,128)(2,1)}, u32[]{:S(2)}, u32[]{:S(2)}) collective-permute-start(bf16[2,2,64,2048]{3,2,1,0:T(8,128)(2,1)} %maximum_select_fusion.4), channel_id=1, source_target_pairs={{0,1},{1,0},{2,3},{3,2},{4,5},{5,4},{6,7},{7,6},{8,9},{9,8},{10,11... | collective-permute-start | bytes 3145736 | tf_op jit(solution)/shard_map/ppermute | solution.py:158
  179.9 35.6 %all-to-all-start.3 = ((bf16[32,512,64]{1,2,0:T(8,128)(2,1)}), bf16[32,512,64]{1,2,0:T(8,128)(2,1)}, u32[]{:S(2)}, u32[]{:S(2)}) async-start(bf16[32,512,64]{1,2,0:T(8,128)(2,1)} %broadcast_in_dim.47), calls=%async_computation.3 | async-start | bytes 4194304 | tf_op jit(solution)/shard_map/all_to_all | solution.py:226
  198.5 107.8 %copy-start.6 = (bf16[5,2048,16]{1,2,0:T(8,128)(2,1)}, bf16[5,2048,16]{1,2,0:T(8,128)(2,1)S(1)}, u32[]{:S(2)}) copy-start(bf16[5,2048,16]{1,2,0:T(8,128)(2,1)S(1)} %copy.263) | copy-start | bytes 983044
  211.9 95.3 %copy-start.40 = (bf16[2,16,2048]{2,1,0:T(8,128)(2,1)}, bf16[2,16,2048]{2,1,0:T(8,128)(2,1)S(1)}, u32[]{:S(2)}) copy-start(bf16[2,16,2048]{2,1,0:T(8,128)(2,1)S(1)} %copy.280) | copy-start | bytes 393220
  221.2 221.6 %all-to-all-start.4 = ((bf16[64,64,1408]{2,1,0:T(8,128)(2,1)}), bf16[64,64,1408]{2,1,0:T(8,128)(2,1)}, u32[]{:S(2)}, u32[]{:S(2)}) async-start(bf16[64,64,1408]{2,1,0:T(8,128)(2,1)} %bitcast.507), calls=%async_computation.4 | async-start | bytes 23068672 | tf_op jit(solution)/shard_map/all_to_all | solution.py:226
  229.8 32.2 %copy-start.78 = (f32[2,256,16]{1,2,0:T(8,128)}, f32[2,256,16]{1,2,0:T(8,128)S(1)}, u32[]{:S(2)}) copy-start(f32[2,256,16]{1,2,0:T(8,128)S(1)} %fusion.87) | copy-start | bytes 98308
  268.9 389.1 %copy-start.63 = (f32[2,256,16]{1,2,0:T(8,128)}, f32[2,256,16]{1,2,0:T(8,128)S(1)}, u32[]{:S(2)}) copy-start(f32[2,256,16]{1,2,0:T(8,128)S(1)} %fusion.140) | copy-start | bytes 98308
  276.6 23.1 %collective-permute-start.2 = (f32[2,2,64,2048]{3,2,1,0:T(8,128)}, f32[2,2,64,2048]{3,2,1,0:T(8,128)}, u32[]{:S(2)}, u32[]{:S(2)}) collective-permute-start(f32[2,2,64,2048]{3,2,1,0:T(8,128)} %dynamic-slice_bitcast_fusion.3), channel_id=1, source_target_pairs={{0,1},{1,0},{2,3},{3,2},{4,5},{5,4},{6,7},{7,6},{8,9},{9,8},{10,11... | collective-permute-start | bytes 6291464 | tf_op jit(solution)/shard_map/ppermute | solution.py:173
  278.8 16.5 %collective-permute-start.8 = (bf16[2,64,2048]{2,1,0:T(8,128)(2,1)S(1)}, bf16[2,64,2048]{2,1,0:T(8,128)(2,1)}, u32[]{:S(2)}, u32[]{:S(2)}) collective-permute-start(bf16[2,64,2048]{2,1,0:T(8,128)(2,1)S(1)} %copy-done.36), channel_id=1, source_target_pairs={{0,2},{1,3},{2,0},{3,1},{4,6},{5,7},{6,4},{7,5},{8,10},{9,11},{10,... | collective-permute-start | bytes 1572872 | tf_op jit(solution)/shard_map/ppermute | solution.py:154
  296.7 9.1 collective-permute-start.9
  303.3 93.1 %collective-permute-start.3 = (f32[2,64,2048]{2,1,0:T(8,128)}, f32[2,64,2048]{2,1,0:T(8,128)}, u32[]{:S(2)}, u32[]{:S(2)}) collective-permute-start(f32[2,64,2048]{2,1,0:T(8,128)} %dynamic-slice_bitcast_fusion.7), channel_id=1, source_target_pairs={{0,2},{1,3},{2,0},{3,1},{4,6},{5,7},{6,4},{7,5},{8,10},{9,11},{10,... | collective-permute-start | bytes 3145736 | tf_op jit(solution)/shard_map/ppermute | solution.py:176
  308.5 288.7 %copy-start.72 = (f32[2,256,16]{1,2,0:T(8,128)}, f32[2,256,16]{1,2,0:T(8,128)S(1)}, u32[]{:S(2)}) copy-start(f32[2,256,16]{1,2,0:T(8,128)S(1)} %convolution_multiply_fusion.15) | copy-start | bytes 98308
  455.9 134.7 %all-to-all-start.5 = ((bf16[32,1408,64]{1,2,0:T(8,128)(2,1)}), bf16[32,1408,64]{1,2,0:T(8,128)(2,1)}, u32[]{:S(2)}, u32[]{:S(2)}) async-start(bf16[32,1408,64]{1,2,0:T(8,128)(2,1)} %broadcast_in_dim.49), calls=%async_computation.5 | async-start | bytes 11534336 | tf_op jit(solution)/shard_map/all_to_all | solution.py:226
  475.8 73.2 %collective-permute-start.4 = (bf16[2,64,2048]{2,1,0:T(8,128)(2,1)}, bf16[2,64,2048]{2,1,0:T(8,128)(2,1)}, u32[]{:S(2)}, u32[]{:S(2)}) collective-permute-start(bf16[2,64,2048]{2,1,0:T(8,128)(2,1)} %multiply_convert_fusion.3), channel_id=1, source_target_pairs={{0,2},{1,3},{2,0},{3,1},{4,6},{5,7},{6,4},{7,5},{8,10},{9,11},{10,... | collective-permute-start | bytes 1572872 | tf_op jit(solution)/shard_map/ppermute | solution.py:154
  484.8 69.5 %copy-start.16 = (bf16[32,44,128]{0,2,1:T(8,128)(2,1)S(1)}, bf16[32,44,128]{0,2,1:T(8,128)(2,1)}, u32[]{:S(2)}) copy-start(bf16[32,44,128]{0,2,1:T(8,128)(2,1)} %copy.288) | copy-start | bytes 1081348
  551.3 20.3 %collective-permute-start.5 = (bf16[2,2,64,2048]{3,2,0,1:T(8,128)(2,1)}, bf16[2,2,64,2048]{3,2,0,1:T(8,128)(2,1)}, u32[]{:S(2)}, u32[]{:S(2)}) collective-permute-start(bf16[2,2,64,2048]{3,2,0,1:T(8,128)(2,1)} %maximum_select_fusion.6), channel_id=1, source_target_pairs={{0,1},{1,0},{2,3},{3,2},{4,5},{5,4},{6,7},{7,6},{8,9},{9,8},{10,11... | collective-permute-start | bytes 3145736 | tf_op jit(solution)/shard_map/ppermute | solution.py:158
  647.4 14.0 %collective-permute-start.10 = (f32[2,2,64,2048]{3,2,1,0:T(8,128)}, f32[2,2,64,2048]{3,2,1,0:T(8,128)}, u32[]{:S(2)}, u32[]{:S(2)}) collective-permute-start(f32[2,2,64,2048]{3,2,1,0:T(8,128)} %dynamic-slice_bitcast_fusion.1), channel_id=1, source_target_pairs={{0,1},{1,0},{2,3},{3,2},{4,5},{5,4},{6,7},{7,6},{8,9},{9,8},{10,11... | collective-permute-start | bytes 6291464 | tf_op jit(solution)/shard_map/ppermute | solution.py:173
  654.4 10.3 %collective-permute-start.6 = (f32[2,2,64,2048]{3,2,1,0:T(8,128)}, f32[2,2,64,2048]{3,2,1,0:T(8,128)}, u32[]{:S(2)}, u32[]{:S(2)}) collective-permute-start(f32[2,2,64,2048]{3,2,1,0:T(8,128)} %dynamic-slice_bitcast_fusion.2), channel_id=1, source_target_pairs={{0,1},{1,0},{2,3},{3,2},{4,5},{5,4},{6,7},{7,6},{8,9},{9,8},{10,11... | collective-permute-start | bytes 6291464 | tf_op jit(solution)/shard_map/ppermute | solution.py:173
  658.6 74.5 %collective-permute-start.18 = (f32[2,2,256,16]{2,3,1,0:T(8,128)}, f32[2,2,256,16]{2,3,1,0:T(8,128)}, u32[]{:S(2)}, u32[]{:S(2)}) collective-permute-start(f32[2,2,256,16]{2,3,1,0:T(8,128)} %pad_maximum_fusion.15), channel_id=1, source_target_pairs={{0,1},{1,0},{2,3},{3,2},{4,5},{5,4},{6,7},{7,6},{8,9},{9,8},{10,11... | collective-permute-start | bytes 196616 | tf_op jit(solution)/shard_map/ppermute | solution.py:181
  660.7 54.0 %copy-start.51 = (f32[2,1,16,1408]{3,2,0,1:T(8,128)}, f32[2,1,16,1408]{3,2,0,1:T(8,128)S(1)}, u32[]{:S(2)}) copy-start(f32[2,1,16,1408]{3,2,0,1:T(8,128)S(1)} %fusion.12) | copy-start | bytes 540676
  664.2 25.8 %collective-permute-start.11 = (f32[2,64,2048]{2,1,0:T(8,128)S(1)}, f32[2,64,2048]{2,1,0:T(8,128)S(1)}, u32[]{:S(2)}, u32[]{:S(2)}) collective-permute-start(f32[2,64,2048]{2,1,0:T(8,128)S(1)} %dynamic-slice_bitcast_fusion.5), channel_id=1, source_target_pairs={{0,2},{1,3},{2,0},{3,1},{4,6},{5,7},{6,4},{7,5},{8,10},{9,11},{10,... | collective-permute-start | bytes 3145736 | tf_op jit(solution)/shard_map/ppermute | solution.py:176
  666.9 23.3 %copy-start.115 = (f32[2,64]{1,0:T(2,128)S(1)}, f32[2,64]{1,0:T(2,128)}, u32[]{:S(2)}) copy-start(f32[2,64]{1,0:T(2,128)} %get-tuple-element.64) | copy-start | bytes 1540
  666.9 45.5 %copy-start.37 = (bf16[2,64,2048]{2,1,0:T(8,128)(2,1)S(1)}, bf16[2,64,2048]{2,1,0:T(8,128)(2,1)}, u32[]{:S(2)}) copy-start(bf16[2,64,2048]{2,1,0:T(8,128)(2,1)} %param.19) | copy-start | bytes 1572868
  666.9 45.5 %copy-start.107 = (f32[2,64]{1,0:T(2,128)S(1)}, f32[2,64]{1,0:T(2,128)}, u32[]{:S(2)}) copy-start(f32[2,64]{1,0:T(2,128)} %copy-done.106) | copy-start | bytes 1540
  667.0 45.5 %collective-permute-start.7 = (f32[2,64,2048]{2,1,0:T(8,128)S(1)}, f32[2,64,2048]{2,1,0:T(8,128)S(1)}, u32[]{:S(2)}, u32[]{:S(2)}) collective-permute-start(f32[2,64,2048]{2,1,0:T(8,128)S(1)} %dynamic-slice_bitcast_fusion.6), channel_id=1, source_target_pairs={{0,2},{1,3},{2,0},{3,1},{4,6},{5,7},{6,4},{7,5},{8,10},{9,11},{10,... | collective-permute-start | bytes 3145736 | tf_op jit(solution)/shard_map/ppermute | solution.py:176
  670.0 44.7 %copy-start.53 = (f32[2,1,16,1408]{3,2,0,1:T(8,128)}, f32[2,1,16,1408]{3,2,0,1:T(8,128)S(1)}, u32[]{:S(2)}) copy-start(f32[2,1,16,1408]{3,2,0,1:T(8,128)S(1)} %fusion.13) | copy-start | bytes 540676
  714.2 13.9 %collective-permute-start.12 = (bf16[2,64,2048]{2,1,0:T(8,128)(2,1)}, bf16[2,64,2048]{2,1,0:T(8,128)(2,1)}, u32[]{:S(2)}, u32[]{:S(2)}) collective-permute-start(bf16[2,64,2048]{2,1,0:T(8,128)(2,1)} %get-tuple-element.62), channel_id=1, source_target_pairs={{0,2},{1,3},{2,0},{3,1},{4,6},{5,7},{6,4},{7,5},{8,10},{9,11},{10,... | collective-permute-start | bytes 1572872 | tf_op jit(solution)/shard_map/ppermute | solution.py:154
  730.9 28.0 %collective-permute-start.13 = (bf16[2,2,64,2048]{3,2,0,1:T(8,128)(2,1)}, bf16[2,2,64,2048]{3,2,0,1:T(8,128)(2,1)}, u32[]{:S(2)}, u32[]{:S(2)}) collective-permute-start(bf16[2,2,64,2048]{3,2,0,1:T(8,128)(2,1)} %maximum_select_fusion.9), channel_id=1, source_target_pairs={{0,1},{1,0},{2,3},{3,2},{4,5},{5,4},{6,7},{7,6},{8,9},{9,8},{10,11... | collective-permute-start | bytes 3145736 | tf_op jit(solution)/shard_map/ppermute | solution.py:158
  734.6 15.6 %collective-permute-start.19 = (f32[2,2,256,16]{2,3,1,0:T(8,128)}, f32[2,2,256,16]{2,3,1,0:T(8,128)}, u32[]{:S(2)}, u32[]{:S(2)}) collective-permute-start(f32[2,2,256,16]{2,3,1,0:T(8,128)} %fusion.123), channel_id=1, source_target_pairs={{0,2},{1,3},{2,0},{3,1},{4,6},{5,7},{6,4},{7,5},{8,10},{9,11},{10,... | collective-permute-start | bytes 196616 | tf_op jit(solution)/shard_map/ppermute | solution.py:182
  851.5 109.5 %all-to-all-start.7 = ((bf16[32,2,12544]{2,1,0:T(2,128)(2,1)}), bf16[32,2,12544]{2,1,0:T(2,128)(2,1)}, u32[]{:S(2)}, u32[]{:S(2)}) async-start(bf16[32,2,12544]{2,1,0:T(2,128)(2,1)} %reshape.786), calls=%async_computation.7 | async-start | bytes 3211264 | tf_op jit(solution)/shard_map/all_to_all | solution.py:451
  859.3 38.4 %collective-permute-start.16 = (f32[5,2,256,16]{2,3,1,0:T(8,128)S(1)}, f32[5,2,256,16]{2,3,1,0:T(8,128)}, u32[]{:S(2)}, u32[]{:S(2)}) collective-permute-start(f32[5,2,256,16]{2,3,1,0:T(8,128)S(1)} %constant_dynamic-update-slice_fusion), channel_id=1, source_target_pairs={{0,1},{1,0},{2,3},{3,2},{4,5},{5,4},{6,7},{7,6},{8,9},{9,8},{10,11... | collective-permute-start | bytes 491528 | tf_op jit(solution)/shard_map/ppermute | solution.py:181
  898.7 7.8 collective-permute-start.17
  905.1 63.6 %collective-permute-start.14 = (f32[2,2,64,2048]{3,2,1,0:T(8,128)}, f32[2,2,64,2048]{3,2,1,0:T(8,128)}, u32[]{:S(2)}, u32[]{:S(2)}) collective-permute-start(f32[2,2,64,2048]{3,2,1,0:T(8,128)} %dynamic-slice_bitcast_fusion), channel_id=1, source_target_pairs={{0,1},{1,0},{2,3},{3,2},{4,5},{5,4},{6,7},{7,6},{8,9},{9,8},{10,11... | collective-permute-start | bytes 6291464 | tf_op jit(solution)/shard_map/ppermute | solution.py:173
  961.0 33.6 %all-to-all-start.6 = ((f32[32,1,14336]{2,1,0:T(1,128)}), f32[32,1,14336]{2,1,0:T(1,128)}, u32[]{:S(2)}, u32[]{:S(2)}) async-start(f32[32,1,14336]{2,1,0:T(1,128)} %copy.330), calls=%async_computation.6 | async-start | bytes 3670016 | tf_op jit(solution)/shard_map/all_to_all | solution.py:433
  972.5 44.2 %collective-permute-start.15 = (f32[2,64,2048]{2,1,0:T(8,128)}, f32[2,64,2048]{2,1,0:T(8,128)S(1)}, u32[]{:S(2)}, u32[]{:S(2)}) collective-permute-start(f32[2,64,2048]{2,1,0:T(8,128)} %dynamic-slice_bitcast_fusion.4), channel_id=1, source_target_pairs={{0,2},{1,3},{2,0},{3,1},{4,6},{5,7},{6,4},{7,5},{8,10},{9,11},{10,... | collective-permute-start | bytes 3145736 | tf_op jit(solution)/shard_map/ppermute | solution.py:176
  990.7 26.1 %copy-start.5 = (bf16[2,64,2048]{2,1,0:T(8,128)(2,1)S(1)}, bf16[2,64,2048]{2,1,0:T(8,128)(2,1)}, u32[]{:S(2)}) copy-start(bf16[2,64,2048]{2,1,0:T(8,128)(2,1)} %param.18) | copy-start | bytes 1572868
  990.7 26.1 %copy-start.93 = (f32[2048]{0:T(1024)S(1)}, f32[2048]{0:T(1024)}, u32[]{:S(2)}) copy-start(f32[2048]{0:T(1024)} %param.26) | copy-start | bytes 24580
  994.6 23.7 %copy-start.114 = (f32[2,64]{1,0:T(2,128)S(1)}, f32[2,64]{1,0:T(2,128)}, u32[]{:S(2)}) copy-start(f32[2,64]{1,0:T(2,128)} %copy-done.113) | copy-start | bytes 1540
  994.6 23.7 %copy-start.39 = (f32[2,64,2048]{2,1,0:T(8,128)S(1)}, f32[2,64,2048]{2,1,0:T(8,128)}, u32[]{:S(2)}) copy-start(f32[2,64,2048]{2,1,0:T(8,128)} %get-tuple-element.63) | copy-start | bytes 3145732
  994.6 23.7 %copy-start.105 = (f32[2,64]{1,0:T(2,128)S(1)}, f32[2,64]{1,0:T(2,128)}, u32[]{:S(2)}) copy-start(f32[2,64]{1,0:T(2,128)} %copy-done.104) | copy-start | bytes 1540
  (106 other events, 593.1 us)

commit v7 on v5

--- a/solution.py
+++ b/solution.py
@@ -125,7 +125,8 @@
     chip_sum = mine + lax.ppermute(theirs, "tok", xor_pairs(count, 1))
     keep = lax.dynamic_index_in_dim(chip_sum, half, axis, keepdims=False)
     send = lax.dynamic_index_in_dim(chip_sum, 1 - half, axis, keepdims=False)
-    return keep + lax.ppermute(send, "tok", xor_pairs(count, 2))
+    got = lax.ppermute(send.astype(jnp.bfloat16), "tok", xor_pairs(count, 2))
+    return keep + got.astype(keep.dtype)
 
 
 def tok_sum(values):

time: 955 us -> 920 us (0.963)
  waiting for transfers between devices: 319 us -> 274 us
    ppermute x4, waiting for transfers between devices: 142 us -> 47.3 us  [tok_scatter(): got = lax.ppermute(send.astype(jnp.bfloat16), 'tok', xor_pairs(count, 2))]
    all_to_all x3, waiting for transfers between devices: 46.2 us -> 96.6 us  [fsdp_gather(): return lax.all_to_all(tiled_in, 'fsdp', 0, axis, tiled=True)]
    ppermute x4, waiting for transfers between devices: 80.4 us -> 66.6 us  [tok_gather(): far = lax.ppermute(values, 'tok', xor_pairs(count, 2))]
    ppermute x4, starting transfers between devices: 6.84 us -> 20.5 us  [tok_scatter(): got = lax.ppermute(send.astype(jnp.bfloat16), 'tok', xor_pairs(count, 2))]
    dynamic_slice x0 -> x8, local copies, waits for them, and re-layouts: none -> 11.8 us  [the longest x4 6.05 us: tok_scatter(): theirs = lax.dynamic_index_in_dim(split, 1 - core, axis + 1, keepdims=False)]
    all_to_all x2, waiting for transfers between devices: 50.4 us -> 62 us  [packed_gather(): lax.all_to_all(tiled_in, axes, 0, 0, tiled=True)]
    unnamed x284 -> x282, local copies, waits for them, and re-layouts: 35.9 us -> 30.3 us
  transfers between devices with their start and end apart: 27 -> 27, of which waited for: 10 -> 11; matrix products, arithmetic and copies ran while one was open for 32% -> 34% of each run, Pallas kernels for 0% -> 0%
where the time goes in v7:
time: 920 us; the launch traced here: 910 us
  waiting for transfers between devices  274 us (30%)
  local copies, waits for them, and re-layouts  233 us (25%)
  matrix products  120 us (13%)
  starting transfers between devices  103 us (11%)
  other arithmetic  92.4 us (10%)
  blocking collectives  80 us (9%)
    all_to_all x3, waiting for transfers between devices, fsdp_gather(): return lax.all_to_all(tiled_in, 'fsdp', 0, axis, tiled=True)  96.6 us
    all_to_all x1, blocking collectives, fsdp_gather(): return lax.all_to_all(tiled_in, 'fsdp', 0, axis, tiled=True)  80 us
    ppermute x4, waiting for transfers between devices, tok_gather(): far = lax.ppermute(values, 'tok', xor_pairs(count, 2))  66.6 us
    all_to_all x2, waiting for transfers between devices, packed_gather(): lax.all_to_all(tiled_in, axes, 0, 0, tiled=True)  62 us
    dot_general x32, matrix products, hp_dot(): jnp.einsum(spec, left, right, precision=highest, preferred_element_type=j...  47.6 us
    ppermute x4, waiting for transfers between devices, tok_scatter(): got = lax.ppermute(send.astype(jnp.bfloat16), 'tok', xor_pairs(count, 2))  47.3 us
    all_to_all x3, starting transfers between devices, fsdp_gather(): return lax.all_to_all(tiled_in, 'fsdp', 0, axis, tiled=True)  32.1 us
    unnamed x282, local copies, waits for them, and re-layouts  30.3 us
  transfers between devices with their start and end apart: 27, of which 11 were waited for; matrix products, arithmetic and copies ran while one was open for 34% of the time, Pallas kernels for 0%

profile of v7, /device:TPU:1, one launch (start us, length us, event | category | flops | bytes accessed | tf_op | source)
XLA Modules:
  0.0 909.8 jit_solution(12532933124149624485)
XLA Ops:
  2.3 80.0 %all_to_all.95 = bf16[96,64,512]{2,1,0:T(8,128)(2,1)S(1)} all-to-all(bf16[96,64,512]{2,1,0:T(8,128)(2,1)S(1)} %bitcast.543), channel_id=1, replica_groups=mesh['fsdp'=32,'tok'=4] {'fsdp'}, dimensions={0} | all-to-all | bytes 12582912 | tf_op jit(solution)/shard_map/all_to_all | solution.py:179
  88.4 9.7 %all-to-all-start.1 = ((bf16[128,112,128]{2,1,0:T(8,128)(2,1)}), bf16[128,112,128]{2,1,0:T(8,128)(2,1)}, u32[]{:S(2)}, u32[]{:S(2)}) async-start(bf16[128,112,128]{2,1,0:T(8,128)(2,1)} %broadcast_in_dim.43), calls=%async_computation.1 | async-start | bytes 7340032 | tf_op jit(solution)/shard_map/all_to_all | solution.py:187
  103.9 41.3 %all-to-all-done.1 = bf16[128,112,128]{2,1,0:T(8,128)(2,1)} async-done(((bf16[128,112,128]{2,1,0:T(8,128)(2,1)}), bf16[128,112,128]{2,1,0:T(8,128)(2,1)}, u32[]{:S(2)}, u32[]{:S(2)}) %all-to-all-start.1) | async-done | bytes 3670048 | tf_op jit(solution)/shard_map/all_to_all | solution.py:187
  145.2 3.5 slice.309
  151.3 4.7 all-to-all-start.2
  161.1 20.6 %all-to-all-done.2 = bf16[32,196,128]{2,1,0:T(8,128)(2,1)S(1)} async-done(((bf16[32,196,128]{2,1,0:T(8,128)(2,1)}), bf16[32,196,128]{2,1,0:T(8,128)(2,1)S(1)}, u32[]{:S(2)}, u32[]{:S(2)}) %all-to-all-start.2) | async-done | bytes 1605664 | tf_op jit(solution)/shard_map/all_to_all | solution.py:187
  184.6 6.6 all-to-all-start.3
  200.8 3.9 constant_dynamic-slice_fusion.15
  218.0 6.7 broadcast_in_dim.48
  224.8 7.9 all-to-all-start.4
  232.6 3.6 constant_dynamic-slice_fusion.11
  245.8 3.8 fusion.48
  252.8 3.8 fusion.45
  259.3 3.5 subtract_convert_fusion
  305.4 13.3 %collective-permute-start.3 = (bf16[2,64,2048]{2,1,0:T(8,128)(2,1)}, bf16[2,64,2048]{2,1,0:T(8,128)(2,1)}, u32[]{:S(2)}, u32[]{:S(2)}) collective-permute-start(bf16[2,64,2048]{2,1,0:T(8,128)(2,1)} %fusion.78), channel_id=1, source_target_pairs={{0,2},{1,3},{2,0},{3,1},{4,6},{5,7},{6,4},{7,5},{8,10},{9,11},{10,... | collective-permute-start | bytes 1572872 | tf_op jit(solution)/shard_map/ppermute | solution.py:128
  324.5 18.9 %collective-permute-done.3 = bf16[2,64,2048]{2,1,0:T(8,128)(2,1)} collective-permute-done((bf16[2,64,2048]{2,1,0:T(8,128)(2,1)}, bf16[2,64,2048]{2,1,0:T(8,128)(2,1)}, u32[]{:S(2)}, u32[]{:S(2)}) %collective-permute-start.3) | collective-permute-done | bytes 524320 | tf_op jit(solution)/shard_map/ppermute | solution.py:128
  345.0 96.3 %all-to-all-done.4 = bf16[64,64,1408]{2,1,0:T(8,128)(2,1)} async-done(((bf16[64,64,1408]{2,1,0:T(8,128)(2,1)}), bf16[64,64,1408]{2,1,0:T(8,128)(2,1)}, u32[]{:S(2)}, u32[]{:S(2)}) %all-to-all-start.4) | async-done | bytes 11534368 | tf_op jit(solution)/shard_map/all_to_all | solution.py:179
  441.3 10.0 %copy.260 = bf16[2,32,64,1408]{3,2,1,0:T(8,128)(2,1)} copy(bf16[2,32,64,1408]{3,2,0,1:T(8,128)(2,1)} %bitcast.67) | data formatting | bytes 23068672 | tf_op jit(solution)/shard_map/all_to_all | solution.py:179
  454.5 17.6 %all-to-all-start.5 = ((bf16[32,1408,64]{1,2,0:T(8,128)(2,1)}), bf16[32,1408,64]{1,2,0:T(8,128)(2,1)}, u32[]{:S(2)}, u32[]{:S(2)}) async-start(bf16[32,1408,64]{1,2,0:T(8,128)(2,1)} %broadcast_in_dim.49), calls=%async_computation.5 | async-start | bytes 11534336 | tf_op jit(solution)/shard_map/all_to_all | solution.py:179
  481.3 61.6 %collective-permute-done.4 = bf16[2,64,2048]{2,1,0:T(8,128)(2,1)} collective-permute-done((bf16[2,64,2048]{2,1,0:T(8,128)(2,1)}, bf16[2,64,2048]{2,1,0:T(8,128)(2,1)}, u32[]{:S(2)}, u32[]{:S(2)}) %collective-permute-start.4) | collective-permute-done | bytes 524320 | tf_op jit(solution)/shard_map/ppermute | solution.py:106
  557.5 6.1 fusion.2
  566.7 5.0 fusion.6
  571.7 6.5 fusion.149
  583.2 3.4 fusion.4
  587.1 3.5 fusion
  598.8 5.9 fusion.147
  620.1 3.8 collective-permute-start.11
  626.8 8.9 collective-permute-done.11
  636.0 10.9 %collective-permute-done.7 = bf16[2,64,2048]{2,1,0:T(8,128)(2,1)S(1)} collective-permute-done((bf16[2,64,2048]{2,1,0:T(8,128)(2,1)S(1)}, bf16[2,64,2048]{2,1,0:T(8,128)(2,1)S(1)}, u32[]{:S(2)}, u32[]{:S(2)}) %collective-permute-start.7) | collective-permute-done | bytes 524320 | tf_op jit(solution)/shard_map/ppermute | solution.py:128
  658.9 5.1 collective-permute-done.12
  699.5 3.8 fusion.51
  726.4 4.2 multiply_add_fusion.5
  733.1 5.5 fusion.28
  742.4 3.8 fusion.76
  751.9 5.3 fusion.32
  795.3 4.0 reduce.2
  801.9 8.6 all-to-all-start.7
  813.5 8.8 reshape.750
  822.3 6.8 constant_dynamic-slice_fusion
  829.1 4.2 copy.343
  833.3 4.2 copy.295
  841.6 4.6 dynamic_update_slice.36
  847.4 4.7 dynamic_update_slice.37
  852.1 4.1 copy.344
  859.5 9.4 %all-to-all-start.6 = ((f32[32,1,14336]{2,1,0:T(1,128)}), f32[32,1,14336]{2,1,0:T(1,128)}, u32[]{:S(2)}, u32[]{:S(2)}) async-start(f32[32,1,14336]{2,1,0:T(1,128)} %copy.301), calls=%async_computation.6 | async-start | bytes 3670016 | tf_op jit(solution)/shard_map/all_to_all | solution.py:385
  875.5 8.4 reshape.771
  883.9 3.4 convert_reduce_fusion
  897.2 8.6 collective-permute-done.15
  (575 shorter events, 322.8 us)
Async XLA Ops:
  88.4 56.9 %all-to-all-start.1 = ((bf16[128,112,128]{2,1,0:T(8,128)(2,1)}), bf16[128,112,128]{2,1,0:T(8,128)(2,1)}, u32[]{:S(2)}, u32[]{:S(2)}) async-start(bf16[128,112,128]{2,1,0:T(8,128)(2,1)} %broadcast_in_dim.43), calls=%async_computation.1 | async-start | bytes 7340032 | tf_op jit(solution)/shard_map/all_to_all | solution.py:187
  98.3 50.4 %copy-start.119 = (f32[2,64]{1,0:T(2,128)}, f32[2,64]{1,0:T(2,128)S(1)}, u32[]{:S(2)}) copy-start(f32[2,64]{1,0:T(2,128)S(1)} %fusion.63) | copy-start | bytes 1540
  98.3 59.4 %copy-start.110 = (f32[2,64]{1,0:T(2,128)}, f32[2,64]{1,0:T(2,128)S(1)}, u32[]{:S(2)}) copy-start(f32[2,64]{1,0:T(2,128)S(1)} %fusion.116) | copy-start | bytes 1540
  99.3 59.4 %collective-permute-start = (bf16[2,64,2048]{2,1,0:T(8,128)(2,1)}, bf16[2,64,2048]{2,1,0:T(8,128)(2,1)S(1)}, u32[]{:S(2)}, u32[]{:S(2)}) collective-permute-start(bf16[2,64,2048]{2,1,0:T(8,128)(2,1)} %fusion.65), channel_id=1, source_target_pairs={{0,2},{1,3},{2,0},{3,1},{4,6},{5,7},{6,4},{7,5},{8,10},{9,11},{10,... | collective-permute-start | bytes 1572872 | tf_op jit(solution)/shard_map/ppermute | solution.py:106
  102.6 191.4 %collective-permute-start.8 = (bf16[2,64,2048]{2,1,0:T(8,128)(2,1)}, bf16[2,64,2048]{2,1,0:T(8,128)(2,1)}, u32[]{:S(2)}, u32[]{:S(2)}) collective-permute-start(bf16[2,64,2048]{2,1,0:T(8,128)(2,1)} %param.19), channel_id=1, source_target_pairs={{0,2},{1,3},{2,0},{3,1},{4,6},{5,7},{6,4},{7,5},{8,10},{9,11},{10,... | collective-permute-start | bytes 1572872 | tf_op jit(solution)/shard_map/ppermute | solution.py:106
  103.8 44.9 %copy-start.115 = (bf16[1408,4]{0,1:T(4,128)(2,1)S(1)}, bf16[1408,4]{0,1:T(4,128)(2,1)}, u32[]{:S(2)}) copy-start(bf16[1408,4]{0,1:T(4,128)(2,1)} %param.34) | copy-start | bytes 33796
  103.9 45.6 %copy-start.123 = (bf16[512,4]{0,1:T(4,128)(2,1)S(1)}, bf16[512,4]{0,1:T(4,128)(2,1)}, u32[]{:S(2)}) copy-start(bf16[512,4]{0,1:T(4,128)(2,1)} %param.33) | copy-start | bytes 12292
  103.9 46.0 %copy-start.112 = (bf16[2,4,1408]{2,1,0:T(4,128)(2,1)S(1)}, bf16[2,4,1408]{2,1,0:T(4,128)(2,1)}, u32[]{:S(2)}) copy-start(bf16[2,4,1408]{2,1,0:T(4,128)(2,1)} %param.32) | copy-start | bytes 67588
  103.9 46.0 %copy-start.114 = (bf16[3,4,512]{2,1,0:T(4,128)(2,1)S(1)}, bf16[3,4,512]{2,1,0:T(4,128)(2,1)}, u32[]{:S(2)}) copy-start(bf16[3,4,512]{2,1,0:T(4,128)(2,1)} %param.31) | copy-start | bytes 36868
  151.3 30.4 %all-to-all-start.2 = ((bf16[32,196,128]{2,1,0:T(8,128)(2,1)}), bf16[32,196,128]{2,1,0:T(8,128)(2,1)S(1)}, u32[]{:S(2)}, u32[]{:S(2)}) async-start(bf16[32,196,128]{2,1,0:T(8,128)(2,1)} %broadcast_in_dim.44), calls=%async_computation.2 | async-start | bytes 3276800 | tf_op jit(solution)/shard_map/all_to_all | solution.py:187
  158.7 24.3 %copy-start.103 = (bf16[512,64]{0,1:T(8,128)(2,1)S(1)}, bf16[512,64]{0,1:T(8,128)(2,1)}, u32[]{:S(2)}) copy-start(bf16[512,64]{0,1:T(8,128)(2,1)} %param.23) | copy-start | bytes 196612
  159.8 38.1 %collective-permute-start.1 = (bf16[2,2,64,2048]{3,2,1,0:T(8,128)(2,1)}, bf16[2,2,64,2048]{3,2,1,0:T(8,128)(2,1)}, u32[]{:S(2)}, u32[]{:S(2)}) collective-permute-start(bf16[2,2,64,2048]{3,2,1,0:T(8,128)(2,1)} %maximum_select_fusion.4), channel_id=1, source_target_pairs={{0,1},{1,0},{2,3},{3,2},{4,5},{5,4},{6,7},{7,6},{8,9},{9,8},{10,11... | collective-permute-start | bytes 3145736 | tf_op jit(solution)/shard_map/ppermute | solution.py:110
  184.6 33.5 %all-to-all-start.3 = ((bf16[32,512,64]{1,2,0:T(8,128)(2,1)}), bf16[32,512,64]{1,2,0:T(8,128)(2,1)}, u32[]{:S(2)}, u32[]{:S(2)}) async-start(bf16[32,512,64]{1,2,0:T(8,128)(2,1)} %broadcast_in_dim.47), calls=%async_computation.3 | async-start | bytes 4194304 | tf_op jit(solution)/shard_map/all_to_all | solution.py:179
  200.0 80.6 %copy-start = (bf16[2,2,2,64,2048]{4,3,2,1,0:T(8,128)(2,1)}, bf16[2,2,2,64,2048]{4,3,2,1,0:T(8,128)(2,1)S(1)}, u32[]{:S(2)}) copy-start(bf16[2,2,2,64,2048]{4,3,2,1,0:T(8,128)(2,1)S(1)} %maximum_select_fusion) | copy-start | bytes 6291460
  208.8 109.8 %copy-start.4 = (bf16[5,2048,16]{1,2,0:T(8,128)(2,1)}, bf16[5,2048,16]{1,2,0:T(8,128)(2,1)S(1)}, u32[]{:S(2)}) copy-start(bf16[5,2048,16]{1,2,0:T(8,128)(2,1)S(1)} %copy.238) | copy-start | bytes 983044
  217.7 27.4 %copy-start.79 = (f32[2,256,16]{1,2,0:T(8,128)}, f32[2,256,16]{1,2,0:T(8,128)S(1)}, u32[]{:S(2)}) copy-start(f32[2,256,16]{1,2,0:T(8,128)S(1)} %fusion.125) | copy-start | bytes 98308
  224.8 216.5 %all-to-all-start.4 = ((bf16[64,64,1408]{2,1,0:T(8,128)(2,1)}), bf16[64,64,1408]{2,1,0:T(8,128)(2,1)}, u32[]{:S(2)}, u32[]{:S(2)}) async-start(bf16[64,64,1408]{2,1,0:T(8,128)(2,1)} %bitcast.512), calls=%async_computation.4 | async-start | bytes 23068672 | tf_op jit(solution)/shard_map/all_to_all | solution.py:179
  237.8 81.6 %copy-start.42 = (bf16[2,16,2048]{2,1,0:T(8,128)(2,1)}, bf16[2,16,2048]{2,1,0:T(8,128)(2,1)S(1)}, u32[]{:S(2)}) copy-start(bf16[2,16,2048]{2,1,0:T(8,128)(2,1)S(1)} %copy.255) | copy-start | bytes 393220
  292.5 9.3 %collective-permute-start.2 = (f32[2,2,64,2048]{3,2,0,1:T(8,128)}, f32[2,2,64,2048]{3,2,0,1:T(8,128)}, u32[]{:S(2)}, u32[]{:S(2)}) collective-permute-start(f32[2,2,64,2048]{3,2,0,1:T(8,128)} %bitcast.502), channel_id=1, source_target_pairs={{0,1},{1,0},{2,3},{3,2},{4,5},{5,4},{6,7},{7,6},{8,9},{9,8},{10,11... | collective-permute-start | bytes 6291464 | tf_op jit(solution)/shard_map/ppermute | solution.py:125
  296.7 3.0 collective-permute-start.9
  305.4 38.0 %collective-permute-start.3 = (bf16[2,64,2048]{2,1,0:T(8,128)(2,1)}, bf16[2,64,2048]{2,1,0:T(8,128)(2,1)}, u32[]{:S(2)}, u32[]{:S(2)}) collective-permute-start(bf16[2,64,2048]{2,1,0:T(8,128)(2,1)} %fusion.78), channel_id=1, source_target_pairs={{0,2},{1,3},{2,0},{3,1},{4,6},{5,7},{6,4},{7,5},{8,10},{9,11},{10,... | collective-permute-start | bytes 1572872 | tf_op jit(solution)/shard_map/ppermute | solution.py:128
  345.0 127.1 %copy-start.116 = (f32[2,64]{1,0:T(2,128)}, f32[2,64]{1,0:T(2,128)S(1)}, u32[]{:S(2)}) copy-start(f32[2,64]{1,0:T(2,128)S(1)} %get-tuple-element.64) | copy-start | bytes 1540
  454.5 117.2 %all-to-all-start.5 = ((bf16[32,1408,64]{1,2,0:T(8,128)(2,1)}), bf16[32,1408,64]{1,2,0:T(8,128)(2,1)}, u32[]{:S(2)}, u32[]{:S(2)}) async-start(bf16[32,1408,64]{1,2,0:T(8,128)(2,1)} %broadcast_in_dim.49), calls=%async_computation.5 | async-start | bytes 11534336 | tf_op jit(solution)/shard_map/all_to_all | solution.py:179
  472.2 81.1 %copy-start.108 = (f32[2,64]{1,0:T(2,128)}, f32[2,64]{1,0:T(2,128)S(1)}, u32[]{:S(2)}) copy-start(f32[2,64]{1,0:T(2,128)S(1)} %fusion.117) | copy-start | bytes 1540
  473.2 69.7 %collective-permute-start.4 = (bf16[2,64,2048]{2,1,0:T(8,128)(2,1)}, bf16[2,64,2048]{2,1,0:T(8,128)(2,1)}, u32[]{:S(2)}, u32[]{:S(2)}) collective-permute-start(bf16[2,64,2048]{2,1,0:T(8,128)(2,1)} %multiply_convert_fusion.3), channel_id=1, source_target_pairs={{0,2},{1,3},{2,0},{3,1},{4,6},{5,7},{6,4},{7,5},{8,10},{9,11},{10,... | collective-permute-start | bytes 1572872 | tf_op jit(solution)/shard_map/ppermute | solution.py:106
  481.1 66.5 %copy-start.100 = (bf16[4,1408,4]{1,2,0:T(4,128)(2,1)S(1)}, bf16[4,1408,4]{1,2,0:T(4,128)(2,1)}, u32[]{:S(2)}) copy-start(bf16[4,1408,4]{1,2,0:T(4,128)(2,1)} %copy.264) | copy-start | bytes 135172
  544.3 10.6 %collective-permute-start.5 = (bf16[2,2,64,2048]{3,2,0,1:T(8,128)(2,1)S(1)}, bf16[2,2,64,2048]{3,2,0,1:T(8,128)(2,1)S(1)}, u32[]{:S(2)}, u32[]{:S(2)}) collective-permute-start(bf16[2,2,64,2048]{3,2,0,1:T(8,128)(2,1)S(1)} %maximum_select_fusion.6), channel_id=1, source_target_pairs={{0,1},{1,0},{2,3},{3,2},{4,5},{5,4},{6,7},{7,6},{8,9},{9,8},{10,11... | collective-permute-start | bytes 3145736 | tf_op jit(solution)/shard_map/ppermute | solution.py:110
  556.8 22.9 %copy-start.101 = (f32[2,256,16]{1,2,0:T(8,128)}, f32[2,256,16]{1,2,0:T(8,128)S(1)}, u32[]{:S(2)}) copy-start(f32[2,256,16]{1,2,0:T(8,128)S(1)} %fusion.136) | copy-start | bytes 98308
  583.1 21.6 %copy-start.32 = (bf16[2,256,1408]{2,1,0:T(8,128)(2,1)}, bf16[2,256,1408]{2,1,0:T(8,128)(2,1)S(1)}, u32[]{:S(2)}) copy-start(bf16[2,256,1408]{2,1,0:T(8,128)(2,1)S(1)} %get-tuple-element.68) | copy-start | bytes 4325380
  598.8 19.2 %collective-permute-start.10 = (f32[2,2,64,2048]{3,2,0,1:T(8,128)}, f32[2,2,64,2048]{3,2,0,1:T(8,128)}, u32[]{:S(2)}, u32[]{:S(2)}) collective-permute-start(f32[2,2,64,2048]{3,2,0,1:T(8,128)} %bitcast.500), channel_id=1, source_target_pairs={{0,1},{1,0},{2,3},{3,2},{4,5},{5,4},{6,7},{7,6},{8,9},{9,8},{10,11... | collective-permute-start | bytes 6291464 | tf_op jit(solution)/shard_map/ppermute | solution.py:125
  610.5 13.4 %collective-permute-start.6 = (f32[2,2,64,2048]{3,2,0,1:T(8,128)}, f32[2,2,64,2048]{3,2,0,1:T(8,128)}, u32[]{:S(2)}, u32[]{:S(2)}) collective-permute-start(f32[2,2,64,2048]{3,2,0,1:T(8,128)} %bitcast.501), channel_id=1, source_target_pairs={{0,1},{1,0},{2,3},{3,2},{4,5},{5,4},{6,7},{7,6},{8,9},{9,8},{10,11... | collective-permute-start | bytes 6291464 | tf_op jit(solution)/shard_map/ppermute | solution.py:125
  613.0 55.6 %collective-permute-start.18 = (f32[2,2,256,16]{2,3,1,0:T(8,128)}, f32[2,2,256,16]{2,3,1,0:T(8,128)}, u32[]{:S(2)}, u32[]{:S(2)}) collective-permute-start(f32[2,2,256,16]{2,3,1,0:T(8,128)} %pad_maximum_fusion.11), channel_id=1, source_target_pairs={{0,1},{1,0},{2,3},{3,2},{4,5},{5,4},{6,7},{7,6},{8,9},{9,8},{10,11... | collective-permute-start | bytes 196616 | tf_op jit(solution)/shard_map/ppermute | solution.py:134
  615.1 37.3 %copy-start.54 = (f32[2,1,16,1408]{3,2,0,1:T(8,128)}, f32[2,1,16,1408]{3,2,0,1:T(8,128)S(1)}, u32[]{:S(2)}) copy-start(f32[2,1,16,1408]{3,2,0,1:T(8,128)S(1)} %fusion.18) | copy-start | bytes 540676
  620.1 15.6 %collective-permute-start.11 = (bf16[2,64,2048]{2,1,0:T(8,128)(2,1)S(1)}, bf16[2,64,2048]{2,1,0:T(8,128)(2,1)S(1)}, u32[]{:S(2)}, u32[]{:S(2)}) collective-permute-start(bf16[2,64,2048]{2,1,0:T(8,128)(2,1)S(1)} %fusion.80), channel_id=1, source_target_pairs={{0,2},{1,3},{2,0},{3,1},{4,6},{5,7},{6,4},{7,5},{8,10},{9,11},{10,... | collective-permute-start | bytes 1572872 | tf_op jit(solution)/shard_map/ppermute | solution.py:128
  626.0 21.0 %copy-start.109 = (f32[2,64]{1,0:T(2,128)S(1)}, f32[2,64]{1,0:T(2,128)}, u32[]{:S(2)}) copy-start(f32[2,64]{1,0:T(2,128)} %copy-done.108) | copy-start | bytes 1540
  626.0 20.9 %collective-permute-start.7 = (bf16[2,64,2048]{2,1,0:T(8,128)(2,1)S(1)}, bf16[2,64,2048]{2,1,0:T(8,128)(2,1)S(1)}, u32[]{:S(2)}, u32[]{:S(2)}) collective-permute-start(bf16[2,64,2048]{2,1,0:T(8,128)(2,1)S(1)} %fusion.79), channel_id=1, source_target_pairs={{0,2},{1,3},{2,0},{3,1},{4,6},{5,7},{6,4},{7,5},{8,10},{9,11},{10,... | collective-permute-start | bytes 1572872 | tf_op jit(solution)/shard_map/ppermute | solution.py:128
  626.8 25.6 %copy-start.56 = (f32[2,1,16,1408]{3,2,0,1:T(8,128)}, f32[2,1,16,1408]{3,2,0,1:T(8,128)S(1)}, u32[]{:S(2)}) copy-start(f32[2,1,16,1408]{3,2,0,1:T(8,128)S(1)} %fusion.19) | copy-start | bytes 540676
  649.7 14.2 %collective-permute-start.12 = (bf16[2,64,2048]{2,1,0:T(8,128)(2,1)}, bf16[2,64,2048]{2,1,0:T(8,128)(2,1)}, u32[]{:S(2)}, u32[]{:S(2)}) collective-permute-start(bf16[2,64,2048]{2,1,0:T(8,128)(2,1)} %get-tuple-element.62), channel_id=1, source_target_pairs={{0,2},{1,3},{2,0},{3,1},{4,6},{5,7},{6,4},{7,5},{8,10},{9,11},{10,... | collective-permute-start | bytes 1572872 | tf_op jit(solution)/shard_map/ppermute | solution.py:106
  654.4 18.4 %copy-start.55 = (f32[2,1,16,1408]{3,2,0,1:T(8,128)S(1)}, f32[2,1,16,1408]{3,2,0,1:T(8,128)}, u32[]{:S(2)}) copy-start(f32[2,1,16,1408]{3,2,0,1:T(8,128)} %copy-done.54) | copy-start | bytes 540676
  654.4 18.4 %copy-start.57 = (f32[2,1,16,1408]{3,2,0,1:T(8,128)S(1)}, f32[2,1,16,1408]{3,2,0,1:T(8,128)}, u32[]{:S(2)}) copy-start(f32[2,1,16,1408]{3,2,0,1:T(8,128)} %copy-done.56) | copy-start | bytes 540676
  666.7 28.6 %collective-permute-start.13 = (bf16[2,2,64,2048]{3,2,0,1:T(8,128)(2,1)}, bf16[2,2,64,2048]{3,2,0,1:T(8,128)(2,1)}, u32[]{:S(2)}, u32[]{:S(2)}) collective-permute-start(bf16[2,2,64,2048]{3,2,0,1:T(8,128)(2,1)} %maximum_select_fusion.9), channel_id=1, source_target_pairs={{0,1},{1,0},{2,3},{3,2},{4,5},{5,4},{6,7},{7,6},{8,9},{9,8},{10,11... | collective-permute-start | bytes 3145736 | tf_op jit(solution)/shard_map/ppermute | solution.py:110
  670.1 17.2 %collective-permute-start.19 = (f32[2,2,256,16]{2,3,1,0:T(8,128)}, f32[2,2,256,16]{2,3,1,0:T(8,128)}, u32[]{:S(2)}, u32[]{:S(2)}) collective-permute-start(f32[2,2,256,16]{2,3,1,0:T(8,128)} %fusion.120), channel_id=1, source_target_pairs={{0,2},{1,3},{2,0},{3,1},{4,6},{5,7},{6,4},{7,5},{8,10},{9,11},{10,... | collective-permute-start | bytes 196616 | tf_op jit(solution)/shard_map/ppermute | solution.py:135
  777.0 91.9 %collective-permute-start.14 = (f32[2,2,64,2048]{3,2,0,1:T(8,128)}, f32[2,2,64,2048]{3,2,0,1:T(8,128)}, u32[]{:S(2)}, u32[]{:S(2)}) collective-permute-start(f32[2,2,64,2048]{3,2,0,1:T(8,128)} %bitcast.499), channel_id=1, source_target_pairs={{0,1},{1,0},{2,3},{3,2},{4,5},{5,4},{6,7},{7,6},{8,9},{9,8},{10,11... | collective-permute-start | bytes 6291464 | tf_op jit(solution)/shard_map/ppermute | solution.py:125
  778.5 11.0 %collective-permute-start.16 = (f32[5,2,256,16]{2,3,1,0:T(8,128)}, f32[5,2,256,16]{2,3,1,0:T(8,128)}, u32[]{:S(2)}, u32[]{:S(2)}) collective-permute-start(f32[5,2,256,16]{2,3,1,0:T(8,128)} %bitcast_dynamic-update-slice_fusion), channel_id=1, source_target_pairs={{0,1},{1,0},{2,3},{3,2},{4,5},{5,4},{6,7},{7,6},{8,9},{9,8},{10,11... | collective-permute-start | bytes 491528 | tf_op jit(solution)/shard_map/ppermute | solution.py:134
  790.6 20.0 %collective-permute-start.17 = (f32[5,2,256,16]{2,3,1,0:T(8,128)S(1)}, f32[5,2,256,16]{2,3,1,0:T(8,128)S(1)}, u32[]{:S(2)}, u32[]{:S(2)}) collective-permute-start(f32[5,2,256,16]{2,3,1,0:T(8,128)S(1)} %add.296), channel_id=1, source_target_pairs={{0,2},{1,3},{2,0},{3,1},{4,6},{5,7},{6,4},{7,5},{8,10},{9,11},{10,... | collective-permute-start | bytes 491528 | tf_op jit(solution)/shard_map/ppermute | solution.py:135
  801.9 57.7 %all-to-all-start.7 = ((bf16[32,2,12544]{2,1,0:T(2,128)(2,1)}), bf16[32,2,12544]{2,1,0:T(2,128)(2,1)}, u32[]{:S(2)}, u32[]{:S(2)}) async-start(bf16[32,2,12544]{2,1,0:T(2,128)(2,1)} %reshape.770), calls=%async_computation.7 | async-start | bytes 3211264 | tf_op jit(solution)/shard_map/all_to_all | solution.py:403
  859.5 33.7 %all-to-all-start.6 = ((f32[32,1,14336]{2,1,0:T(1,128)}), f32[32,1,14336]{2,1,0:T(1,128)}, u32[]{:S(2)}, u32[]{:S(2)}) async-start(f32[32,1,14336]{2,1,0:T(1,128)} %copy.301), calls=%async_computation.6 | async-start | bytes 3670016 | tf_op jit(solution)/shard_map/all_to_all | solution.py:385
  872.3 33.6 %collective-permute-start.15 = (bf16[2,64,2048]{2,1,0:T(8,128)(2,1)}, bf16[2,64,2048]{2,1,0:T(8,128)(2,1)}, u32[]{:S(2)}, u32[]{:S(2)}) collective-permute-start(bf16[2,64,2048]{2,1,0:T(8,128)(2,1)} %fusion.81), channel_id=1, source_target_pairs={{0,2},{1,3},{2,0},{3,1},{4,6},{5,7},{6,4},{7,5},{8,10},{9,11},{10,... | collective-permute-start | bytes 1572872 | tf_op jit(solution)/shard_map/ppermute | solution.py:128
  (118 other events, 625.4 us)

commit v8 on v4

--- a/solution.py
+++ b/solution.py
@@ -125,13 +125,96 @@
     chip_sum = mine + lax.ppermute(theirs, "tok", xor_pairs(count, 1))
     keep = lax.dynamic_index_in_dim(chip_sum, half, axis, keepdims=False)
     send = lax.dynamic_index_in_dim(chip_sum, 1 - half, axis, keepdims=False)
-    return keep + lax.ppermute(send, "tok", xor_pairs(count, 2))
+    got = lax.ppermute(send.astype(jnp.bfloat16), "tok", xor_pairs(count, 2))
+    return keep + got.astype(keep.dtype)
 
 
 def tok_sum(values):
     count = lax.axis_size("tok")
     chip_sum = values + lax.ppermute(values, "tok", xor_pairs(count, 1))
     return chip_sum + lax.ppermute(chip_sum, "tok", xor_pairs(count, 2))
+
+
+def fsdp_coords():
+    me = lax.axis_index("fsdp")
+    return {"x": me // 8, "z": (me // 4) % 2, "y": me % 4}
+
+
+def fsdp_pairs(kind, step):
+    pairs = []
+    for x in range(4):
+        for z in range(2):
+            for y in range(4):
+                if kind == "z":
+                    target = (x * 2 + 1 - z) * 4 + y
+                elif kind == "x":
+                    target = (((x + step) % 4) * 2 + z) * 4 + y
+                else:
+                    target = (x * 2 + z) * 4 + (y + step) % 4
+                pairs.append(((x * 2 + z) * 4 + y, target))
+    return pairs
+
+
+def put(buffer, piece, axis, offset):
+    start = [0] * buffer.ndim
+    start[axis] = offset
+    return lax.dynamic_update_slice(buffer, piece, start)
+
+
+def grow(pieces, axes, factor):
+    return [
+        jnp.zeros(p.shape[:ax] + (p.shape[ax] * factor,) + p.shape[ax + 1 :], p.dtype)
+        for p, ax in zip(pieces, axes)
+    ]
+
+
+def halves(pieces, axes, second):
+    out = []
+    for p, ax in zip(pieces, axes):
+        n = p.shape[ax] // 2
+        out.append(lax.slice_in_dim(p, n if second else 0, 2 * n if second else n, axis=ax))
+    return out
+
+
+def pair_stage(stacks, axes, coord):
+    other = lax.ppermute(stacks, "fsdp", fsdp_pairs("z", 1))
+    outs = []
+    for mine, theirs, buffer, ax in zip(stacks, other, grow(stacks, axes, 2), axes):
+        n = mine.shape[ax]
+        buffer = put(buffer, mine, ax, coord * n)
+        outs.append(put(buffer, theirs, ax, (1 - coord) * n))
+    return outs
+
+
+def ring_stage(stacks, axes, kind, coord):
+    from_left = lax.ppermute(stacks, "fsdp", fsdp_pairs(kind, 1))
+    from_right = lax.ppermute(stacks, "fsdp", fsdp_pairs(kind, -1))
+    split = stacks[0].shape[axes[0]] > 1
+    if split:
+        far_left = lax.ppermute(halves(from_left, axes, False), "fsdp", fsdp_pairs(kind, 1))
+        far_right = lax.ppermute(halves(from_right, axes, True), "fsdp", fsdp_pairs(kind, -1))
+    else:
+        far_left = lax.ppermute(from_left, "fsdp", fsdp_pairs(kind, 1))
+    outs = []
+    for i, (buffer, ax) in enumerate(zip(grow(stacks, axes, 4), axes)):
+        n = stacks[i].shape[ax]
+        buffer = put(buffer, stacks[i], ax, coord * n)
+        buffer = put(buffer, from_right[i], ax, ((coord + 1) % 4) * n)
+        buffer = put(buffer, from_left[i], ax, ((coord + 3) % 4) * n)
+        buffer = put(buffer, far_left[i], ax, ((coord + 2) % 4) * n)
+        if split:
+            buffer = put(buffer, far_right[i], ax, ((coord + 2) % 4) * n + n // 2)
+        outs.append(buffer)
+    return outs
+
+
+def torus_gather(route_a, axes_a, route_b, axes_b):
+    coord = fsdp_coords()
+    route_a = ring_stage(route_a, axes_a, "y", coord["y"])
+    route_b = ring_stage(route_b, axes_b, "x", coord["x"])
+    both = pair_stage(route_a + route_b, axes_a + axes_b, coord["z"])
+    route_a, route_b = both[: len(route_a)], both[len(route_a) :]
+    return ring_stage(route_a, axes_a, "x", coord["x"]), ring_stage(route_b, axes_b, "y", coord["y"])
 
 
 def hp_dot(left, right, spec):
@@ -172,34 +255,43 @@
     fsdp_rows = w_qkv.shape[1]
     groups_per_adapter = RANK // b_qkv.shape[1]
 
-    def fsdp_gather(values, axis):
-        tiled_in = jnp.broadcast_to(values[None], (fsdp_count,) + values.shape)
-        tiled_in = tiled_in.reshape((fsdp_count * values.shape[0],) + values.shape[1:])
-        return lax.all_to_all(tiled_in, "fsdp", 0, axis, tiled=True)
-
-    def packed_gather(small, axes):
-        count = 1
-        for name in axes:
-            count *= lax.axis_size(name)
-        flat = jnp.concatenate([p.reshape(-1, COLS) for p in small], axis=0)
-        tiled_in = jnp.broadcast_to(flat[None], (count,) + flat.shape).reshape(-1, COLS)
-        got = lax.all_to_all(tiled_in, axes, 0, 0, tiled=True).reshape((count,) + flat.shape)
-        out = []
-        start = 0
-        for p in small:
-            rows = p.size // COLS
-            out.append(got[:, start : start + rows].reshape((count,) + p.shape))
-            start += rows
-        return out
-
-    w_qkv_full = fsdp_gather(w_qkv, 1)
-    g_ain, g_brows = packed_gather([a_in, b_rows], ("fsdp", "tok"))
-    g_bqkv, g_bgateup, g_aout, g_adown = packed_gather([b_qkv, b_gateup, a_out, a_down], ("fsdp",))
-    w_out_full = fsdp_gather(w_out, 1)
-    w_gateup_full = fsdp_gather(w_gateup, 1)
-    w_down_full = fsdp_gather(w_down, 1)
-    a_in_full = jnp.moveaxis(g_ain, 0, 1).reshape(5, D, COLS)
-    b_rows_full = jnp.moveaxis(g_brows, 0, 2).reshape(2, COLS, D)
+    a_in_tok = tok_gather(a_in)
+    b_rows_tok = tok_gather(b_rows)
+    small = [a_in_tok, b_rows_tok, b_qkv, b_gateup, a_out, a_down]
+    small_flat = jnp.concatenate([p.reshape(-1, COLS) for p in small])
+    (g_qkv, g_out, g_down, g_small), (g_gateup,) = torus_gather(
+        [w_qkv[:, None], w_out[None], w_down[None], small_flat[None]],
+        [1, 0, 0, 0],
+        [w_gateup[:, None]],
+        [1],
+    )
+    w_qkv_full = g_qkv.reshape(3, D, qw_here)
+    w_out_full = jnp.moveaxis(g_out, 0, 1).reshape(qw_here, D)
+    w_down_full = jnp.moveaxis(g_down, 0, 1).reshape(ff_here, D)
+    w_gateup_perm = g_gateup.reshape(2, D, ff_here)
+    unpacked = []
+    start = 0
+    for p in small:
+        rows = p.size // COLS
+        unpacked.append(g_small[:, start : start + rows].reshape((fsdp_count,) + p.shape))
+        start += rows
+    (g_ain, g_brows, g_bqkv, g_bgateup, g_aout, g_adown) = unpacked
+    a_in_full = jnp.transpose(g_ain, (2, 0, 1, 3, 4)).reshape(5, D, COLS)
+    b_rows_full = jnp.transpose(g_brows, (2, 3, 0, 1, 4)).reshape(2, COLS, D)
+
+    def to_yzx(values):
+        lead = values.shape[:-1]
+        split = values.reshape(lead + (4, 2, 4, D // fsdp_count))
+        n = len(lead)
+        order = tuple(range(n)) + (n + 2, n + 1, n, n + 3)
+        return jnp.transpose(split, order).reshape(values.shape)
+
+    def from_yzx(values):
+        lead = values.shape[:-1]
+        split = values.reshape(lead + (4, 2, 4, D // fsdp_count))
+        n = len(lead)
+        order = tuple(range(n)) + (n + 2, n + 1, n, n + 3)
+        return jnp.transpose(split, order).reshape(values.shape)
 
     def pick_cols(values, axis):
         return jnp.stack(
@@ -228,9 +320,11 @@
     def scatter_rows(values):
         return tok_scatter(values.reshape(seqs, tok_count, local_len, values.shape[-1]), 1)
 
-    def column_forward(rows_full, weight, down_sel, up_sel):
+    def column_forward(rows_full, weight, down_sel, up_sel, rows_for_weight=None):
+        if rows_for_weight is None:
+            rows_for_weight = rows_full
         lowrank = jnp.einsum("std,sdr->str", rows_full, down_sel, preferred_element_type=jnp.float32)
-        linear = jnp.einsum("std,de->ste", rows_full, weight, preferred_element_type=jnp.float32)
+        linear = jnp.einsum("std,de->ste", rows_for_weight, weight, preferred_element_type=jnp.float32)
         return linear + adapter_scale * hp_dot(lowrank, up_sel.astype(jnp.float32), "str,sre->ste"), lowrank
 
     def row_forward(rows_here, weight, down_sel, up_sel):
@@ -267,8 +361,9 @@
     hidden = inputs_rows + attn_rows
     normed_ffn, norm_ffn_pull = jax.vjp(partial(rows_norm, gain_vector=gain_ffn), hidden)
     ffn_full = gather_rows(normed_ffn.astype(jnp.bfloat16))
-    gate_lin, gate_low = column_forward(ffn_full, w_gateup_full[0], a_in_sel[:, 3], b_gateup_sel[:, 0])
-    up_lin, up_low = column_forward(ffn_full, w_gateup_full[1], a_in_sel[:, 4], b_gateup_sel[:, 1])
+    ffn_perm = to_yzx(ffn_full)
+    gate_lin, gate_low = column_forward(ffn_full, w_gateup_perm[0], a_in_sel[:, 3], b_gateup_sel[:, 0], ffn_perm)
+    up_lin, up_low = column_forward(ffn_full, w_gateup_perm[1], a_in_sel[:, 4], b_gateup_sel[:, 1], ffn_perm)
     product_float, swiglu_pull = jax.vjp(swiglu, gate_lin, up_lin)
     product = product_float.astype(jnp.bfloat16)
     ffn_rows, down_low = row_forward(product, w_down_full, a_down_sel, b_rows_sel[:, 1])
@@ -286,7 +381,7 @@
         ) + hp_dot(grad_low, down_sel.astype(jnp.float32), "str,sdr->std")
         return grad_inputs, grad_down
 
-    def column_backward(rows_full, entries):
+    def column_backward(rows_full, entries, weight_order=None):
         running = None
         grad_lows = []
         grads_up = []
@@ -295,9 +390,10 @@
             grad_low = adapter_scale * hp_dot(grad_float, up_sel.astype(jnp.float32), "ste,sre->str")
             grads_up.append(adapter_scale * hp_dot(lowrank, grad_float, "str,ste->sre"))
             grad_lows.append(grad_low)
-            term = jnp.einsum(
-                "ste,de->std", grad_rows, weight, preferred_element_type=jnp.float32
-            ) + hp_dot(grad_low, down_sel.astype(jnp.float32), "str,sdr->std")
+            main_term = jnp.einsum("ste,de->std", grad_rows, weight, preferred_element_type=jnp.float32)
+            if weight_order is not None:
+                main_term = weight_order(main_term)
+            term = main_term + hp_dot(grad_low, down_sel.astype(jnp.float32), "str,sdr->std")
             running = term if running is None else running + term
         return scatter_rows(running), grad_lows, grads_up
 
@@ -315,9 +411,10 @@
     grad_ffn_rows, ffn_grad_lows, ffn_grads_up = column_backward(
         ffn_full,
         (
-            (grad_gate.astype(jnp.bfloat16), w_gateup_full[0], a_in_sel[:, 3], b_gateup_sel[:, 0], gate_low),
-            (grad_up.astype(jnp.bfloat16), w_gateup_full[1], a_in_sel[:, 4], b_gateup_sel[:, 1], up_low),
+            (grad_gate.astype(jnp.bfloat16), w_gateup_perm[0], a_in_sel[:, 3], b_gateup_sel[:, 0], gate_low),
+            (grad_up.astype(jnp.bfloat16), w_gateup_perm[1], a_in_sel[:, 4], b_gateup_sel[:, 1], up_low),
         ),
+        from_yzx,
     )
     grad_hidden = tangent + norm_ffn_pull(grad_ffn_rows)[0]
     grad_attn_full = gather_rows(grad_hidden.astype(jnp.bfloat16))

time: 984 us -> 839 us (0.85)
  waiting for transfers between devices: 325 us -> 141 us
  local copies, waits for them, and re-layouts: 237 us -> 355 us
  blocking collectives: 87.4 us -> 0 us
  matrix products: 114 us -> 126 us
    all_to_all x4 -> x0, waiting for transfers between devices: 91.5 us -> none  [fsdp_gather(): return lax.all_to_all(tiled_in, 'fsdp', 0, axis, tiled=True)]
    all_to_all x2 -> x0, blocking collectives: 87.4 us -> none  [packed_gather(): lax.all_to_all(tiled_in, axes, 0, 0, tiled=True)]
    ppermute x4 -> x6, waiting for transfers between devices: 95.1 us -> 10.5 us  [tok_gather(): far = lax.ppermute(values, 'tok', xor_pairs(count, 2))]
    dynamic_update_slice x0 -> x57, local copies, waits for them, and re-layouts: none -> 63.8 us  [put(): return lax.dynamic_update_slice(buffer, piece, start)]
    all_to_all x4 -> x0, starting transfers between devices: 33.5 us -> none  [fsdp_gather(): return lax.all_to_all(tiled_in, 'fsdp', 0, axis, tiled=True)]
    ppermute x4 -> x44, starting transfers between devices: 20.5 us -> 44.9 us  [the longest x10 20.3 us: ring_stage(): from_right = lax.ppermute(stacks, 'fsdp', fsdp_pairs(kind, -1))]
    slice x14 -> x20, local copies, waits for them, and re-layouts: 19.9 us -> 42.7 us  [the longest x9 18.9 us: per_device(): g_small[:, start:start + rows].reshape((fsdp_count,) + p.shape)]
    ppermute x4, starting transfers between devices: 4.19 us -> 20 us  [tok_scatter(): chip_sum = mine + lax.ppermute(theirs, 'tok', xor_pairs(count, 1))]
  transfers between devices with their start and end apart: 26 -> 66, of which waited for: 12 -> 23; matrix products, arithmetic and copies ran while one was open for 28% -> 48% of each run, Pallas kernels for 0% -> 0%
where the time goes in v8:
time: 839 us; the launch traced here: 825 us
  local copies, waits for them, and re-layouts  355 us (42%)
  waiting for transfers between devices  141 us (17%)
  matrix products  126 us (15%)
  starting transfers between devices  111 us (13%)
  other arithmetic  82.6 us (10%)
  between operations  8.73 us (1%)
    dynamic_update_slice x57, local copies, waits for them, and re-layouts, put(): return lax.dynamic_update_slice(buffer, piece, start)  63.8 us
    dot_general x32, matrix products, hp_dot(): jnp.einsum(spec, left, right, precision=highest, preferred_element_type=j...  51.3 us
    unnamed x289, local copies, waits for them, and re-layouts  34.8 us
    ppermute x4, waiting for transfers between devices, tok_scatter(): got = lax.ppermute(send.astype(jnp.bfloat16), 'tok', xor_pairs(count, 2))  34 us
    ppermute x5, waiting for transfers between devices, pair_stage(): other = lax.ppermute(stacks, 'fsdp', fsdp_pairs('z', 1))  28.8 us
    dot_general x5, matrix products, column_backward(): jnp.einsum('ste,de->std', grad_rows, weight, preferred_element_type=jnp.f...  25.8 us
    ppermute x10, waiting for transfers between devices, ring_stage(): from_left = lax.ppermute(stacks, 'fsdp', fsdp_pairs(kind, 1))  23.5 us
    ppermute x10, starting transfers between devices, ring_stage(): from_right = lax.ppermute(stacks, 'fsdp', fsdp_pairs(kind, -1))  20.3 us
  transfers between devices with their start and end apart: 66, of which 23 were waited for; matrix products, arithmetic and copies ran while one was open for 48% of the time, Pallas kernels for 0%

profile of v8, /device:TPU:1, one launch (start us, length us, event | category | flops | bytes accessed | tf_op | source)
XLA Modules:
  0.0 824.7 jit_solution(7288744359608756226)
XLA Ops:
  30.8 4.1 collective-permute-done.10
  56.3 5.5 collective-permute-done.43
  83.0 4.6 collective-permute-done.25
  102.8 13.2 %collective-permute-start.1 = (bf16[2,2,64,2048]{3,2,1,0:T(8,128)(2,1)S(1)}, bf16[2,2,64,2048]{3,2,1,0:T(8,128)(2,1)S(1)}, u32[]{:S(2)}, u32[]{:S(2)}) collective-permute-start(bf16[2,2,64,2048]{3,2,1,0:T(8,128)(2,1)S(1)} %maximum_select_fusion.4), channel_id=1, source_target_pairs={{0,1},{1,0},{2,3},{3,2},{4,5},{5,4},{6,7},{7,6},{8,9},{9,8},{10,11... | collective-permute-start | bytes 3145736 | tf_op jit(solution)/shard_map/ppermute | solution.py:110
  125.2 8.8 %collective-permute-done.5 = bf16[3,4,64,512]{3,2,1,0:T(8,128)(2,1)S(1)} collective-permute-done((bf16[3,4,64,512]{3,2,1,0:T(8,128)(2,1)S(1)}, bf16[3,4,64,512]{3,2,1,0:T(8,128)(2,1)S(1)}, u32[]{:S(2)}, u32[]{:S(2)}) %collective-permute-start.5) | collective-permute-done | bytes 786464 | tf_op jit(solution)/shard_map/ppermute | solution.py:180
  149.6 15.4 %collective-permute-done.37 = bf16[2,4,64,1408]{3,2,1,0:T(8,128)(2,1)S(1)} collective-permute-done((bf16[2,4,64,1408]{3,2,1,0:T(8,128)(2,1)}, bf16[2,4,64,1408]{3,2,1,0:T(8,128)(2,1)S(1)}, u32[]{:S(2)}, u32[]{:S(2)}) %collective-permute-start.37) | collective-permute-done | bytes 1441824 | tf_op jit(solution)/shard_map/ppermute | solution.py:180
  168.0 5.6 broadcast_in_dim.149
  187.7 6.5 collective-permute-done.46
  206.6 14.5 %collective-permute-done.7 = bf16[3,8,64,512]{3,2,1,0:T(8,128)(2,1)} collective-permute-done((bf16[3,8,64,512]{3,2,1,0:T(8,128)(2,1)}, bf16[3,8,64,512]{3,2,1,0:T(8,128)(2,1)}, u32[]{:S(2)}, u32[]{:S(2)}) %collective-permute-start.7) | collective-permute-done | bytes 1572896 | tf_op jit(solution)/shard_map/ppermute | solution.py:190
  223.2 4.7 collective-permute-done.6
  236.7 5.3 collective-permute-done.21
  280.0 4.7 copy.307
  284.8 6.4 copy.308
  296.3 4.5 constant_dynamic-slice_fusion.8
  326.6 5.7 fusion.97
  338.5 4.1 convolution_add_fusion.5
  362.8 19.7 %collective-permute-start.30 = (f32[2,2,64,2048]{3,2,0,1:T(8,128)}, f32[2,2,64,2048]{3,2,0,1:T(8,128)}, u32[]{:S(2)}, u32[]{:S(2)}) collective-permute-start(f32[2,2,64,2048]{3,2,0,1:T(8,128)} %bitcast.537), channel_id=1, source_target_pairs={{0,1},{1,0},{2,3},{3,2},{4,5},{5,4},{6,7},{7,6},{8,9},{9,8},{10,11... | collective-permute-start | bytes 6291464 | tf_op jit(solution)/shard_map/ppermute | solution.py:125
  389.7 7.7 convolution_add_fusion
  413.7 5.8 collective-permute-done.31
  421.8 11.6 %collective-permute-done.40 = bf16[2,4,64,1408]{3,2,1,0:T(8,128)(2,1)S(1)} collective-permute-done((bf16[2,4,64,1408]{3,2,1,0:T(8,128)(2,1)S(1)}, bf16[2,4,64,1408]{3,2,1,0:T(8,128)(2,1)S(1)}, u32[]{:S(2)}, u32[]{:S(2)}) %collective-permute-start.40) | collective-permute-done | bytes 1441824 | tf_op jit(solution)/shard_map/ppermute | solution.py:194
  437.7 9.4 %fusion.96 = (bf16[1,32,64,1408]{3,2,1,0:T(8,128)(2,1)}, bf16[1,32,64,1408]{3,2,1,0:T(8,128)(2,1)}) fusion(bf16[2,32,64,1408]{3,2,1,0:T(8,128)(2,1)} %constant_dynamic-update-slice_fusion.17), kind=kLoop, calls=%fused_computation.343 | loop fusion | bytes 23068672 | tf_op jit(solution)/shard_map/slice | solution.py:365
  449.6 5.7 select_n.517
  458.1 7.1 copy.314
  469.1 5.9 convolution_add_fusion.1
  475.0 6.3 fusion.2
  487.7 5.4 copy.336
  495.6 6.2 convolution_bitcast_fusion.3
  504.2 5.4 copy.334
  512.6 4.4 add_add_fusion.1
  545.7 9.2 %collective-permute-done.55 = bf16[2,64,2048]{2,1,0:T(8,128)(2,1)S(1)} collective-permute-done((bf16[2,64,2048]{2,1,0:T(8,128)(2,1)S(1)}, bf16[2,64,2048]{2,1,0:T(8,128)(2,1)S(1)}, u32[]{:S(2)}, u32[]{:S(2)}) %collective-permute-start.55) | collective-permute-done | bytes 524320 | tf_op jit(solution)/shard_map/ppermute | solution.py:128
  555.2 10.9 %collective-permute-done.51 = bf16[2,64,2048]{2,1,0:T(8,128)(2,1)S(1)} collective-permute-done((bf16[2,64,2048]{2,1,0:T(8,128)(2,1)S(1)}, bf16[2,64,2048]{2,1,0:T(8,128)(2,1)S(1)}, u32[]{:S(2)}, u32[]{:S(2)}) %collective-permute-start.51) | collective-permute-done | bytes 524320 | tf_op jit(solution)/shard_map/ppermute | solution.py:128
  575.9 6.4 collective-permute-done.56
  644.1 4.3 multiply_add_fusion.5
  650.8 5.3 fusion.107
  671.8 4.9 fusion.108
  685.2 5.7 add_add_fusion
  714.8 4.0 reduce.2
  721.2 6.7 all-to-all-start.1
  730.9 8.8 %reshape.871 = f32[5,2,32,4,16,16]{4,3,2,5,1,0:T(4,128)} reshape(f32[5,2,2048,16]{2,3,1,0:T(8,128)S(1)} %copy.359) | data formatting | bytes 2621440 | tf_op jit(solution)/shard_map/reshape | solution.py:402
  739.7 6.8 constant_dynamic-slice_fusion
  746.5 4.2 copy.412
  750.7 4.2 copy.360
  759.0 5.3 dynamic_update_slice.256
  765.6 5.3 dynamic_update_slice.257
  770.9 4.1 copy.413
  778.4 7.8 all-to-all-start
  790.5 8.3 %reshape.896 = bf16[32,1,25088]{2,1,0:T(2,128)(2,1)S(1)} reshape(bf16[32,2,12544]{2,1,0:T(2,128)(2,1)} %all-to-all-done.1) | data formatting | bytes 3211264
  812.6 8.2 collective-permute-done.59
  (742 shorter events, 481.1 us)
Async XLA Ops:
  0.7 61.2 %collective-permute-start.2 = (bf16[3,1,64,512]{3,2,0,1:T(8,128)(2,1)}, bf16[3,1,64,512]{3,2,0,1:T(8,128)(2,1)}, u32[]{:S(2)}, u32[]{:S(2)}) collective-permute-start(bf16[3,1,64,512]{3,2,0,1:T(8,128)(2,1)} %bitcast.662), channel_id=1, source_target_pairs={{0,12},{4,0},{8,4},{12,8},{16,28},{20,16},{24,20},{28,24},{32,44},... | collective-permute-start | bytes 589832 | tf_op jit(solution)/shard_map/ppermute | solution.py:191
  4.3 59.5 %collective-permute-start.3 = (bf16[3,1,64,512]{3,2,0,1:T(8,128)(2,1)}, bf16[3,1,64,512]{3,2,0,1:T(8,128)(2,1)}, u32[]{:S(2)}, u32[]{:S(2)}) collective-permute-start(bf16[3,1,64,512]{3,2,0,1:T(8,128)(2,1)} %bitcast.663), channel_id=1, source_target_pairs={{0,4},{4,8},{8,12},{12,0},{16,20},{20,24},{24,28},{28,16},{32,36},... | collective-permute-start | bytes 589832 | tf_op jit(solution)/shard_map/ppermute | solution.py:190
  4.3 41.2 %collective-permute-start.22 = (bf16[1,512,64]{1,2,0:T(8,128)(2,1)}, bf16[1,512,64]{1,2,0:T(8,128)(2,1)}, u32[]{:S(2)}, u32[]{:S(2)}) collective-permute-start(bf16[1,512,64]{1,2,0:T(8,128)(2,1)} %bitcast.672), channel_id=1, source_target_pairs={{0,12},{4,0},{8,4},{12,8},{16,28},{20,16},{24,20},{28,24},{32,44},... | collective-permute-start | bytes 196616 | tf_op jit(solution)/shard_map/ppermute | solution.py:191
  7.0 38.6 %collective-permute-start.23 = (bf16[1,512,64]{1,2,0:T(8,128)(2,1)}, bf16[1,512,64]{1,2,0:T(8,128)(2,1)}, u32[]{:S(2)}, u32[]{:S(2)}) collective-permute-start(bf16[1,512,64]{1,2,0:T(8,128)(2,1)} %bitcast.673), channel_id=1, source_target_pairs={{0,4},{4,8},{8,12},{12,0},{16,20},{20,24},{24,28},{28,16},{32,36},... | collective-permute-start | bytes 196616 | tf_op jit(solution)/shard_map/ppermute | solution.py:190
  7.0 23.6 %collective-permute-start.12 = (bf16[2,128,16]{1,2,0:T(8,128)(2,1)}, bf16[2,128,16]{1,2,0:T(8,128)(2,1)S(1)}, u32[]{:S(2)}, u32[]{:S(2)}) collective-permute-start(bf16[2,128,16]{1,2,0:T(8,128)(2,1)} %param.35), channel_id=1, source_target_pairs={{0,2},{1,3},{2,0},{3,1},{4,6},{5,7},{6,4},{7,5},{8,10},{9,11},{10,... | collective-permute-start | bytes 24584 | tf_op jit(solution)/shard_map/ppermute | solution.py:106
  40.5 33.0 %collective-permute-start.34 = (bf16[2,1,64,1408]{3,2,0,1:T(8,128)(2,1)}, bf16[2,1,64,1408]{3,2,0,1:T(8,128)(2,1)S(1)}, u32[]{:S(2)}, u32[]{:S(2)}) collective-permute-start(bf16[2,1,64,1408]{3,2,0,1:T(8,128)(2,1)} %bitcast.659), channel_id=1, source_target_pairs={{0,96},{4,100},{8,104},{12,108},{16,112},{20,116},{24,120},{28,124... | collective-permute-start | bytes 1081352 | tf_op jit(solution)/shard_map/ppermute | solution.py:191
  45.5 28.8 %collective-permute-start.35 = (bf16[2,1,64,1408]{3,2,0,1:T(8,128)(2,1)}, bf16[2,1,64,1408]{3,2,0,1:T(8,128)(2,1)S(1)}, u32[]{:S(2)}, u32[]{:S(2)}) collective-permute-start(bf16[2,1,64,1408]{3,2,0,1:T(8,128)(2,1)} %bitcast.660), channel_id=1, source_target_pairs={{0,32},{4,36},{8,40},{12,44},{16,48},{20,52},{24,56},{28,60},{32,6... | collective-permute-start | bytes 1081352 | tf_op jit(solution)/shard_map/ppermute | solution.py:190
  61.8 31.2 %collective-permute-start = (bf16[2,64,2048]{2,1,0:T(8,128)(2,1)S(1)}, bf16[2,64,2048]{2,1,0:T(8,128)(2,1)S(1)}, u32[]{:S(2)}, u32[]{:S(2)}) collective-permute-start(bf16[2,64,2048]{2,1,0:T(8,128)(2,1)S(1)} %copy-done.76), channel_id=1, source_target_pairs={{0,2},{1,3},{2,0},{3,1},{4,6},{5,7},{6,4},{7,5},{8,10},{9,11},{10,... | collective-permute-start | bytes 1572872 | tf_op jit(solution)/shard_map/ppermute | solution.py:106
  69.6 26.0 %collective-permute-start.52 = (bf16[2,64,2048]{2,1,0:T(8,128)(2,1)S(1)}, bf16[2,64,2048]{2,1,0:T(8,128)(2,1)S(1)}, u32[]{:S(2)}, u32[]{:S(2)}) collective-permute-start(bf16[2,64,2048]{2,1,0:T(8,128)(2,1)S(1)} %copy-done.34), channel_id=1, source_target_pairs={{0,2},{1,3},{2,0},{3,1},{4,6},{5,7},{6,4},{7,5},{8,10},{9,11},{10,... | collective-permute-start | bytes 1572872 | tf_op jit(solution)/shard_map/ppermute | solution.py:106
  72.5 15.1 %collective-permute-start.25 = (bf16[4,512,64]{1,2,0:T(8,128)(2,1)S(1)}, bf16[4,512,64]{1,2,0:T(8,128)(2,1)S(1)}, u32[]{:S(2)}, u32[]{:S(2)}) collective-permute-start(bf16[4,512,64]{1,2,0:T(8,128)(2,1)S(1)} %constant_dynamic-update-slice_fusion.31), channel_id=1, source_target_pairs={{0,16},{4,20},{8,24},{12,28},{16,0},{20,4},{24,8},{28,12},{32,48},... | collective-permute-start | bytes 786440 | tf_op jit(solution)/shard_map/ppermute | solution.py:180
  73.5 17.0 %collective-permute-start.4 = (bf16[3,1,64,512]{3,2,0,1:T(8,128)(2,1)}, bf16[3,1,64,512]{3,2,0,1:T(8,128)(2,1)S(1)}, u32[]{:S(2)}, u32[]{:S(2)}) collective-permute-start(bf16[3,1,64,512]{3,2,0,1:T(8,128)(2,1)} %collective-permute-done.3), channel_id=1, source_target_pairs={{0,4},{4,8},{8,12},{12,0},{16,20},{20,24},{24,28},{28,16},{32,36},... | collective-permute-start | bytes 589832 | tf_op jit(solution)/shard_map/ppermute | solution.py:197
  81.6 42.0 %collective-permute-start.45 = (bf16[4,1408,64]{1,2,0:T(8,128)(2,1)S(1)}, bf16[4,1408,64]{1,2,0:T(8,128)(2,1)S(1)}, u32[]{:S(2)}, u32[]{:S(2)}) collective-permute-start(bf16[4,1408,64]{1,2,0:T(8,128)(2,1)S(1)} %constant_dynamic-update-slice_fusion.13), channel_id=1, source_target_pairs={{0,16},{4,20},{8,24},{12,28},{16,0},{20,4},{24,8},{28,12},{32,48},... | collective-permute-start | bytes 2162696 | tf_op jit(solution)/shard_map/ppermute | solution.py:180
  90.5 27.5 %collective-permute-start.17 = (bf16[4,644,128]{2,0,1:T(4,128)(2,1)S(1)}, bf16[4,644,128]{2,0,1:T(4,128)(2,1)S(1)}, u32[]{:S(2)}, u32[]{:S(2)}) collective-permute-start(bf16[4,644,128]{2,0,1:T(4,128)(2,1)S(1)} %copy.284), channel_id=1, source_target_pairs={{0,16},{4,20},{8,24},{12,28},{16,0},{20,4},{24,8},{28,12},{32,48},... | collective-permute-start | bytes 1978376 | tf_op jit(solution)/shard_map/ppermute | solution.py:180
  95.6 21.3 %collective-permute-start.27 = (bf16[8,512,64]{1,2,0:T(8,128)(2,1)S(1)}, bf16[8,512,64]{1,2,0:T(8,128)(2,1)S(1)}, u32[]{:S(2)}, u32[]{:S(2)}) collective-permute-start(bf16[8,512,64]{1,2,0:T(8,128)(2,1)S(1)} %constant_dynamic-update-slice_fusion.29), channel_id=1, source_target_pairs={{0,32},{4,36},{8,40},{12,44},{16,48},{20,52},{24,56},{28,60},{32,6... | collective-permute-start | bytes 1572872 | tf_op jit(solution)/shard_map/ppermute | solution.py:190
  96.1 37.9 %collective-permute-start.5 = (bf16[3,4,64,512]{3,2,1,0:T(8,128)(2,1)S(1)}, bf16[3,4,64,512]{3,2,1,0:T(8,128)(2,1)S(1)}, u32[]{:S(2)}, u32[]{:S(2)}) collective-permute-start(bf16[3,4,64,512]{3,2,1,0:T(8,128)(2,1)S(1)} %bitcast_dynamic-update-slice_fusion.5), channel_id=1, source_target_pairs={{0,16},{4,20},{8,24},{12,28},{16,0},{20,4},{24,8},{28,12},{32,48},... | collective-permute-start | bytes 2359304 | tf_op jit(solution)/shard_map/ppermute | solution.py:180
  102.8 45.5 %collective-permute-start.1 = (bf16[2,2,64,2048]{3,2,1,0:T(8,128)(2,1)S(1)}, bf16[2,2,64,2048]{3,2,1,0:T(8,128)(2,1)S(1)}, u32[]{:S(2)}, u32[]{:S(2)}) collective-permute-start(bf16[2,2,64,2048]{3,2,1,0:T(8,128)(2,1)S(1)} %maximum_select_fusion.4), channel_id=1, source_target_pairs={{0,1},{1,0},{2,3},{3,2},{4,5},{5,4},{6,7},{7,6},{8,9},{9,8},{10,11... | collective-permute-start | bytes 3145736 | tf_op jit(solution)/shard_map/ppermute | solution.py:110
  116.9 28.9 %collective-permute-start.53 = (bf16[2,2,64,2048]{3,2,0,1:T(8,128)(2,1)S(1)}, bf16[2,2,64,2048]{3,2,0,1:T(8,128)(2,1)S(1)}, u32[]{:S(2)}, u32[]{:S(2)}) collective-permute-start(bf16[2,2,64,2048]{3,2,0,1:T(8,128)(2,1)S(1)} %maximum_select_fusion.7), channel_id=1, source_target_pairs={{0,1},{1,0},{2,3},{3,2},{4,5},{5,4},{6,7},{7,6},{8,9},{9,8},{10,11... | collective-permute-start | bytes 3145736 | tf_op jit(solution)/shard_map/ppermute | solution.py:110
  117.9 17.6 %collective-permute-start.28 = (bf16[4,512,64]{1,2,0:T(8,128)(2,1)S(1)}, bf16[4,512,64]{1,2,0:T(8,128)(2,1)S(1)}, u32[]{:S(2)}, u32[]{:S(2)}) collective-permute-start(bf16[4,512,64]{1,2,0:T(8,128)(2,1)S(1)} %slice.378), channel_id=1, source_target_pairs={{0,32},{4,36},{8,40},{12,44},{16,48},{20,52},{24,56},{28,60},{32,6... | collective-permute-start | bytes 786440 | tf_op jit(solution)/shard_map/ppermute | solution.py:194
  123.6 41.4 %collective-permute-start.37 = (bf16[2,4,64,1408]{3,2,1,0:T(8,128)(2,1)}, bf16[2,4,64,1408]{3,2,1,0:T(8,128)(2,1)S(1)}, u32[]{:S(2)}, u32[]{:S(2)}) collective-permute-start(bf16[2,4,64,1408]{3,2,1,0:T(8,128)(2,1)} %bitcast_dynamic-update-slice_fusion.1), channel_id=1, source_target_pairs={{0,16},{4,20},{8,24},{12,28},{16,0},{20,4},{24,8},{28,12},{32,48},... | collective-permute-start | bytes 4325384 | tf_op jit(solution)/shard_map/ppermute | solution.py:180
  135.5 31.0 %collective-permute-start.19 = (bf16[8,644,128]{2,0,1:T(8,128)(2,1)}, bf16[8,644,128]{2,0,1:T(8,128)(2,1)}, u32[]{:S(2)}, u32[]{:S(2)}) collective-permute-start(bf16[8,644,128]{2,0,1:T(8,128)(2,1)} %copy.286), channel_id=1, source_target_pairs={{0,32},{4,36},{8,40},{12,44},{16,48},{20,52},{24,56},{28,60},{32,6... | collective-permute-start | bytes 3956744 | tf_op jit(solution)/shard_map/ppermute | solution.py:190
  140.1 38.6 %collective-permute-start.18 = (bf16[8,644,128]{2,0,1:T(8,128)(2,1)}, bf16[8,644,128]{2,0,1:T(8,128)(2,1)}, u32[]{:S(2)}, u32[]{:S(2)}) collective-permute-start(bf16[8,644,128]{2,0,1:T(8,128)(2,1)} %copy.286), channel_id=1, source_target_pairs={{0,96},{4,100},{8,104},{12,108},{16,112},{20,116},{24,120},{28,124... | collective-permute-start | bytes 3956744 | tf_op jit(solution)/shard_map/ppermute | solution.py:191
  145.9 48.3 %collective-permute-start.46 = (bf16[8,1408,64]{1,2,0:T(8,128)(2,1)}, bf16[8,1408,64]{1,2,0:T(8,128)(2,1)}, u32[]{:S(2)}, u32[]{:S(2)}) collective-permute-start(bf16[8,1408,64]{1,2,0:T(8,128)(2,1)} %constant_dynamic-update-slice_fusion.11), channel_id=1, source_target_pairs={{0,96},{4,100},{8,104},{12,108},{16,112},{20,116},{24,120},{28,124... | collective-permute-start | bytes 4325384 | tf_op jit(solution)/shard_map/ppermute | solution.py:191
  148.4 49.3 %collective-permute-start.47 = (bf16[8,1408,64]{1,2,0:T(8,128)(2,1)}, bf16[8,1408,64]{1,2,0:T(8,128)(2,1)}, u32[]{:S(2)}, u32[]{:S(2)}) collective-permute-start(bf16[8,1408,64]{1,2,0:T(8,128)(2,1)} %constant_dynamic-update-slice_fusion.11), channel_id=1, source_target_pairs={{0,32},{4,36},{8,40},{12,44},{16,48},{20,52},{24,56},{28,60},{32,6... | collective-permute-start | bytes 4325384 | tf_op jit(solution)/shard_map/ppermute | solution.py:190
  165.0 62.9 %collective-permute-start.6 = (bf16[3,8,64,512]{3,2,1,0:T(8,128)(2,1)}, bf16[3,8,64,512]{3,2,1,0:T(8,128)(2,1)}, u32[]{:S(2)}, u32[]{:S(2)}) collective-permute-start(bf16[3,8,64,512]{3,2,1,0:T(8,128)(2,1)} %constant_dynamic-update-slice_fusion.46), channel_id=1, source_target_pairs={{0,96},{4,100},{8,104},{12,108},{16,112},{20,116},{24,120},{28,124... | collective-permute-start | bytes 4718600 | tf_op jit(solution)/shard_map/ppermute | solution.py:191
  166.5 54.6 %collective-permute-start.7 = (bf16[3,8,64,512]{3,2,1,0:T(8,128)(2,1)}, bf16[3,8,64,512]{3,2,1,0:T(8,128)(2,1)}, u32[]{:S(2)}, u32[]{:S(2)}) collective-permute-start(bf16[3,8,64,512]{3,2,1,0:T(8,128)(2,1)} %constant_dynamic-update-slice_fusion.46), channel_id=1, source_target_pairs={{0,32},{4,36},{8,40},{12,44},{16,48},{20,52},{24,56},{28,60},{32,6... | collective-permute-start | bytes 4718600 | tf_op jit(solution)/shard_map/ppermute | solution.py:190
  178.7 220.2 %collective-permute-start.38 = (bf16[2,8,64,1408]{3,2,1,0:T(8,128)(2,1)}, bf16[2,8,64,1408]{3,2,1,0:T(8,128)(2,1)}, u32[]{:S(2)}, u32[]{:S(2)}) collective-permute-start(bf16[2,8,64,1408]{3,2,1,0:T(8,128)(2,1)} %constant_dynamic-update-slice_fusion.22), channel_id=1, source_target_pairs={{0,12},{4,0},{8,4},{12,8},{16,28},{20,16},{24,20},{28,24},{32,44},... | collective-permute-start | bytes 8650760 | tf_op jit(solution)/shard_map/ppermute | solution.py:191
  194.2 41.1 %collective-permute-start.20 = (bf16[4,644,128]{2,0,1:T(4,128)(2,1)S(1)}, bf16[4,644,128]{2,0,1:T(4,128)(2,1)S(1)}, u32[]{:S(2)}, u32[]{:S(2)}) collective-permute-start(bf16[4,644,128]{2,0,1:T(4,128)(2,1)S(1)} %slice.357), channel_id=1, source_target_pairs={{0,32},{4,36},{8,40},{12,44},{16,48},{20,52},{24,56},{28,60},{32,6... | collective-permute-start | bytes 1978376 | tf_op jit(solution)/shard_map/ppermute | solution.py:194
  197.6 44.4 %collective-permute-start.21 = (bf16[4,644,128]{2,0,1:T(4,128)(2,1)S(1)}, bf16[4,644,128]{2,0,1:T(4,128)(2,1)S(1)}, u32[]{:S(2)}, u32[]{:S(2)}) collective-permute-start(bf16[4,644,128]{2,0,1:T(4,128)(2,1)S(1)} %slice.358), channel_id=1, source_target_pairs={{0,96},{4,100},{8,104},{12,108},{16,112},{20,116},{24,120},{28,124... | collective-permute-start | bytes 1978376 | tf_op jit(solution)/shard_map/ppermute | solution.py:195
  221.1 176.3 %collective-permute-start.39 = (bf16[2,8,64,1408]{3,2,1,0:T(8,128)(2,1)}, bf16[2,8,64,1408]{3,2,1,0:T(8,128)(2,1)}, u32[]{:S(2)}, u32[]{:S(2)}) collective-permute-start(bf16[2,8,64,1408]{3,2,1,0:T(8,128)(2,1)} %constant_dynamic-update-slice_fusion.22), channel_id=1, source_target_pairs={{0,4},{4,8},{8,12},{12,0},{16,20},{20,24},{24,28},{28,16},{32,36},... | collective-permute-start | bytes 8650760 | tf_op jit(solution)/shard_map/ppermute | solution.py:190
  227.9 157.6 %collective-permute-start.48 = (bf16[4,1408,64]{1,2,0:T(8,128)(2,1)}, bf16[4,1408,64]{1,2,0:T(8,128)(2,1)}, u32[]{:S(2)}, u32[]{:S(2)}) collective-permute-start(bf16[4,1408,64]{1,2,0:T(8,128)(2,1)} %slice.393), channel_id=1, source_target_pairs={{0,32},{4,36},{8,40},{12,44},{16,48},{20,52},{24,56},{28,60},{32,6... | collective-permute-start | bytes 2162696 | tf_op jit(solution)/shard_map/ppermute | solution.py:194
  235.2 86.8 %collective-permute-start.8 = (bf16[3,4,64,512]{3,2,1,0:T(8,128)(2,1)}, bf16[3,4,64,512]{3,2,1,0:T(8,128)(2,1)}, u32[]{:S(2)}, u32[]{:S(2)}) collective-permute-start(bf16[3,4,64,512]{3,2,1,0:T(8,128)(2,1)} %slice.354), channel_id=1, source_target_pairs={{0,32},{4,36},{8,40},{12,44},{16,48},{20,52},{24,56},{28,60},{32,6... | collective-permute-start | bytes 2359304 | tf_op jit(solution)/shard_map/ppermute | solution.py:194
  242.0 82.5 %collective-permute-start.9 = (bf16[3,4,64,512]{3,2,1,0:T(8,128)(2,1)}, bf16[3,4,64,512]{3,2,1,0:T(8,128)(2,1)}, u32[]{:S(2)}, u32[]{:S(2)}) collective-permute-start(bf16[3,4,64,512]{3,2,1,0:T(8,128)(2,1)} %slice.355), channel_id=1, source_target_pairs={{0,96},{4,100},{8,104},{12,108},{16,112},{20,116},{24,120},{28,124... | collective-permute-start | bytes 2359304 | tf_op jit(solution)/shard_map/ppermute | solution.py:195
  322.1 65.6 %collective-permute-start.49 = (bf16[4,1408,64]{1,2,0:T(8,128)(2,1)}, bf16[4,1408,64]{1,2,0:T(8,128)(2,1)}, u32[]{:S(2)}, u32[]{:S(2)}) collective-permute-start(bf16[4,1408,64]{1,2,0:T(8,128)(2,1)} %slice.394), channel_id=1, source_target_pairs={{0,96},{4,100},{8,104},{12,108},{16,112},{20,116},{24,120},{28,124... | collective-permute-start | bytes 2162696 | tf_op jit(solution)/shard_map/ppermute | solution.py:195
  362.8 40.3 %collective-permute-start.30 = (f32[2,2,64,2048]{3,2,0,1:T(8,128)}, f32[2,2,64,2048]{3,2,0,1:T(8,128)}, u32[]{:S(2)}, u32[]{:S(2)}) collective-permute-start(f32[2,2,64,2048]{3,2,0,1:T(8,128)} %bitcast.537), channel_id=1, source_target_pairs={{0,1},{1,0},{2,3},{3,2},{4,5},{5,4},{6,7},{7,6},{8,9},{9,8},{10,11... | collective-permute-start | bytes 6291464 | tf_op jit(solution)/shard_map/ppermute | solution.py:125
  398.8 34.5 %collective-permute-start.40 = (bf16[2,4,64,1408]{3,2,1,0:T(8,128)(2,1)S(1)}, bf16[2,4,64,1408]{3,2,1,0:T(8,128)(2,1)S(1)}, u32[]{:S(2)}, u32[]{:S(2)}) collective-permute-start(bf16[2,4,64,1408]{3,2,1,0:T(8,128)(2,1)S(1)} %slice.384), channel_id=1, source_target_pairs={{0,4},{4,8},{8,12},{12,0},{16,20},{20,24},{24,28},{28,16},{32,36},... | collective-permute-start | bytes 4325384 | tf_op jit(solution)/shard_map/ppermute | solution.py:194
  400.4 34.2 %collective-permute-start.41 = (bf16[2,4,64,1408]{3,2,1,0:T(8,128)(2,1)S(1)}, bf16[2,4,64,1408]{3,2,1,0:T(8,128)(2,1)S(1)}, u32[]{:S(2)}, u32[]{:S(2)}) collective-permute-start(bf16[2,4,64,1408]{3,2,1,0:T(8,128)(2,1)S(1)} %slice.385), channel_id=1, source_target_pairs={{0,12},{4,0},{8,4},{12,8},{16,28},{20,16},{24,20},{28,24},{32,44},... | collective-permute-start | bytes 4325384 | tf_op jit(solution)/shard_map/ppermute | solution.py:195
  420.0 15.8 %collective-permute-start.32 = (bf16[2,64,2048]{2,1,0:T(8,128)(2,1)S(1)}, bf16[2,64,2048]{2,1,0:T(8,128)(2,1)S(1)}, u32[]{:S(2)}, u32[]{:S(2)}) collective-permute-start(bf16[2,64,2048]{2,1,0:T(8,128)(2,1)S(1)} %multiply_convert_fusion.3), channel_id=1, source_target_pairs={{0,2},{1,3},{2,0},{3,1},{4,6},{5,7},{6,4},{7,5},{8,10},{9,11},{10,... | collective-permute-start | bytes 1572872 | tf_op jit(solution)/shard_map/ppermute | solution.py:106
  520.1 17.4 %collective-permute-start.54 = (f32[2,2,64,2048]{3,2,0,1:T(8,128)}, f32[2,2,64,2048]{3,2,0,1:T(8,128)}, u32[]{:S(2)}, u32[]{:S(2)}) collective-permute-start(f32[2,2,64,2048]{3,2,0,1:T(8,128)} %bitcast.535), channel_id=1, source_target_pairs={{0,1},{1,0},{2,3},{3,2},{4,5},{5,4},{6,7},{7,6},{8,9},{9,8},{10,11... | collective-permute-start | bytes 6291464 | tf_op jit(solution)/shard_map/ppermute | solution.py:125
  532.2 54.7 %collective-permute-start.62 = (f32[2,2,256,16]{2,3,1,0:T(8,128)}, f32[2,2,256,16]{2,3,1,0:T(8,128)}, u32[]{:S(2)}, u32[]{:S(2)}) collective-permute-start(f32[2,2,256,16]{2,3,1,0:T(8,128)} %pad_maximum_fusion.11), channel_id=1, source_target_pairs={{0,1},{1,0},{2,3},{3,2},{4,5},{5,4},{6,7},{7,6},{8,9},{9,8},{10,11... | collective-permute-start | bytes 196616 | tf_op jit(solution)/shard_map/ppermute | solution.py:134
  539.7 15.1 %collective-permute-start.55 = (bf16[2,64,2048]{2,1,0:T(8,128)(2,1)S(1)}, bf16[2,64,2048]{2,1,0:T(8,128)(2,1)S(1)}, u32[]{:S(2)}, u32[]{:S(2)}) collective-permute-start(bf16[2,64,2048]{2,1,0:T(8,128)(2,1)S(1)} %fusion.32), channel_id=1, source_target_pairs={{0,2},{1,3},{2,0},{3,1},{4,6},{5,7},{6,4},{7,5},{8,10},{9,11},{10,... | collective-permute-start | bytes 1572872 | tf_op jit(solution)/shard_map/ppermute | solution.py:128
  543.2 22.8 %collective-permute-start.51 = (bf16[2,64,2048]{2,1,0:T(8,128)(2,1)S(1)}, bf16[2,64,2048]{2,1,0:T(8,128)(2,1)S(1)}, u32[]{:S(2)}, u32[]{:S(2)}) collective-permute-start(bf16[2,64,2048]{2,1,0:T(8,128)(2,1)S(1)} %fusion.31), channel_id=1, source_target_pairs={{0,2},{1,3},{2,0},{3,1},{4,6},{5,7},{6,4},{7,5},{8,10},{9,11},{10,... | collective-permute-start | bytes 1572872 | tf_op jit(solution)/shard_map/ppermute | solution.py:128
  585.2 27.7 %collective-permute-start.57 = (bf16[2,2,64,2048]{3,2,0,1:T(8,128)(2,1)}, bf16[2,2,64,2048]{3,2,0,1:T(8,128)(2,1)}, u32[]{:S(2)}, u32[]{:S(2)}) collective-permute-start(bf16[2,2,64,2048]{3,2,0,1:T(8,128)(2,1)} %maximum_select_fusion.9), channel_id=1, source_target_pairs={{0,1},{1,0},{2,3},{3,2},{4,5},{5,4},{6,7},{7,6},{8,9},{9,8},{10,11... | collective-permute-start | bytes 3145736 | tf_op jit(solution)/shard_map/ppermute | solution.py:110
  588.3 16.4 %collective-permute-start.63 = (f32[2,2,256,16]{2,3,1,0:T(8,128)}, f32[2,2,256,16]{2,3,1,0:T(8,128)}, u32[]{:S(2)}, u32[]{:S(2)}) collective-permute-start(f32[2,2,256,16]{2,3,1,0:T(8,128)} %fusion.73), channel_id=1, source_target_pairs={{0,2},{1,3},{2,0},{3,1},{4,6},{5,7},{6,4},{7,5},{8,10},{9,11},{10,... | collective-permute-start | bytes 196616 | tf_op jit(solution)/shard_map/ppermute | solution.py:135
  694.4 91.8 %collective-permute-start.58 = (f32[2,2,64,2048]{3,2,0,1:T(8,128)}, f32[2,2,64,2048]{3,2,0,1:T(8,128)}, u32[]{:S(2)}, u32[]{:S(2)}) collective-permute-start(f32[2,2,64,2048]{3,2,0,1:T(8,128)} %bitcast.534), channel_id=1, source_target_pairs={{0,1},{1,0},{2,3},{3,2},{4,5},{5,4},{6,7},{7,6},{8,9},{9,8},{10,11... | collective-permute-start | bytes 6291464 | tf_op jit(solution)/shard_map/ppermute | solution.py:125
  708.6 19.3 %collective-permute-start.61 = (f32[5,2,256,16]{2,3,1,0:T(8,128)S(1)}, f32[5,2,256,16]{2,3,1,0:T(8,128)S(1)}, u32[]{:S(2)}, u32[]{:S(2)}) collective-permute-start(f32[5,2,256,16]{2,3,1,0:T(8,128)S(1)} %add.543), channel_id=1, source_target_pairs={{0,2},{1,3},{2,0},{3,1},{4,6},{5,7},{6,4},{7,5},{8,10},{9,11},{10,... | collective-permute-start | bytes 491528 | tf_op jit(solution)/shard_map/ppermute | solution.py:135
  721.2 57.1 %all-to-all-start.1 = ((bf16[32,2,12544]{2,1,0:T(2,128)(2,1)}), bf16[32,2,12544]{2,1,0:T(2,128)(2,1)}, u32[]{:S(2)}, u32[]{:S(2)}) async-start(bf16[32,2,12544]{2,1,0:T(2,128)(2,1)} %reshape.895), calls=%async_computation.1 | async-start | bytes 3211264 | tf_op jit(solution)/shard_map/all_to_all | solution.py:494
  778.4 30.3 %all-to-all-start = ((f32[32,1,14336]{2,1,0:T(1,128)}), f32[32,1,14336]{2,1,0:T(1,128)}, u32[]{:S(2)}, u32[]{:S(2)}) async-start(f32[32,1,14336]{2,1,0:T(1,128)} %copy.366), calls=%async_computation | async-start | bytes 3670016 | tf_op jit(solution)/shard_map/all_to_all | solution.py:476
  789.6 31.2 %collective-permute-start.59 = (bf16[2,64,2048]{2,1,0:T(8,128)(2,1)}, bf16[2,64,2048]{2,1,0:T(8,128)(2,1)}, u32[]{:S(2)}, u32[]{:S(2)}) collective-permute-start(bf16[2,64,2048]{2,1,0:T(8,128)(2,1)} %fusion.33), channel_id=1, source_target_pairs={{0,2},{1,3},{2,0},{3,1},{4,6},{5,7},{6,4},{7,5},{8,10},{9,11},{10,... | collective-permute-start | bytes 1572872 | tf_op jit(solution)/shard_map/ppermute | solution.py:128
  (154 other events, 2255.7 us)

commit v9 on v8

--- a/solution.py
+++ b/solution.py
@@ -440,36 +440,32 @@
     grad_tokens = grad_hidden + norm_attn_pull(grad_attn_rows)[0]
 
     grad_lows = tok_sum(jnp.stack(attn_grad_lows + ffn_grad_lows))
-    grad_a_in_all = jnp.concatenate(
+    onehot = (
+        jnp.arange(COLS)[None, None, :] == offsets[:, None, None] + jnp.arange(RANK)[None, :, None]
+    ).astype(jnp.float32)
+    wide_lows = hp_dot(grad_lows, onehot, "pstr,src->pstc")
+    dense_a_in = jnp.concatenate(
         [
-            hp_dot(normed_full.astype(jnp.float32), grad_lows[:3], "std,pstr->psdr"),
-            hp_dot(ffn_full.astype(jnp.float32), grad_lows[3:], "std,pstr->psdr"),
+            hp_dot(normed_full.astype(jnp.float32), wide_lows[:3], "std,pstc->pdc"),
+            hp_dot(ffn_full.astype(jnp.float32), wide_lows[3:], "std,pstc->pdc"),
         ]
     )
-    grad_a_in_part = mine_of(grad_a_in_all, 2)
-    grad_b_rows_all = adapter_scale * jnp.stack(
-        [
-            hp_dot(row_lows[0], grad_attn_full.astype(jnp.float32), "str,std->srd"),
-            hp_dot(row_lows[1], grad_ffn_full.astype(jnp.float32), "str,std->srd"),
-        ]
-    )
-    grad_b_rows_part = mine_of(grad_b_rows_all, 3)
-
-    def place(part, axis, total):
-        shape = list(part.shape[1:])
-        shape[axis] = total
-        dense = jnp.zeros(shape, jnp.float32)
-        for s in range(seqs):
-            current = lax.dynamic_slice_in_dim(dense, offsets[s], RANK, axis)
-            dense = lax.dynamic_update_slice_in_dim(dense, current + part[s], offsets[s], axis)
-        return dense
-
-    dense_a_in = place(jnp.moveaxis(grad_a_in_part, 1, 0), 3, COLS)
-    dense_b_rows = place(jnp.moveaxis(grad_b_rows_part, 1, 0), 1, COLS)
+    a_in_mine = lax.dynamic_index_in_dim(
+        dense_a_in.reshape(5, fsdp_count, tok_count, RANK, COLS), me_tok, 2, keepdims=False
+    )
+    wide_row_lows = hp_dot(row_lows, onehot, "qstr,src->qstc")
+    dense_b_rows = adapter_scale * hp_dot(
+        wide_row_lows,
+        jnp.stack([grad_attn_full, grad_ffn_full]).astype(jnp.float32),
+        "qstc,qstd->qcd",
+    )
+    b_rows_mine = lax.dynamic_index_in_dim(
+        dense_b_rows.reshape(2, COLS, fsdp_count, tok_count, RANK), me_tok, 3, keepdims=False
+    )
     wide = jnp.concatenate(
         [
-            jnp.moveaxis(dense_a_in, 1, 0).reshape(fsdp_count, -1),
-            jnp.moveaxis(dense_b_rows, 2, 0).reshape(fsdp_count, -1),
+            jnp.moveaxis(a_in_mine, 1, 0).reshape(fsdp_count, -1),
+            jnp.moveaxis(b_rows_mine, 2, 0).reshape(fsdp_count, -1),
         ],
         axis=1,
     )
@@ -477,10 +473,10 @@
     a_in_block = wide_sum[: 5 * 16 * COLS].reshape(5, 16, COLS)
     b_rows_block = wide_sum[5 * 16 * COLS :].reshape(2, COLS, 16)
 
-    dense_b_qkv = place(jnp.stack(attn_grads_up, 1), 1, COLS)
-    dense_b_gateup = place(jnp.stack(ffn_grads_up, 1), 1, COLS)
-    dense_a_out = place(grad_a_out, 1, COLS)
-    dense_a_down = place(grad_a_down, 1, COLS)
+    dense_b_qkv = hp_dot(onehot, jnp.stack(attn_grads_up, 1), "src,spre->pce")
+    dense_b_gateup = hp_dot(onehot, jnp.stack(ffn_grads_up, 1), "src,spre->pce")
+    dense_a_out = hp_dot(grad_a_out, onehot, "sdr,src->dc")
+    dense_a_down = hp_dot(grad_a_down, onehot, "sdr,src->dc")
     per = COLS // fsdp_count
     narrow = jnp.concatenate(
         [

time: 839 us -> 785 us (0.936)
  local copies, waits for them, and re-layouts: 355 us -> 307 us
  other arithmetic: 82.6 us -> 68.2 us
    dynamic_update_slice x11 -> x0, local copies, waits for them, and re-layouts: 20 us -> none  [place(): lax.dynamic_update_slice_in_dim(dense, current + part[s], offsets[s], axis)]
    reshape x3 -> x1, local copies, waits for them, and re-layouts: 15.1 us -> 2.16 us  [per_device(): jnp.moveaxis(b_rows_mine, 2, 0).reshape(fsdp_count, -1)]
    dynamic_slice x3 -> x0, local copies, waits for them, and re-layouts: 12.8 us -> none  [mine_of(): return lax.dynamic_index_in_dim(split, me_tok, axis + 1, keepdims=False)]
    dot_general x32 -> x37, matrix products: 51.3 us -> 58 us  [hp_dot(): jnp.einsum(spec, left, right, precision=highest, preferred_element_type=j...]
    unnamed x289 -> x286, local copies, waits for them, and re-layouts: 34.8 us -> 33.3 us
  transfers between devices with their start and end apart: 66 -> 66, of which waited for: 23 -> 24; matrix products, arithmetic and copies ran while one was open for 48% -> 46% of each run, Pallas kernels for 0% -> 0%
where the time goes in v9:
time: 785 us; the launch traced here: 772 us
  local copies, waits for them, and re-layouts  307 us (39%)
  waiting for transfers between devices  145 us (18%)
  matrix products  132 us (17%)
  starting transfers between devices  111 us (14%)
  other arithmetic  68.2 us (9%)
  between operations  8.55 us (1%)
    dynamic_update_slice x57, local copies, waits for them, and re-layouts, put(): return lax.dynamic_update_slice(buffer, piece, start)  63.8 us
    dot_general x37, matrix products, hp_dot(): jnp.einsum(spec, left, right, precision=highest, preferred_element_type=j...  58 us
    ppermute x4, waiting for transfers between devices, tok_scatter(): got = lax.ppermute(send.astype(jnp.bfloat16), 'tok', xor_pairs(count, 2))  33.4 us
    unnamed x286, local copies, waits for them, and re-layouts  33.3 us
    ppermute x5, waiting for transfers between devices, pair_stage(): other = lax.ppermute(stacks, 'fsdp', fsdp_pairs('z', 1))  29.2 us
    dot_general x5, matrix products, column_backward(): jnp.einsum('ste,de->std', grad_rows, weight, preferred_element_type=jnp.f...  26 us
    ppermute x10, waiting for transfers between devices, ring_stage(): from_left = lax.ppermute(stacks, 'fsdp', fsdp_pairs(kind, 1))  23.6 us
    ppermute x4, starting transfers between devices, tok_scatter(): chip_sum = mine + lax.ppermute(theirs, 'tok', xor_pairs(count, 1))  20.4 us
  transfers between devices with their start and end apart: 66, of which 24 were waited for; matrix products, arithmetic and copies ran while one was open for 46% of the time, Pallas kernels for 0%

profile of v9, /device:TPU:1, one launch (start us, length us, event | category | flops | bytes accessed | tf_op | source)
XLA Modules:
  0.0 772.3 jit_solution(14383381800204862555)
XLA Ops:
  30.7 4.1 collective-permute-done.10
  52.3 3.9 collective-permute-done.42
  56.2 5.5 collective-permute-done.43
  82.7 4.8 collective-permute-done.25
  102.6 13.3 %collective-permute-start.1 = (bf16[2,2,64,2048]{3,2,1,0:T(8,128)(2,1)S(1)}, bf16[2,2,64,2048]{3,2,1,0:T(8,128)(2,1)S(1)}, u32[]{:S(2)}, u32[]{:S(2)}) collective-permute-start(bf16[2,2,64,2048]{3,2,1,0:T(8,128)(2,1)S(1)} %maximum_select_fusion.4), channel_id=1, source_target_pairs={{0,1},{1,0},{2,3},{3,2},{4,5},{5,4},{6,7},{7,6},{8,9},{9,8},{10,11... | collective-permute-start | bytes 3145736 | tf_op jit(solution)/shard_map/ppermute | solution.py:110
  125.1 8.8 %collective-permute-done.5 = bf16[3,4,64,512]{3,2,1,0:T(8,128)(2,1)S(1)} collective-permute-done((bf16[3,4,64,512]{3,2,1,0:T(8,128)(2,1)S(1)}, bf16[3,4,64,512]{3,2,1,0:T(8,128)(2,1)S(1)}, u32[]{:S(2)}, u32[]{:S(2)}) %collective-permute-start.5) | collective-permute-done | bytes 786464 | tf_op jit(solution)/shard_map/ppermute | solution.py:180
  149.4 15.6 %collective-permute-done.37 = bf16[2,4,64,1408]{3,2,1,0:T(8,128)(2,1)S(1)} collective-permute-done((bf16[2,4,64,1408]{3,2,1,0:T(8,128)(2,1)}, bf16[2,4,64,1408]{3,2,1,0:T(8,128)(2,1)S(1)}, u32[]{:S(2)}, u32[]{:S(2)}) %collective-permute-start.37) | collective-permute-done | bytes 1441824 | tf_op jit(solution)/shard_map/ppermute | solution.py:180
  168.1 5.8 broadcast_in_dim.134
  173.8 3.7 constant_dynamic-update-slice_fusion.21
  187.9 6.1 collective-permute-done.46
  206.4 14.6 %collective-permute-done.7 = bf16[3,8,64,512]{3,2,1,0:T(8,128)(2,1)} collective-permute-done((bf16[3,8,64,512]{3,2,1,0:T(8,128)(2,1)}, bf16[3,8,64,512]{3,2,1,0:T(8,128)(2,1)}, u32[]{:S(2)}, u32[]{:S(2)}) %collective-permute-start.7) | collective-permute-done | bytes 1572896 | tf_op jit(solution)/shard_map/ppermute | solution.py:190
  223.1 4.6 collective-permute-done.6
  236.6 5.3 collective-permute-done.21
  252.0 3.9 constant_dynamic-slice_fusion.14
  279.7 4.7 copy.302
  284.5 6.4 copy.303
  296.0 4.5 constant_dynamic-slice_fusion.7
  326.1 5.7 fusion.121
  337.9 4.1 convolution_add_fusion.5
  362.3 20.1 %collective-permute-start.30 = (f32[2,2,64,2048]{3,2,0,1:T(8,128)}, f32[2,2,64,2048]{3,2,0,1:T(8,128)}, u32[]{:S(2)}, u32[]{:S(2)}) collective-permute-start(f32[2,2,64,2048]{3,2,0,1:T(8,128)} %bitcast.537), channel_id=1, source_target_pairs={{0,1},{1,0},{2,3},{3,2},{4,5},{5,4},{6,7},{7,6},{8,9},{9,8},{10,11... | collective-permute-start | bytes 6291464 | tf_op jit(solution)/shard_map/ppermute | solution.py:125
  389.6 7.6 convolution_add_fusion
  410.0 3.7 constant_dynamic-update-slice_fusion.19
  413.7 5.7 collective-permute-done.31
  421.7 11.5 %collective-permute-done.40 = bf16[2,4,64,1408]{3,2,1,0:T(8,128)(2,1)S(1)} collective-permute-done((bf16[2,4,64,1408]{3,2,1,0:T(8,128)(2,1)S(1)}, bf16[2,4,64,1408]{3,2,1,0:T(8,128)(2,1)S(1)}, u32[]{:S(2)}, u32[]{:S(2)}) %collective-permute-start.40) | collective-permute-done | bytes 1441824 | tf_op jit(solution)/shard_map/ppermute | solution.py:194
  437.7 9.4 %fusion.120 = (bf16[1,32,64,1408]{3,2,1,0:T(8,128)(2,1)}, bf16[1,32,64,1408]{3,2,1,0:T(8,128)(2,1)}) fusion(bf16[2,32,64,1408]{3,2,1,0:T(8,128)(2,1)} %constant_dynamic-update-slice_fusion.17), kind=kLoop, calls=%fused_computation.351 | loop fusion | bytes 23068672 | tf_op jit(solution)/shard_map/slice | solution.py:365
  449.5 5.5 select_n.519
  457.8 7.1 copy.309
  468.8 5.9 convolution_add_fusion.1
  474.8 6.3 fusion.6
  487.6 5.4 copy.331
  495.4 6.5 convolution_bitcast_fusion.5
  504.2 5.4 copy.329
  512.4 4.4 add_add_fusion.1
  540.6 8.6 %collective-permute-done.55 = bf16[2,64,2048]{2,1,0:T(8,128)(2,1)S(1)} collective-permute-done((bf16[2,64,2048]{2,1,0:T(8,128)(2,1)S(1)}, bf16[2,64,2048]{2,1,0:T(8,128)(2,1)S(1)}, u32[]{:S(2)}, u32[]{:S(2)}) %collective-permute-start.55) | collective-permute-done | bytes 524320 | tf_op jit(solution)/shard_map/ppermute | solution.py:128
  549.5 10.9 %collective-permute-done.51 = bf16[2,64,2048]{2,1,0:T(8,128)(2,1)S(1)} collective-permute-done((bf16[2,64,2048]{2,1,0:T(8,128)(2,1)S(1)}, bf16[2,64,2048]{2,1,0:T(8,128)(2,1)S(1)}, u32[]{:S(2)}, u32[]{:S(2)}) %collective-permute-start.51) | collective-permute-done | bytes 524320 | tf_op jit(solution)/shard_map/ppermute | solution.py:128
  566.5 9.2 %collective-permute-done.56 = bf16[2,64,2048]{2,1,0:T(8,128)(2,1)S(1)} collective-permute-done((bf16[2,64,2048]{2,1,0:T(8,128)(2,1)S(1)}, bf16[2,64,2048]{2,1,0:T(8,128)(2,1)S(1)}, u32[]{:S(2)}, u32[]{:S(2)}) %collective-permute-start.56) | collective-permute-done | bytes 524320 | tf_op jit(solution)/shard_map/ppermute | solution.py:106
  601.4 3.8 convolution_add_fusion.3
  626.2 4.6 multiply_add_fusion.5
  635.1 5.0 fusion.131
  644.8 5.2 fusion.132
  659.2 5.7 add_add_fusion
  679.4 4.8 fusion.11
  693.4 4.0 reduce.2
  699.9 6.6 all-to-all-start.1
  714.6 5.9 copy.353
  727.7 6.1 all-to-all-start
  738.2 8.2 %reshape.966 = bf16[32,1,25088]{2,1,0:T(2,128)(2,1)S(1)} reshape(bf16[32,2,12544]{2,1,0:T(2,128)(2,1)} %all-to-all-done.1) | data formatting | bytes 3211264
  760.2 8.2 %collective-permute-done.59 = bf16[2,64,2048]{2,1,0:T(8,128)(2,1)} collective-permute-done((bf16[2,64,2048]{2,1,0:T(8,128)(2,1)}, bf16[2,64,2048]{2,1,0:T(8,128)(2,1)}, u32[]{:S(2)}, u32[]{:S(2)}) %collective-permute-start.59) | collective-permute-done | bytes 524320 | tf_op jit(solution)/shard_map/ppermute | solution.py:128
  (705 shorter events, 437.3 us)
Async XLA Ops:
  0.7 61.1 %collective-permute-start.2 = (bf16[3,1,64,512]{3,2,0,1:T(8,128)(2,1)}, bf16[3,1,64,512]{3,2,0,1:T(8,128)(2,1)}, u32[]{:S(2)}, u32[]{:S(2)}) collective-permute-start(bf16[3,1,64,512]{3,2,0,1:T(8,128)(2,1)} %bitcast.665), channel_id=1, source_target_pairs={{0,12},{4,0},{8,4},{12,8},{16,28},{20,16},{24,20},{28,24},{32,44},... | collective-permute-start | bytes 589832 | tf_op jit(solution)/shard_map/ppermute | solution.py:191
  4.3 59.5 %collective-permute-start.3 = (bf16[3,1,64,512]{3,2,0,1:T(8,128)(2,1)}, bf16[3,1,64,512]{3,2,0,1:T(8,128)(2,1)}, u32[]{:S(2)}, u32[]{:S(2)}) collective-permute-start(bf16[3,1,64,512]{3,2,0,1:T(8,128)(2,1)} %bitcast.666), channel_id=1, source_target_pairs={{0,4},{4,8},{8,12},{12,0},{16,20},{20,24},{24,28},{28,16},{32,36},... | collective-permute-start | bytes 589832 | tf_op jit(solution)/shard_map/ppermute | solution.py:190
  4.3 41.1 %collective-permute-start.22 = (bf16[1,512,64]{1,2,0:T(8,128)(2,1)}, bf16[1,512,64]{1,2,0:T(8,128)(2,1)}, u32[]{:S(2)}, u32[]{:S(2)}) collective-permute-start(bf16[1,512,64]{1,2,0:T(8,128)(2,1)} %bitcast.675), channel_id=1, source_target_pairs={{0,12},{4,0},{8,4},{12,8},{16,28},{20,16},{24,20},{28,24},{32,44},... | collective-permute-start | bytes 196616 | tf_op jit(solution)/shard_map/ppermute | solution.py:191
  7.0 38.6 %collective-permute-start.23 = (bf16[1,512,64]{1,2,0:T(8,128)(2,1)}, bf16[1,512,64]{1,2,0:T(8,128)(2,1)}, u32[]{:S(2)}, u32[]{:S(2)}) collective-permute-start(bf16[1,512,64]{1,2,0:T(8,128)(2,1)} %bitcast.676), channel_id=1, source_target_pairs={{0,4},{4,8},{8,12},{12,0},{16,20},{20,24},{24,28},{28,16},{32,36},... | collective-permute-start | bytes 196616 | tf_op jit(solution)/shard_map/ppermute | solution.py:190
  7.0 23.6 %collective-permute-start.12 = (bf16[2,128,16]{1,2,0:T(8,128)(2,1)}, bf16[2,128,16]{1,2,0:T(8,128)(2,1)S(1)}, u32[]{:S(2)}, u32[]{:S(2)}) collective-permute-start(bf16[2,128,16]{1,2,0:T(8,128)(2,1)} %param.35), channel_id=1, source_target_pairs={{0,2},{1,3},{2,0},{3,1},{4,6},{5,7},{6,4},{7,5},{8,10},{9,11},{10,... | collective-permute-start | bytes 24584 | tf_op jit(solution)/shard_map/ppermute | solution.py:106
  40.4 33.0 %collective-permute-start.34 = (bf16[2,1,64,1408]{3,2,0,1:T(8,128)(2,1)}, bf16[2,1,64,1408]{3,2,0,1:T(8,128)(2,1)S(1)}, u32[]{:S(2)}, u32[]{:S(2)}) collective-permute-start(bf16[2,1,64,1408]{3,2,0,1:T(8,128)(2,1)} %bitcast.662), channel_id=1, source_target_pairs={{0,96},{4,100},{8,104},{12,108},{16,112},{20,116},{24,120},{28,124... | collective-permute-start | bytes 1081352 | tf_op jit(solution)/shard_map/ppermute | solution.py:191
  45.5 28.8 %collective-permute-start.35 = (bf16[2,1,64,1408]{3,2,0,1:T(8,128)(2,1)}, bf16[2,1,64,1408]{3,2,0,1:T(8,128)(2,1)S(1)}, u32[]{:S(2)}, u32[]{:S(2)}) collective-permute-start(bf16[2,1,64,1408]{3,2,0,1:T(8,128)(2,1)} %bitcast.663), channel_id=1, source_target_pairs={{0,32},{4,36},{8,40},{12,44},{16,48},{20,52},{24,56},{28,60},{32,6... | collective-permute-start | bytes 1081352 | tf_op jit(solution)/shard_map/ppermute | solution.py:190
  61.7 31.1 %collective-permute-start = (bf16[2,64,2048]{2,1,0:T(8,128)(2,1)S(1)}, bf16[2,64,2048]{2,1,0:T(8,128)(2,1)S(1)}, u32[]{:S(2)}, u32[]{:S(2)}) collective-permute-start(bf16[2,64,2048]{2,1,0:T(8,128)(2,1)S(1)} %copy-done.70), channel_id=1, source_target_pairs={{0,2},{1,3},{2,0},{3,1},{4,6},{5,7},{6,4},{7,5},{8,10},{9,11},{10,... | collective-permute-start | bytes 1572872 | tf_op jit(solution)/shard_map/ppermute | solution.py:106
  69.5 26.0 %collective-permute-start.52 = (bf16[2,64,2048]{2,1,0:T(8,128)(2,1)S(1)}, bf16[2,64,2048]{2,1,0:T(8,128)(2,1)S(1)}, u32[]{:S(2)}, u32[]{:S(2)}) collective-permute-start(bf16[2,64,2048]{2,1,0:T(8,128)(2,1)S(1)} %copy-done.34), channel_id=1, source_target_pairs={{0,2},{1,3},{2,0},{3,1},{4,6},{5,7},{6,4},{7,5},{8,10},{9,11},{10,... | collective-permute-start | bytes 1572872 | tf_op jit(solution)/shard_map/ppermute | solution.py:106
  72.4 15.1 %collective-permute-start.25 = (bf16[4,512,64]{1,2,0:T(8,128)(2,1)S(1)}, bf16[4,512,64]{1,2,0:T(8,128)(2,1)S(1)}, u32[]{:S(2)}, u32[]{:S(2)}) collective-permute-start(bf16[4,512,64]{1,2,0:T(8,128)(2,1)S(1)} %constant_dynamic-update-slice_fusion.31), channel_id=1, source_target_pairs={{0,16},{4,20},{8,24},{12,28},{16,0},{20,4},{24,8},{28,12},{32,48},... | collective-permute-start | bytes 786440 | tf_op jit(solution)/shard_map/ppermute | solution.py:180
  73.4 17.0 %collective-permute-start.4 = (bf16[3,1,64,512]{3,2,0,1:T(8,128)(2,1)}, bf16[3,1,64,512]{3,2,0,1:T(8,128)(2,1)S(1)}, u32[]{:S(2)}, u32[]{:S(2)}) collective-permute-start(bf16[3,1,64,512]{3,2,0,1:T(8,128)(2,1)} %collective-permute-done.3), channel_id=1, source_target_pairs={{0,4},{4,8},{8,12},{12,0},{16,20},{20,24},{24,28},{28,16},{32,36},... | collective-permute-start | bytes 589832 | tf_op jit(solution)/shard_map/ppermute | solution.py:197
  81.5 42.0 %collective-permute-start.45 = (bf16[4,1408,64]{1,2,0:T(8,128)(2,1)S(1)}, bf16[4,1408,64]{1,2,0:T(8,128)(2,1)S(1)}, u32[]{:S(2)}, u32[]{:S(2)}) collective-permute-start(bf16[4,1408,64]{1,2,0:T(8,128)(2,1)S(1)} %constant_dynamic-update-slice_fusion.13), channel_id=1, source_target_pairs={{0,16},{4,20},{8,24},{12,28},{16,0},{20,4},{24,8},{28,12},{32,48},... | collective-permute-start | bytes 2162696 | tf_op jit(solution)/shard_map/ppermute | solution.py:180
  90.4 27.4 %collective-permute-start.17 = (bf16[4,644,128]{2,0,1:T(4,128)(2,1)S(1)}, bf16[4,644,128]{2,0,1:T(4,128)(2,1)S(1)}, u32[]{:S(2)}, u32[]{:S(2)}) collective-permute-start(bf16[4,644,128]{2,0,1:T(4,128)(2,1)S(1)} %copy.279), channel_id=1, source_target_pairs={{0,16},{4,20},{8,24},{12,28},{16,0},{20,4},{24,8},{28,12},{32,48},... | collective-permute-start | bytes 1978376 | tf_op jit(solution)/shard_map/ppermute | solution.py:180
  95.5 21.3 %collective-permute-start.27 = (bf16[8,512,64]{1,2,0:T(8,128)(2,1)S(1)}, bf16[8,512,64]{1,2,0:T(8,128)(2,1)S(1)}, u32[]{:S(2)}, u32[]{:S(2)}) collective-permute-start(bf16[8,512,64]{1,2,0:T(8,128)(2,1)S(1)} %constant_dynamic-update-slice_fusion.29), channel_id=1, source_target_pairs={{0,32},{4,36},{8,40},{12,44},{16,48},{20,52},{24,56},{28,60},{32,6... | collective-permute-start | bytes 1572872 | tf_op jit(solution)/shard_map/ppermute | solution.py:190
  96.0 37.9 %collective-permute-start.5 = (bf16[3,4,64,512]{3,2,1,0:T(8,128)(2,1)S(1)}, bf16[3,4,64,512]{3,2,1,0:T(8,128)(2,1)S(1)}, u32[]{:S(2)}, u32[]{:S(2)}) collective-permute-start(bf16[3,4,64,512]{3,2,1,0:T(8,128)(2,1)S(1)} %bitcast_dynamic-update-slice_fusion.5), channel_id=1, source_target_pairs={{0,16},{4,20},{8,24},{12,28},{16,0},{20,4},{24,8},{28,12},{32,48},... | collective-permute-start | bytes 2359304 | tf_op jit(solution)/shard_map/ppermute | solution.py:180
  102.6 45.5 %collective-permute-start.1 = (bf16[2,2,64,2048]{3,2,1,0:T(8,128)(2,1)S(1)}, bf16[2,2,64,2048]{3,2,1,0:T(8,128)(2,1)S(1)}, u32[]{:S(2)}, u32[]{:S(2)}) collective-permute-start(bf16[2,2,64,2048]{3,2,1,0:T(8,128)(2,1)S(1)} %maximum_select_fusion.4), channel_id=1, source_target_pairs={{0,1},{1,0},{2,3},{3,2},{4,5},{5,4},{6,7},{7,6},{8,9},{9,8},{10,11... | collective-permute-start | bytes 3145736 | tf_op jit(solution)/shard_map/ppermute | solution.py:110
  116.8 28.9 %collective-permute-start.53 = (bf16[2,2,64,2048]{3,2,0,1:T(8,128)(2,1)S(1)}, bf16[2,2,64,2048]{3,2,0,1:T(8,128)(2,1)S(1)}, u32[]{:S(2)}, u32[]{:S(2)}) collective-permute-start(bf16[2,2,64,2048]{3,2,0,1:T(8,128)(2,1)S(1)} %maximum_select_fusion.7), channel_id=1, source_target_pairs={{0,1},{1,0},{2,3},{3,2},{4,5},{5,4},{6,7},{7,6},{8,9},{9,8},{10,11... | collective-permute-start | bytes 3145736 | tf_op jit(solution)/shard_map/ppermute | solution.py:110
  117.8 17.6 %collective-permute-start.28 = (bf16[4,512,64]{1,2,0:T(8,128)(2,1)S(1)}, bf16[4,512,64]{1,2,0:T(8,128)(2,1)S(1)}, u32[]{:S(2)}, u32[]{:S(2)}) collective-permute-start(bf16[4,512,64]{1,2,0:T(8,128)(2,1)S(1)} %slice.304), channel_id=1, source_target_pairs={{0,32},{4,36},{8,40},{12,44},{16,48},{20,52},{24,56},{28,60},{32,6... | collective-permute-start | bytes 786440 | tf_op jit(solution)/shard_map/ppermute | solution.py:194
  123.5 41.4 %collective-permute-start.37 = (bf16[2,4,64,1408]{3,2,1,0:T(8,128)(2,1)}, bf16[2,4,64,1408]{3,2,1,0:T(8,128)(2,1)S(1)}, u32[]{:S(2)}, u32[]{:S(2)}) collective-permute-start(bf16[2,4,64,1408]{3,2,1,0:T(8,128)(2,1)} %bitcast_dynamic-update-slice_fusion.1), channel_id=1, source_target_pairs={{0,16},{4,20},{8,24},{12,28},{16,0},{20,4},{24,8},{28,12},{32,48},... | collective-permute-start | bytes 4325384 | tf_op jit(solution)/shard_map/ppermute | solution.py:180
  135.4 31.0 %collective-permute-start.19 = (bf16[8,644,128]{2,0,1:T(8,128)(2,1)}, bf16[8,644,128]{2,0,1:T(8,128)(2,1)}, u32[]{:S(2)}, u32[]{:S(2)}) collective-permute-start(bf16[8,644,128]{2,0,1:T(8,128)(2,1)} %copy.281), channel_id=1, source_target_pairs={{0,32},{4,36},{8,40},{12,44},{16,48},{20,52},{24,56},{28,60},{32,6... | collective-permute-start | bytes 3956744 | tf_op jit(solution)/shard_map/ppermute | solution.py:190
  140.0 39.0 %collective-permute-start.18 = (bf16[8,644,128]{2,0,1:T(8,128)(2,1)}, bf16[8,644,128]{2,0,1:T(8,128)(2,1)}, u32[]{:S(2)}, u32[]{:S(2)}) collective-permute-start(bf16[8,644,128]{2,0,1:T(8,128)(2,1)} %copy.281), channel_id=1, source_target_pairs={{0,96},{4,100},{8,104},{12,108},{16,112},{20,116},{24,120},{28,124... | collective-permute-start | bytes 3956744 | tf_op jit(solution)/shard_map/ppermute | solution.py:191
  145.7 48.3 %collective-permute-start.46 = (bf16[8,1408,64]{1,2,0:T(8,128)(2,1)}, bf16[8,1408,64]{1,2,0:T(8,128)(2,1)}, u32[]{:S(2)}, u32[]{:S(2)}) collective-permute-start(bf16[8,1408,64]{1,2,0:T(8,128)(2,1)} %constant_dynamic-update-slice_fusion.11), channel_id=1, source_target_pairs={{0,96},{4,100},{8,104},{12,108},{16,112},{20,116},{24,120},{28,124... | collective-permute-start | bytes 4325384 | tf_op jit(solution)/shard_map/ppermute | solution.py:191
  148.2 49.3 %collective-permute-start.47 = (bf16[8,1408,64]{1,2,0:T(8,128)(2,1)}, bf16[8,1408,64]{1,2,0:T(8,128)(2,1)}, u32[]{:S(2)}, u32[]{:S(2)}) collective-permute-start(bf16[8,1408,64]{1,2,0:T(8,128)(2,1)} %constant_dynamic-update-slice_fusion.11), channel_id=1, source_target_pairs={{0,32},{4,36},{8,40},{12,44},{16,48},{20,52},{24,56},{28,60},{32,6... | collective-permute-start | bytes 4325384 | tf_op jit(solution)/shard_map/ppermute | solution.py:190
  164.9 62.8 %collective-permute-start.6 = (bf16[3,8,64,512]{3,2,1,0:T(8,128)(2,1)}, bf16[3,8,64,512]{3,2,1,0:T(8,128)(2,1)}, u32[]{:S(2)}, u32[]{:S(2)}) collective-permute-start(bf16[3,8,64,512]{3,2,1,0:T(8,128)(2,1)} %constant_dynamic-update-slice_fusion.46), channel_id=1, source_target_pairs={{0,96},{4,100},{8,104},{12,108},{16,112},{20,116},{24,120},{28,124... | collective-permute-start | bytes 4718600 | tf_op jit(solution)/shard_map/ppermute | solution.py:191
  166.5 54.6 %collective-permute-start.7 = (bf16[3,8,64,512]{3,2,1,0:T(8,128)(2,1)}, bf16[3,8,64,512]{3,2,1,0:T(8,128)(2,1)}, u32[]{:S(2)}, u32[]{:S(2)}) collective-permute-start(bf16[3,8,64,512]{3,2,1,0:T(8,128)(2,1)} %constant_dynamic-update-slice_fusion.46), channel_id=1, source_target_pairs={{0,32},{4,36},{8,40},{12,44},{16,48},{20,52},{24,56},{28,60},{32,6... | collective-permute-start | bytes 4718600 | tf_op jit(solution)/shard_map/ppermute | solution.py:190
  179.0 219.8 %collective-permute-start.38 = (bf16[2,8,64,1408]{3,2,1,0:T(8,128)(2,1)}, bf16[2,8,64,1408]{3,2,1,0:T(8,128)(2,1)}, u32[]{:S(2)}, u32[]{:S(2)}) collective-permute-start(bf16[2,8,64,1408]{3,2,1,0:T(8,128)(2,1)} %constant_dynamic-update-slice_fusion.22), channel_id=1, source_target_pairs={{0,12},{4,0},{8,4},{12,8},{16,28},{20,16},{24,20},{28,24},{32,44},... | collective-permute-start | bytes 8650760 | tf_op jit(solution)/shard_map/ppermute | solution.py:191
  194.0 41.2 %collective-permute-start.20 = (bf16[4,644,128]{2,0,1:T(4,128)(2,1)S(1)}, bf16[4,644,128]{2,0,1:T(4,128)(2,1)S(1)}, u32[]{:S(2)}, u32[]{:S(2)}) collective-permute-start(bf16[4,644,128]{2,0,1:T(4,128)(2,1)S(1)} %slice.283), channel_id=1, source_target_pairs={{0,32},{4,36},{8,40},{12,44},{16,48},{20,52},{24,56},{28,60},{32,6... | collective-permute-start | bytes 1978376 | tf_op jit(solution)/shard_map/ppermute | solution.py:194
  197.4 44.4 %collective-permute-start.21 = (bf16[4,644,128]{2,0,1:T(4,128)(2,1)S(1)}, bf16[4,644,128]{2,0,1:T(4,128)(2,1)S(1)}, u32[]{:S(2)}, u32[]{:S(2)}) collective-permute-start(bf16[4,644,128]{2,0,1:T(4,128)(2,1)S(1)} %slice.284), channel_id=1, source_target_pairs={{0,96},{4,100},{8,104},{12,108},{16,112},{20,116},{24,120},{28,124... | collective-permute-start | bytes 1978376 | tf_op jit(solution)/shard_map/ppermute | solution.py:195
  221.0 176.3 %collective-permute-start.39 = (bf16[2,8,64,1408]{3,2,1,0:T(8,128)(2,1)}, bf16[2,8,64,1408]{3,2,1,0:T(8,128)(2,1)}, u32[]{:S(2)}, u32[]{:S(2)}) collective-permute-start(bf16[2,8,64,1408]{3,2,1,0:T(8,128)(2,1)} %constant_dynamic-update-slice_fusion.22), channel_id=1, source_target_pairs={{0,4},{4,8},{8,12},{12,0},{16,20},{20,24},{24,28},{28,16},{32,36},... | collective-permute-start | bytes 8650760 | tf_op jit(solution)/shard_map/ppermute | solution.py:190
  227.7 157.6 %collective-permute-start.48 = (bf16[4,1408,64]{1,2,0:T(8,128)(2,1)}, bf16[4,1408,64]{1,2,0:T(8,128)(2,1)}, u32[]{:S(2)}, u32[]{:S(2)}) collective-permute-start(bf16[4,1408,64]{1,2,0:T(8,128)(2,1)} %slice.319), channel_id=1, source_target_pairs={{0,32},{4,36},{8,40},{12,44},{16,48},{20,52},{24,56},{28,60},{32,6... | collective-permute-start | bytes 2162696 | tf_op jit(solution)/shard_map/ppermute | solution.py:194
  235.2 86.6 %collective-permute-start.8 = (bf16[3,4,64,512]{3,2,1,0:T(8,128)(2,1)}, bf16[3,4,64,512]{3,2,1,0:T(8,128)(2,1)}, u32[]{:S(2)}, u32[]{:S(2)}) collective-permute-start(bf16[3,4,64,512]{3,2,1,0:T(8,128)(2,1)} %slice.280), channel_id=1, source_target_pairs={{0,32},{4,36},{8,40},{12,44},{16,48},{20,52},{24,56},{28,60},{32,6... | collective-permute-start | bytes 2359304 | tf_op jit(solution)/shard_map/ppermute | solution.py:194
  241.8 82.2 %collective-permute-start.9 = (bf16[3,4,64,512]{3,2,1,0:T(8,128)(2,1)}, bf16[3,4,64,512]{3,2,1,0:T(8,128)(2,1)}, u32[]{:S(2)}, u32[]{:S(2)}) collective-permute-start(bf16[3,4,64,512]{3,2,1,0:T(8,128)(2,1)} %slice.281), channel_id=1, source_target_pairs={{0,96},{4,100},{8,104},{12,108},{16,112},{20,116},{24,120},{28,124... | collective-permute-start | bytes 2359304 | tf_op jit(solution)/shard_map/ppermute | solution.py:195
  321.7 65.8 %collective-permute-start.49 = (bf16[4,1408,64]{1,2,0:T(8,128)(2,1)}, bf16[4,1408,64]{1,2,0:T(8,128)(2,1)}, u32[]{:S(2)}, u32[]{:S(2)}) collective-permute-start(bf16[4,1408,64]{1,2,0:T(8,128)(2,1)} %slice.320), channel_id=1, source_target_pairs={{0,96},{4,100},{8,104},{12,108},{16,112},{20,116},{24,120},{28,124... | collective-permute-start | bytes 2162696 | tf_op jit(solution)/shard_map/ppermute | solution.py:195
  362.3 40.7 %collective-permute-start.30 = (f32[2,2,64,2048]{3,2,0,1:T(8,128)}, f32[2,2,64,2048]{3,2,0,1:T(8,128)}, u32[]{:S(2)}, u32[]{:S(2)}) collective-permute-start(f32[2,2,64,2048]{3,2,0,1:T(8,128)} %bitcast.537), channel_id=1, source_target_pairs={{0,1},{1,0},{2,3},{3,2},{4,5},{5,4},{6,7},{7,6},{8,9},{9,8},{10,11... | collective-permute-start | bytes 6291464 | tf_op jit(solution)/shard_map/ppermute | solution.py:125
  398.7 34.5 %collective-permute-start.40 = (bf16[2,4,64,1408]{3,2,1,0:T(8,128)(2,1)S(1)}, bf16[2,4,64,1408]{3,2,1,0:T(8,128)(2,1)S(1)}, u32[]{:S(2)}, u32[]{:S(2)}) collective-permute-start(bf16[2,4,64,1408]{3,2,1,0:T(8,128)(2,1)S(1)} %slice.310), channel_id=1, source_target_pairs={{0,4},{4,8},{8,12},{12,0},{16,20},{20,24},{24,28},{28,16},{32,36},... | collective-permute-start | bytes 4325384 | tf_op jit(solution)/shard_map/ppermute | solution.py:194
  400.3 34.2 %collective-permute-start.41 = (bf16[2,4,64,1408]{3,2,1,0:T(8,128)(2,1)S(1)}, bf16[2,4,64,1408]{3,2,1,0:T(8,128)(2,1)S(1)}, u32[]{:S(2)}, u32[]{:S(2)}) collective-permute-start(bf16[2,4,64,1408]{3,2,1,0:T(8,128)(2,1)S(1)} %slice.311), channel_id=1, source_target_pairs={{0,12},{4,0},{8,4},{12,8},{16,28},{20,16},{24,20},{28,24},{32,44},... | collective-permute-start | bytes 4325384 | tf_op jit(solution)/shard_map/ppermute | solution.py:195
  405.0 14.5 %collective-permute-start.31 = (bf16[2,64,2048]{2,1,0:T(8,128)(2,1)S(1)}, bf16[2,64,2048]{2,1,0:T(8,128)(2,1)S(1)}, u32[]{:S(2)}, u32[]{:S(2)}) collective-permute-start(bf16[2,64,2048]{2,1,0:T(8,128)(2,1)S(1)} %fusion.43), channel_id=1, source_target_pairs={{0,2},{1,3},{2,0},{3,1},{4,6},{5,7},{6,4},{7,5},{8,10},{9,11},{10,... | collective-permute-start | bytes 1572872 | tf_op jit(solution)/shard_map/ppermute | solution.py:128
  419.9 15.8 %collective-permute-start.32 = (bf16[2,64,2048]{2,1,0:T(8,128)(2,1)S(1)}, bf16[2,64,2048]{2,1,0:T(8,128)(2,1)S(1)}, u32[]{:S(2)}, u32[]{:S(2)}) collective-permute-start(bf16[2,64,2048]{2,1,0:T(8,128)(2,1)S(1)} %multiply_convert_fusion.3), channel_id=1, source_target_pairs={{0,2},{1,3},{2,0},{3,1},{4,6},{5,7},{6,4},{7,5},{8,10},{9,11},{10,... | collective-permute-start | bytes 1572872 | tf_op jit(solution)/shard_map/ppermute | solution.py:106
  534.6 14.6 %collective-permute-start.55 = (bf16[2,64,2048]{2,1,0:T(8,128)(2,1)S(1)}, bf16[2,64,2048]{2,1,0:T(8,128)(2,1)S(1)}, u32[]{:S(2)}, u32[]{:S(2)}) collective-permute-start(bf16[2,64,2048]{2,1,0:T(8,128)(2,1)S(1)} %fusion.45), channel_id=1, source_target_pairs={{0,2},{1,3},{2,0},{3,1},{4,6},{5,7},{6,4},{7,5},{8,10},{9,11},{10,... | collective-permute-start | bytes 1572872 | tf_op jit(solution)/shard_map/ppermute | solution.py:128
  538.2 22.2 %collective-permute-start.51 = (bf16[2,64,2048]{2,1,0:T(8,128)(2,1)S(1)}, bf16[2,64,2048]{2,1,0:T(8,128)(2,1)S(1)}, u32[]{:S(2)}, u32[]{:S(2)}) collective-permute-start(bf16[2,64,2048]{2,1,0:T(8,128)(2,1)S(1)} %fusion.44), channel_id=1, source_target_pairs={{0,2},{1,3},{2,0},{3,1},{4,6},{5,7},{6,4},{7,5},{8,10},{9,11},{10,... | collective-permute-start | bytes 1572872 | tf_op jit(solution)/shard_map/ppermute | solution.py:128
  563.5 16.5 %collective-permute-start.62 = (f32[2,2,256,16]{2,3,1,0:T(8,128)S(1)}, f32[2,2,256,16]{2,3,1,0:T(8,128)S(1)}, u32[]{:S(2)}, u32[]{:S(2)}) collective-permute-start(f32[2,2,256,16]{2,3,1,0:T(8,128)S(1)} %pad_maximum_fusion.9), channel_id=1, source_target_pairs={{0,1},{1,0},{2,3},{3,2},{4,5},{5,4},{6,7},{7,6},{8,9},{9,8},{10,11... | collective-permute-start | bytes 196616 | tf_op jit(solution)/shard_map/ppermute | solution.py:134
  576.9 20.3 %collective-permute-start.57 = (bf16[2,2,64,2048]{3,2,0,1:T(8,128)(2,1)}, bf16[2,2,64,2048]{3,2,0,1:T(8,128)(2,1)}, u32[]{:S(2)}, u32[]{:S(2)}) collective-permute-start(bf16[2,2,64,2048]{3,2,0,1:T(8,128)(2,1)} %maximum_select_fusion.9), channel_id=1, source_target_pairs={{0,1},{1,0},{2,3},{3,2},{4,5},{5,4},{6,7},{7,6},{8,9},{9,8},{10,11... | collective-permute-start | bytes 3145736 | tf_op jit(solution)/shard_map/ppermute | solution.py:110
  580.7 14.2 %collective-permute-start.63 = (f32[2,2,256,16]{2,3,1,0:T(8,128)}, f32[2,2,256,16]{2,3,1,0:T(8,128)}, u32[]{:S(2)}, u32[]{:S(2)}) collective-permute-start(f32[2,2,256,16]{2,3,1,0:T(8,128)} %fusion.97), channel_id=1, source_target_pairs={{0,2},{1,3},{2,0},{3,1},{4,6},{5,7},{6,4},{7,5},{8,10},{9,11},{10,... | collective-permute-start | bytes 196616 | tf_op jit(solution)/shard_map/ppermute | solution.py:135
  668.3 65.5 %collective-permute-start.58 = (f32[2,2,64,2048]{3,2,0,1:T(8,128)}, f32[2,2,64,2048]{3,2,0,1:T(8,128)}, u32[]{:S(2)}, u32[]{:S(2)}) collective-permute-start(f32[2,2,64,2048]{3,2,0,1:T(8,128)} %bitcast.534), channel_id=1, source_target_pairs={{0,1},{1,0},{2,3},{3,2},{4,5},{5,4},{6,7},{7,6},{8,9},{9,8},{10,11... | collective-permute-start | bytes 6291464 | tf_op jit(solution)/shard_map/ppermute | solution.py:125
  677.7 28.8 %collective-permute-start.61 = (f32[5,2,256,16]{2,3,1,0:T(8,128)S(1)}, f32[5,2,256,16]{2,3,1,0:T(8,128)S(1)}, u32[]{:S(2)}, u32[]{:S(2)}) collective-permute-start(f32[5,2,256,16]{2,3,1,0:T(8,128)S(1)} %add.528), channel_id=1, source_target_pairs={{0,2},{1,3},{2,0},{3,1},{4,6},{5,7},{6,4},{7,5},{8,10},{9,11},{10,... | collective-permute-start | bytes 491528 | tf_op jit(solution)/shard_map/ppermute | solution.py:135
  699.9 27.8 %all-to-all-start.1 = ((bf16[32,2,12544]{2,1,0:T(2,128)(2,1)}), bf16[32,2,12544]{2,1,0:T(2,128)(2,1)}, u32[]{:S(2)}, u32[]{:S(2)}) async-start(bf16[32,2,12544]{2,1,0:T(2,128)(2,1)} %reshape.965), calls=%async_computation.1 | async-start | bytes 3211264 | tf_op jit(solution)/shard_map/all_to_all | solution.py:490
  727.7 28.5 %all-to-all-start = ((f32[32,1,14336]{2,1,0:T(1,128)}), f32[32,1,14336]{2,1,0:T(1,128)}, u32[]{:S(2)}, u32[]{:S(2)}) async-start(f32[32,1,14336]{2,1,0:T(1,128)} %copy.360), calls=%async_computation | async-start | bytes 3670016 | tf_op jit(solution)/shard_map/all_to_all | solution.py:472
  737.1 31.2 %collective-permute-start.59 = (bf16[2,64,2048]{2,1,0:T(8,128)(2,1)}, bf16[2,64,2048]{2,1,0:T(8,128)(2,1)}, u32[]{:S(2)}, u32[]{:S(2)}) collective-permute-start(bf16[2,64,2048]{2,1,0:T(8,128)(2,1)} %fusion.46), channel_id=1, source_target_pairs={{0,2},{1,3},{2,0},{3,1},{4,6},{5,7},{6,4},{7,5},{8,10},{9,11},{10,... | collective-permute-start | bytes 1572872 | tf_op jit(solution)/shard_map/ppermute | solution.py:128
  (152 other events, 2250.0 us)

commit v10 on v9

--- a/solution.py
+++ b/solution.py
@@ -127,6 +127,39 @@
     send = lax.dynamic_index_in_dim(chip_sum, 1 - half, axis, keepdims=False)
     got = lax.ppermute(send.astype(jnp.bfloat16), "tok", xor_pairs(count, 2))
     return keep + got.astype(keep.dtype)
+
+
+def tok_gather_rel(values, axis):
+    count = lax.axis_size("tok")
+    far = lax.ppermute(values, "tok", xor_pairs(count, 2))
+    pair = jnp.stack([values, far], axis)
+    near = lax.ppermute(pair, "tok", xor_pairs(count, 1))
+    full = jnp.stack([pair, near], axis + 1)
+    return full.reshape(values.shape[:axis] + (count,) + values.shape[axis:])
+
+
+def tok_scatter_rel(blocks, axis):
+    count = lax.axis_size("tok")
+    split = blocks.reshape(blocks.shape[:axis] + (2, 2) + blocks.shape[axis + 1 :])
+    mine = lax.index_in_dim(split, 0, axis + 1, keepdims=False)
+    theirs = lax.index_in_dim(split, 1, axis + 1, keepdims=False)
+    chip_sum = mine + lax.ppermute(theirs, "tok", xor_pairs(count, 1))
+    keep = lax.index_in_dim(chip_sum, 0, axis, keepdims=False)
+    send = lax.index_in_dim(chip_sum, 1, axis, keepdims=False)
+    got = lax.ppermute(send.astype(jnp.bfloat16), "tok", xor_pairs(count, 2))
+    return keep + got.astype(keep.dtype)
+
+
+def tok_sum_rows(values, axis):
+    count = lax.axis_size("tok")
+    shape = values.shape
+    split_shape = shape[:axis] + (2, 2, shape[axis] // 4) + shape[axis + 1 :]
+
+    def swapped(other, block_axis):
+        return jnp.flip(other.reshape(split_shape), axis + block_axis).reshape(shape)
+
+    chip_sum = values + swapped(lax.ppermute(values, "tok", xor_pairs(count, 1)), 1)
+    return chip_sum + swapped(lax.ppermute(chip_sum, "tok", xor_pairs(count, 2)), 0)
 
 
 def tok_sum(values):
@@ -250,7 +283,8 @@
     ff_here = w_gateup.shape[2]
     heads_here = qw_here // VALUE_DIM
     lambda_here = lax.dynamic_slice_in_dim(lambda_head, me_tok * heads_here, heads_here)
-    positions = jnp.arange(length)
+    rows_at = jnp.arange(length)
+    positions = (me_tok ^ (rows_at // local_len)) * local_len + rows_at % local_len
     offsets = adapter_id * RANK
     fsdp_rows = w_qkv.shape[1]
     groups_per_adapter = RANK // b_qkv.shape[1]
@@ -314,11 +348,11 @@
     a_down_sel = jnp.moveaxis(pick_groups(g_adown), 1, 2).reshape(seqs, ff_here, RANK)
 
     def gather_rows(values):
-        full = tok_gather(values, 1)
+        full = tok_gather_rel(values, 1)
         return full.reshape(seqs, length, values.shape[-1])
 
     def scatter_rows(values):
-        return tok_scatter(values.reshape(seqs, tok_count, local_len, values.shape[-1]), 1)
+        return tok_scatter_rel(values.reshape(seqs, tok_count, local_len, values.shape[-1]), 1)
 
     def column_forward(rows_full, weight, down_sel, up_sel, rows_for_weight=None):
         if rows_for_weight is None:
@@ -334,6 +368,7 @@
         return scatter_rows(total), lowrank
 
     inputs_rows = tokens.astype(jnp.float32)
+    segments = jnp.take(segments, positions, axis=1)
     allowed = (segments[:, :, None] == segments[:, None, :]) & (
         positions[:, None] >= positions[None, :]
     )[None]
@@ -368,7 +403,7 @@
     product = product_float.astype(jnp.bfloat16)
     ffn_rows, down_low = row_forward(product, w_down_full, a_down_sel, b_rows_sel[:, 1])
     output = (hidden + ffn_rows).astype(jnp.bfloat16)
-    row_lows = tok_sum(jnp.stack([out_low, down_low]))
+    row_lows = tok_sum_rows(jnp.stack([out_low, down_low]), 2)
 
     tangent = cotangent.astype(jnp.float32)
 
@@ -439,7 +474,7 @@
     )
     grad_tokens = grad_hidden + norm_attn_pull(grad_attn_rows)[0]
 
-    grad_lows = tok_sum(jnp.stack(attn_grad_lows + ffn_grad_lows))
+    grad_lows = tok_sum_rows(jnp.stack(attn_grad_lows + ffn_grad_lows), 2)
     onehot = (
         jnp.arange(COLS)[None, None, :] == offsets[:, None, None] + jnp.arange(RANK)[None, :, None]
     ).astype(jnp.float32)

time: 785 us -> 807 us (1.028)
  local copies, waits for them, and re-layouts: 307 us -> 326 us
    ppermute x12 -> x20, starting transfers between devices: 30.9 us -> 52.3 us  [the longest x4 20.4 us: tok_scatter_rel(): chip_sum = mine + lax.ppermute(theirs, 'tok', xor_pairs(count, 1))]
    ppermute x6 -> x2, starting transfers between devices: 19.5 us -> 3.03 us  [tok_gather(): near = lax.ppermute(pair, 'tok', xor_pairs(count, 1))]
    dynamic_slice x8 -> x0, local copies, waits for them, and re-layouts: 11.7 us -> none  [the longest x4 5.99 us: tok_scatter(): theirs = lax.dynamic_index_in_dim(split, 1 - core, axis + 1, keepdims=False)]
    ppermute x6 -> x2, waiting for transfers between devices: 13.3 us -> 2.73 us  [tok_gather(): far = lax.ppermute(values, 'tok', xor_pairs(count, 2))]
    ppermute x12 -> x20, waiting for transfers between devices: 33.4 us -> 42.5 us  [the longest x4 32.4 us: tok_scatter_rel(): got = lax.ppermute(send.astype(jnp.bfloat16), 'tok', xor_pairs(count, 2))]
    reshape x0 -> x8, local copies, waits for them, and re-layouts: none -> 8.5 us  [the longest x4 4.54 us: swapped(): other.reshape(split_shape)]
    unnamed x286 -> x269, local copies, waits for them, and re-layouts: 33.3 us -> 41.6 us
  transfers between devices with their start and end apart: 66 -> 66, of which waited for: 24 -> 25; matrix products, arithmetic and copies ran while one was open for 46% -> 46% of each run, Pallas kernels for 0% -> 0%
where the time goes in v10:
time: 807 us; the launch traced here: 793 us
  local copies, waits for them, and re-layouts  326 us (40%)
  waiting for transfers between devices  144 us (18%)
  matrix products  137 us (17%)
  starting transfers between devices  111 us (14%)
  other arithmetic  66.7 us (8%)
  between operations  8.56 us (1%)
    dot_general x37, matrix products, hp_dot(): jnp.einsum(spec, left, right, precision=highest, preferred_element_type=j...  64 us
    dynamic_update_slice x57, local copies, waits for them, and re-layouts, put(): return lax.dynamic_update_slice(buffer, piece, start)  63.3 us
    unnamed x269, local copies, waits for them, and re-layouts  41.6 us
    ppermute x4, waiting for transfers between devices, tok_scatter_rel(): got = lax.ppermute(send.astype(jnp.bfloat16), 'tok', xor_pairs(count, 2))  32.4 us
    ppermute x5, waiting for transfers between devices, pair_stage(): other = lax.ppermute(stacks, 'fsdp', fsdp_pairs('z', 1))  29.2 us
    dot_general x5, matrix products, column_backward(): jnp.einsum('ste,de->std', grad_rows, weight, preferred_element_type=jnp.f...  26.1 us
    ppermute x10, waiting for transfers between devices, ring_stage(): from_left = lax.ppermute(stacks, 'fsdp', fsdp_pairs(kind, 1))  23.5 us
    ppermute x10, starting transfers between devices, ring_stage(): from_right = lax.ppermute(stacks, 'fsdp', fsdp_pairs(kind, -1))  20.8 us
  transfers between devices with their start and end apart: 66, of which 25 were waited for; matrix products, arithmetic and copies ran while one was open for 46% of the time, Pallas kernels for 0%

profile of v10, /device:TPU:1, one launch (start us, length us, event | category | flops | bytes accessed | tf_op | source)
XLA Modules:
  0.0 793.4 jit_solution(5759197958089276382)
XLA Ops:
  0.7 3.6 collective-permute-start.2
  54.2 3.9 collective-permute-done.42
  58.1 5.5 collective-permute-done.43
  84.5 4.8 collective-permute-done.25
  104.1 13.6 %collective-permute-start.1 = (bf16[2,2,64,2048]{3,2,0,1:T(8,128)(2,1)S(1)}, bf16[2,2,64,2048]{3,2,0,1:T(8,128)(2,1)S(1)}, u32[]{:S(2)}, u32[]{:S(2)}) collective-permute-start(bf16[2,2,64,2048]{3,2,0,1:T(8,128)(2,1)S(1)} %get-tuple-element.80), channel_id=1, source_target_pairs={{0,1},{1,0},{2,3},{3,2},{4,5},{5,4},{6,7},{7,6},{8,9},{9,8},{10,11... | collective-permute-start | bytes 3145736 | tf_op jit(solution)/shard_map/ppermute | solution.py:136
  126.9 8.9 %collective-permute-done.5 = bf16[3,4,64,512]{3,2,1,0:T(8,128)(2,1)S(1)} collective-permute-done((bf16[3,4,64,512]{3,2,1,0:T(8,128)(2,1)S(1)}, bf16[3,4,64,512]{3,2,1,0:T(8,128)(2,1)S(1)}, u32[]{:S(2)}, u32[]{:S(2)}) %collective-permute-start.5) | collective-permute-done | bytes 786464 | tf_op jit(solution)/shard_map/ppermute | solution.py:213
  151.3 15.5 %collective-permute-done.37 = bf16[2,4,64,1408]{3,2,1,0:T(8,128)(2,1)S(1)} collective-permute-done((bf16[2,4,64,1408]{3,2,1,0:T(8,128)(2,1)}, bf16[2,4,64,1408]{3,2,1,0:T(8,128)(2,1)S(1)}, u32[]{:S(2)}, u32[]{:S(2)}) %collective-permute-start.37) | collective-permute-done | bytes 1441824 | tf_op jit(solution)/shard_map/ppermute | solution.py:213
  170.0 5.6 broadcast_in_dim.146
  189.7 6.4 collective-permute-done.46
  208.4 14.5 %collective-permute-done.7 = bf16[3,8,64,512]{3,2,1,0:T(8,128)(2,1)} collective-permute-done((bf16[3,8,64,512]{3,2,1,0:T(8,128)(2,1)}, bf16[3,8,64,512]{3,2,1,0:T(8,128)(2,1)}, u32[]{:S(2)}, u32[]{:S(2)}) %collective-permute-start.7) | collective-permute-done | bytes 1572896 | tf_op jit(solution)/shard_map/ppermute | solution.py:223
  225.0 4.8 collective-permute-done.6
  238.0 5.9 collective-permute-done.21
  253.3 3.8 constant_dynamic-slice_fusion.6
  277.5 4.8 copy.298
  282.3 6.4 copy.299
  293.8 4.5 constant_dynamic-slice_fusion.1
  323.3 5.7 fusion.141
  335.3 4.1 convolution_add_fusion.5
  360.4 19.9 %collective-permute-start.30 = (f32[2,2,64,2048]{3,2,0,1:T(8,128)}, f32[2,2,64,2048]{3,2,0,1:T(8,128)}, u32[]{:S(2)}, u32[]{:S(2)}) collective-permute-start(f32[2,2,64,2048]{3,2,0,1:T(8,128)} %bitcast.570), channel_id=1, source_target_pairs={{0,1},{1,0},{2,3},{3,2},{4,5},{5,4},{6,7},{7,6},{8,9},{9,8},{10,11... | collective-permute-start | bytes 6291464 | tf_op jit(solution)/shard_map/ppermute | solution.py:146
  390.1 7.6 convolution_add_fusion
  410.4 3.6 constant_dynamic-update-slice_fusion.19
  414.0 5.8 collective-permute-done.31
  422.4 11.2 %collective-permute-done.40 = bf16[2,4,64,1408]{3,2,1,0:T(8,128)(2,1)S(1)} collective-permute-done((bf16[2,4,64,1408]{3,2,1,0:T(8,128)(2,1)S(1)}, bf16[2,4,64,1408]{3,2,1,0:T(8,128)(2,1)S(1)}, u32[]{:S(2)}, u32[]{:S(2)}) %collective-permute-start.40) | collective-permute-done | bytes 1441824 | tf_op jit(solution)/shard_map/ppermute | solution.py:227
  438.0 9.5 %fusion.140 = (bf16[1,32,64,1408]{3,2,1,0:T(8,128)(2,1)}, bf16[1,32,64,1408]{3,2,1,0:T(8,128)(2,1)}) fusion(bf16[2,32,64,1408]{3,2,1,0:T(8,128)(2,1)} %constant_dynamic-update-slice_fusion.17), kind=kLoop, calls=%fused_computation.371 | loop fusion | bytes 23068672 | tf_op jit(solution)/shard_map/slice | solution.py:400
  447.8 5.5 reshape_reshape_reshape.3
  455.9 7.0 copy.305
  466.9 5.9 convolution_add_fusion.1
  472.8 6.3 fusion.6
  480.2 3.6 convolution_bitcast_fusion.4
  486.2 5.4 copy.325
  494.1 6.3 convolution_bitcast_fusion.5
  502.7 5.4 copy.323
  510.9 4.4 add_add_fusion.1
  533.0 9.2 %collective-permute-done.55 = bf16[2,64,2048]{2,1,0:T(8,128)(2,1)} collective-permute-done((bf16[2,64,2048]{2,1,0:T(8,128)(2,1)}, bf16[2,64,2048]{2,1,0:T(8,128)(2,1)}, u32[]{:S(2)}, u32[]{:S(2)}) %collective-permute-start.55) | collective-permute-done | bytes 524320 | tf_op jit(solution)/shard_map/ppermute | solution.py:149
  544.2 9.2 %collective-permute-done.51 = bf16[2,64,2048]{2,1,0:T(8,128)(2,1)} collective-permute-done((bf16[2,64,2048]{2,1,0:T(8,128)(2,1)}, bf16[2,64,2048]{2,1,0:T(8,128)(2,1)}, u32[]{:S(2)}, u32[]{:S(2)}) %collective-permute-start.51) | collective-permute-done | bytes 524320 | tf_op jit(solution)/shard_map/ppermute | solution.py:149
  561.6 9.5 %collective-permute-done.56 = bf16[2,64,2048]{2,1,0:T(8,128)(2,1)S(1)} collective-permute-done((bf16[2,64,2048]{2,1,0:T(8,128)(2,1)S(1)}, bf16[2,64,2048]{2,1,0:T(8,128)(2,1)S(1)}, u32[]{:S(2)}, u32[]{:S(2)}) %collective-permute-start.56) | collective-permute-done | bytes 524320 | tf_op jit(solution)/shard_map/ppermute | solution.py:134
  612.5 3.8 convolution_add_fusion.3
  639.7 4.6 multiply_add_fusion.5
  649.6 5.3 fusion.155
  658.9 5.1 fusion.156
  674.1 5.8 add_add_fusion
  698.7 5.5 fusion.11
  713.1 4.0 reduce.2
  719.6 6.6 all-to-all-start.1
  735.8 5.9 copy.347
  747.5 7.4 all-to-all-start
  759.4 8.2 %reshape.807 = bf16[32,1,25088]{2,1,0:T(2,128)(2,1)S(1)} reshape(bf16[32,2,12544]{2,1,0:T(2,128)(2,1)} %all-to-all-done.1) | data formatting | bytes 3211264
  781.2 8.2 %collective-permute-done.59 = bf16[2,64,2048]{2,1,0:T(8,128)(2,1)} collective-permute-done((bf16[2,64,2048]{2,1,0:T(8,128)(2,1)}, bf16[2,64,2048]{2,1,0:T(8,128)(2,1)}, u32[]{:S(2)}, u32[]{:S(2)}) %collective-permute-start.59) | collective-permute-done | bytes 524320 | tf_op jit(solution)/shard_map/ppermute | solution.py:149
  (697 shorter events, 456.6 us)
Async XLA Ops:
  0.7 63.0 %collective-permute-start.2 = (bf16[3,1,64,512]{3,2,0,1:T(8,128)(2,1)}, bf16[3,1,64,512]{3,2,0,1:T(8,128)(2,1)}, u32[]{:S(2)}, u32[]{:S(2)}) collective-permute-start(bf16[3,1,64,512]{3,2,0,1:T(8,128)(2,1)} %bitcast.695), channel_id=1, source_target_pairs={{0,12},{4,0},{8,4},{12,8},{16,28},{20,16},{24,20},{28,24},{32,44},... | collective-permute-start | bytes 589832 | tf_op jit(solution)/shard_map/ppermute | solution.py:224
  4.3 61.4 %collective-permute-start.3 = (bf16[3,1,64,512]{3,2,0,1:T(8,128)(2,1)}, bf16[3,1,64,512]{3,2,0,1:T(8,128)(2,1)}, u32[]{:S(2)}, u32[]{:S(2)}) collective-permute-start(bf16[3,1,64,512]{3,2,0,1:T(8,128)(2,1)} %bitcast.696), channel_id=1, source_target_pairs={{0,4},{4,8},{8,12},{12,0},{16,20},{20,24},{24,28},{28,16},{32,36},... | collective-permute-start | bytes 589832 | tf_op jit(solution)/shard_map/ppermute | solution.py:223
  4.3 43.0 %collective-permute-start.22 = (bf16[1,512,64]{1,2,0:T(8,128)(2,1)}, bf16[1,512,64]{1,2,0:T(8,128)(2,1)}, u32[]{:S(2)}, u32[]{:S(2)}) collective-permute-start(bf16[1,512,64]{1,2,0:T(8,128)(2,1)} %bitcast.705), channel_id=1, source_target_pairs={{0,12},{4,0},{8,4},{12,8},{16,28},{20,16},{24,20},{28,24},{32,44},... | collective-permute-start | bytes 196616 | tf_op jit(solution)/shard_map/ppermute | solution.py:224
  7.0 40.5 %collective-permute-start.23 = (bf16[1,512,64]{1,2,0:T(8,128)(2,1)}, bf16[1,512,64]{1,2,0:T(8,128)(2,1)}, u32[]{:S(2)}, u32[]{:S(2)}) collective-permute-start(bf16[1,512,64]{1,2,0:T(8,128)(2,1)} %bitcast.706), channel_id=1, source_target_pairs={{0,4},{4,8},{8,12},{12,0},{16,20},{20,24},{24,28},{28,16},{32,36},... | collective-permute-start | bytes 196616 | tf_op jit(solution)/shard_map/ppermute | solution.py:223
  7.0 24.1 %collective-permute-start.12 = (bf16[2,128,16]{1,2,0:T(8,128)(2,1)}, bf16[2,128,16]{1,2,0:T(8,128)(2,1)}, u32[]{:S(2)}, u32[]{:S(2)}) collective-permute-start(bf16[2,128,16]{1,2,0:T(8,128)(2,1)} %param.35), channel_id=1, source_target_pairs={{0,2},{1,3},{2,0},{3,1},{4,6},{5,7},{6,4},{7,5},{8,10},{9,11},{10,... | collective-permute-start | bytes 24584 | tf_op jit(solution)/shard_map/ppermute | solution.py:106
  42.3 33.0 %collective-permute-start.34 = (bf16[2,1,64,1408]{3,2,0,1:T(8,128)(2,1)S(1)}, bf16[2,1,64,1408]{3,2,0,1:T(8,128)(2,1)S(1)}, u32[]{:S(2)}, u32[]{:S(2)}) collective-permute-start(bf16[2,1,64,1408]{3,2,0,1:T(8,128)(2,1)S(1)} %bitcast.692), channel_id=1, source_target_pairs={{0,96},{4,100},{8,104},{12,108},{16,112},{20,116},{24,120},{28,124... | collective-permute-start | bytes 1081352 | tf_op jit(solution)/shard_map/ppermute | solution.py:224
  47.3 28.8 %collective-permute-start.35 = (bf16[2,1,64,1408]{3,2,0,1:T(8,128)(2,1)S(1)}, bf16[2,1,64,1408]{3,2,0,1:T(8,128)(2,1)S(1)}, u32[]{:S(2)}, u32[]{:S(2)}) collective-permute-start(bf16[2,1,64,1408]{3,2,0,1:T(8,128)(2,1)S(1)} %bitcast.693), channel_id=1, source_target_pairs={{0,32},{4,36},{8,40},{12,44},{16,48},{20,52},{24,56},{28,60},{32,6... | collective-permute-start | bytes 1081352 | tf_op jit(solution)/shard_map/ppermute | solution.py:223
  63.6 30.8 %collective-permute-start = (bf16[2,64,2048]{2,1,0:T(8,128)(2,1)S(1)}, bf16[2,64,2048]{2,1,0:T(8,128)(2,1)S(1)}, u32[]{:S(2)}, u32[]{:S(2)}) collective-permute-start(bf16[2,64,2048]{2,1,0:T(8,128)(2,1)S(1)} %fusion.37), channel_id=1, source_target_pairs={{0,2},{1,3},{2,0},{3,1},{4,6},{5,7},{6,4},{7,5},{8,10},{9,11},{10,... | collective-permute-start | bytes 1572872 | tf_op jit(solution)/shard_map/ppermute | solution.py:134
  71.4 25.9 %collective-permute-start.52 = (bf16[2,64,2048]{2,1,0:T(8,128)(2,1)S(1)}, bf16[2,64,2048]{2,1,0:T(8,128)(2,1)S(1)}, u32[]{:S(2)}, u32[]{:S(2)}) collective-permute-start(bf16[2,64,2048]{2,1,0:T(8,128)(2,1)S(1)} %copy-done.43), channel_id=1, source_target_pairs={{0,2},{1,3},{2,0},{3,1},{4,6},{5,7},{6,4},{7,5},{8,10},{9,11},{10,... | collective-permute-start | bytes 1572872 | tf_op jit(solution)/shard_map/ppermute | solution.py:134
  74.3 15.1 %collective-permute-start.25 = (bf16[4,512,64]{1,2,0:T(8,128)(2,1)S(1)}, bf16[4,512,64]{1,2,0:T(8,128)(2,1)S(1)}, u32[]{:S(2)}, u32[]{:S(2)}) collective-permute-start(bf16[4,512,64]{1,2,0:T(8,128)(2,1)S(1)} %constant_dynamic-update-slice_fusion.31), channel_id=1, source_target_pairs={{0,16},{4,20},{8,24},{12,28},{16,0},{20,4},{24,8},{28,12},{32,48},... | collective-permute-start | bytes 786440 | tf_op jit(solution)/shard_map/ppermute | solution.py:213
  75.3 16.6 %collective-permute-start.4 = (bf16[3,1,64,512]{3,2,0,1:T(8,128)(2,1)}, bf16[3,1,64,512]{3,2,0,1:T(8,128)(2,1)S(1)}, u32[]{:S(2)}, u32[]{:S(2)}) collective-permute-start(bf16[3,1,64,512]{3,2,0,1:T(8,128)(2,1)} %collective-permute-done.3), channel_id=1, source_target_pairs={{0,4},{4,8},{8,12},{12,0},{16,20},{20,24},{24,28},{28,16},{32,36},... | collective-permute-start | bytes 589832 | tf_op jit(solution)/shard_map/ppermute | solution.py:230
  83.3 41.9 %collective-permute-start.45 = (bf16[4,1408,64]{1,2,0:T(8,128)(2,1)S(1)}, bf16[4,1408,64]{1,2,0:T(8,128)(2,1)S(1)}, u32[]{:S(2)}, u32[]{:S(2)}) collective-permute-start(bf16[4,1408,64]{1,2,0:T(8,128)(2,1)S(1)} %constant_dynamic-update-slice_fusion.13), channel_id=1, source_target_pairs={{0,16},{4,20},{8,24},{12,28},{16,0},{20,4},{24,8},{28,12},{32,48},... | collective-permute-start | bytes 2162696 | tf_op jit(solution)/shard_map/ppermute | solution.py:213
  91.9 27.8 %collective-permute-start.17 = (bf16[4,644,128]{2,0,1:T(4,128)(2,1)S(1)}, bf16[4,644,128]{2,0,1:T(4,128)(2,1)S(1)}, u32[]{:S(2)}, u32[]{:S(2)}) collective-permute-start(bf16[4,644,128]{2,0,1:T(4,128)(2,1)S(1)} %copy.272), channel_id=1, source_target_pairs={{0,16},{4,20},{8,24},{12,28},{16,0},{20,4},{24,8},{28,12},{32,48},... | collective-permute-start | bytes 1978376 | tf_op jit(solution)/shard_map/ppermute | solution.py:213
  97.3 21.4 %collective-permute-start.27 = (bf16[8,512,64]{1,2,0:T(8,128)(2,1)S(1)}, bf16[8,512,64]{1,2,0:T(8,128)(2,1)S(1)}, u32[]{:S(2)}, u32[]{:S(2)}) collective-permute-start(bf16[8,512,64]{1,2,0:T(8,128)(2,1)S(1)} %constant_dynamic-update-slice_fusion.29), channel_id=1, source_target_pairs={{0,32},{4,36},{8,40},{12,44},{16,48},{20,52},{24,56},{28,60},{32,6... | collective-permute-start | bytes 1572872 | tf_op jit(solution)/shard_map/ppermute | solution.py:223
  97.5 38.3 %collective-permute-start.5 = (bf16[3,4,64,512]{3,2,1,0:T(8,128)(2,1)S(1)}, bf16[3,4,64,512]{3,2,1,0:T(8,128)(2,1)S(1)}, u32[]{:S(2)}, u32[]{:S(2)}) collective-permute-start(bf16[3,4,64,512]{3,2,1,0:T(8,128)(2,1)S(1)} %bitcast_dynamic-update-slice_fusion.5), channel_id=1, source_target_pairs={{0,16},{4,20},{8,24},{12,28},{16,0},{20,4},{24,8},{28,12},{32,48},... | collective-permute-start | bytes 2359304 | tf_op jit(solution)/shard_map/ppermute | solution.py:213
  104.1 43.5 %collective-permute-start.1 = (bf16[2,2,64,2048]{3,2,0,1:T(8,128)(2,1)S(1)}, bf16[2,2,64,2048]{3,2,0,1:T(8,128)(2,1)S(1)}, u32[]{:S(2)}, u32[]{:S(2)}) collective-permute-start(bf16[2,2,64,2048]{3,2,0,1:T(8,128)(2,1)S(1)} %get-tuple-element.80), channel_id=1, source_target_pairs={{0,1},{1,0},{2,3},{3,2},{4,5},{5,4},{6,7},{7,6},{8,9},{9,8},{10,11... | collective-permute-start | bytes 3145736 | tf_op jit(solution)/shard_map/ppermute | solution.py:136
  118.7 30.0 %collective-permute-start.53 = (bf16[2,2,64,2048]{3,2,0,1:T(8,128)(2,1)S(1)}, bf16[2,2,64,2048]{3,2,0,1:T(8,128)(2,1)S(1)}, u32[]{:S(2)}, u32[]{:S(2)}) collective-permute-start(bf16[2,2,64,2048]{3,2,0,1:T(8,128)(2,1)S(1)} %get-tuple-element.74), channel_id=1, source_target_pairs={{0,1},{1,0},{2,3},{3,2},{4,5},{5,4},{6,7},{7,6},{8,9},{9,8},{10,11... | collective-permute-start | bytes 3145736 | tf_op jit(solution)/shard_map/ppermute | solution.py:136
  119.6 17.7 %collective-permute-start.28 = (bf16[4,512,64]{1,2,0:T(8,128)(2,1)S(1)}, bf16[4,512,64]{1,2,0:T(8,128)(2,1)S(1)}, u32[]{:S(2)}, u32[]{:S(2)}) collective-permute-start(bf16[4,512,64]{1,2,0:T(8,128)(2,1)S(1)} %slice.374), channel_id=1, source_target_pairs={{0,32},{4,36},{8,40},{12,44},{16,48},{20,52},{24,56},{28,60},{32,6... | collective-permute-start | bytes 786440 | tf_op jit(solution)/shard_map/ppermute | solution.py:227
  125.3 41.5 %collective-permute-start.37 = (bf16[2,4,64,1408]{3,2,1,0:T(8,128)(2,1)}, bf16[2,4,64,1408]{3,2,1,0:T(8,128)(2,1)S(1)}, u32[]{:S(2)}, u32[]{:S(2)}) collective-permute-start(bf16[2,4,64,1408]{3,2,1,0:T(8,128)(2,1)} %bitcast_dynamic-update-slice_fusion.1), channel_id=1, source_target_pairs={{0,16},{4,20},{8,24},{12,28},{16,0},{20,4},{24,8},{28,12},{32,48},... | collective-permute-start | bytes 4325384 | tf_op jit(solution)/shard_map/ppermute | solution.py:213
  137.3 31.0 %collective-permute-start.19 = (bf16[8,644,128]{2,0,1:T(8,128)(2,1)}, bf16[8,644,128]{2,0,1:T(8,128)(2,1)}, u32[]{:S(2)}, u32[]{:S(2)}) collective-permute-start(bf16[8,644,128]{2,0,1:T(8,128)(2,1)} %copy.274), channel_id=1, source_target_pairs={{0,32},{4,36},{8,40},{12,44},{16,48},{20,52},{24,56},{28,60},{32,6... | collective-permute-start | bytes 3956744 | tf_op jit(solution)/shard_map/ppermute | solution.py:223
  141.9 38.8 %collective-permute-start.18 = (bf16[8,644,128]{2,0,1:T(8,128)(2,1)}, bf16[8,644,128]{2,0,1:T(8,128)(2,1)}, u32[]{:S(2)}, u32[]{:S(2)}) collective-permute-start(bf16[8,644,128]{2,0,1:T(8,128)(2,1)} %copy.274), channel_id=1, source_target_pairs={{0,96},{4,100},{8,104},{12,108},{16,112},{20,116},{24,120},{28,124... | collective-permute-start | bytes 3956744 | tf_op jit(solution)/shard_map/ppermute | solution.py:224
  147.7 48.4 %collective-permute-start.46 = (bf16[8,1408,64]{1,2,0:T(8,128)(2,1)}, bf16[8,1408,64]{1,2,0:T(8,128)(2,1)}, u32[]{:S(2)}, u32[]{:S(2)}) collective-permute-start(bf16[8,1408,64]{1,2,0:T(8,128)(2,1)} %constant_dynamic-update-slice_fusion.11), channel_id=1, source_target_pairs={{0,96},{4,100},{8,104},{12,108},{16,112},{20,116},{24,120},{28,124... | collective-permute-start | bytes 4325384 | tf_op jit(solution)/shard_map/ppermute | solution.py:224
  148.7 50.1 %collective-permute-start.47 = (bf16[8,1408,64]{1,2,0:T(8,128)(2,1)}, bf16[8,1408,64]{1,2,0:T(8,128)(2,1)}, u32[]{:S(2)}, u32[]{:S(2)}) collective-permute-start(bf16[8,1408,64]{1,2,0:T(8,128)(2,1)} %constant_dynamic-update-slice_fusion.11), channel_id=1, source_target_pairs={{0,32},{4,36},{8,40},{12,44},{16,48},{20,52},{24,56},{28,60},{32,6... | collective-permute-start | bytes 4325384 | tf_op jit(solution)/shard_map/ppermute | solution.py:223
  166.8 63.0 %collective-permute-start.6 = (bf16[3,8,64,512]{3,2,1,0:T(8,128)(2,1)}, bf16[3,8,64,512]{3,2,1,0:T(8,128)(2,1)}, u32[]{:S(2)}, u32[]{:S(2)}) collective-permute-start(bf16[3,8,64,512]{3,2,1,0:T(8,128)(2,1)} %constant_dynamic-update-slice_fusion.46), channel_id=1, source_target_pairs={{0,96},{4,100},{8,104},{12,108},{16,112},{20,116},{24,120},{28,124... | collective-permute-start | bytes 4718600 | tf_op jit(solution)/shard_map/ppermute | solution.py:224
  168.3 54.6 %collective-permute-start.7 = (bf16[3,8,64,512]{3,2,1,0:T(8,128)(2,1)}, bf16[3,8,64,512]{3,2,1,0:T(8,128)(2,1)}, u32[]{:S(2)}, u32[]{:S(2)}) collective-permute-start(bf16[3,8,64,512]{3,2,1,0:T(8,128)(2,1)} %constant_dynamic-update-slice_fusion.46), channel_id=1, source_target_pairs={{0,32},{4,36},{8,40},{12,44},{16,48},{20,52},{24,56},{28,60},{32,6... | collective-permute-start | bytes 4718600 | tf_op jit(solution)/shard_map/ppermute | solution.py:223
  180.7 218.5 %collective-permute-start.38 = (bf16[2,8,64,1408]{3,2,1,0:T(8,128)(2,1)}, bf16[2,8,64,1408]{3,2,1,0:T(8,128)(2,1)}, u32[]{:S(2)}, u32[]{:S(2)}) collective-permute-start(bf16[2,8,64,1408]{3,2,1,0:T(8,128)(2,1)} %constant_dynamic-update-slice_fusion.22), channel_id=1, source_target_pairs={{0,12},{4,0},{8,4},{12,8},{16,28},{20,16},{24,20},{28,24},{32,44},... | collective-permute-start | bytes 8650760 | tf_op jit(solution)/shard_map/ppermute | solution.py:224
  196.1 41.0 %collective-permute-start.20 = (bf16[4,644,128]{2,0,1:T(4,128)(2,1)S(1)}, bf16[4,644,128]{2,0,1:T(4,128)(2,1)S(1)}, u32[]{:S(2)}, u32[]{:S(2)}) collective-permute-start(bf16[4,644,128]{2,0,1:T(4,128)(2,1)S(1)} %slice.353), channel_id=1, source_target_pairs={{0,32},{4,36},{8,40},{12,44},{16,48},{20,52},{24,56},{28,60},{32,6... | collective-permute-start | bytes 1978376 | tf_op jit(solution)/shard_map/ppermute | solution.py:227
  198.8 45.1 %collective-permute-start.21 = (bf16[4,644,128]{2,0,1:T(4,128)(2,1)S(1)}, bf16[4,644,128]{2,0,1:T(4,128)(2,1)S(1)}, u32[]{:S(2)}, u32[]{:S(2)}) collective-permute-start(bf16[4,644,128]{2,0,1:T(4,128)(2,1)S(1)} %slice.354), channel_id=1, source_target_pairs={{0,96},{4,100},{8,104},{12,108},{16,112},{20,116},{24,120},{28,124... | collective-permute-start | bytes 1978376 | tf_op jit(solution)/shard_map/ppermute | solution.py:228
  222.9 174.8 %collective-permute-start.39 = (bf16[2,8,64,1408]{3,2,1,0:T(8,128)(2,1)}, bf16[2,8,64,1408]{3,2,1,0:T(8,128)(2,1)}, u32[]{:S(2)}, u32[]{:S(2)}) collective-permute-start(bf16[2,8,64,1408]{3,2,1,0:T(8,128)(2,1)} %constant_dynamic-update-slice_fusion.22), channel_id=1, source_target_pairs={{0,4},{4,8},{8,12},{12,0},{16,20},{20,24},{24,28},{28,16},{32,36},... | collective-permute-start | bytes 8650760 | tf_op jit(solution)/shard_map/ppermute | solution.py:223
  229.8 156.0 %collective-permute-start.48 = (bf16[4,1408,64]{1,2,0:T(8,128)(2,1)}, bf16[4,1408,64]{1,2,0:T(8,128)(2,1)}, u32[]{:S(2)}, u32[]{:S(2)}) collective-permute-start(bf16[4,1408,64]{1,2,0:T(8,128)(2,1)} %slice.393), channel_id=1, source_target_pairs={{0,32},{4,36},{8,40},{12,44},{16,48},{20,52},{24,56},{28,60},{32,6... | collective-permute-start | bytes 2162696 | tf_op jit(solution)/shard_map/ppermute | solution.py:227
  237.0 82.0 %collective-permute-start.8 = (bf16[3,4,64,512]{3,2,1,0:T(8,128)(2,1)}, bf16[3,4,64,512]{3,2,1,0:T(8,128)(2,1)}, u32[]{:S(2)}, u32[]{:S(2)}) collective-permute-start(bf16[3,4,64,512]{3,2,1,0:T(8,128)(2,1)} %slice.350), channel_id=1, source_target_pairs={{0,32},{4,36},{8,40},{12,44},{16,48},{20,52},{24,56},{28,60},{32,6... | collective-permute-start | bytes 2359304 | tf_op jit(solution)/shard_map/ppermute | solution.py:227
  243.9 77.4 %collective-permute-start.9 = (bf16[3,4,64,512]{3,2,1,0:T(8,128)(2,1)}, bf16[3,4,64,512]{3,2,1,0:T(8,128)(2,1)}, u32[]{:S(2)}, u32[]{:S(2)}) collective-permute-start(bf16[3,4,64,512]{3,2,1,0:T(8,128)(2,1)} %slice.351), channel_id=1, source_target_pairs={{0,96},{4,100},{8,104},{12,108},{16,112},{20,116},{24,120},{28,124... | collective-permute-start | bytes 2359304 | tf_op jit(solution)/shard_map/ppermute | solution.py:228
  319.0 69.0 %collective-permute-start.49 = (bf16[4,1408,64]{1,2,0:T(8,128)(2,1)}, bf16[4,1408,64]{1,2,0:T(8,128)(2,1)}, u32[]{:S(2)}, u32[]{:S(2)}) collective-permute-start(bf16[4,1408,64]{1,2,0:T(8,128)(2,1)} %slice.394), channel_id=1, source_target_pairs={{0,96},{4,100},{8,104},{12,108},{16,112},{20,116},{24,120},{28,124... | collective-permute-start | bytes 2162696 | tf_op jit(solution)/shard_map/ppermute | solution.py:228
  360.4 43.0 %collective-permute-start.30 = (f32[2,2,64,2048]{3,2,0,1:T(8,128)}, f32[2,2,64,2048]{3,2,0,1:T(8,128)}, u32[]{:S(2)}, u32[]{:S(2)}) collective-permute-start(f32[2,2,64,2048]{3,2,0,1:T(8,128)} %bitcast.570), channel_id=1, source_target_pairs={{0,1},{1,0},{2,3},{3,2},{4,5},{5,4},{6,7},{7,6},{8,9},{9,8},{10,11... | collective-permute-start | bytes 6291464 | tf_op jit(solution)/shard_map/ppermute | solution.py:146
  399.2 34.5 %collective-permute-start.40 = (bf16[2,4,64,1408]{3,2,1,0:T(8,128)(2,1)S(1)}, bf16[2,4,64,1408]{3,2,1,0:T(8,128)(2,1)S(1)}, u32[]{:S(2)}, u32[]{:S(2)}) collective-permute-start(bf16[2,4,64,1408]{3,2,1,0:T(8,128)(2,1)S(1)} %slice.384), channel_id=1, source_target_pairs={{0,4},{4,8},{8,12},{12,0},{16,20},{20,24},{24,28},{28,16},{32,36},... | collective-permute-start | bytes 4325384 | tf_op jit(solution)/shard_map/ppermute | solution.py:227
  400.7 34.1 %collective-permute-start.41 = (bf16[2,4,64,1408]{3,2,1,0:T(8,128)(2,1)S(1)}, bf16[2,4,64,1408]{3,2,1,0:T(8,128)(2,1)S(1)}, u32[]{:S(2)}, u32[]{:S(2)}) collective-permute-start(bf16[2,4,64,1408]{3,2,1,0:T(8,128)(2,1)S(1)} %slice.385), channel_id=1, source_target_pairs={{0,12},{4,0},{8,4},{12,8},{16,28},{20,16},{24,20},{28,24},{32,44},... | collective-permute-start | bytes 4325384 | tf_op jit(solution)/shard_map/ppermute | solution.py:228
  405.4 14.5 %collective-permute-start.31 = (bf16[2,64,2048]{2,1,0:T(8,128)(2,1)S(1)}, bf16[2,64,2048]{2,1,0:T(8,128)(2,1)S(1)}, u32[]{:S(2)}, u32[]{:S(2)}) collective-permute-start(bf16[2,64,2048]{2,1,0:T(8,128)(2,1)S(1)} %fusion.50), channel_id=1, source_target_pairs={{0,2},{1,3},{2,0},{3,1},{4,6},{5,7},{6,4},{7,5},{8,10},{9,11},{10,... | collective-permute-start | bytes 1572872 | tf_op jit(solution)/shard_map/ppermute | solution.py:149
  420.9 15.2 %collective-permute-start.32 = (bf16[2,64,2048]{2,1,0:T(8,128)(2,1)S(1)}, bf16[2,64,2048]{2,1,0:T(8,128)(2,1)S(1)}, u32[]{:S(2)}, u32[]{:S(2)}) collective-permute-start(bf16[2,64,2048]{2,1,0:T(8,128)(2,1)S(1)} %multiply_convert_fusion.3), channel_id=1, source_target_pairs={{0,2},{1,3},{2,0},{3,1},{4,6},{5,7},{6,4},{7,5},{8,10},{9,11},{10,... | collective-permute-start | bytes 1572872 | tf_op jit(solution)/shard_map/ppermute | solution.py:134
  526.9 15.3 %collective-permute-start.55 = (bf16[2,64,2048]{2,1,0:T(8,128)(2,1)}, bf16[2,64,2048]{2,1,0:T(8,128)(2,1)}, u32[]{:S(2)}, u32[]{:S(2)}) collective-permute-start(bf16[2,64,2048]{2,1,0:T(8,128)(2,1)} %fusion.52), channel_id=1, source_target_pairs={{0,2},{1,3},{2,0},{3,1},{4,6},{5,7},{6,4},{7,5},{8,10},{9,11},{10,... | collective-permute-start | bytes 1572872 | tf_op jit(solution)/shard_map/ppermute | solution.py:149
  530.6 22.8 %collective-permute-start.51 = (bf16[2,64,2048]{2,1,0:T(8,128)(2,1)}, bf16[2,64,2048]{2,1,0:T(8,128)(2,1)}, u32[]{:S(2)}, u32[]{:S(2)}) collective-permute-start(bf16[2,64,2048]{2,1,0:T(8,128)(2,1)} %fusion.51), channel_id=1, source_target_pairs={{0,2},{1,3},{2,0},{3,1},{4,6},{5,7},{6,4},{7,5},{8,10},{9,11},{10,... | collective-permute-start | bytes 1572872 | tf_op jit(solution)/shard_map/ppermute | solution.py:149
  558.4 18.4 %collective-permute-start.62 = (f32[2,2,256,16]{2,3,1,0:T(8,128)S(1)}, f32[2,2,256,16]{2,3,1,0:T(8,128)}, u32[]{:S(2)}, u32[]{:S(2)}) collective-permute-start(f32[2,2,256,16]{2,3,1,0:T(8,128)S(1)} %pad_maximum_fusion.15), channel_id=1, source_target_pairs={{0,1},{1,0},{2,3},{3,2},{4,5},{5,4},{6,7},{7,6},{8,9},{9,8},{10,11... | collective-permute-start | bytes 196616 | tf_op jit(solution)/shard_map/ppermute | solution.py:161
  572.6 36.0 %collective-permute-start.57 = (bf16[2,2,64,2048]{3,2,0,1:T(8,128)(2,1)}, bf16[2,2,64,2048]{3,2,0,1:T(8,128)(2,1)}, u32[]{:S(2)}, u32[]{:S(2)}) collective-permute-start(bf16[2,2,64,2048]{3,2,0,1:T(8,128)(2,1)} %get-tuple-element.71), channel_id=1, source_target_pairs={{0,1},{1,0},{2,3},{3,2},{4,5},{5,4},{6,7},{7,6},{8,9},{9,8},{10,11... | collective-permute-start | bytes 3145736 | tf_op jit(solution)/shard_map/ppermute | solution.py:136
  583.3 18.2 %collective-permute-start.63 = (f32[2,2,256,16]{2,3,1,0:T(8,128)}, f32[2,2,256,16]{2,3,1,0:T(8,128)}, u32[]{:S(2)}, u32[]{:S(2)}) collective-permute-start(f32[2,2,256,16]{2,3,1,0:T(8,128)} %fusion.113), channel_id=1, source_target_pairs={{0,2},{1,3},{2,0},{3,1},{4,6},{5,7},{6,4},{7,5},{8,10},{9,11},{10,... | collective-permute-start | bytes 196616 | tf_op jit(solution)/shard_map/ppermute | solution.py:162
  683.3 71.5 %collective-permute-start.58 = (f32[2,2,64,2048]{3,2,0,1:T(8,128)}, f32[2,2,64,2048]{3,2,0,1:T(8,128)}, u32[]{:S(2)}, u32[]{:S(2)}) collective-permute-start(f32[2,2,64,2048]{3,2,0,1:T(8,128)} %bitcast.567), channel_id=1, source_target_pairs={{0,1},{1,0},{2,3},{3,2},{4,5},{5,4},{6,7},{7,6},{8,9},{9,8},{10,11... | collective-permute-start | bytes 6291464 | tf_op jit(solution)/shard_map/ppermute | solution.py:146
  696.8 29.4 %collective-permute-start.61 = (f32[5,2,256,16]{2,3,1,0:T(8,128)S(1)}, f32[5,2,256,16]{2,3,1,0:T(8,128)S(1)}, u32[]{:S(2)}, u32[]{:S(2)}) collective-permute-start(f32[5,2,256,16]{2,3,1,0:T(8,128)S(1)} %add.596), channel_id=1, source_target_pairs={{0,2},{1,3},{2,0},{3,1},{4,6},{5,7},{6,4},{7,5},{8,10},{9,11},{10,... | collective-permute-start | bytes 491528 | tf_op jit(solution)/shard_map/ppermute | solution.py:162
  719.6 27.9 %all-to-all-start.1 = ((bf16[32,2,12544]{2,1,0:T(2,128)(2,1)}), bf16[32,2,12544]{2,1,0:T(2,128)(2,1)}, u32[]{:S(2)}, u32[]{:S(2)}) async-start(bf16[32,2,12544]{2,1,0:T(2,128)(2,1)} %reshape.806), calls=%async_computation.1 | async-start | bytes 3211264 | tf_op jit(solution)/shard_map/all_to_all | solution.py:525
  747.5 29.8 %all-to-all-start = ((f32[32,1,14336]{2,1,0:T(1,128)}), f32[32,1,14336]{2,1,0:T(1,128)}, u32[]{:S(2)}, u32[]{:S(2)}) async-start(f32[32,1,14336]{2,1,0:T(1,128)} %copy.354), calls=%async_computation | async-start | bytes 3670016 | tf_op jit(solution)/shard_map/all_to_all | solution.py:507
  758.3 31.2 %collective-permute-start.59 = (bf16[2,64,2048]{2,1,0:T(8,128)(2,1)}, bf16[2,64,2048]{2,1,0:T(8,128)(2,1)}, u32[]{:S(2)}, u32[]{:S(2)}) collective-permute-start(bf16[2,64,2048]{2,1,0:T(8,128)(2,1)} %fusion.53), channel_id=1, source_target_pairs={{0,2},{1,3},{2,0},{3,1},{4,6},{5,7},{6,4},{7,5},{8,10},{9,11},{10,... | collective-permute-start | bytes 1572872 | tf_op jit(solution)/shard_map/ppermute | solution.py:149
  (141 other events, 1178.1 us)

commit v11 on v9

--- a/solution.py
+++ b/solution.py
@@ -462,40 +462,41 @@
     b_rows_mine = lax.dynamic_index_in_dim(
         dense_b_rows.reshape(2, COLS, fsdp_count, tok_count, RANK), me_tok, 3, keepdims=False
     )
-    wide = jnp.concatenate(
+    def reduce_to_owners(parts, kind):
+        rows = [p.size // (fsdp_count * COLS) for p in parts]
+        packed = jnp.concatenate(
+            [p.reshape(fsdp_count, r, COLS) for p, r in zip(parts, rows)], axis=1
+        ).astype(kind)
+        total = lax.all_to_all(packed, "fsdp", 0, 0, tiled=False).astype(jnp.float32).sum(0)
+        out = []
+        start = 0
+        for p, r in zip(parts, rows):
+            out.append(total[start : start + r].reshape(p.shape[1:]))
+            start += r
+        return out
+
+    per = COLS // fsdp_count
+    dense_b_gateup = hp_dot(onehot, jnp.stack(ffn_grads_up, 1), "src,spre->pce")
+    dense_a_down = hp_dot(grad_a_down, onehot, "sdr,src->dc")
+    b_gateup_block, a_down_block = reduce_to_owners(
         [
-            jnp.moveaxis(a_in_mine, 1, 0).reshape(fsdp_count, -1),
-            jnp.moveaxis(b_rows_mine, 2, 0).reshape(fsdp_count, -1),
+            jnp.moveaxis(dense_b_gateup.reshape(2, fsdp_count, per, ff_here), 1, 0),
+            jnp.moveaxis(dense_a_down.reshape(ff_here, fsdp_count, per), 1, 0),
         ],
-        axis=1,
-    )
-    wide_sum = lax.all_to_all(wide, "fsdp", 0, 0, tiled=False).sum(0)
-    a_in_block = wide_sum[: 5 * 16 * COLS].reshape(5, 16, COLS)
-    b_rows_block = wide_sum[5 * 16 * COLS :].reshape(2, COLS, 16)
-
+        jnp.bfloat16,
+    )
     dense_b_qkv = hp_dot(onehot, jnp.stack(attn_grads_up, 1), "src,spre->pce")
-    dense_b_gateup = hp_dot(onehot, jnp.stack(ffn_grads_up, 1), "src,spre->pce")
     dense_a_out = hp_dot(grad_a_out, onehot, "sdr,src->dc")
-    dense_a_down = hp_dot(grad_a_down, onehot, "sdr,src->dc")
-    per = COLS // fsdp_count
-    narrow = jnp.concatenate(
+    b_qkv_block, a_out_block = reduce_to_owners(
         [
-            jnp.moveaxis(dense_b_qkv.reshape(3, fsdp_count, per, qw_here), 1, 0).reshape(fsdp_count, -1),
-            jnp.moveaxis(dense_b_gateup.reshape(2, fsdp_count, per, ff_here), 1, 0).reshape(fsdp_count, -1),
-            jnp.moveaxis(dense_a_out.reshape(qw_here, fsdp_count, per), 1, 0).reshape(fsdp_count, -1),
-            jnp.moveaxis(dense_a_down.reshape(ff_here, fsdp_count, per), 1, 0).reshape(fsdp_count, -1),
+            jnp.moveaxis(dense_b_qkv.reshape(3, fsdp_count, per, qw_here), 1, 0),
+            jnp.moveaxis(dense_a_out.reshape(qw_here, fsdp_count, per), 1, 0),
         ],
-        axis=1,
-    ).astype(jnp.bfloat16)
-    narrow_sum = lax.all_to_all(narrow, "fsdp", 0, 0, tiled=False).astype(jnp.float32).sum(0)
-    sizes = [3 * per * qw_here, 2 * per * ff_here, qw_here * per, ff_here * per]
-    cuts = [0]
-    for size in sizes:
-        cuts.append(cuts[-1] + size)
-    b_qkv_block = narrow_sum[cuts[0] : cuts[1]].reshape(3, per, qw_here)
-    b_gateup_block = narrow_sum[cuts[1] : cuts[2]].reshape(2, per, ff_here)
-    a_out_block = narrow_sum[cuts[2] : cuts[3]].reshape(qw_here, per)
-    a_down_block = narrow_sum[cuts[3] : cuts[4]].reshape(ff_here, per)
+        jnp.bfloat16,
+    )
+    a_in_block, b_rows_block = reduce_to_owners(
+        [jnp.moveaxis(a_in_mine, 1, 0), jnp.moveaxis(b_rows_mine, 2, 0)], jnp.float32
+    )
 
     return (
         output,

time: 785 us -> 786 us (level)
  local copies, waits for them, and re-layouts: 307 us -> 288 us
  starting transfers between devices: 111 us -> 123 us
    unnamed x286 -> x283, local copies, waits for them, and re-layouts: 33.3 us -> 22 us
    all_to_all x2 -> x3, starting transfers between devices: 12.7 us -> 21.6 us  [reduce_to_owners(): lax.all_to_all(packed, 'fsdp', 0, 0, tiled=False).astype(jnp.float32).sum(0)]
  transfers between devices with their start and end apart: 66 -> 67, of which waited for: 24 -> 23; matrix products, arithmetic and copies ran while one was open for 46% -> 52% of each run, Pallas kernels for 0% -> 0%
where the time goes in v11:
time: 786 us; the launch traced here: 773 us
  local copies, waits for them, and re-layouts  288 us (37%)
  waiting for transfers between devices  152 us (19%)
  matrix products  134 us (17%)
  starting transfers between devices  123 us (16%)
  other arithmetic  67 us (9%)
  between operations  8.78 us (1%)
    dynamic_update_slice x57, local copies, waits for them, and re-layouts, put(): return lax.dynamic_update_slice(buffer, piece, start)  63.9 us
    dot_general x37, matrix products, hp_dot(): jnp.einsum(spec, left, right, precision=highest, preferred_element_type=j...  59.9 us
    ppermute x4, waiting for transfers between devices, tok_scatter(): got = lax.ppermute(send.astype(jnp.bfloat16), 'tok', xor_pairs(count, 2))  34.9 us
    ppermute x5, waiting for transfers between devices, pair_stage(): other = lax.ppermute(stacks, 'fsdp', fsdp_pairs('z', 1))  29.1 us
    dot_general x5, matrix products, column_backward(): jnp.einsum('ste,de->std', grad_rows, weight, preferred_element_type=jnp.f...  25.8 us
    ppermute x10, waiting for transfers between devices, ring_stage(): from_left = lax.ppermute(stacks, 'fsdp', fsdp_pairs(kind, 1))  23.6 us
    unnamed x283, local copies, waits for them, and re-layouts  22 us
    all_to_all x3, starting transfers between devices, reduce_to_owners(): lax.all_to_all(packed, 'fsdp', 0, 0, tiled=False).astype(jnp.float32).sum(0)  21.6 us
  transfers between devices with their start and end apart: 67, of which 23 were waited for; matrix products, arithmetic and copies ran while one was open for 52% of the time, Pallas kernels for 0%

profile of v11, /device:TPU:1, one launch (start us, length us, event | category | flops | bytes accessed | tf_op | source)
XLA Modules:
  0.0 773.0 jit_solution(369148597148661421)
XLA Ops:
  30.7 4.1 collective-permute-done.10
  52.3 3.9 collective-permute-done.42
  56.2 5.5 collective-permute-done.43
  82.6 4.8 collective-permute-done.25
  102.6 13.3 %collective-permute-start.1 = (bf16[2,2,64,2048]{3,2,1,0:T(8,128)(2,1)S(1)}, bf16[2,2,64,2048]{3,2,1,0:T(8,128)(2,1)S(1)}, u32[]{:S(2)}, u32[]{:S(2)}) collective-permute-start(bf16[2,2,64,2048]{3,2,1,0:T(8,128)(2,1)S(1)} %maximum_select_fusion.4), channel_id=1, source_target_pairs={{0,1},{1,0},{2,3},{3,2},{4,5},{5,4},{6,7},{7,6},{8,9},{9,8},{10,11... | collective-permute-start | bytes 3145736 | tf_op jit(solution)/shard_map/ppermute | solution.py:110
  125.2 8.7 %collective-permute-done.5 = bf16[3,4,64,512]{3,2,1,0:T(8,128)(2,1)S(1)} collective-permute-done((bf16[3,4,64,512]{3,2,1,0:T(8,128)(2,1)S(1)}, bf16[3,4,64,512]{3,2,1,0:T(8,128)(2,1)S(1)}, u32[]{:S(2)}, u32[]{:S(2)}) %collective-permute-start.5) | collective-permute-done | bytes 786464 | tf_op jit(solution)/shard_map/ppermute | solution.py:180
  149.4 15.5 %collective-permute-done.37 = bf16[2,4,64,1408]{3,2,1,0:T(8,128)(2,1)S(1)} collective-permute-done((bf16[2,4,64,1408]{3,2,1,0:T(8,128)(2,1)}, bf16[2,4,64,1408]{3,2,1,0:T(8,128)(2,1)S(1)}, u32[]{:S(2)}, u32[]{:S(2)}) %collective-permute-start.37) | collective-permute-done | bytes 1441824 | tf_op jit(solution)/shard_map/ppermute | solution.py:180
  168.0 5.8 broadcast_in_dim.134
  187.9 6.0 collective-permute-done.46
  206.4 14.6 %collective-permute-done.7 = bf16[3,8,64,512]{3,2,1,0:T(8,128)(2,1)} collective-permute-done((bf16[3,8,64,512]{3,2,1,0:T(8,128)(2,1)}, bf16[3,8,64,512]{3,2,1,0:T(8,128)(2,1)}, u32[]{:S(2)}, u32[]{:S(2)}) %collective-permute-start.7) | collective-permute-done | bytes 1572896 | tf_op jit(solution)/shard_map/ppermute | solution.py:190
  223.1 4.6 collective-permute-done.6
  236.5 5.3 collective-permute-done.21
  252.0 3.9 constant_dynamic-slice_fusion.14
  279.8 4.7 copy.302
  284.5 6.4 copy.303
  296.0 4.5 constant_dynamic-slice_fusion.7
  326.2 5.7 fusion.121
  337.9 4.1 convolution_add_fusion.5
  362.3 20.0 %collective-permute-start.30 = (f32[2,2,64,2048]{3,2,0,1:T(8,128)}, f32[2,2,64,2048]{3,2,0,1:T(8,128)}, u32[]{:S(2)}, u32[]{:S(2)}) collective-permute-start(f32[2,2,64,2048]{3,2,0,1:T(8,128)} %bitcast.532), channel_id=1, source_target_pairs={{0,1},{1,0},{2,3},{3,2},{4,5},{5,4},{6,7},{7,6},{8,9},{9,8},{10,11... | collective-permute-start | bytes 6291464 | tf_op jit(solution)/shard_map/ppermute | solution.py:125
  389.5 7.6 convolution_add_fusion
  409.9 3.7 constant_dynamic-update-slice_fusion.19
  413.7 5.7 collective-permute-done.31
  421.6 11.5 %collective-permute-done.40 = bf16[2,4,64,1408]{3,2,1,0:T(8,128)(2,1)S(1)} collective-permute-done((bf16[2,4,64,1408]{3,2,1,0:T(8,128)(2,1)S(1)}, bf16[2,4,64,1408]{3,2,1,0:T(8,128)(2,1)S(1)}, u32[]{:S(2)}, u32[]{:S(2)}) %collective-permute-start.40) | collective-permute-done | bytes 1441824 | tf_op jit(solution)/shard_map/ppermute | solution.py:194
  437.6 9.4 %fusion.120 = (bf16[1,32,64,1408]{3,2,1,0:T(8,128)(2,1)}, bf16[1,32,64,1408]{3,2,1,0:T(8,128)(2,1)}) fusion(bf16[2,32,64,1408]{3,2,1,0:T(8,128)(2,1)} %constant_dynamic-update-slice_fusion.17), kind=kLoop, calls=%fused_computation.352 | loop fusion | bytes 23068672 | tf_op jit(solution)/shard_map/slice | solution.py:365
  449.4 5.5 select_n.519
  457.7 7.1 copy.309
  468.7 5.9 convolution_add_fusion.1
  474.7 6.3 fusion.6
  481.4 3.6 convolution_bitcast_fusion.4
  487.4 5.4 copy.331
  495.3 6.3 convolution_bitcast_fusion.5
  503.9 5.4 copy.329
  512.2 4.4 add_add_fusion.1
  542.8 8.6 %collective-permute-done.55 = bf16[2,64,2048]{2,1,0:T(8,128)(2,1)S(1)} collective-permute-done((bf16[2,64,2048]{2,1,0:T(8,128)(2,1)S(1)}, bf16[2,64,2048]{2,1,0:T(8,128)(2,1)S(1)}, u32[]{:S(2)}, u32[]{:S(2)}) %collective-permute-start.55) | collective-permute-done | bytes 524320 | tf_op jit(solution)/shard_map/ppermute | solution.py:128
  551.8 10.9 %collective-permute-done.51 = bf16[2,64,2048]{2,1,0:T(8,128)(2,1)S(1)} collective-permute-done((bf16[2,64,2048]{2,1,0:T(8,128)(2,1)S(1)}, bf16[2,64,2048]{2,1,0:T(8,128)(2,1)S(1)}, u32[]{:S(2)}, u32[]{:S(2)}) %collective-permute-start.51) | collective-permute-done | bytes 524320 | tf_op jit(solution)/shard_map/ppermute | solution.py:128
  569.6 8.4 %collective-permute-done.56 = bf16[2,64,2048]{2,1,0:T(8,128)(2,1)S(1)} collective-permute-done((bf16[2,64,2048]{2,1,0:T(8,128)(2,1)S(1)}, bf16[2,64,2048]{2,1,0:T(8,128)(2,1)S(1)}, u32[]{:S(2)}, u32[]{:S(2)}) %collective-permute-start.56) | collective-permute-done | bytes 524320 | tf_op jit(solution)/shard_map/ppermute | solution.py:106
  597.2 6.3 all-to-all-start.2
  610.0 3.8 convolution_add_fusion.3
  634.8 4.6 multiply_add_fusion.5
  643.7 5.0 fusion.131
  653.4 5.2 fusion.132
  667.8 5.7 add_add_fusion
  705.2 7.5 all-to-all-start.1
  712.7 4.3 pad_maximum_fusion
  717.0 5.9 copy.353
  725.9 7.8 %all-to-all-start = ((f32[32,112,128]{2,1,0:T(8,128)}), f32[32,112,128]{2,1,0:T(8,128)}, u32[]{:S(2)}, u32[]{:S(2)}) async-start(f32[32,112,128]{2,1,0:T(8,128)} %pad_maximum_fusion.2), calls=%async_computation | async-start | bytes 3670016 | tf_op jit(solution)/shard_map/all_to_all | solution.py:470
  744.9 11.1 %all-to-all-done = f32[32,112,128]{2,1,0:T(8,128)} async-done(((f32[32,112,128]{2,1,0:T(8,128)}), f32[32,112,128]{2,1,0:T(8,128)}, u32[]{:S(2)}, u32[]{:S(2)}) %all-to-all-start) | async-done | bytes 1835040 | tf_op jit(solution)/shard_map/all_to_all | solution.py:470
  759.0 9.8 %collective-permute-done.59 = bf16[2,64,2048]{2,1,0:T(8,128)(2,1)} collective-permute-done((bf16[2,64,2048]{2,1,0:T(8,128)(2,1)}, bf16[2,64,2048]{2,1,0:T(8,128)(2,1)}, u32[]{:S(2)}, u32[]{:S(2)}) %collective-permute-start.59) | collective-permute-done | bytes 524320 | tf_op jit(solution)/shard_map/ppermute | solution.py:128
  (703 shorter events, 429.8 us)
Async XLA Ops:
  0.7 61.1 %collective-permute-start.2 = (bf16[3,1,64,512]{3,2,0,1:T(8,128)(2,1)}, bf16[3,1,64,512]{3,2,0,1:T(8,128)(2,1)}, u32[]{:S(2)}, u32[]{:S(2)}) collective-permute-start(bf16[3,1,64,512]{3,2,0,1:T(8,128)(2,1)} %bitcast.658), channel_id=1, source_target_pairs={{0,12},{4,0},{8,4},{12,8},{16,28},{20,16},{24,20},{28,24},{32,44},... | collective-permute-start | bytes 589832 | tf_op jit(solution)/shard_map/ppermute | solution.py:191
  4.3 59.4 %collective-permute-start.3 = (bf16[3,1,64,512]{3,2,0,1:T(8,128)(2,1)}, bf16[3,1,64,512]{3,2,0,1:T(8,128)(2,1)}, u32[]{:S(2)}, u32[]{:S(2)}) collective-permute-start(bf16[3,1,64,512]{3,2,0,1:T(8,128)(2,1)} %bitcast.659), channel_id=1, source_target_pairs={{0,4},{4,8},{8,12},{12,0},{16,20},{20,24},{24,28},{28,16},{32,36},... | collective-permute-start | bytes 589832 | tf_op jit(solution)/shard_map/ppermute | solution.py:190
  4.3 41.1 %collective-permute-start.22 = (bf16[1,512,64]{1,2,0:T(8,128)(2,1)}, bf16[1,512,64]{1,2,0:T(8,128)(2,1)}, u32[]{:S(2)}, u32[]{:S(2)}) collective-permute-start(bf16[1,512,64]{1,2,0:T(8,128)(2,1)} %bitcast.668), channel_id=1, source_target_pairs={{0,12},{4,0},{8,4},{12,8},{16,28},{20,16},{24,20},{28,24},{32,44},... | collective-permute-start | bytes 196616 | tf_op jit(solution)/shard_map/ppermute | solution.py:191
  7.0 38.5 %collective-permute-start.23 = (bf16[1,512,64]{1,2,0:T(8,128)(2,1)}, bf16[1,512,64]{1,2,0:T(8,128)(2,1)}, u32[]{:S(2)}, u32[]{:S(2)}) collective-permute-start(bf16[1,512,64]{1,2,0:T(8,128)(2,1)} %bitcast.669), channel_id=1, source_target_pairs={{0,4},{4,8},{8,12},{12,0},{16,20},{20,24},{24,28},{28,16},{32,36},... | collective-permute-start | bytes 196616 | tf_op jit(solution)/shard_map/ppermute | solution.py:190
  7.0 23.5 %collective-permute-start.12 = (bf16[2,128,16]{1,2,0:T(8,128)(2,1)}, bf16[2,128,16]{1,2,0:T(8,128)(2,1)S(1)}, u32[]{:S(2)}, u32[]{:S(2)}) collective-permute-start(bf16[2,128,16]{1,2,0:T(8,128)(2,1)} %param.35), channel_id=1, source_target_pairs={{0,2},{1,3},{2,0},{3,1},{4,6},{5,7},{6,4},{7,5},{8,10},{9,11},{10,... | collective-permute-start | bytes 24584 | tf_op jit(solution)/shard_map/ppermute | solution.py:106
  40.4 33.0 %collective-permute-start.34 = (bf16[2,1,64,1408]{3,2,0,1:T(8,128)(2,1)}, bf16[2,1,64,1408]{3,2,0,1:T(8,128)(2,1)S(1)}, u32[]{:S(2)}, u32[]{:S(2)}) collective-permute-start(bf16[2,1,64,1408]{3,2,0,1:T(8,128)(2,1)} %bitcast.655), channel_id=1, source_target_pairs={{0,96},{4,100},{8,104},{12,108},{16,112},{20,116},{24,120},{28,124... | collective-permute-start | bytes 1081352 | tf_op jit(solution)/shard_map/ppermute | solution.py:191
  45.4 28.8 %collective-permute-start.35 = (bf16[2,1,64,1408]{3,2,0,1:T(8,128)(2,1)}, bf16[2,1,64,1408]{3,2,0,1:T(8,128)(2,1)S(1)}, u32[]{:S(2)}, u32[]{:S(2)}) collective-permute-start(bf16[2,1,64,1408]{3,2,0,1:T(8,128)(2,1)} %bitcast.656), channel_id=1, source_target_pairs={{0,32},{4,36},{8,40},{12,44},{16,48},{20,52},{24,56},{28,60},{32,6... | collective-permute-start | bytes 1081352 | tf_op jit(solution)/shard_map/ppermute | solution.py:190
  61.7 31.1 %collective-permute-start = (bf16[2,64,2048]{2,1,0:T(8,128)(2,1)S(1)}, bf16[2,64,2048]{2,1,0:T(8,128)(2,1)S(1)}, u32[]{:S(2)}, u32[]{:S(2)}) collective-permute-start(bf16[2,64,2048]{2,1,0:T(8,128)(2,1)S(1)} %copy-done.70), channel_id=1, source_target_pairs={{0,2},{1,3},{2,0},{3,1},{4,6},{5,7},{6,4},{7,5},{8,10},{9,11},{10,... | collective-permute-start | bytes 1572872 | tf_op jit(solution)/shard_map/ppermute | solution.py:106
  69.5 26.0 %collective-permute-start.52 = (bf16[2,64,2048]{2,1,0:T(8,128)(2,1)S(1)}, bf16[2,64,2048]{2,1,0:T(8,128)(2,1)S(1)}, u32[]{:S(2)}, u32[]{:S(2)}) collective-permute-start(bf16[2,64,2048]{2,1,0:T(8,128)(2,1)S(1)} %copy-done.31), channel_id=1, source_target_pairs={{0,2},{1,3},{2,0},{3,1},{4,6},{5,7},{6,4},{7,5},{8,10},{9,11},{10,... | collective-permute-start | bytes 1572872 | tf_op jit(solution)/shard_map/ppermute | solution.py:106
  72.4 15.1 %collective-permute-start.25 = (bf16[4,512,64]{1,2,0:T(8,128)(2,1)S(1)}, bf16[4,512,64]{1,2,0:T(8,128)(2,1)S(1)}, u32[]{:S(2)}, u32[]{:S(2)}) collective-permute-start(bf16[4,512,64]{1,2,0:T(8,128)(2,1)S(1)} %constant_dynamic-update-slice_fusion.31), channel_id=1, source_target_pairs={{0,16},{4,20},{8,24},{12,28},{16,0},{20,4},{24,8},{28,12},{32,48},... | collective-permute-start | bytes 786440 | tf_op jit(solution)/shard_map/ppermute | solution.py:180
  73.4 17.0 %collective-permute-start.4 = (bf16[3,1,64,512]{3,2,0,1:T(8,128)(2,1)}, bf16[3,1,64,512]{3,2,0,1:T(8,128)(2,1)S(1)}, u32[]{:S(2)}, u32[]{:S(2)}) collective-permute-start(bf16[3,1,64,512]{3,2,0,1:T(8,128)(2,1)} %collective-permute-done.3), channel_id=1, source_target_pairs={{0,4},{4,8},{8,12},{12,0},{16,20},{20,24},{24,28},{28,16},{32,36},... | collective-permute-start | bytes 589832 | tf_op jit(solution)/shard_map/ppermute | solution.py:197
  81.4 42.1 %collective-permute-start.45 = (bf16[4,1408,64]{1,2,0:T(8,128)(2,1)S(1)}, bf16[4,1408,64]{1,2,0:T(8,128)(2,1)S(1)}, u32[]{:S(2)}, u32[]{:S(2)}) collective-permute-start(bf16[4,1408,64]{1,2,0:T(8,128)(2,1)S(1)} %constant_dynamic-update-slice_fusion.13), channel_id=1, source_target_pairs={{0,16},{4,20},{8,24},{12,28},{16,0},{20,4},{24,8},{28,12},{32,48},... | collective-permute-start | bytes 2162696 | tf_op jit(solution)/shard_map/ppermute | solution.py:180
  90.4 27.5 %collective-permute-start.17 = (bf16[4,644,128]{2,0,1:T(4,128)(2,1)S(1)}, bf16[4,644,128]{2,0,1:T(4,128)(2,1)S(1)}, u32[]{:S(2)}, u32[]{:S(2)}) collective-permute-start(bf16[4,644,128]{2,0,1:T(4,128)(2,1)S(1)} %copy.279), channel_id=1, source_target_pairs={{0,16},{4,20},{8,24},{12,28},{16,0},{20,4},{24,8},{28,12},{32,48},... | collective-permute-start | bytes 1978376 | tf_op jit(solution)/shard_map/ppermute | solution.py:180
  95.5 21.2 %collective-permute-start.27 = (bf16[8,512,64]{1,2,0:T(8,128)(2,1)S(1)}, bf16[8,512,64]{1,2,0:T(8,128)(2,1)S(1)}, u32[]{:S(2)}, u32[]{:S(2)}) collective-permute-start(bf16[8,512,64]{1,2,0:T(8,128)(2,1)S(1)} %constant_dynamic-update-slice_fusion.29), channel_id=1, source_target_pairs={{0,32},{4,36},{8,40},{12,44},{16,48},{20,52},{24,56},{28,60},{32,6... | collective-permute-start | bytes 1572872 | tf_op jit(solution)/shard_map/ppermute | solution.py:190
  96.0 37.9 %collective-permute-start.5 = (bf16[3,4,64,512]{3,2,1,0:T(8,128)(2,1)S(1)}, bf16[3,4,64,512]{3,2,1,0:T(8,128)(2,1)S(1)}, u32[]{:S(2)}, u32[]{:S(2)}) collective-permute-start(bf16[3,4,64,512]{3,2,1,0:T(8,128)(2,1)S(1)} %bitcast_dynamic-update-slice_fusion.5), channel_id=1, source_target_pairs={{0,16},{4,20},{8,24},{12,28},{16,0},{20,4},{24,8},{28,12},{32,48},... | collective-permute-start | bytes 2359304 | tf_op jit(solution)/shard_map/ppermute | solution.py:180
  102.6 45.5 %collective-permute-start.1 = (bf16[2,2,64,2048]{3,2,1,0:T(8,128)(2,1)S(1)}, bf16[2,2,64,2048]{3,2,1,0:T(8,128)(2,1)S(1)}, u32[]{:S(2)}, u32[]{:S(2)}) collective-permute-start(bf16[2,2,64,2048]{3,2,1,0:T(8,128)(2,1)S(1)} %maximum_select_fusion.4), channel_id=1, source_target_pairs={{0,1},{1,0},{2,3},{3,2},{4,5},{5,4},{6,7},{7,6},{8,9},{9,8},{10,11... | collective-permute-start | bytes 3145736 | tf_op jit(solution)/shard_map/ppermute | solution.py:110
  116.8 29.0 %collective-permute-start.53 = (bf16[2,2,64,2048]{3,2,0,1:T(8,128)(2,1)S(1)}, bf16[2,2,64,2048]{3,2,0,1:T(8,128)(2,1)S(1)}, u32[]{:S(2)}, u32[]{:S(2)}) collective-permute-start(bf16[2,2,64,2048]{3,2,0,1:T(8,128)(2,1)S(1)} %maximum_select_fusion.7), channel_id=1, source_target_pairs={{0,1},{1,0},{2,3},{3,2},{4,5},{5,4},{6,7},{7,6},{8,9},{9,8},{10,11... | collective-permute-start | bytes 3145736 | tf_op jit(solution)/shard_map/ppermute | solution.py:110
  117.9 17.6 %collective-permute-start.28 = (bf16[4,512,64]{1,2,0:T(8,128)(2,1)S(1)}, bf16[4,512,64]{1,2,0:T(8,128)(2,1)S(1)}, u32[]{:S(2)}, u32[]{:S(2)}) collective-permute-start(bf16[4,512,64]{1,2,0:T(8,128)(2,1)S(1)} %slice.260), channel_id=1, source_target_pairs={{0,32},{4,36},{8,40},{12,44},{16,48},{20,52},{24,56},{28,60},{32,6... | collective-permute-start | bytes 786440 | tf_op jit(solution)/shard_map/ppermute | solution.py:194
  123.6 41.3 %collective-permute-start.37 = (bf16[2,4,64,1408]{3,2,1,0:T(8,128)(2,1)}, bf16[2,4,64,1408]{3,2,1,0:T(8,128)(2,1)S(1)}, u32[]{:S(2)}, u32[]{:S(2)}) collective-permute-start(bf16[2,4,64,1408]{3,2,1,0:T(8,128)(2,1)} %bitcast_dynamic-update-slice_fusion.1), channel_id=1, source_target_pairs={{0,16},{4,20},{8,24},{12,28},{16,0},{20,4},{24,8},{28,12},{32,48},... | collective-permute-start | bytes 4325384 | tf_op jit(solution)/shard_map/ppermute | solution.py:180
  135.4 31.0 %collective-permute-start.19 = (bf16[8,644,128]{2,0,1:T(8,128)(2,1)}, bf16[8,644,128]{2,0,1:T(8,128)(2,1)}, u32[]{:S(2)}, u32[]{:S(2)}) collective-permute-start(bf16[8,644,128]{2,0,1:T(8,128)(2,1)} %copy.281), channel_id=1, source_target_pairs={{0,32},{4,36},{8,40},{12,44},{16,48},{20,52},{24,56},{28,60},{32,6... | collective-permute-start | bytes 3956744 | tf_op jit(solution)/shard_map/ppermute | solution.py:190
  139.9 39.0 %collective-permute-start.18 = (bf16[8,644,128]{2,0,1:T(8,128)(2,1)}, bf16[8,644,128]{2,0,1:T(8,128)(2,1)}, u32[]{:S(2)}, u32[]{:S(2)}) collective-permute-start(bf16[8,644,128]{2,0,1:T(8,128)(2,1)} %copy.281), channel_id=1, source_target_pairs={{0,96},{4,100},{8,104},{12,108},{16,112},{20,116},{24,120},{28,124... | collective-permute-start | bytes 3956744 | tf_op jit(solution)/shard_map/ppermute | solution.py:191
  145.7 48.3 %collective-permute-start.46 = (bf16[8,1408,64]{1,2,0:T(8,128)(2,1)}, bf16[8,1408,64]{1,2,0:T(8,128)(2,1)}, u32[]{:S(2)}, u32[]{:S(2)}) collective-permute-start(bf16[8,1408,64]{1,2,0:T(8,128)(2,1)} %constant_dynamic-update-slice_fusion.11), channel_id=1, source_target_pairs={{0,96},{4,100},{8,104},{12,108},{16,112},{20,116},{24,120},{28,124... | collective-permute-start | bytes 4325384 | tf_op jit(solution)/shard_map/ppermute | solution.py:191
  148.1 49.3 %collective-permute-start.47 = (bf16[8,1408,64]{1,2,0:T(8,128)(2,1)}, bf16[8,1408,64]{1,2,0:T(8,128)(2,1)}, u32[]{:S(2)}, u32[]{:S(2)}) collective-permute-start(bf16[8,1408,64]{1,2,0:T(8,128)(2,1)} %constant_dynamic-update-slice_fusion.11), channel_id=1, source_target_pairs={{0,32},{4,36},{8,40},{12,44},{16,48},{20,52},{24,56},{28,60},{32,6... | collective-permute-start | bytes 4325384 | tf_op jit(solution)/shard_map/ppermute | solution.py:190
  164.9 62.8 %collective-permute-start.6 = (bf16[3,8,64,512]{3,2,1,0:T(8,128)(2,1)}, bf16[3,8,64,512]{3,2,1,0:T(8,128)(2,1)}, u32[]{:S(2)}, u32[]{:S(2)}) collective-permute-start(bf16[3,8,64,512]{3,2,1,0:T(8,128)(2,1)} %constant_dynamic-update-slice_fusion.46), channel_id=1, source_target_pairs={{0,96},{4,100},{8,104},{12,108},{16,112},{20,116},{24,120},{28,124... | collective-permute-start | bytes 4718600 | tf_op jit(solution)/shard_map/ppermute | solution.py:191
  166.4 54.6 %collective-permute-start.7 = (bf16[3,8,64,512]{3,2,1,0:T(8,128)(2,1)}, bf16[3,8,64,512]{3,2,1,0:T(8,128)(2,1)}, u32[]{:S(2)}, u32[]{:S(2)}) collective-permute-start(bf16[3,8,64,512]{3,2,1,0:T(8,128)(2,1)} %constant_dynamic-update-slice_fusion.46), channel_id=1, source_target_pairs={{0,32},{4,36},{8,40},{12,44},{16,48},{20,52},{24,56},{28,60},{32,6... | collective-permute-start | bytes 4718600 | tf_op jit(solution)/shard_map/ppermute | solution.py:190
  178.9 219.8 %collective-permute-start.38 = (bf16[2,8,64,1408]{3,2,1,0:T(8,128)(2,1)}, bf16[2,8,64,1408]{3,2,1,0:T(8,128)(2,1)}, u32[]{:S(2)}, u32[]{:S(2)}) collective-permute-start(bf16[2,8,64,1408]{3,2,1,0:T(8,128)(2,1)} %constant_dynamic-update-slice_fusion.22), channel_id=1, source_target_pairs={{0,12},{4,0},{8,4},{12,8},{16,28},{20,16},{24,20},{28,24},{32,44},... | collective-permute-start | bytes 8650760 | tf_op jit(solution)/shard_map/ppermute | solution.py:191
  194.0 41.1 %collective-permute-start.20 = (bf16[4,644,128]{2,0,1:T(4,128)(2,1)S(1)}, bf16[4,644,128]{2,0,1:T(4,128)(2,1)S(1)}, u32[]{:S(2)}, u32[]{:S(2)}) collective-permute-start(bf16[4,644,128]{2,0,1:T(4,128)(2,1)S(1)} %slice.239), channel_id=1, source_target_pairs={{0,32},{4,36},{8,40},{12,44},{16,48},{20,52},{24,56},{28,60},{32,6... | collective-permute-start | bytes 1978376 | tf_op jit(solution)/shard_map/ppermute | solution.py:194
  197.4 44.4 %collective-permute-start.21 = (bf16[4,644,128]{2,0,1:T(4,128)(2,1)S(1)}, bf16[4,644,128]{2,0,1:T(4,128)(2,1)S(1)}, u32[]{:S(2)}, u32[]{:S(2)}) collective-permute-start(bf16[4,644,128]{2,0,1:T(4,128)(2,1)S(1)} %slice.240), channel_id=1, source_target_pairs={{0,96},{4,100},{8,104},{12,108},{16,112},{20,116},{24,120},{28,124... | collective-permute-start | bytes 1978376 | tf_op jit(solution)/shard_map/ppermute | solution.py:195
  221.0 176.2 %collective-permute-start.39 = (bf16[2,8,64,1408]{3,2,1,0:T(8,128)(2,1)}, bf16[2,8,64,1408]{3,2,1,0:T(8,128)(2,1)}, u32[]{:S(2)}, u32[]{:S(2)}) collective-permute-start(bf16[2,8,64,1408]{3,2,1,0:T(8,128)(2,1)} %constant_dynamic-update-slice_fusion.22), channel_id=1, source_target_pairs={{0,4},{4,8},{8,12},{12,0},{16,20},{20,24},{24,28},{28,16},{32,36},... | collective-permute-start | bytes 8650760 | tf_op jit(solution)/shard_map/ppermute | solution.py:190
  227.7 157.6 %collective-permute-start.48 = (bf16[4,1408,64]{1,2,0:T(8,128)(2,1)}, bf16[4,1408,64]{1,2,0:T(8,128)(2,1)}, u32[]{:S(2)}, u32[]{:S(2)}) collective-permute-start(bf16[4,1408,64]{1,2,0:T(8,128)(2,1)} %slice.275), channel_id=1, source_target_pairs={{0,32},{4,36},{8,40},{12,44},{16,48},{20,52},{24,56},{28,60},{32,6... | collective-permute-start | bytes 2162696 | tf_op jit(solution)/shard_map/ppermute | solution.py:194
  235.1 86.6 %collective-permute-start.8 = (bf16[3,4,64,512]{3,2,1,0:T(8,128)(2,1)}, bf16[3,4,64,512]{3,2,1,0:T(8,128)(2,1)}, u32[]{:S(2)}, u32[]{:S(2)}) collective-permute-start(bf16[3,4,64,512]{3,2,1,0:T(8,128)(2,1)} %slice.236), channel_id=1, source_target_pairs={{0,32},{4,36},{8,40},{12,44},{16,48},{20,52},{24,56},{28,60},{32,6... | collective-permute-start | bytes 2359304 | tf_op jit(solution)/shard_map/ppermute | solution.py:194
  241.8 82.1 %collective-permute-start.9 = (bf16[3,4,64,512]{3,2,1,0:T(8,128)(2,1)}, bf16[3,4,64,512]{3,2,1,0:T(8,128)(2,1)}, u32[]{:S(2)}, u32[]{:S(2)}) collective-permute-start(bf16[3,4,64,512]{3,2,1,0:T(8,128)(2,1)} %slice.237), channel_id=1, source_target_pairs={{0,96},{4,100},{8,104},{12,108},{16,112},{20,116},{24,120},{28,124... | collective-permute-start | bytes 2359304 | tf_op jit(solution)/shard_map/ppermute | solution.py:195
  321.7 65.8 %collective-permute-start.49 = (bf16[4,1408,64]{1,2,0:T(8,128)(2,1)}, bf16[4,1408,64]{1,2,0:T(8,128)(2,1)}, u32[]{:S(2)}, u32[]{:S(2)}) collective-permute-start(bf16[4,1408,64]{1,2,0:T(8,128)(2,1)} %slice.276), channel_id=1, source_target_pairs={{0,96},{4,100},{8,104},{12,108},{16,112},{20,116},{24,120},{28,124... | collective-permute-start | bytes 2162696 | tf_op jit(solution)/shard_map/ppermute | solution.py:195
  362.3 40.7 %collective-permute-start.30 = (f32[2,2,64,2048]{3,2,0,1:T(8,128)}, f32[2,2,64,2048]{3,2,0,1:T(8,128)}, u32[]{:S(2)}, u32[]{:S(2)}) collective-permute-start(f32[2,2,64,2048]{3,2,0,1:T(8,128)} %bitcast.532), channel_id=1, source_target_pairs={{0,1},{1,0},{2,3},{3,2},{4,5},{5,4},{6,7},{7,6},{8,9},{9,8},{10,11... | collective-permute-start | bytes 6291464 | tf_op jit(solution)/shard_map/ppermute | solution.py:125
  398.7 34.5 %collective-permute-start.40 = (bf16[2,4,64,1408]{3,2,1,0:T(8,128)(2,1)S(1)}, bf16[2,4,64,1408]{3,2,1,0:T(8,128)(2,1)S(1)}, u32[]{:S(2)}, u32[]{:S(2)}) collective-permute-start(bf16[2,4,64,1408]{3,2,1,0:T(8,128)(2,1)S(1)} %slice.266), channel_id=1, source_target_pairs={{0,4},{4,8},{8,12},{12,0},{16,20},{20,24},{24,28},{28,16},{32,36},... | collective-permute-start | bytes 4325384 | tf_op jit(solution)/shard_map/ppermute | solution.py:194
  400.2 34.1 %collective-permute-start.41 = (bf16[2,4,64,1408]{3,2,1,0:T(8,128)(2,1)S(1)}, bf16[2,4,64,1408]{3,2,1,0:T(8,128)(2,1)S(1)}, u32[]{:S(2)}, u32[]{:S(2)}) collective-permute-start(bf16[2,4,64,1408]{3,2,1,0:T(8,128)(2,1)S(1)} %slice.267), channel_id=1, source_target_pairs={{0,12},{4,0},{8,4},{12,8},{16,28},{20,16},{24,20},{28,24},{32,44},... | collective-permute-start | bytes 4325384 | tf_op jit(solution)/shard_map/ppermute | solution.py:195
  404.9 14.5 %collective-permute-start.31 = (bf16[2,64,2048]{2,1,0:T(8,128)(2,1)S(1)}, bf16[2,64,2048]{2,1,0:T(8,128)(2,1)S(1)}, u32[]{:S(2)}, u32[]{:S(2)}) collective-permute-start(bf16[2,64,2048]{2,1,0:T(8,128)(2,1)S(1)} %fusion.43), channel_id=1, source_target_pairs={{0,2},{1,3},{2,0},{3,1},{4,6},{5,7},{6,4},{7,5},{8,10},{9,11},{10,... | collective-permute-start | bytes 1572872 | tf_op jit(solution)/shard_map/ppermute | solution.py:128
  419.9 15.8 %collective-permute-start.32 = (bf16[2,64,2048]{2,1,0:T(8,128)(2,1)S(1)}, bf16[2,64,2048]{2,1,0:T(8,128)(2,1)S(1)}, u32[]{:S(2)}, u32[]{:S(2)}) collective-permute-start(bf16[2,64,2048]{2,1,0:T(8,128)(2,1)S(1)} %multiply_convert_fusion.3), channel_id=1, source_target_pairs={{0,2},{1,3},{2,0},{3,1},{4,6},{5,7},{6,4},{7,5},{8,10},{9,11},{10,... | collective-permute-start | bytes 1572872 | tf_op jit(solution)/shard_map/ppermute | solution.py:106
  520.0 13.8 %collective-permute-start.54 = (f32[2,2,64,2048]{3,2,0,1:T(8,128)}, f32[2,2,64,2048]{3,2,0,1:T(8,128)}, u32[]{:S(2)}, u32[]{:S(2)}) collective-permute-start(f32[2,2,64,2048]{3,2,0,1:T(8,128)} %bitcast.530), channel_id=1, source_target_pairs={{0,1},{1,0},{2,3},{3,2},{4,5},{5,4},{6,7},{7,6},{8,9},{9,8},{10,11... | collective-permute-start | bytes 6291464 | tf_op jit(solution)/shard_map/ppermute | solution.py:125
  536.4 15.0 %collective-permute-start.55 = (bf16[2,64,2048]{2,1,0:T(8,128)(2,1)S(1)}, bf16[2,64,2048]{2,1,0:T(8,128)(2,1)S(1)}, u32[]{:S(2)}, u32[]{:S(2)}) collective-permute-start(bf16[2,64,2048]{2,1,0:T(8,128)(2,1)S(1)} %fusion.45), channel_id=1, source_target_pairs={{0,2},{1,3},{2,0},{3,1},{4,6},{5,7},{6,4},{7,5},{8,10},{9,11},{10,... | collective-permute-start | bytes 1572872 | tf_op jit(solution)/shard_map/ppermute | solution.py:128
  540.4 22.2 %collective-permute-start.51 = (bf16[2,64,2048]{2,1,0:T(8,128)(2,1)S(1)}, bf16[2,64,2048]{2,1,0:T(8,128)(2,1)S(1)}, u32[]{:S(2)}, u32[]{:S(2)}) collective-permute-start(bf16[2,64,2048]{2,1,0:T(8,128)(2,1)S(1)} %fusion.44), channel_id=1, source_target_pairs={{0,2},{1,3},{2,0},{3,1},{4,6},{5,7},{6,4},{7,5},{8,10},{9,11},{10,... | collective-permute-start | bytes 1572872 | tf_op jit(solution)/shard_map/ppermute | solution.py:128
  566.4 25.6 %collective-permute-start.62 = (f32[2,2,256,16]{2,3,1,0:T(8,128)}, f32[2,2,256,16]{2,3,1,0:T(8,128)}, u32[]{:S(2)}, u32[]{:S(2)}) collective-permute-start(f32[2,2,256,16]{2,3,1,0:T(8,128)} %pad_maximum_fusion.11), channel_id=1, source_target_pairs={{0,1},{1,0},{2,3},{3,2},{4,5},{5,4},{6,7},{7,6},{8,9},{9,8},{10,11... | collective-permute-start | bytes 196616 | tf_op jit(solution)/shard_map/ppermute | solution.py:134
  579.2 26.7 %collective-permute-start.57 = (bf16[2,2,64,2048]{3,2,0,1:T(8,128)(2,1)}, bf16[2,2,64,2048]{3,2,0,1:T(8,128)(2,1)}, u32[]{:S(2)}, u32[]{:S(2)}) collective-permute-start(bf16[2,2,64,2048]{3,2,0,1:T(8,128)(2,1)} %maximum_select_fusion.9), channel_id=1, source_target_pairs={{0,1},{1,0},{2,3},{3,2},{4,5},{5,4},{6,7},{7,6},{8,9},{9,8},{10,11... | collective-permute-start | bytes 3145736 | tf_op jit(solution)/shard_map/ppermute | solution.py:110
  597.2 108.0 %all-to-all-start.2 = ((bf16[32,132,128]{2,1,0:T(8,128)(2,1)}), bf16[32,132,128]{2,1,0:T(8,128)(2,1)}, u32[]{:S(2)}, u32[]{:S(2)}) async-start(bf16[32,132,128]{2,1,0:T(8,128)(2,1)} %pad_maximum_fusion.3), calls=%async_computation.2 | async-start | bytes 2228224 | tf_op jit(solution)/shard_map/all_to_all | solution.py:470
  676.9 56.8 %collective-permute-start.58 = (f32[2,2,64,2048]{3,2,0,1:T(8,128)}, f32[2,2,64,2048]{3,2,0,1:T(8,128)}, u32[]{:S(2)}, u32[]{:S(2)}) collective-permute-start(f32[2,2,64,2048]{3,2,0,1:T(8,128)} %bitcast.529), channel_id=1, source_target_pairs={{0,1},{1,0},{2,3},{3,2},{4,5},{5,4},{6,7},{7,6},{8,9},{9,8},{10,11... | collective-permute-start | bytes 6291464 | tf_op jit(solution)/shard_map/ppermute | solution.py:125
  705.2 20.7 %all-to-all-start.1 = ((bf16[32,64,128]{2,1,0:T(8,128)(2,1)}), bf16[32,64,128]{2,1,0:T(8,128)(2,1)}, u32[]{:S(2)}, u32[]{:S(2)}) async-start(bf16[32,64,128]{2,1,0:T(8,128)(2,1)} %pad_maximum_fusion.8), calls=%async_computation.1 | async-start | bytes 1048576 | tf_op jit(solution)/shard_map/all_to_all | solution.py:470
  725.9 30.2 %all-to-all-start = ((f32[32,112,128]{2,1,0:T(8,128)}), f32[32,112,128]{2,1,0:T(8,128)}, u32[]{:S(2)}, u32[]{:S(2)}) async-start(f32[32,112,128]{2,1,0:T(8,128)} %pad_maximum_fusion.2), calls=%async_computation | async-start | bytes 3670016 | tf_op jit(solution)/shard_map/all_to_all | solution.py:470
  737.0 31.8 %collective-permute-start.59 = (bf16[2,64,2048]{2,1,0:T(8,128)(2,1)}, bf16[2,64,2048]{2,1,0:T(8,128)(2,1)}, u32[]{:S(2)}, u32[]{:S(2)}) collective-permute-start(bf16[2,64,2048]{2,1,0:T(8,128)(2,1)} %fusion.46), channel_id=1, source_target_pairs={{0,2},{1,3},{2,0},{3,1},{4,6},{5,7},{6,4},{7,5},{8,10},{9,11},{10,... | collective-permute-start | bytes 1572872 | tf_op jit(solution)/shard_map/ppermute | solution.py:128
  (153 other events, 2308.5 us)

commit v12 on v11

--- a/solution.py
+++ b/solution.py
@@ -268,7 +268,9 @@
     w_qkv_full = g_qkv.reshape(3, D, qw_here)
     w_out_full = jnp.moveaxis(g_out, 0, 1).reshape(qw_here, D)
     w_down_full = jnp.moveaxis(g_down, 0, 1).reshape(ff_here, D)
-    w_gateup_perm = g_gateup.reshape(2, D, ff_here)
+    w_gateup_perm = jnp.transpose(
+        g_gateup.reshape(2, 4, 2, 4, D // fsdp_count, ff_here), (0, 3, 2, 1, 4, 5)
+    ).reshape(2, D, ff_here)
     unpacked = []
     start = 0
     for p in small:
@@ -361,9 +363,8 @@
     hidden = inputs_rows + attn_rows
     normed_ffn, norm_ffn_pull = jax.vjp(partial(rows_norm, gain_vector=gain_ffn), hidden)
     ffn_full = gather_rows(normed_ffn.astype(jnp.bfloat16))
-    ffn_perm = to_yzx(ffn_full)
-    gate_lin, gate_low = column_forward(ffn_full, w_gateup_perm[0], a_in_sel[:, 3], b_gateup_sel[:, 0], ffn_perm)
-    up_lin, up_low = column_forward(ffn_full, w_gateup_perm[1], a_in_sel[:, 4], b_gateup_sel[:, 1], ffn_perm)
+    gate_lin, gate_low = column_forward(ffn_full, w_gateup_perm[0], a_in_sel[:, 3], b_gateup_sel[:, 0])
+    up_lin, up_low = column_forward(ffn_full, w_gateup_perm[1], a_in_sel[:, 4], b_gateup_sel[:, 1])
     product_float, swiglu_pull = jax.vjp(swiglu, gate_lin, up_lin)
     product = product_float.astype(jnp.bfloat16)
     ffn_rows, down_low = row_forward(product, w_down_full, a_down_sel, b_rows_sel[:, 1])
@@ -414,7 +415,6 @@
             (grad_gate.astype(jnp.bfloat16), w_gateup_perm[0], a_in_sel[:, 3], b_gateup_sel[:, 0], gate_low),
             (grad_up.astype(jnp.bfloat16), w_gateup_perm[1], a_in_sel[:, 4], b_gateup_sel[:, 1], up_low),
         ),
-        from_yzx,
     )
     grad_hidden = tangent + norm_ffn_pull(grad_ffn_rows)[0]
     grad_attn_full = gather_rows(grad_hidden.astype(jnp.bfloat16))

time: 786 us -> 748 us (0.952)
  local copies, waits for them, and re-layouts: 288 us -> 271 us
  waiting for transfers between devices: 152 us -> 139 us
  matrix products: 134 us -> 125 us
    ppermute x10, waiting for transfers between devices: 15.3 us -> 1.9 us  [ring_stage(): from_right = lax.ppermute(stacks, 'fsdp', fsdp_pairs(kind, -1))]
    transpose x3 -> x0, local copies, waits for them, and re-layouts: 11.8 us -> none  [the longest x1 7.08 us: to_yzx(): return jnp.transpose(split, order).reshape(values.shape)]
    reshape x2 -> x0, local copies, waits for them, and re-layouts: 10.8 us -> none  [from_yzx(): return jnp.transpose(split, order).reshape(values.shape)]
    unnamed x283 -> x277, local copies, waits for them, and re-layouts: 22 us -> 23 us
  transfers between devices with their start and end apart: 67 -> 67, of which waited for: 23 -> 24; matrix products, arithmetic and copies ran while one was open for 52% -> 55% of each run, Pallas kernels for 0% -> 0%
where the time goes in v12:
time: 748 us; the launch traced here: 735 us
  local copies, waits for them, and re-layouts  271 us (36%)
  waiting for transfers between devices  139 us (19%)
  starting transfers between devices  126 us (17%)
  matrix products  125 us (17%)
  other arithmetic  65.8 us (9%)
  between operations  8.71 us (1%)
    dynamic_update_slice x57, local copies, waits for them, and re-layouts, put(): return lax.dynamic_update_slice(buffer, piece, start)  66.9 us
    dot_general x37, matrix products, hp_dot(): jnp.einsum(spec, left, right, precision=highest, preferred_element_type=j...  61 us
    ppermute x4, waiting for transfers between devices, tok_scatter(): got = lax.ppermute(send.astype(jnp.bfloat16), 'tok', xor_pairs(count, 2))  36.2 us
    ppermute x5, waiting for transfers between devices, pair_stage(): other = lax.ppermute(stacks, 'fsdp', fsdp_pairs('z', 1))  25.3 us
    ppermute x10, starting transfers between devices, ring_stage(): from_right = lax.ppermute(stacks, 'fsdp', fsdp_pairs(kind, -1))  25 us
    dot_general x5, matrix products, column_backward(): jnp.einsum('ste,de->std', grad_rows, weight, preferred_element_type=jnp.f...  24.6 us
    unnamed x277, local copies, waits for them, and re-layouts  23 us
    ppermute x4, starting transfers between devices, tok_scatter(): chip_sum = mine + lax.ppermute(theirs, 'tok', xor_pairs(count, 1))  21.7 us
  transfers between devices with their start and end apart: 67, of which 24 were waited for; matrix products, arithmetic and copies ran while one was open for 55% of the time, Pallas kernels for 0%

profile of v12, /device:TPU:1, one launch (start us, length us, event | category | flops | bytes accessed | tf_op | source)
XLA Modules:
  0.0 734.8 jit_solution(3738616696094019975)
XLA Ops:
  0.7 3.6 collective-permute-start.42
  7.0 3.6 collective-permute-start.12
  31.0 4.1 collective-permute-done.10
  65.5 5.3 collective-permute-done.44
  73.7 5.6 collective-permute-done.16
  96.9 6.9 collective-permute-start.1
  118.3 7.3 collective-permute-done.5
  139.7 16.8 %collective-permute-done.37 = bf16[2,4,64,1408]{3,2,1,0:T(8,128)(2,1)S(1)} collective-permute-done((bf16[2,4,64,1408]{3,2,1,0:T(8,128)(2,1)}, bf16[2,4,64,1408]{3,2,1,0:T(8,128)(2,1)S(1)}, u32[]{:S(2)}, u32[]{:S(2)}) %collective-permute-start.37) | collective-permute-done | bytes 1441824 | tf_op jit(solution)/shard_map/ppermute | solution.py:180
  159.8 5.7 broadcast_in_dim.134
  165.5 3.6 constant_dynamic-update-slice_fusion.21
  170.6 3.6 collective-permute-start.38
  194.3 17.5 %collective-permute-done.7 = bf16[3,8,64,512]{3,2,1,0:T(8,128)(2,1)} collective-permute-done((bf16[3,8,64,512]{3,2,1,0:T(8,128)(2,1)}, bf16[3,8,64,512]{3,2,1,0:T(8,128)(2,1)}, u32[]{:S(2)}, u32[]{:S(2)}) %collective-permute-start.7) | collective-permute-done | bytes 1572896 | tf_op jit(solution)/shard_map/ppermute | solution.py:190
  222.1 3.8 collective-permute-done.20
  229.3 3.7 collective-permute-start.9
  238.4 3.7 constant_dynamic-slice_fusion.14
  252.9 4.8 copy.277
  257.7 6.4 copy.278
  264.1 3.5 constant_dynamic-slice_fusion.10
  296.0 5.8 fusion.121
  307.9 4.1 convolution_add_fusion.2
  333.3 20.8 %collective-permute-start.30 = (f32[2,2,64,2048]{3,2,0,1:T(8,128)}, f32[2,2,64,2048]{3,2,0,1:T(8,128)}, u32[]{:S(2)}, u32[]{:S(2)}) collective-permute-start(f32[2,2,64,2048]{3,2,0,1:T(8,128)} %bitcast.503), channel_id=1, source_target_pairs={{0,1},{1,0},{2,3},{3,2},{4,5},{5,4},{6,7},{7,6},{8,9},{9,8},{10,11... | collective-permute-start | bytes 6291464 | tf_op jit(solution)/shard_map/ppermute | solution.py:125
  386.5 3.7 constant_dynamic-update-slice_fusion.20
  390.2 3.6 constant_dynamic-update-slice_fusion.19
  393.8 5.5 collective-permute-done.31
  401.8 11.2 %collective-permute-done.40 = bf16[2,4,64,1408]{3,2,1,0:T(8,128)(2,1)S(1)} collective-permute-done((bf16[2,4,64,1408]{3,2,1,0:T(8,128)(2,1)S(1)}, bf16[2,4,64,1408]{3,2,1,0:T(8,128)(2,1)S(1)}, u32[]{:S(2)}, u32[]{:S(2)}) %collective-permute-start.40) | collective-permute-done | bytes 1441824 | tf_op jit(solution)/shard_map/ppermute | solution.py:194
  417.6 9.7 %fusion.120 = (bf16[1,4,2,4,64,1408]{5,4,1,2,3,0:T(8,128)(2,1)}, bf16[1,4,2,4,64,1408]{5,4,1,2,3,0:T(8,128)(2,1)}) fusion(bf16[2,4,2,4,64,1408]{5,4,1,2,3,0:T(8,128)(2,1)} %bitcast.80), kind=kLoop, calls=%fused_computation.348 | loop fusion | bytes 23068672 | tf_op jit(solution)/shard_map/slice | solution.py:366
  427.3 3.3 copy.286
  434.4 3.4 fusion.128
  438.5 3.4 fusion.127
  448.2 7.1 fusion.8
  455.8 5.0 fusion.132
  461.3 3.4 fusion.133
  475.6 3.5 multiply_add_fusion
  495.5 9.2 %collective-permute-done.55 = bf16[2,64,2048]{2,1,0:T(8,128)(2,1)S(1)} collective-permute-done((bf16[2,64,2048]{2,1,0:T(8,128)(2,1)S(1)}, bf16[2,64,2048]{2,1,0:T(8,128)(2,1)S(1)}, u32[]{:S(2)}, u32[]{:S(2)}) %collective-permute-start.55) | collective-permute-done | bytes 524320 | tf_op jit(solution)/shard_map/ppermute | solution.py:128
  505.0 10.9 %collective-permute-done.51 = bf16[2,64,2048]{2,1,0:T(8,128)(2,1)S(1)} collective-permute-done((bf16[2,64,2048]{2,1,0:T(8,128)(2,1)S(1)}, bf16[2,64,2048]{2,1,0:T(8,128)(2,1)S(1)}, u32[]{:S(2)}, u32[]{:S(2)}) %collective-permute-start.51) | collective-permute-done | bytes 524320 | tf_op jit(solution)/shard_map/ppermute | solution.py:128
  521.9 9.9 %collective-permute-done.56 = bf16[2,64,2048]{2,1,0:T(8,128)(2,1)S(1)} collective-permute-done((bf16[2,64,2048]{2,1,0:T(8,128)(2,1)S(1)}, bf16[2,64,2048]{2,1,0:T(8,128)(2,1)S(1)}, u32[]{:S(2)}, u32[]{:S(2)}) %collective-permute-start.56) | collective-permute-done | bytes 524320 | tf_op jit(solution)/shard_map/ppermute | solution.py:106
  549.8 5.6 all-to-all-start.2
  561.9 3.8 convolution_add_fusion.1
  590.4 4.6 multiply_add_fusion.5
  601.8 5.2 fusion.135
  612.5 5.2 fusion.136
  634.2 5.8 add_add_fusion
  666.3 7.5 %all-to-all-start.1 = ((bf16[32,64,128]{2,1,0:T(8,128)(2,1)}), bf16[32,64,128]{2,1,0:T(8,128)(2,1)}, u32[]{:S(2)}, u32[]{:S(2)}) async-start(bf16[32,64,128]{2,1,0:T(8,128)(2,1)} %pad_maximum_fusion.8), calls=%async_computation.1 | async-start | bytes 1048576 | tf_op jit(solution)/shard_map/all_to_all | solution.py:470
  673.8 4.4 pad_maximum_fusion
  678.2 5.9 copy.318
  687.0 7.8 %all-to-all-start = ((f32[32,112,128]{2,1,0:T(8,128)}), f32[32,112,128]{2,1,0:T(8,128)}, u32[]{:S(2)}, u32[]{:S(2)}) async-start(f32[32,112,128]{2,1,0:T(8,128)} %pad_maximum_fusion.2), calls=%async_computation | async-start | bytes 3670016 | tf_op jit(solution)/shard_map/all_to_all | solution.py:470
  706.8 10.2 %all-to-all-done = f32[32,112,128]{2,1,0:T(8,128)} async-done(((f32[32,112,128]{2,1,0:T(8,128)}), f32[32,112,128]{2,1,0:T(8,128)}, u32[]{:S(2)}, u32[]{:S(2)}) %all-to-all-start) | async-done | bytes 1835040 | tf_op jit(solution)/shard_map/all_to_all | solution.py:470
  720.0 10.6 %collective-permute-done.59 = bf16[2,64,2048]{2,1,0:T(8,128)(2,1)} collective-permute-done((bf16[2,64,2048]{2,1,0:T(8,128)(2,1)}, bf16[2,64,2048]{2,1,0:T(8,128)(2,1)}, u32[]{:S(2)}, u32[]{:S(2)}) %collective-permute-start.59) | collective-permute-done | bytes 524320 | tf_op jit(solution)/shard_map/ppermute | solution.py:128
  (691 shorter events, 416.7 us)
Async XLA Ops:
  0.7 51.8 %collective-permute-start.42 = (bf16[1,1408,64]{1,2,0:T(8,128)(2,1)}, bf16[1,1408,64]{1,2,0:T(8,128)(2,1)}, u32[]{:S(2)}, u32[]{:S(2)}) collective-permute-start(bf16[1,1408,64]{1,2,0:T(8,128)(2,1)} %bitcast.627), channel_id=1, source_target_pairs={{0,12},{4,0},{8,4},{12,8},{16,28},{20,16},{24,20},{28,24},{32,44},... | collective-permute-start | bytes 540680 | tf_op jit(solution)/shard_map/ppermute | solution.py:191
  4.3 49.2 %collective-permute-start.43 = (bf16[1,1408,64]{1,2,0:T(8,128)(2,1)}, bf16[1,1408,64]{1,2,0:T(8,128)(2,1)}, u32[]{:S(2)}, u32[]{:S(2)}) collective-permute-start(bf16[1,1408,64]{1,2,0:T(8,128)(2,1)} %bitcast.628), channel_id=1, source_target_pairs={{0,4},{4,8},{8,12},{12,0},{16,20},{20,24},{24,28},{28,16},{32,36},... | collective-permute-start | bytes 540680 | tf_op jit(solution)/shard_map/ppermute | solution.py:190
  4.3 39.7 %collective-permute-start.22 = (bf16[1,512,64]{1,2,0:T(8,128)(2,1)}, bf16[1,512,64]{1,2,0:T(8,128)(2,1)}, u32[]{:S(2)}, u32[]{:S(2)}) collective-permute-start(bf16[1,512,64]{1,2,0:T(8,128)(2,1)} %bitcast.633), channel_id=1, source_target_pairs={{0,12},{4,0},{8,4},{12,8},{16,28},{20,16},{24,20},{28,24},{32,44},... | collective-permute-start | bytes 196616 | tf_op jit(solution)/shard_map/ppermute | solution.py:191
  7.0 37.2 %collective-permute-start.23 = (bf16[1,512,64]{1,2,0:T(8,128)(2,1)}, bf16[1,512,64]{1,2,0:T(8,128)(2,1)}, u32[]{:S(2)}, u32[]{:S(2)}) collective-permute-start(bf16[1,512,64]{1,2,0:T(8,128)(2,1)} %bitcast.634), channel_id=1, source_target_pairs={{0,4},{4,8},{8,12},{12,0},{16,20},{20,24},{24,28},{28,16},{32,36},... | collective-permute-start | bytes 196616 | tf_op jit(solution)/shard_map/ppermute | solution.py:190
  7.0 23.9 %collective-permute-start.12 = (bf16[2,128,16]{1,2,0:T(8,128)(2,1)}, bf16[2,128,16]{1,2,0:T(8,128)(2,1)S(1)}, u32[]{:S(2)}, u32[]{:S(2)}) collective-permute-start(bf16[2,128,16]{1,2,0:T(8,128)(2,1)} %param.35), channel_id=1, source_target_pairs={{0,2},{1,3},{2,0},{3,1},{4,6},{5,7},{6,4},{7,5},{8,10},{9,11},{10,... | collective-permute-start | bytes 24584 | tf_op jit(solution)/shard_map/ppermute | solution.py:106
  40.5 24.1 %collective-permute-start.34 = (bf16[2,1,64,1408]{3,2,1,0:T(8,128)(2,1)}, bf16[2,1,64,1408]{3,2,1,0:T(8,128)(2,1)S(1)}, u32[]{:S(2)}, u32[]{:S(2)}) collective-permute-start(bf16[2,1,64,1408]{3,2,1,0:T(8,128)(2,1)} %bitcast.620), channel_id=1, source_target_pairs={{0,96},{4,100},{8,104},{12,108},{16,112},{20,116},{24,120},{28,124... | collective-permute-start | bytes 1081352 | tf_op jit(solution)/shard_map/ppermute | solution.py:191
  44.1 28.9 %collective-permute-start.35 = (bf16[2,1,64,1408]{3,2,1,0:T(8,128)(2,1)}, bf16[2,1,64,1408]{3,2,1,0:T(8,128)(2,1)S(1)}, u32[]{:S(2)}, u32[]{:S(2)}) collective-permute-start(bf16[2,1,64,1408]{3,2,1,0:T(8,128)(2,1)} %bitcast.621), channel_id=1, source_target_pairs={{0,32},{4,36},{8,40},{12,44},{16,48},{20,52},{24,56},{28,60},{32,6... | collective-permute-start | bytes 1081352 | tf_op jit(solution)/shard_map/ppermute | solution.py:190
  53.6 33.7 %collective-permute-start = (bf16[2,64,2048]{2,1,0:T(8,128)(2,1)S(1)}, bf16[2,64,2048]{2,1,0:T(8,128)(2,1)S(1)}, u32[]{:S(2)}, u32[]{:S(2)}) collective-permute-start(bf16[2,64,2048]{2,1,0:T(8,128)(2,1)S(1)} %copy-done.73), channel_id=1, source_target_pairs={{0,2},{1,3},{2,0},{3,1},{4,6},{5,7},{6,4},{7,5},{8,10},{9,11},{10,... | collective-permute-start | bytes 1572872 | tf_op jit(solution)/shard_map/ppermute | solution.py:106
  59.6 30.8 %collective-permute-start.52 = (bf16[2,64,2048]{2,1,0:T(8,128)(2,1)S(1)}, bf16[2,64,2048]{2,1,0:T(8,128)(2,1)S(1)}, u32[]{:S(2)}, u32[]{:S(2)}) collective-permute-start(bf16[2,64,2048]{2,1,0:T(8,128)(2,1)S(1)} %copy-done.33), channel_id=1, source_target_pairs={{0,2},{1,3},{2,0},{3,1},{4,6},{5,7},{6,4},{7,5},{8,10},{9,11},{10,... | collective-permute-start | bytes 1572872 | tf_op jit(solution)/shard_map/ppermute | solution.py:106
  64.0 17.7 %collective-permute-start.25 = (bf16[4,512,64]{1,2,0:T(8,128)(2,1)S(1)}, bf16[4,512,64]{1,2,0:T(8,128)(2,1)S(1)}, u32[]{:S(2)}, u32[]{:S(2)}) collective-permute-start(bf16[4,512,64]{1,2,0:T(8,128)(2,1)S(1)} %copy-done.66), channel_id=1, source_target_pairs={{0,16},{4,20},{8,24},{12,28},{16,0},{20,4},{24,8},{28,12},{32,48},... | collective-permute-start | bytes 786440 | tf_op jit(solution)/shard_map/ppermute | solution.py:180
  79.3 35.0 %collective-permute-start.45 = (bf16[4,1408,64]{1,2,0:T(8,128)(2,1)S(1)}, bf16[4,1408,64]{1,2,0:T(8,128)(2,1)S(1)}, u32[]{:S(2)}, u32[]{:S(2)}) collective-permute-start(bf16[4,1408,64]{1,2,0:T(8,128)(2,1)S(1)} %constant_dynamic-update-slice_fusion.13), channel_id=1, source_target_pairs={{0,16},{4,20},{8,24},{12,28},{16,0},{20,4},{24,8},{28,12},{32,48},... | collective-permute-start | bytes 2162696 | tf_op jit(solution)/shard_map/ppermute | solution.py:180
  84.2 24.5 %collective-permute-start.17 = (bf16[4,644,128]{2,0,1:T(4,128)(2,1)S(1)}, bf16[4,644,128]{2,0,1:T(4,128)(2,1)S(1)}, u32[]{:S(2)}, u32[]{:S(2)}) collective-permute-start(bf16[4,644,128]{2,0,1:T(4,128)(2,1)S(1)} %copy.254), channel_id=1, source_target_pairs={{0,16},{4,20},{8,24},{12,28},{16,0},{20,4},{24,8},{28,12},{32,48},... | collective-permute-start | bytes 1978376 | tf_op jit(solution)/shard_map/ppermute | solution.py:180
  90.4 14.3 %collective-permute-start.27 = (bf16[8,512,64]{1,2,0:T(8,128)(2,1)S(1)}, bf16[8,512,64]{1,2,0:T(8,128)(2,1)S(1)}, u32[]{:S(2)}, u32[]{:S(2)}) collective-permute-start(bf16[8,512,64]{1,2,0:T(8,128)(2,1)S(1)} %constant_dynamic-update-slice_fusion.33), channel_id=1, source_target_pairs={{0,32},{4,36},{8,40},{12,44},{16,48},{20,52},{24,56},{28,60},{32,6... | collective-permute-start | bytes 1572872 | tf_op jit(solution)/shard_map/ppermute | solution.py:190
  90.8 34.7 %collective-permute-start.5 = (bf16[3,4,64,512]{3,2,1,0:T(8,128)(2,1)S(1)}, bf16[3,4,64,512]{3,2,1,0:T(8,128)(2,1)S(1)}, u32[]{:S(2)}, u32[]{:S(2)}) collective-permute-start(bf16[3,4,64,512]{3,2,1,0:T(8,128)(2,1)S(1)} %bitcast_dynamic-update-slice_fusion.1), channel_id=1, source_target_pairs={{0,16},{4,20},{8,24},{12,28},{16,0},{20,4},{24,8},{28,12},{32,48},... | collective-permute-start | bytes 2359304 | tf_op jit(solution)/shard_map/ppermute | solution.py:180
  96.9 41.8 %collective-permute-start.1 = (bf16[2,2,64,2048]{3,2,1,0:T(8,128)(2,1)S(1)}, bf16[2,2,64,2048]{3,2,1,0:T(8,128)(2,1)S(1)}, u32[]{:S(2)}, u32[]{:S(2)}) collective-permute-start(bf16[2,2,64,2048]{3,2,1,0:T(8,128)(2,1)S(1)} %maximum_select_fusion.4), channel_id=1, source_target_pairs={{0,1},{1,0},{2,3},{3,2},{4,5},{5,4},{6,7},{7,6},{8,9},{9,8},{10,11... | collective-permute-start | bytes 3145736 | tf_op jit(solution)/shard_map/ppermute | solution.py:110
  104.7 31.2 %collective-permute-start.53 = (bf16[2,2,64,2048]{3,2,0,1:T(8,128)(2,1)S(1)}, bf16[2,2,64,2048]{3,2,0,1:T(8,128)(2,1)S(1)}, u32[]{:S(2)}, u32[]{:S(2)}) collective-permute-start(bf16[2,2,64,2048]{3,2,0,1:T(8,128)(2,1)S(1)} %maximum_select_fusion.7), channel_id=1, source_target_pairs={{0,1},{1,0},{2,3},{3,2},{4,5},{5,4},{6,7},{7,6},{8,9},{9,8},{10,11... | collective-permute-start | bytes 3145736 | tf_op jit(solution)/shard_map/ppermute | solution.py:110
  114.3 42.3 %collective-permute-start.37 = (bf16[2,4,64,1408]{3,2,1,0:T(8,128)(2,1)}, bf16[2,4,64,1408]{3,2,1,0:T(8,128)(2,1)S(1)}, u32[]{:S(2)}, u32[]{:S(2)}) collective-permute-start(bf16[2,4,64,1408]{3,2,1,0:T(8,128)(2,1)} %constant_dynamic-update-slice_fusion.24), channel_id=1, source_target_pairs={{0,16},{4,20},{8,24},{12,28},{16,0},{20,4},{24,8},{28,12},{32,48},... | collective-permute-start | bytes 4325384 | tf_op jit(solution)/shard_map/ppermute | solution.py:180
  115.6 14.5 %collective-permute-start.29 = (bf16[4,512,64]{1,2,0:T(8,128)(2,1)S(1)}, bf16[4,512,64]{1,2,0:T(8,128)(2,1)S(1)}, u32[]{:S(2)}, u32[]{:S(2)}) collective-permute-start(bf16[4,512,64]{1,2,0:T(8,128)(2,1)S(1)} %slice.261), channel_id=1, source_target_pairs={{0,96},{4,100},{8,104},{12,108},{16,112},{20,116},{24,120},{28,124... | collective-permute-start | bytes 786440 | tf_op jit(solution)/shard_map/ppermute | solution.py:195
  125.5 33.0 %collective-permute-start.19 = (bf16[8,644,128]{2,0,1:T(8,128)(2,1)}, bf16[8,644,128]{2,0,1:T(8,128)(2,1)}, u32[]{:S(2)}, u32[]{:S(2)}) collective-permute-start(bf16[8,644,128]{2,0,1:T(8,128)(2,1)} %copy.256), channel_id=1, source_target_pairs={{0,32},{4,36},{8,40},{12,44},{16,48},{20,52},{24,56},{28,60},{32,6... | collective-permute-start | bytes 3956744 | tf_op jit(solution)/shard_map/ppermute | solution.py:190
  130.1 40.5 %collective-permute-start.18 = (bf16[8,644,128]{2,0,1:T(8,128)(2,1)}, bf16[8,644,128]{2,0,1:T(8,128)(2,1)}, u32[]{:S(2)}, u32[]{:S(2)}) collective-permute-start(bf16[8,644,128]{2,0,1:T(8,128)(2,1)} %copy.256), channel_id=1, source_target_pairs={{0,96},{4,100},{8,104},{12,108},{16,112},{20,116},{24,120},{28,124... | collective-permute-start | bytes 3956744 | tf_op jit(solution)/shard_map/ppermute | solution.py:191
  135.9 45.7 %collective-permute-start.46 = (bf16[8,1408,64]{1,2,0:T(8,128)(2,1)}, bf16[8,1408,64]{1,2,0:T(8,128)(2,1)}, u32[]{:S(2)}, u32[]{:S(2)}) collective-permute-start(bf16[8,1408,64]{1,2,0:T(8,128)(2,1)} %constant_dynamic-update-slice_fusion.11), channel_id=1, source_target_pairs={{0,96},{4,100},{8,104},{12,108},{16,112},{20,116},{24,120},{28,124... | collective-permute-start | bytes 4325384 | tf_op jit(solution)/shard_map/ppermute | solution.py:191
  138.7 46.7 %collective-permute-start.47 = (bf16[8,1408,64]{1,2,0:T(8,128)(2,1)}, bf16[8,1408,64]{1,2,0:T(8,128)(2,1)}, u32[]{:S(2)}, u32[]{:S(2)}) collective-permute-start(bf16[8,1408,64]{1,2,0:T(8,128)(2,1)} %constant_dynamic-update-slice_fusion.11), channel_id=1, source_target_pairs={{0,32},{4,36},{8,40},{12,44},{16,48},{20,52},{24,56},{28,60},{32,6... | collective-permute-start | bytes 4325384 | tf_op jit(solution)/shard_map/ppermute | solution.py:190
  156.5 60.3 %collective-permute-start.6 = (bf16[3,8,64,512]{3,2,1,0:T(8,128)(2,1)}, bf16[3,8,64,512]{3,2,1,0:T(8,128)(2,1)}, u32[]{:S(2)}, u32[]{:S(2)}) collective-permute-start(bf16[3,8,64,512]{3,2,1,0:T(8,128)(2,1)} %constant_dynamic-update-slice_fusion.50), channel_id=1, source_target_pairs={{0,96},{4,100},{8,104},{12,108},{16,112},{20,116},{24,120},{28,124... | collective-permute-start | bytes 4718600 | tf_op jit(solution)/shard_map/ppermute | solution.py:191
  158.5 53.2 %collective-permute-start.7 = (bf16[3,8,64,512]{3,2,1,0:T(8,128)(2,1)}, bf16[3,8,64,512]{3,2,1,0:T(8,128)(2,1)}, u32[]{:S(2)}, u32[]{:S(2)}) collective-permute-start(bf16[3,8,64,512]{3,2,1,0:T(8,128)(2,1)} %constant_dynamic-update-slice_fusion.50), channel_id=1, source_target_pairs={{0,32},{4,36},{8,40},{12,44},{16,48},{20,52},{24,56},{28,60},{32,6... | collective-permute-start | bytes 4718600 | tf_op jit(solution)/shard_map/ppermute | solution.py:190
  170.6 208.0 %collective-permute-start.38 = (bf16[2,8,64,1408]{3,2,1,0:T(8,128)(2,1)}, bf16[2,8,64,1408]{3,2,1,0:T(8,128)(2,1)}, u32[]{:S(2)}, u32[]{:S(2)}) collective-permute-start(bf16[2,8,64,1408]{3,2,1,0:T(8,128)(2,1)} %constant_dynamic-update-slice_fusion.22), channel_id=1, source_target_pairs={{0,12},{4,0},{8,4},{12,8},{16,28},{20,16},{24,20},{28,24},{32,44},... | collective-permute-start | bytes 8650760 | tf_op jit(solution)/shard_map/ppermute | solution.py:191
  181.6 44.3 %collective-permute-start.20 = (bf16[4,644,128]{2,0,1:T(4,128)(2,1)S(1)}, bf16[4,644,128]{2,0,1:T(4,128)(2,1)S(1)}, u32[]{:S(2)}, u32[]{:S(2)}) collective-permute-start(bf16[4,644,128]{2,0,1:T(4,128)(2,1)S(1)} %slice.239), channel_id=1, source_target_pairs={{0,32},{4,36},{8,40},{12,44},{16,48},{20,52},{24,56},{28,60},{32,6... | collective-permute-start | bytes 1978376 | tf_op jit(solution)/shard_map/ppermute | solution.py:194
  185.4 43.9 %collective-permute-start.21 = (bf16[4,644,128]{2,0,1:T(4,128)(2,1)S(1)}, bf16[4,644,128]{2,0,1:T(4,128)(2,1)S(1)}, u32[]{:S(2)}, u32[]{:S(2)}) collective-permute-start(bf16[4,644,128]{2,0,1:T(4,128)(2,1)S(1)} %slice.240), channel_id=1, source_target_pairs={{0,96},{4,100},{8,104},{12,108},{16,112},{20,116},{24,120},{28,124... | collective-permute-start | bytes 1978376 | tf_op jit(solution)/shard_map/ppermute | solution.py:195
  211.7 165.3 %collective-permute-start.39 = (bf16[2,8,64,1408]{3,2,1,0:T(8,128)(2,1)}, bf16[2,8,64,1408]{3,2,1,0:T(8,128)(2,1)}, u32[]{:S(2)}, u32[]{:S(2)}) collective-permute-start(bf16[2,8,64,1408]{3,2,1,0:T(8,128)(2,1)} %constant_dynamic-update-slice_fusion.22), channel_id=1, source_target_pairs={{0,4},{4,8},{8,12},{12,0},{16,20},{20,24},{24,28},{28,16},{32,36},... | collective-permute-start | bytes 8650760 | tf_op jit(solution)/shard_map/ppermute | solution.py:190
  216.8 156.2 %collective-permute-start.48 = (bf16[4,1408,64]{1,2,0:T(8,128)(2,1)}, bf16[4,1408,64]{1,2,0:T(8,128)(2,1)}, u32[]{:S(2)}, u32[]{:S(2)}) collective-permute-start(bf16[4,1408,64]{1,2,0:T(8,128)(2,1)} %slice.275), channel_id=1, source_target_pairs={{0,32},{4,36},{8,40},{12,44},{16,48},{20,52},{24,56},{28,60},{32,6... | collective-permute-start | bytes 2162696 | tf_op jit(solution)/shard_map/ppermute | solution.py:194
  225.9 65.7 %collective-permute-start.8 = (bf16[3,4,64,512]{3,2,1,0:T(8,128)(2,1)}, bf16[3,4,64,512]{3,2,1,0:T(8,128)(2,1)}, u32[]{:S(2)}, u32[]{:S(2)}) collective-permute-start(bf16[3,4,64,512]{3,2,1,0:T(8,128)(2,1)} %slice.236), channel_id=1, source_target_pairs={{0,32},{4,36},{8,40},{12,44},{16,48},{20,52},{24,56},{28,60},{32,6... | collective-permute-start | bytes 2359304 | tf_op jit(solution)/shard_map/ppermute | solution.py:194
  229.3 64.6 %collective-permute-start.9 = (bf16[3,4,64,512]{3,2,1,0:T(8,128)(2,1)}, bf16[3,4,64,512]{3,2,1,0:T(8,128)(2,1)}, u32[]{:S(2)}, u32[]{:S(2)}) collective-permute-start(bf16[3,4,64,512]{3,2,1,0:T(8,128)(2,1)} %slice.237), channel_id=1, source_target_pairs={{0,96},{4,100},{8,104},{12,108},{16,112},{20,116},{24,120},{28,124... | collective-permute-start | bytes 2359304 | tf_op jit(solution)/shard_map/ppermute | solution.py:195
  291.6 83.5 %collective-permute-start.49 = (bf16[4,1408,64]{1,2,0:T(8,128)(2,1)}, bf16[4,1408,64]{1,2,0:T(8,128)(2,1)}, u32[]{:S(2)}, u32[]{:S(2)}) collective-permute-start(bf16[4,1408,64]{1,2,0:T(8,128)(2,1)} %slice.276), channel_id=1, source_target_pairs={{0,96},{4,100},{8,104},{12,108},{16,112},{20,116},{24,120},{28,124... | collective-permute-start | bytes 2162696 | tf_op jit(solution)/shard_map/ppermute | solution.py:195
  333.3 49.6 %collective-permute-start.30 = (f32[2,2,64,2048]{3,2,0,1:T(8,128)}, f32[2,2,64,2048]{3,2,0,1:T(8,128)}, u32[]{:S(2)}, u32[]{:S(2)}) collective-permute-start(f32[2,2,64,2048]{3,2,0,1:T(8,128)} %bitcast.503), channel_id=1, source_target_pairs={{0,1},{1,0},{2,3},{3,2},{4,5},{5,4},{6,7},{7,6},{8,9},{9,8},{10,11... | collective-permute-start | bytes 6291464 | tf_op jit(solution)/shard_map/ppermute | solution.py:125
  378.6 34.5 %collective-permute-start.40 = (bf16[2,4,64,1408]{3,2,1,0:T(8,128)(2,1)S(1)}, bf16[2,4,64,1408]{3,2,1,0:T(8,128)(2,1)S(1)}, u32[]{:S(2)}, u32[]{:S(2)}) collective-permute-start(bf16[2,4,64,1408]{3,2,1,0:T(8,128)(2,1)S(1)} %slice.266), channel_id=1, source_target_pairs={{0,4},{4,8},{8,12},{12,0},{16,20},{20,24},{24,28},{28,16},{32,36},... | collective-permute-start | bytes 4325384 | tf_op jit(solution)/shard_map/ppermute | solution.py:194
  380.3 34.0 %collective-permute-start.41 = (bf16[2,4,64,1408]{3,2,1,0:T(8,128)(2,1)S(1)}, bf16[2,4,64,1408]{3,2,1,0:T(8,128)(2,1)S(1)}, u32[]{:S(2)}, u32[]{:S(2)}) collective-permute-start(bf16[2,4,64,1408]{3,2,1,0:T(8,128)(2,1)S(1)} %slice.267), channel_id=1, source_target_pairs={{0,12},{4,0},{8,4},{12,8},{16,28},{20,16},{24,20},{28,24},{32,44},... | collective-permute-start | bytes 4325384 | tf_op jit(solution)/shard_map/ppermute | solution.py:195
  384.8 14.5 %collective-permute-start.31 = (bf16[2,64,2048]{2,1,0:T(8,128)(2,1)S(1)}, bf16[2,64,2048]{2,1,0:T(8,128)(2,1)S(1)}, u32[]{:S(2)}, u32[]{:S(2)}) collective-permute-start(bf16[2,64,2048]{2,1,0:T(8,128)(2,1)S(1)} %fusion.43), channel_id=1, source_target_pairs={{0,2},{1,3},{2,0},{3,1},{4,6},{5,7},{6,4},{7,5},{8,10},{9,11},{10,... | collective-permute-start | bytes 1572872 | tf_op jit(solution)/shard_map/ppermute | solution.py:128
  399.8 15.8 %collective-permute-start.32 = (bf16[2,64,2048]{2,1,0:T(8,128)(2,1)S(1)}, bf16[2,64,2048]{2,1,0:T(8,128)(2,1)S(1)}, u32[]{:S(2)}, u32[]{:S(2)}) collective-permute-start(bf16[2,64,2048]{2,1,0:T(8,128)(2,1)S(1)} %multiply_convert_fusion.3), channel_id=1, source_target_pairs={{0,2},{1,3},{2,0},{3,1},{4,6},{5,7},{6,4},{7,5},{8,10},{9,11},{10,... | collective-permute-start | bytes 1572872 | tf_op jit(solution)/shard_map/ppermute | solution.py:106
  416.7 15.7 %collective-permute-start.33 = (bf16[2,2,64,2048]{3,2,0,1:T(8,128)(2,1)}, bf16[2,2,64,2048]{3,2,0,1:T(8,128)(2,1)S(1)}, u32[]{:S(2)}, u32[]{:S(2)}) collective-permute-start(bf16[2,2,64,2048]{3,2,0,1:T(8,128)(2,1)} %maximum_select_fusion.6), channel_id=1, source_target_pairs={{0,1},{1,0},{2,3},{3,2},{4,5},{5,4},{6,7},{7,6},{8,9},{9,8},{10,11... | collective-permute-start | bytes 3145736 | tf_op jit(solution)/shard_map/ppermute | solution.py:110
  489.5 15.1 %collective-permute-start.55 = (bf16[2,64,2048]{2,1,0:T(8,128)(2,1)S(1)}, bf16[2,64,2048]{2,1,0:T(8,128)(2,1)S(1)}, u32[]{:S(2)}, u32[]{:S(2)}) collective-permute-start(bf16[2,64,2048]{2,1,0:T(8,128)(2,1)S(1)} %fusion.45), channel_id=1, source_target_pairs={{0,2},{1,3},{2,0},{3,1},{4,6},{5,7},{6,4},{7,5},{8,10},{9,11},{10,... | collective-permute-start | bytes 1572872 | tf_op jit(solution)/shard_map/ppermute | solution.py:128
  493.3 22.5 %collective-permute-start.51 = (bf16[2,64,2048]{2,1,0:T(8,128)(2,1)S(1)}, bf16[2,64,2048]{2,1,0:T(8,128)(2,1)S(1)}, u32[]{:S(2)}, u32[]{:S(2)}) collective-permute-start(bf16[2,64,2048]{2,1,0:T(8,128)(2,1)S(1)} %fusion.44), channel_id=1, source_target_pairs={{0,2},{1,3},{2,0},{3,1},{4,6},{5,7},{6,4},{7,5},{8,10},{9,11},{10,... | collective-permute-start | bytes 1572872 | tf_op jit(solution)/shard_map/ppermute | solution.py:128
  519.2 25.9 %collective-permute-start.62 = (f32[2,2,256,16]{2,3,1,0:T(8,128)S(1)}, f32[2,2,256,16]{2,3,1,0:T(8,128)S(1)}, u32[]{:S(2)}, u32[]{:S(2)}) collective-permute-start(f32[2,2,256,16]{2,3,1,0:T(8,128)S(1)} %pad_maximum_fusion.11), channel_id=1, source_target_pairs={{0,1},{1,0},{2,3},{3,2},{4,5},{5,4},{6,7},{7,6},{8,9},{9,8},{10,11... | collective-permute-start | bytes 196616 | tf_op jit(solution)/shard_map/ppermute | solution.py:134
  532.9 24.7 %collective-permute-start.57 = (bf16[2,2,64,2048]{3,2,0,1:T(8,128)(2,1)}, bf16[2,2,64,2048]{3,2,0,1:T(8,128)(2,1)}, u32[]{:S(2)}, u32[]{:S(2)}) collective-permute-start(bf16[2,2,64,2048]{3,2,0,1:T(8,128)(2,1)} %maximum_select_fusion.9), channel_id=1, source_target_pairs={{0,1},{1,0},{2,3},{3,2},{4,5},{5,4},{6,7},{7,6},{8,9},{9,8},{10,11... | collective-permute-start | bytes 3145736 | tf_op jit(solution)/shard_map/ppermute | solution.py:110
  549.8 116.5 %all-to-all-start.2 = ((bf16[32,132,128]{2,1,0:T(8,128)(2,1)}), bf16[32,132,128]{2,1,0:T(8,128)(2,1)}, u32[]{:S(2)}, u32[]{:S(2)}) async-start(bf16[32,132,128]{2,1,0:T(8,128)(2,1)} %pad_maximum_fusion.3), calls=%async_computation.2 | async-start | bytes 2228224 | tf_op jit(solution)/shard_map/all_to_all | solution.py:470
  621.9 22.5 %collective-permute-start.60 = (f32[5,2,256,16]{2,3,1,0:T(8,128)}, f32[5,2,256,16]{2,3,1,0:T(8,128)S(1)}, u32[]{:S(2)}, u32[]{:S(2)}) collective-permute-start(f32[5,2,256,16]{2,3,1,0:T(8,128)} %bitcast_dynamic-update-slice_fusion.4), channel_id=1, source_target_pairs={{0,1},{1,0},{2,3},{3,2},{4,5},{5,4},{6,7},{7,6},{8,9},{9,8},{10,11... | collective-permute-start | bytes 491528 | tf_op jit(solution)/shard_map/ppermute | solution.py:134
  643.4 51.4 %collective-permute-start.58 = (f32[2,2,64,2048]{3,2,0,1:T(8,128)}, f32[2,2,64,2048]{3,2,0,1:T(8,128)}, u32[]{:S(2)}, u32[]{:S(2)}) collective-permute-start(f32[2,2,64,2048]{3,2,0,1:T(8,128)} %bitcast.500), channel_id=1, source_target_pairs={{0,1},{1,0},{2,3},{3,2},{4,5},{5,4},{6,7},{7,6},{8,9},{9,8},{10,11... | collective-permute-start | bytes 6291464 | tf_op jit(solution)/shard_map/ppermute | solution.py:125
  666.3 20.7 %all-to-all-start.1 = ((bf16[32,64,128]{2,1,0:T(8,128)(2,1)}), bf16[32,64,128]{2,1,0:T(8,128)(2,1)}, u32[]{:S(2)}, u32[]{:S(2)}) async-start(bf16[32,64,128]{2,1,0:T(8,128)(2,1)} %pad_maximum_fusion.8), calls=%async_computation.1 | async-start | bytes 1048576 | tf_op jit(solution)/shard_map/all_to_all | solution.py:470
  687.0 30.0 %all-to-all-start = ((f32[32,112,128]{2,1,0:T(8,128)}), f32[32,112,128]{2,1,0:T(8,128)}, u32[]{:S(2)}, u32[]{:S(2)}) async-start(f32[32,112,128]{2,1,0:T(8,128)} %pad_maximum_fusion.2), calls=%async_computation | async-start | bytes 3670016 | tf_op jit(solution)/shard_map/all_to_all | solution.py:470
  698.1 32.5 %collective-permute-start.59 = (bf16[2,64,2048]{2,1,0:T(8,128)(2,1)}, bf16[2,64,2048]{2,1,0:T(8,128)(2,1)}, u32[]{:S(2)}, u32[]{:S(2)}) collective-permute-start(bf16[2,64,2048]{2,1,0:T(8,128)(2,1)} %fusion.46), channel_id=1, source_target_pairs={{0,2},{1,3},{2,0},{3,1},{4,6},{5,7},{6,4},{7,5},{8,10},{9,11},{10,... | collective-permute-start | bytes 1572872 | tf_op jit(solution)/shard_map/ppermute | solution.py:128
  (150 other events, 1467.3 us)

commit v13 on v12

--- a/solution.py
+++ b/solution.py
@@ -279,7 +279,6 @@
         start += rows
     (g_ain, g_brows, g_bqkv, g_bgateup, g_aout, g_adown) = unpacked
     a_in_full = jnp.transpose(g_ain, (2, 0, 1, 3, 4)).reshape(5, D, COLS)
-    b_rows_full = jnp.transpose(g_brows, (2, 3, 0, 1, 4)).reshape(2, COLS, D)
 
     def to_yzx(values):
         lead = values.shape[:-1]
@@ -309,7 +308,14 @@
         )
 
     a_in_sel = pick_cols(a_in_full, 2)
-    b_rows_sel = pick_cols(b_rows_full, 1)
+    b_rows_sel = jnp.stack(
+        [
+            jnp.transpose(
+                lax.dynamic_slice_in_dim(g_brows, offsets[s], RANK, 3), (2, 3, 0, 1, 4)
+            ).reshape(2, RANK, D)
+            for s in range(seqs)
+        ]
+    )
     b_qkv_sel = jnp.moveaxis(pick_groups(g_bqkv), 1, 2).reshape(seqs, 3, RANK, qw_here)
     b_gateup_sel = jnp.moveaxis(pick_groups(g_bgateup), 1, 2).reshape(seqs, 2, RANK, ff_here)
     a_out_sel = jnp.moveaxis(pick_groups(g_aout), 1, 2).reshape(seqs, qw_here, RANK)
@@ -444,14 +450,15 @@
         jnp.arange(COLS)[None, None, :] == offsets[:, None, None] + jnp.arange(RANK)[None, :, None]
     ).astype(jnp.float32)
     wide_lows = hp_dot(grad_lows, onehot, "pstr,src->pstc")
-    dense_a_in = jnp.concatenate(
+    def a_in_rows_mine(dense):
+        split = dense.reshape(dense.shape[0], fsdp_count, tok_count, RANK, COLS)
+        return lax.dynamic_index_in_dim(split, me_tok, 2, keepdims=False)
+
+    a_in_mine = jnp.concatenate(
         [
-            hp_dot(normed_full.astype(jnp.float32), wide_lows[:3], "std,pstc->pdc"),
-            hp_dot(ffn_full.astype(jnp.float32), wide_lows[3:], "std,pstc->pdc"),
+            a_in_rows_mine(hp_dot(normed_full.astype(jnp.float32), wide_lows[:3], "std,pstc->pdc")),
+            a_in_rows_mine(hp_dot(ffn_full.astype(jnp.float32), wide_lows[3:], "std,pstc->pdc")),
         ]
-    )
-    a_in_mine = lax.dynamic_index_in_dim(
-        dense_a_in.reshape(5, fsdp_count, tok_count, RANK, COLS), me_tok, 2, keepdims=False
     )
     wide_row_lows = hp_dot(row_lows, onehot, "qstr,src->qstc")
     dense_b_rows = adapter_scale * hp_dot(

time: 748 us -> 749 us (level)
    dynamic_slice x6 -> x3, local copies, waits for them, and re-layouts: 15.2 us -> 8.2 us  [pick_cols(): lax.dynamic_slice_in_dim(values, offsets[s], RANK, axis)]
    unnamed x277 -> x251, local copies, waits for them, and re-layouts: 23 us -> 23.6 us
  transfers between devices with their start and end apart: 67 -> 67, of which waited for: 24 -> 22; matrix products, arithmetic and copies ran while one was open for 55% -> 54% of each run, Pallas kernels for 0% -> 0%
where the time goes in v13:
time: 749 us; the launch traced here: 736 us
  local copies, waits for them, and re-layouts  271 us (36%)
  waiting for transfers between devices  142 us (19%)
  starting transfers between devices  124 us (17%)
  matrix products  122 us (16%)
  other arithmetic  67.9 us (9%)
  between operations  8.52 us (1%)
    dynamic_update_slice x57, local copies, waits for them, and re-layouts, put(): return lax.dynamic_update_slice(buffer, piece, start)  66.6 us
    dot_general x37, matrix products, hp_dot(): jnp.einsum(spec, left, right, precision=highest, preferred_element_type=j...  59.4 us
    ppermute x4, waiting for transfers between devices, tok_scatter(): got = lax.ppermute(send.astype(jnp.bfloat16), 'tok', xor_pairs(count, 2))  37.4 us
    ppermute x10, starting transfers between devices, ring_stage(): from_right = lax.ppermute(stacks, 'fsdp', fsdp_pairs(kind, -1))  25 us
    ppermute x5, waiting for transfers between devices, pair_stage(): other = lax.ppermute(stacks, 'fsdp', fsdp_pairs('z', 1))  24.3 us
    unnamed x251, local copies, waits for them, and re-layouts  23.6 us
    dot_general x5, matrix products, column_backward(): jnp.einsum('ste,de->std', grad_rows, weight, preferred_element_type=jnp.f...  23.1 us
    ppermute x4, starting transfers between devices, tok_scatter(): chip_sum = mine + lax.ppermute(theirs, 'tok', xor_pairs(count, 1))  21.2 us
  transfers between devices with their start and end apart: 67, of which 22 were waited for; matrix products, arithmetic and copies ran while one was open for 54% of the time, Pallas kernels for 0%

profile of v13, /device:TPU:1, one launch (start us, length us, event | category | flops | bytes accessed | tf_op | source)
XLA Modules:
  0.0 736.1 jit_solution(17910692008921743512)
XLA Ops:
  0.7 3.6 collective-permute-start.42
  7.0 3.6 collective-permute-start.12
  74.4 5.3 collective-permute-done.44
  82.7 5.7 collective-permute-done.16
  105.8 7.4 %collective-permute-start.1 = (bf16[2,2,64,2048]{3,2,1,0:T(8,128)(2,1)S(1)}, bf16[2,2,64,2048]{3,2,1,0:T(8,128)(2,1)S(1)}, u32[]{:S(2)}, u32[]{:S(2)}) collective-permute-start(bf16[2,2,64,2048]{3,2,1,0:T(8,128)(2,1)S(1)} %maximum_select_fusion.4), channel_id=1, source_target_pairs={{0,1},{1,0},{2,3},{3,2},{4,5},{5,4},{6,7},{7,6},{8,9},{9,8},{10,11... | collective-permute-start | bytes 3145736 | tf_op jit(solution)/shard_map/ppermute | solution.py:110
  127.8 6.5 collective-permute-done.5
  148.2 17.0 %collective-permute-done.37 = bf16[2,4,64,1408]{3,2,1,0:T(8,128)(2,1)S(1)} collective-permute-done((bf16[2,4,64,1408]{3,2,1,0:T(8,128)(2,1)}, bf16[2,4,64,1408]{3,2,1,0:T(8,128)(2,1)S(1)}, u32[]{:S(2)}, u32[]{:S(2)}) %collective-permute-start.37) | collective-permute-done | bytes 1441824 | tf_op jit(solution)/shard_map/ppermute | solution.py:180
  168.9 5.7 broadcast_in_dim.134
  174.7 3.6 constant_dynamic-update-slice_fusion.21
  179.8 3.6 collective-permute-start.38
  203.4 16.6 %collective-permute-done.7 = bf16[3,8,64,512]{3,2,1,0:T(8,128)(2,1)} collective-permute-done((bf16[3,8,64,512]{3,2,1,0:T(8,128)(2,1)}, bf16[3,8,64,512]{3,2,1,0:T(8,128)(2,1)}, u32[]{:S(2)}, u32[]{:S(2)}) %collective-permute-start.7) | collective-permute-done | bytes 1572896 | tf_op jit(solution)/shard_map/ppermute | solution.py:190
  235.1 3.5 collective-permute-done.21
  238.6 3.4 collective-permute-start.9
  247.5 3.9 constant_dynamic-slice_fusion.12
  280.5 4.8 copy.281
  308.7 5.9 fusion.121
  320.7 4.1 convolution_add_fusion.2
  346.0 20.3 %collective-permute-start.30 = (f32[2,2,64,2048]{3,2,0,1:T(8,128)}, f32[2,2,64,2048]{3,2,0,1:T(8,128)}, u32[]{:S(2)}, u32[]{:S(2)}) collective-permute-start(f32[2,2,64,2048]{3,2,0,1:T(8,128)} %bitcast.507), channel_id=1, source_target_pairs={{0,1},{1,0},{2,3},{3,2},{4,5},{5,4},{6,7},{7,6},{8,9},{9,8},{10,11... | collective-permute-start | bytes 6291464 | tf_op jit(solution)/shard_map/ppermute | solution.py:125
  372.1 3.5 copy.294
  375.6 3.4 copy.295
  399.7 3.6 constant_dynamic-update-slice_fusion.20
  403.3 3.6 constant_dynamic-update-slice_fusion.19
  406.9 5.7 collective-permute-done.31
  415.0 11.3 %collective-permute-done.40 = bf16[2,4,64,1408]{3,2,1,0:T(8,128)(2,1)S(1)} collective-permute-done((bf16[2,4,64,1408]{3,2,1,0:T(8,128)(2,1)S(1)}, bf16[2,4,64,1408]{3,2,1,0:T(8,128)(2,1)S(1)}, u32[]{:S(2)}, u32[]{:S(2)}) %collective-permute-start.40) | collective-permute-done | bytes 1441824 | tf_op jit(solution)/shard_map/ppermute | solution.py:194
  430.9 9.7 %fusion.120 = (bf16[1,4,2,4,64,1408]{5,4,1,2,3,0:T(8,128)(2,1)}, bf16[1,4,2,4,64,1408]{5,4,1,2,3,0:T(8,128)(2,1)}) fusion(bf16[2,4,2,4,64,1408]{5,4,1,2,3,0:T(8,128)(2,1)} %bitcast.80), kind=kLoop, calls=%fused_computation.349 | loop fusion | bytes 23068672 | tf_op jit(solution)/shard_map/slice | solution.py:372
  448.5 3.4 fusion.128
  452.7 3.4 fusion.127
  462.4 6.7 fusion.8
  469.6 5.0 fusion.132
  475.1 3.4 fusion.133
  489.4 3.5 multiply_add_fusion
  507.9 9.2 %collective-permute-done.55 = bf16[2,64,2048]{2,1,0:T(8,128)(2,1)S(1)} collective-permute-done((bf16[2,64,2048]{2,1,0:T(8,128)(2,1)S(1)}, bf16[2,64,2048]{2,1,0:T(8,128)(2,1)S(1)}, u32[]{:S(2)}, u32[]{:S(2)}) %collective-permute-start.55) | collective-permute-done | bytes 524320 | tf_op jit(solution)/shard_map/ppermute | solution.py:128
  517.5 10.9 %collective-permute-done.51 = bf16[2,64,2048]{2,1,0:T(8,128)(2,1)S(1)} collective-permute-done((bf16[2,64,2048]{2,1,0:T(8,128)(2,1)S(1)}, bf16[2,64,2048]{2,1,0:T(8,128)(2,1)S(1)}, u32[]{:S(2)}, u32[]{:S(2)}) %collective-permute-start.51) | collective-permute-done | bytes 524320 | tf_op jit(solution)/shard_map/ppermute | solution.py:128
  534.3 9.9 %collective-permute-done.56 = bf16[2,64,2048]{2,1,0:T(8,128)(2,1)S(1)} collective-permute-done((bf16[2,64,2048]{2,1,0:T(8,128)(2,1)S(1)}, bf16[2,64,2048]{2,1,0:T(8,128)(2,1)S(1)}, u32[]{:S(2)}, u32[]{:S(2)}) %collective-permute-start.56) | collective-permute-done | bytes 524320 | tf_op jit(solution)/shard_map/ppermute | solution.py:106
  561.1 5.6 all-to-all-start.2
  571.8 3.8 convolution_add_fusion.1
  597.4 3.9 multiply_add_fusion.5
  608.1 4.6 fusion.135
  617.5 4.4 fusion.136
  631.7 5.8 add_add_fusion
  659.3 4.4 convolution_bitcast_fusion
  663.6 3.7 copy.323
  667.4 4.3 convolution_bitcast_fusion.2
  673.6 7.4 %all-to-all-start.1 = ((bf16[32,64,128]{2,1,0:T(8,128)(2,1)}), bf16[32,64,128]{2,1,0:T(8,128)(2,1)S(1)}, u32[]{:S(2)}, u32[]{:S(2)}) async-start(bf16[32,64,128]{2,1,0:T(8,128)(2,1)} %pad_maximum_fusion.7), calls=%async_computation.1 | async-start | bytes 1048576 | tf_op jit(solution)/shard_map/all_to_all | solution.py:477
  683.8 7.2 all-to-all-done.1
  691.0 5.0 all-to-all-start
  707.9 9.4 %all-to-all-done = f32[32,112,128]{2,1,0:T(8,128)} async-done(((f32[32,112,128]{2,1,0:T(8,128)}), f32[32,112,128]{2,1,0:T(8,128)}, u32[]{:S(2)}, u32[]{:S(2)}) %all-to-all-start) | async-done | bytes 1835040 | tf_op jit(solution)/shard_map/all_to_all | solution.py:477
  720.3 11.6 %collective-permute-done.59 = bf16[2,64,2048]{2,1,0:T(8,128)(2,1)} collective-permute-done((bf16[2,64,2048]{2,1,0:T(8,128)(2,1)}, bf16[2,64,2048]{2,1,0:T(8,128)(2,1)}, u32[]{:S(2)}, u32[]{:S(2)}) %collective-permute-start.59) | collective-permute-done | bytes 524320 | tf_op jit(solution)/shard_map/ppermute | solution.py:128
  (668 shorter events, 425.8 us)
Async XLA Ops:
  0.7 60.8 %collective-permute-start.42 = (bf16[1,1408,64]{1,2,0:T(8,128)(2,1)}, bf16[1,1408,64]{1,2,0:T(8,128)(2,1)}, u32[]{:S(2)}, u32[]{:S(2)}) collective-permute-start(bf16[1,1408,64]{1,2,0:T(8,128)(2,1)} %bitcast.630), channel_id=1, source_target_pairs={{0,12},{4,0},{8,4},{12,8},{16,28},{20,16},{24,20},{28,24},{32,44},... | collective-permute-start | bytes 540680 | tf_op jit(solution)/shard_map/ppermute | solution.py:191
  4.3 58.2 %collective-permute-start.43 = (bf16[1,1408,64]{1,2,0:T(8,128)(2,1)}, bf16[1,1408,64]{1,2,0:T(8,128)(2,1)}, u32[]{:S(2)}, u32[]{:S(2)}) collective-permute-start(bf16[1,1408,64]{1,2,0:T(8,128)(2,1)} %bitcast.631), channel_id=1, source_target_pairs={{0,4},{4,8},{8,12},{12,0},{16,20},{20,24},{24,28},{28,16},{32,36},... | collective-permute-start | bytes 540680 | tf_op jit(solution)/shard_map/ppermute | solution.py:190
  4.3 48.7 %collective-permute-start.22 = (bf16[1,512,64]{1,2,0:T(8,128)(2,1)}, bf16[1,512,64]{1,2,0:T(8,128)(2,1)}, u32[]{:S(2)}, u32[]{:S(2)}) collective-permute-start(bf16[1,512,64]{1,2,0:T(8,128)(2,1)} %bitcast.636), channel_id=1, source_target_pairs={{0,12},{4,0},{8,4},{12,8},{16,28},{20,16},{24,20},{28,24},{32,44},... | collective-permute-start | bytes 196616 | tf_op jit(solution)/shard_map/ppermute | solution.py:191
  7.0 46.2 %collective-permute-start.23 = (bf16[1,512,64]{1,2,0:T(8,128)(2,1)}, bf16[1,512,64]{1,2,0:T(8,128)(2,1)}, u32[]{:S(2)}, u32[]{:S(2)}) collective-permute-start(bf16[1,512,64]{1,2,0:T(8,128)(2,1)} %bitcast.637), channel_id=1, source_target_pairs={{0,4},{4,8},{8,12},{12,0},{16,20},{20,24},{24,28},{28,16},{32,36},... | collective-permute-start | bytes 196616 | tf_op jit(solution)/shard_map/ppermute | solution.py:190
  7.0 27.7 %collective-permute-start.12 = (bf16[2,128,16]{1,2,0:T(8,128)(2,1)}, bf16[2,128,16]{1,2,0:T(8,128)(2,1)}, u32[]{:S(2)}, u32[]{:S(2)}) collective-permute-start(bf16[2,128,16]{1,2,0:T(8,128)(2,1)} %param.35), channel_id=1, source_target_pairs={{0,2},{1,3},{2,0},{3,1},{4,6},{5,7},{6,4},{7,5},{8,10},{9,11},{10,... | collective-permute-start | bytes 24584 | tf_op jit(solution)/shard_map/ppermute | solution.py:106
  47.2 26.3 %collective-permute-start.34 = (bf16[2,1,64,1408]{3,2,1,0:T(8,128)(2,1)}, bf16[2,1,64,1408]{3,2,1,0:T(8,128)(2,1)S(1)}, u32[]{:S(2)}, u32[]{:S(2)}) collective-permute-start(bf16[2,1,64,1408]{3,2,1,0:T(8,128)(2,1)} %bitcast.623), channel_id=1, source_target_pairs={{0,96},{4,100},{8,104},{12,108},{16,112},{20,116},{24,120},{28,124... | collective-permute-start | bytes 1081352 | tf_op jit(solution)/shard_map/ppermute | solution.py:191
  53.0 28.9 %collective-permute-start.35 = (bf16[2,1,64,1408]{3,2,1,0:T(8,128)(2,1)}, bf16[2,1,64,1408]{3,2,1,0:T(8,128)(2,1)S(1)}, u32[]{:S(2)}, u32[]{:S(2)}) collective-permute-start(bf16[2,1,64,1408]{3,2,1,0:T(8,128)(2,1)} %bitcast.624), channel_id=1, source_target_pairs={{0,32},{4,36},{8,40},{12,44},{16,48},{20,52},{24,56},{28,60},{32,6... | collective-permute-start | bytes 1081352 | tf_op jit(solution)/shard_map/ppermute | solution.py:190
  62.5 33.6 %collective-permute-start = (bf16[2,64,2048]{2,1,0:T(8,128)(2,1)S(1)}, bf16[2,64,2048]{2,1,0:T(8,128)(2,1)S(1)}, u32[]{:S(2)}, u32[]{:S(2)}) collective-permute-start(bf16[2,64,2048]{2,1,0:T(8,128)(2,1)S(1)} %copy-done.65), channel_id=1, source_target_pairs={{0,2},{1,3},{2,0},{3,1},{4,6},{5,7},{6,4},{7,5},{8,10},{9,11},{10,... | collective-permute-start | bytes 1572872 | tf_op jit(solution)/shard_map/ppermute | solution.py:106
  68.6 30.7 %collective-permute-start.52 = (bf16[2,64,2048]{2,1,0:T(8,128)(2,1)S(1)}, bf16[2,64,2048]{2,1,0:T(8,128)(2,1)S(1)}, u32[]{:S(2)}, u32[]{:S(2)}) collective-permute-start(bf16[2,64,2048]{2,1,0:T(8,128)(2,1)S(1)} %copy-done.35), channel_id=1, source_target_pairs={{0,2},{1,3},{2,0},{3,1},{4,6},{5,7},{6,4},{7,5},{8,10},{9,11},{10,... | collective-permute-start | bytes 1572872 | tf_op jit(solution)/shard_map/ppermute | solution.py:106
  73.0 17.5 %collective-permute-start.25 = (bf16[4,512,64]{1,2,0:T(8,128)(2,1)}, bf16[4,512,64]{1,2,0:T(8,128)(2,1)S(1)}, u32[]{:S(2)}, u32[]{:S(2)}) collective-permute-start(bf16[4,512,64]{1,2,0:T(8,128)(2,1)} %constant_dynamic-update-slice_fusion.35), channel_id=1, source_target_pairs={{0,16},{4,20},{8,24},{12,28},{16,0},{20,4},{24,8},{28,12},{32,48},... | collective-permute-start | bytes 786440 | tf_op jit(solution)/shard_map/ppermute | solution.py:180
  88.4 34.9 %collective-permute-start.45 = (bf16[4,1408,64]{1,2,0:T(8,128)(2,1)S(1)}, bf16[4,1408,64]{1,2,0:T(8,128)(2,1)S(1)}, u32[]{:S(2)}, u32[]{:S(2)}) collective-permute-start(bf16[4,1408,64]{1,2,0:T(8,128)(2,1)S(1)} %constant_dynamic-update-slice_fusion.13), channel_id=1, source_target_pairs={{0,16},{4,20},{8,24},{12,28},{16,0},{20,4},{24,8},{28,12},{32,48},... | collective-permute-start | bytes 2162696 | tf_op jit(solution)/shard_map/ppermute | solution.py:180
  93.0 24.6 %collective-permute-start.17 = (bf16[4,644,128]{2,0,1:T(4,128)(2,1)S(1)}, bf16[4,644,128]{2,0,1:T(4,128)(2,1)S(1)}, u32[]{:S(2)}, u32[]{:S(2)}) collective-permute-start(bf16[4,644,128]{2,0,1:T(4,128)(2,1)S(1)} %copy.258), channel_id=1, source_target_pairs={{0,16},{4,20},{8,24},{12,28},{16,0},{20,4},{24,8},{28,12},{32,48},... | collective-permute-start | bytes 1978376 | tf_op jit(solution)/shard_map/ppermute | solution.py:180
  99.2 14.9 %collective-permute-start.27 = (bf16[8,512,64]{1,2,0:T(8,128)(2,1)S(1)}, bf16[8,512,64]{1,2,0:T(8,128)(2,1)S(1)}, u32[]{:S(2)}, u32[]{:S(2)}) collective-permute-start(bf16[8,512,64]{1,2,0:T(8,128)(2,1)S(1)} %constant_dynamic-update-slice_fusion.33), channel_id=1, source_target_pairs={{0,32},{4,36},{8,40},{12,44},{16,48},{20,52},{24,56},{28,60},{32,6... | collective-permute-start | bytes 1572872 | tf_op jit(solution)/shard_map/ppermute | solution.py:190
  99.7 34.6 %collective-permute-start.5 = (bf16[3,4,64,512]{3,2,1,0:T(8,128)(2,1)S(1)}, bf16[3,4,64,512]{3,2,1,0:T(8,128)(2,1)S(1)}, u32[]{:S(2)}, u32[]{:S(2)}) collective-permute-start(bf16[3,4,64,512]{3,2,1,0:T(8,128)(2,1)S(1)} %bitcast_dynamic-update-slice_fusion.1), channel_id=1, source_target_pairs={{0,16},{4,20},{8,24},{12,28},{16,0},{20,4},{24,8},{28,12},{32,48},... | collective-permute-start | bytes 2359304 | tf_op jit(solution)/shard_map/ppermute | solution.py:180
  105.8 41.5 %collective-permute-start.1 = (bf16[2,2,64,2048]{3,2,1,0:T(8,128)(2,1)S(1)}, bf16[2,2,64,2048]{3,2,1,0:T(8,128)(2,1)S(1)}, u32[]{:S(2)}, u32[]{:S(2)}) collective-permute-start(bf16[2,2,64,2048]{3,2,1,0:T(8,128)(2,1)S(1)} %maximum_select_fusion.4), channel_id=1, source_target_pairs={{0,1},{1,0},{2,3},{3,2},{4,5},{5,4},{6,7},{7,6},{8,9},{9,8},{10,11... | collective-permute-start | bytes 3145736 | tf_op jit(solution)/shard_map/ppermute | solution.py:110
  114.1 30.4 %collective-permute-start.53 = (bf16[2,2,64,2048]{3,2,0,1:T(8,128)(2,1)S(1)}, bf16[2,2,64,2048]{3,2,0,1:T(8,128)(2,1)S(1)}, u32[]{:S(2)}, u32[]{:S(2)}) collective-permute-start(bf16[2,2,64,2048]{3,2,0,1:T(8,128)(2,1)S(1)} %maximum_select_fusion.7), channel_id=1, source_target_pairs={{0,1},{1,0},{2,3},{3,2},{4,5},{5,4},{6,7},{7,6},{8,9},{9,8},{10,11... | collective-permute-start | bytes 3145736 | tf_op jit(solution)/shard_map/ppermute | solution.py:110
  123.3 41.9 %collective-permute-start.37 = (bf16[2,4,64,1408]{3,2,1,0:T(8,128)(2,1)}, bf16[2,4,64,1408]{3,2,1,0:T(8,128)(2,1)S(1)}, u32[]{:S(2)}, u32[]{:S(2)}) collective-permute-start(bf16[2,4,64,1408]{3,2,1,0:T(8,128)(2,1)} %constant_dynamic-update-slice_fusion.24), channel_id=1, source_target_pairs={{0,16},{4,20},{8,24},{12,28},{16,0},{20,4},{24,8},{28,12},{32,48},... | collective-permute-start | bytes 4325384 | tf_op jit(solution)/shard_map/ppermute | solution.py:180
  134.3 33.0 %collective-permute-start.19 = (bf16[8,644,128]{2,0,1:T(8,128)(2,1)}, bf16[8,644,128]{2,0,1:T(8,128)(2,1)}, u32[]{:S(2)}, u32[]{:S(2)}) collective-permute-start(bf16[8,644,128]{2,0,1:T(8,128)(2,1)} %copy.260), channel_id=1, source_target_pairs={{0,32},{4,36},{8,40},{12,44},{16,48},{20,52},{24,56},{28,60},{32,6... | collective-permute-start | bytes 3956744 | tf_op jit(solution)/shard_map/ppermute | solution.py:190
  138.8 41.0 %collective-permute-start.18 = (bf16[8,644,128]{2,0,1:T(8,128)(2,1)}, bf16[8,644,128]{2,0,1:T(8,128)(2,1)}, u32[]{:S(2)}, u32[]{:S(2)}) collective-permute-start(bf16[8,644,128]{2,0,1:T(8,128)(2,1)} %copy.260), channel_id=1, source_target_pairs={{0,96},{4,100},{8,104},{12,108},{16,112},{20,116},{24,120},{28,124... | collective-permute-start | bytes 3956744 | tf_op jit(solution)/shard_map/ppermute | solution.py:191
  144.6 46.2 %collective-permute-start.46 = (bf16[8,1408,64]{1,2,0:T(8,128)(2,1)}, bf16[8,1408,64]{1,2,0:T(8,128)(2,1)}, u32[]{:S(2)}, u32[]{:S(2)}) collective-permute-start(bf16[8,1408,64]{1,2,0:T(8,128)(2,1)} %constant_dynamic-update-slice_fusion.11), channel_id=1, source_target_pairs={{0,96},{4,100},{8,104},{12,108},{16,112},{20,116},{24,120},{28,124... | collective-permute-start | bytes 4325384 | tf_op jit(solution)/shard_map/ppermute | solution.py:191
  147.2 47.9 %collective-permute-start.47 = (bf16[8,1408,64]{1,2,0:T(8,128)(2,1)}, bf16[8,1408,64]{1,2,0:T(8,128)(2,1)}, u32[]{:S(2)}, u32[]{:S(2)}) collective-permute-start(bf16[8,1408,64]{1,2,0:T(8,128)(2,1)} %constant_dynamic-update-slice_fusion.11), channel_id=1, source_target_pairs={{0,32},{4,36},{8,40},{12,44},{16,48},{20,52},{24,56},{28,60},{32,6... | collective-permute-start | bytes 4325384 | tf_op jit(solution)/shard_map/ppermute | solution.py:190
  165.3 60.1 %collective-permute-start.6 = (bf16[3,8,64,512]{3,2,1,0:T(8,128)(2,1)}, bf16[3,8,64,512]{3,2,1,0:T(8,128)(2,1)}, u32[]{:S(2)}, u32[]{:S(2)}) collective-permute-start(bf16[3,8,64,512]{3,2,1,0:T(8,128)(2,1)} %constant_dynamic-update-slice_fusion.50), channel_id=1, source_target_pairs={{0,96},{4,100},{8,104},{12,108},{16,112},{20,116},{24,120},{28,124... | collective-permute-start | bytes 4718600 | tf_op jit(solution)/shard_map/ppermute | solution.py:191
  167.3 52.8 %collective-permute-start.7 = (bf16[3,8,64,512]{3,2,1,0:T(8,128)(2,1)}, bf16[3,8,64,512]{3,2,1,0:T(8,128)(2,1)}, u32[]{:S(2)}, u32[]{:S(2)}) collective-permute-start(bf16[3,8,64,512]{3,2,1,0:T(8,128)(2,1)} %constant_dynamic-update-slice_fusion.50), channel_id=1, source_target_pairs={{0,32},{4,36},{8,40},{12,44},{16,48},{20,52},{24,56},{28,60},{32,6... | collective-permute-start | bytes 4718600 | tf_op jit(solution)/shard_map/ppermute | solution.py:190
  179.8 212.1 %collective-permute-start.38 = (bf16[2,8,64,1408]{3,2,1,0:T(8,128)(2,1)}, bf16[2,8,64,1408]{3,2,1,0:T(8,128)(2,1)}, u32[]{:S(2)}, u32[]{:S(2)}) collective-permute-start(bf16[2,8,64,1408]{3,2,1,0:T(8,128)(2,1)} %constant_dynamic-update-slice_fusion.22), channel_id=1, source_target_pairs={{0,12},{4,0},{8,4},{12,8},{16,28},{20,16},{24,20},{28,24},{32,44},... | collective-permute-start | bytes 8650760 | tf_op jit(solution)/shard_map/ppermute | solution.py:191
  190.8 43.4 %collective-permute-start.20 = (bf16[4,644,128]{2,0,1:T(4,128)(2,1)S(1)}, bf16[4,644,128]{2,0,1:T(4,128)(2,1)S(1)}, u32[]{:S(2)}, u32[]{:S(2)}) collective-permute-start(bf16[4,644,128]{2,0,1:T(4,128)(2,1)S(1)} %slice.239), channel_id=1, source_target_pairs={{0,32},{4,36},{8,40},{12,44},{16,48},{20,52},{24,56},{28,60},{32,6... | collective-permute-start | bytes 1978376 | tf_op jit(solution)/shard_map/ppermute | solution.py:194
  195.1 43.5 %collective-permute-start.21 = (bf16[4,644,128]{2,0,1:T(4,128)(2,1)S(1)}, bf16[4,644,128]{2,0,1:T(4,128)(2,1)S(1)}, u32[]{:S(2)}, u32[]{:S(2)}) collective-permute-start(bf16[4,644,128]{2,0,1:T(4,128)(2,1)S(1)} %slice.240), channel_id=1, source_target_pairs={{0,96},{4,100},{8,104},{12,108},{16,112},{20,116},{24,120},{28,124... | collective-permute-start | bytes 1978376 | tf_op jit(solution)/shard_map/ppermute | solution.py:195
  220.0 170.3 %collective-permute-start.39 = (bf16[2,8,64,1408]{3,2,1,0:T(8,128)(2,1)}, bf16[2,8,64,1408]{3,2,1,0:T(8,128)(2,1)}, u32[]{:S(2)}, u32[]{:S(2)}) collective-permute-start(bf16[2,8,64,1408]{3,2,1,0:T(8,128)(2,1)} %constant_dynamic-update-slice_fusion.22), channel_id=1, source_target_pairs={{0,4},{4,8},{8,12},{12,0},{16,20},{20,24},{24,28},{28,16},{32,36},... | collective-permute-start | bytes 8650760 | tf_op jit(solution)/shard_map/ppermute | solution.py:190
  225.4 160.9 %collective-permute-start.48 = (bf16[4,1408,64]{1,2,0:T(8,128)(2,1)}, bf16[4,1408,64]{1,2,0:T(8,128)(2,1)}, u32[]{:S(2)}, u32[]{:S(2)}) collective-permute-start(bf16[4,1408,64]{1,2,0:T(8,128)(2,1)} %slice.275), channel_id=1, source_target_pairs={{0,32},{4,36},{8,40},{12,44},{16,48},{20,52},{24,56},{28,60},{32,6... | collective-permute-start | bytes 2162696 | tf_op jit(solution)/shard_map/ppermute | solution.py:194
  234.2 69.5 %collective-permute-start.8 = (bf16[3,4,64,512]{3,2,1,0:T(8,128)(2,1)}, bf16[3,4,64,512]{3,2,1,0:T(8,128)(2,1)}, u32[]{:S(2)}, u32[]{:S(2)}) collective-permute-start(bf16[3,4,64,512]{3,2,1,0:T(8,128)(2,1)} %slice.236), channel_id=1, source_target_pairs={{0,32},{4,36},{8,40},{12,44},{16,48},{20,52},{24,56},{28,60},{32,6... | collective-permute-start | bytes 2359304 | tf_op jit(solution)/shard_map/ppermute | solution.py:194
  238.6 67.9 %collective-permute-start.9 = (bf16[3,4,64,512]{3,2,1,0:T(8,128)(2,1)}, bf16[3,4,64,512]{3,2,1,0:T(8,128)(2,1)}, u32[]{:S(2)}, u32[]{:S(2)}) collective-permute-start(bf16[3,4,64,512]{3,2,1,0:T(8,128)(2,1)} %slice.237), channel_id=1, source_target_pairs={{0,96},{4,100},{8,104},{12,108},{16,112},{20,116},{24,120},{28,124... | collective-permute-start | bytes 2359304 | tf_op jit(solution)/shard_map/ppermute | solution.py:195
  303.7 84.6 %collective-permute-start.49 = (bf16[4,1408,64]{1,2,0:T(8,128)(2,1)}, bf16[4,1408,64]{1,2,0:T(8,128)(2,1)}, u32[]{:S(2)}, u32[]{:S(2)}) collective-permute-start(bf16[4,1408,64]{1,2,0:T(8,128)(2,1)} %slice.276), channel_id=1, source_target_pairs={{0,96},{4,100},{8,104},{12,108},{16,112},{20,116},{24,120},{28,124... | collective-permute-start | bytes 2162696 | tf_op jit(solution)/shard_map/ppermute | solution.py:195
  346.0 50.1 %collective-permute-start.30 = (f32[2,2,64,2048]{3,2,0,1:T(8,128)}, f32[2,2,64,2048]{3,2,0,1:T(8,128)}, u32[]{:S(2)}, u32[]{:S(2)}) collective-permute-start(f32[2,2,64,2048]{3,2,0,1:T(8,128)} %bitcast.507), channel_id=1, source_target_pairs={{0,1},{1,0},{2,3},{3,2},{4,5},{5,4},{6,7},{7,6},{8,9},{9,8},{10,11... | collective-permute-start | bytes 6291464 | tf_op jit(solution)/shard_map/ppermute | solution.py:125
  391.8 34.5 %collective-permute-start.40 = (bf16[2,4,64,1408]{3,2,1,0:T(8,128)(2,1)S(1)}, bf16[2,4,64,1408]{3,2,1,0:T(8,128)(2,1)S(1)}, u32[]{:S(2)}, u32[]{:S(2)}) collective-permute-start(bf16[2,4,64,1408]{3,2,1,0:T(8,128)(2,1)S(1)} %slice.266), channel_id=1, source_target_pairs={{0,4},{4,8},{8,12},{12,0},{16,20},{20,24},{24,28},{28,16},{32,36},... | collective-permute-start | bytes 4325384 | tf_op jit(solution)/shard_map/ppermute | solution.py:194
  393.5 34.0 %collective-permute-start.41 = (bf16[2,4,64,1408]{3,2,1,0:T(8,128)(2,1)S(1)}, bf16[2,4,64,1408]{3,2,1,0:T(8,128)(2,1)S(1)}, u32[]{:S(2)}, u32[]{:S(2)}) collective-permute-start(bf16[2,4,64,1408]{3,2,1,0:T(8,128)(2,1)S(1)} %slice.267), channel_id=1, source_target_pairs={{0,12},{4,0},{8,4},{12,8},{16,28},{20,16},{24,20},{28,24},{32,44},... | collective-permute-start | bytes 4325384 | tf_op jit(solution)/shard_map/ppermute | solution.py:195
  398.1 14.5 %collective-permute-start.31 = (bf16[2,64,2048]{2,1,0:T(8,128)(2,1)S(1)}, bf16[2,64,2048]{2,1,0:T(8,128)(2,1)S(1)}, u32[]{:S(2)}, u32[]{:S(2)}) collective-permute-start(bf16[2,64,2048]{2,1,0:T(8,128)(2,1)S(1)} %fusion.43), channel_id=1, source_target_pairs={{0,2},{1,3},{2,0},{3,1},{4,6},{5,7},{6,4},{7,5},{8,10},{9,11},{10,... | collective-permute-start | bytes 1572872 | tf_op jit(solution)/shard_map/ppermute | solution.py:128
  413.1 15.8 %collective-permute-start.32 = (bf16[2,64,2048]{2,1,0:T(8,128)(2,1)S(1)}, bf16[2,64,2048]{2,1,0:T(8,128)(2,1)S(1)}, u32[]{:S(2)}, u32[]{:S(2)}) collective-permute-start(bf16[2,64,2048]{2,1,0:T(8,128)(2,1)S(1)} %multiply_convert_fusion.3), channel_id=1, source_target_pairs={{0,2},{1,3},{2,0},{3,1},{4,6},{5,7},{6,4},{7,5},{8,10},{9,11},{10,... | collective-permute-start | bytes 1572872 | tf_op jit(solution)/shard_map/ppermute | solution.py:106
  429.9 15.8 %collective-permute-start.33 = (bf16[2,2,64,2048]{3,2,0,1:T(8,128)(2,1)}, bf16[2,2,64,2048]{3,2,0,1:T(8,128)(2,1)}, u32[]{:S(2)}, u32[]{:S(2)}) collective-permute-start(bf16[2,2,64,2048]{3,2,0,1:T(8,128)(2,1)} %maximum_select_fusion.6), channel_id=1, source_target_pairs={{0,1},{1,0},{2,3},{3,2},{4,5},{5,4},{6,7},{7,6},{8,9},{9,8},{10,11... | collective-permute-start | bytes 3145736 | tf_op jit(solution)/shard_map/ppermute | solution.py:110
  502.0 15.1 %collective-permute-start.55 = (bf16[2,64,2048]{2,1,0:T(8,128)(2,1)S(1)}, bf16[2,64,2048]{2,1,0:T(8,128)(2,1)S(1)}, u32[]{:S(2)}, u32[]{:S(2)}) collective-permute-start(bf16[2,64,2048]{2,1,0:T(8,128)(2,1)S(1)} %fusion.45), channel_id=1, source_target_pairs={{0,2},{1,3},{2,0},{3,1},{4,6},{5,7},{6,4},{7,5},{8,10},{9,11},{10,... | collective-permute-start | bytes 1572872 | tf_op jit(solution)/shard_map/ppermute | solution.py:128
  505.7 22.6 %collective-permute-start.51 = (bf16[2,64,2048]{2,1,0:T(8,128)(2,1)S(1)}, bf16[2,64,2048]{2,1,0:T(8,128)(2,1)S(1)}, u32[]{:S(2)}, u32[]{:S(2)}) collective-permute-start(bf16[2,64,2048]{2,1,0:T(8,128)(2,1)S(1)} %fusion.44), channel_id=1, source_target_pairs={{0,2},{1,3},{2,0},{3,1},{4,6},{5,7},{6,4},{7,5},{8,10},{9,11},{10,... | collective-permute-start | bytes 1572872 | tf_op jit(solution)/shard_map/ppermute | solution.py:128
  530.1 14.2 %collective-permute-start.56 = (bf16[2,64,2048]{2,1,0:T(8,128)(2,1)S(1)}, bf16[2,64,2048]{2,1,0:T(8,128)(2,1)S(1)}, u32[]{:S(2)}, u32[]{:S(2)}) collective-permute-start(bf16[2,64,2048]{2,1,0:T(8,128)(2,1)S(1)} %get-tuple-element.34), channel_id=1, source_target_pairs={{0,2},{1,3},{2,0},{3,1},{4,6},{5,7},{6,4},{7,5},{8,10},{9,11},{10,... | collective-permute-start | bytes 1572872 | tf_op jit(solution)/shard_map/ppermute | solution.py:106
  531.6 24.7 %collective-permute-start.62 = (f32[2,2,256,16]{2,3,1,0:T(8,128)S(1)}, f32[2,2,256,16]{2,3,1,0:T(8,128)}, u32[]{:S(2)}, u32[]{:S(2)}) collective-permute-start(f32[2,2,256,16]{2,3,1,0:T(8,128)S(1)} %pad_maximum_fusion.10), channel_id=1, source_target_pairs={{0,1},{1,0},{2,3},{3,2},{4,5},{5,4},{6,7},{7,6},{8,9},{9,8},{10,11... | collective-permute-start | bytes 196616 | tf_op jit(solution)/shard_map/ppermute | solution.py:134
  545.4 22.8 %collective-permute-start.57 = (bf16[2,2,64,2048]{3,2,0,1:T(8,128)(2,1)}, bf16[2,2,64,2048]{3,2,0,1:T(8,128)(2,1)}, u32[]{:S(2)}, u32[]{:S(2)}) collective-permute-start(bf16[2,2,64,2048]{3,2,0,1:T(8,128)(2,1)} %maximum_select_fusion.9), channel_id=1, source_target_pairs={{0,1},{1,0},{2,3},{3,2},{4,5},{5,4},{6,7},{7,6},{8,9},{9,8},{10,11... | collective-permute-start | bytes 3145736 | tf_op jit(solution)/shard_map/ppermute | solution.py:110
  561.1 112.4 %all-to-all-start.2 = ((bf16[32,132,128]{2,1,0:T(8,128)(2,1)}), bf16[32,132,128]{2,1,0:T(8,128)(2,1)}, u32[]{:S(2)}, u32[]{:S(2)}) async-start(bf16[32,132,128]{2,1,0:T(8,128)(2,1)} %pad_maximum_fusion.2), calls=%async_computation.2 | async-start | bytes 2228224 | tf_op jit(solution)/shard_map/all_to_all | solution.py:477
  625.5 20.8 %collective-permute-start.60 = (f32[5,2,256,16]{2,3,1,0:T(8,128)}, f32[5,2,256,16]{2,3,1,0:T(8,128)S(1)}, u32[]{:S(2)}, u32[]{:S(2)}) collective-permute-start(f32[5,2,256,16]{2,3,1,0:T(8,128)} %bitcast_dynamic-update-slice_fusion.4), channel_id=1, source_target_pairs={{0,1},{1,0},{2,3},{3,2},{4,5},{5,4},{6,7},{7,6},{8,9},{9,8},{10,11... | collective-permute-start | bytes 491528 | tf_op jit(solution)/shard_map/ppermute | solution.py:134
  640.6 55.4 %collective-permute-start.58 = (f32[2,2,64,2048]{3,2,0,1:T(8,128)}, f32[2,2,64,2048]{3,2,0,1:T(8,128)}, u32[]{:S(2)}, u32[]{:S(2)}) collective-permute-start(f32[2,2,64,2048]{3,2,0,1:T(8,128)} %bitcast.504), channel_id=1, source_target_pairs={{0,1},{1,0},{2,3},{3,2},{4,5},{5,4},{6,7},{7,6},{8,9},{9,8},{10,11... | collective-permute-start | bytes 6291464 | tf_op jit(solution)/shard_map/ppermute | solution.py:125
  673.6 17.5 %all-to-all-start.1 = ((bf16[32,64,128]{2,1,0:T(8,128)(2,1)}), bf16[32,64,128]{2,1,0:T(8,128)(2,1)S(1)}, u32[]{:S(2)}, u32[]{:S(2)}) async-start(bf16[32,64,128]{2,1,0:T(8,128)(2,1)} %pad_maximum_fusion.7), calls=%async_computation.1 | async-start | bytes 1048576 | tf_op jit(solution)/shard_map/all_to_all | solution.py:477
  691.0 26.2 %all-to-all-start = ((f32[32,112,128]{2,1,0:T(8,128)}), f32[32,112,128]{2,1,0:T(8,128)}, u32[]{:S(2)}, u32[]{:S(2)}) async-start(f32[32,112,128]{2,1,0:T(8,128)} %pad_maximum_fusion.1), calls=%async_computation | async-start | bytes 3670016 | tf_op jit(solution)/shard_map/all_to_all | solution.py:477
  699.4 32.6 %collective-permute-start.59 = (bf16[2,64,2048]{2,1,0:T(8,128)(2,1)}, bf16[2,64,2048]{2,1,0:T(8,128)(2,1)}, u32[]{:S(2)}, u32[]{:S(2)}) collective-permute-start(bf16[2,64,2048]{2,1,0:T(8,128)(2,1)} %fusion.46), channel_id=1, source_target_pairs={{0,2},{1,3},{2,0},{3,1},{4,6},{5,7},{6,4},{7,5},{8,10},{9,11},{10,... | collective-permute-start | bytes 1572872 | tf_op jit(solution)/shard_map/ppermute | solution.py:128
  (137 other events, 1158.6 us)

commit v14 on v12

--- a/solution.py
+++ b/solution.py
@@ -259,14 +259,16 @@
     b_rows_tok = tok_gather(b_rows)
     small = [a_in_tok, b_rows_tok, b_qkv, b_gateup, a_out, a_down]
     small_flat = jnp.concatenate([p.reshape(-1, COLS) for p in small])
-    (g_qkv, g_out, g_down, g_small), (g_gateup,) = torus_gather(
-        [w_qkv[:, None], w_out[None], w_down[None], small_flat[None]],
-        [1, 0, 0, 0],
-        [w_gateup[:, None]],
-        [1],
+    (g_qkv, g_down, g_small), (g_gateup, g_out) = torus_gather(
+        [w_qkv[:, None], w_down[None], small_flat[None]],
+        [1, 0, 0],
+        [w_gateup[:, None], w_out[None]],
+        [1, 0],
     )
     w_qkv_full = g_qkv.reshape(3, D, qw_here)
-    w_out_full = jnp.moveaxis(g_out, 0, 1).reshape(qw_here, D)
+    w_out_full = jnp.transpose(
+        g_out.reshape(4, 2, 4, qw_here, D // fsdp_count), (3, 2, 1, 0, 4)
+    ).reshape(qw_here, D)
     w_down_full = jnp.moveaxis(g_down, 0, 1).reshape(ff_here, D)
     w_gateup_perm = jnp.transpose(
         g_gateup.reshape(2, 4, 2, 4, D // fsdp_count, ff_here), (0, 3, 2, 1, 4, 5)

time: 748 us -> 752 us (level)
  waiting for transfers between devices: 139 us -> 152 us
    ppermute x5, waiting for transfers between devices: 12.7 us -> 20.5 us  [ring_stage(): far_left = lax.ppermute(from_left, 'fsdp', fsdp_pairs(kind, 1))]
    unnamed x277 -> x283, local copies, waits for them, and re-layouts: 23 us -> 23.3 us
  transfers between devices with their start and end apart: 67 -> 67, of which waited for: 24 -> 27; matrix products, arithmetic and copies ran while one was open for 55% -> 54% of each run, Pallas kernels for 0% -> 0%
where the time goes in v14:
time: 752 us; the launch traced here: 739 us
  local copies, waits for them, and re-layouts  266 us (35%)
  waiting for transfers between devices  152 us (20%)
  starting transfers between devices  125 us (17%)
  matrix products  122 us (16%)
  other arithmetic  65.9 us (9%)
  between operations  8.78 us (1%)
    dynamic_update_slice x57, local copies, waits for them, and re-layouts, put(): return lax.dynamic_update_slice(buffer, piece, start)  61.8 us
    dot_general x37, matrix products, hp_dot(): jnp.einsum(spec, left, right, precision=highest, preferred_element_type=j...  61.1 us
    ppermute x4, waiting for transfers between devices, tok_scatter(): got = lax.ppermute(send.astype(jnp.bfloat16), 'tok', xor_pairs(count, 2))  35.8 us
    ppermute x5, waiting for transfers between devices, pair_stage(): other = lax.ppermute(stacks, 'fsdp', fsdp_pairs('z', 1))  29.1 us
    dot_general x5, matrix products, column_backward(): jnp.einsum('ste,de->std', grad_rows, weight, preferred_element_type=jnp.f...  24.7 us
    ppermute x10, starting transfers between devices, ring_stage(): from_right = lax.ppermute(stacks, 'fsdp', fsdp_pairs(kind, -1))  24.1 us
    unnamed x283, local copies, waits for them, and re-layouts  23.3 us
    all_to_all x3, starting transfers between devices, reduce_to_owners(): lax.all_to_all(packed, 'fsdp', 0, 0, tiled=False).astype(jnp.float32).sum(0)  21.5 us
  transfers between devices with their start and end apart: 67, of which 27 were waited for; matrix products, arithmetic and copies ran while one was open for 54% of the time, Pallas kernels for 0%

profile of v14, /device:TPU:1, one launch (start us, length us, event | category | flops | bytes accessed | tf_op | source)
XLA Modules:
  0.0 739.5 jit_solution(16337166100219662455)
XLA Ops:
  0.7 3.6 collective-permute-start.42
  6.8 3.6 collective-permute-start.12
  29.9 4.1 collective-permute-done.10
  46.2 9.1 %collective-permute-done.24 = bf16[1,512,64]{1,2,0:T(8,128)(2,1)S(1)} collective-permute-done((bf16[1,512,64]{1,2,0:T(8,128)(2,1)}, bf16[1,512,64]{1,2,0:T(8,128)(2,1)S(1)}, u32[]{:S(2)}, u32[]{:S(2)}) %collective-permute-start.24) | collective-permute-done | bytes 65568 | tf_op jit(solution)/shard_map/ppermute | solution.py:197
  73.0 5.3 collective-permute-done.44
  81.2 5.6 collective-permute-done.16
  102.7 7.0 collective-permute-start.1
  111.6 4.6 collective-permute-done.17
  126.4 6.6 collective-permute-done.5
  146.9 17.1 %collective-permute-done.37 = bf16[2,4,64,1408]{3,2,1,0:T(8,128)(2,1)S(1)} collective-permute-done((bf16[2,4,64,1408]{3,2,1,0:T(8,128)(2,1)}, bf16[2,4,64,1408]{3,2,1,0:T(8,128)(2,1)S(1)}, u32[]{:S(2)}, u32[]{:S(2)}) %collective-permute-start.37) | collective-permute-done | bytes 1441824 | tf_op jit(solution)/shard_map/ppermute | solution.py:180
  166.7 5.7 broadcast_in_dim.134
  172.4 3.7 constant_dynamic-update-slice_fusion.21
  177.6 3.6 collective-permute-start.38
  200.8 18.6 %collective-permute-done.7 = bf16[3,8,64,512]{3,2,1,0:T(8,128)(2,1)} collective-permute-done((bf16[3,8,64,512]{3,2,1,0:T(8,128)(2,1)}, bf16[3,8,64,512]{3,2,1,0:T(8,128)(2,1)}, u32[]{:S(2)}, u32[]{:S(2)}) %collective-permute-start.7) | collective-permute-done | bytes 1572896 | tf_op jit(solution)/shard_map/ppermute | solution.py:190
  227.8 5.7 collective-permute-done.20
  235.9 3.7 collective-permute-start.9
  245.0 3.7 constant_dynamic-slice_fusion.14
  259.5 4.7 copy.276
  264.2 6.4 copy.277
  270.7 3.5 constant_dynamic-slice_fusion.10
  302.5 5.8 fusion.121
  314.4 4.1 convolution_add_fusion.2
  338.2 20.4 %collective-permute-start.30 = (f32[2,2,64,2048]{3,2,0,1:T(8,128)}, f32[2,2,64,2048]{3,2,0,1:T(8,128)}, u32[]{:S(2)}, u32[]{:S(2)}) collective-permute-start(f32[2,2,64,2048]{3,2,0,1:T(8,128)} %bitcast.504), channel_id=1, source_target_pairs={{0,1},{1,0},{2,3},{3,2},{4,5},{5,4},{6,7},{7,6},{8,9},{9,8},{10,11... | collective-permute-start | bytes 6291464 | tf_op jit(solution)/shard_map/ppermute | solution.py:125
  391.5 3.6 constant_dynamic-update-slice_fusion.20
  395.1 3.6 constant_dynamic-update-slice_fusion.19
  398.7 5.1 collective-permute-done.31
  406.8 10.8 %collective-permute-done.40 = bf16[2,4,64,1408]{3,2,1,0:T(8,128)(2,1)S(1)} collective-permute-done((bf16[2,4,64,1408]{3,2,1,0:T(8,128)(2,1)S(1)}, bf16[2,4,64,1408]{3,2,1,0:T(8,128)(2,1)S(1)}, u32[]{:S(2)}, u32[]{:S(2)}) %collective-permute-start.40) | collective-permute-done | bytes 1441824 | tf_op jit(solution)/shard_map/ppermute | solution.py:194
  422.2 9.7 %fusion.120 = (bf16[1,4,2,4,64,1408]{5,4,1,2,3,0:T(8,128)(2,1)}, bf16[1,4,2,4,64,1408]{5,4,1,2,3,0:T(8,128)(2,1)}) fusion(bf16[2,4,2,4,64,1408]{5,4,1,2,3,0:T(8,128)(2,1)} %bitcast.81), kind=kLoop, calls=%fused_computation.348 | loop fusion | bytes 23068672 | tf_op jit(solution)/shard_map/slice | solution.py:368
  438.9 3.4 fusion.128
  443.1 3.4 fusion.127
  452.8 7.1 fusion.8
  460.4 5.1 fusion.132
  466.0 3.4 fusion.133
  480.3 3.5 multiply_add_fusion
  500.2 9.2 %collective-permute-done.55 = bf16[2,64,2048]{2,1,0:T(8,128)(2,1)S(1)} collective-permute-done((bf16[2,64,2048]{2,1,0:T(8,128)(2,1)S(1)}, bf16[2,64,2048]{2,1,0:T(8,128)(2,1)S(1)}, u32[]{:S(2)}, u32[]{:S(2)}) %collective-permute-start.55) | collective-permute-done | bytes 524320 | tf_op jit(solution)/shard_map/ppermute | solution.py:128
  509.7 10.9 %collective-permute-done.51 = bf16[2,64,2048]{2,1,0:T(8,128)(2,1)S(1)} collective-permute-done((bf16[2,64,2048]{2,1,0:T(8,128)(2,1)S(1)}, bf16[2,64,2048]{2,1,0:T(8,128)(2,1)S(1)}, u32[]{:S(2)}, u32[]{:S(2)}) %collective-permute-start.51) | collective-permute-done | bytes 524320 | tf_op jit(solution)/shard_map/ppermute | solution.py:128
  527.0 9.5 %collective-permute-done.56 = bf16[2,64,2048]{2,1,0:T(8,128)(2,1)S(1)} collective-permute-done((bf16[2,64,2048]{2,1,0:T(8,128)(2,1)S(1)}, bf16[2,64,2048]{2,1,0:T(8,128)(2,1)S(1)}, u32[]{:S(2)}, u32[]{:S(2)}) %collective-permute-start.56) | collective-permute-done | bytes 524320 | tf_op jit(solution)/shard_map/ppermute | solution.py:106
  554.9 6.3 all-to-all-start.2
  594.9 4.5 multiply_add_fusion.5
  606.2 5.2 fusion.135
  616.9 5.2 fusion.136
  638.7 5.8 add_add_fusion
  670.8 7.5 %all-to-all-start.1 = ((bf16[32,64,128]{2,1,0:T(8,128)(2,1)}), bf16[32,64,128]{2,1,0:T(8,128)(2,1)}, u32[]{:S(2)}, u32[]{:S(2)}) async-start(bf16[32,64,128]{2,1,0:T(8,128)(2,1)} %pad_maximum_fusion.8), calls=%async_computation.1 | async-start | bytes 1048576 | tf_op jit(solution)/shard_map/all_to_all | solution.py:472
  678.3 4.4 pad_maximum_fusion
  682.7 5.9 copy.317
  691.6 7.8 %all-to-all-start = ((f32[32,112,128]{2,1,0:T(8,128)}), f32[32,112,128]{2,1,0:T(8,128)}, u32[]{:S(2)}, u32[]{:S(2)}) async-start(f32[32,112,128]{2,1,0:T(8,128)} %pad_maximum_fusion.2), calls=%async_computation | async-start | bytes 3670016 | tf_op jit(solution)/shard_map/all_to_all | solution.py:472
  711.4 10.2 %all-to-all-done = f32[32,112,128]{2,1,0:T(8,128)} async-done(((f32[32,112,128]{2,1,0:T(8,128)}), f32[32,112,128]{2,1,0:T(8,128)}, u32[]{:S(2)}, u32[]{:S(2)}) %all-to-all-start) | async-done | bytes 1835040 | tf_op jit(solution)/shard_map/all_to_all | solution.py:472
  724.6 10.6 %collective-permute-done.59 = bf16[2,64,2048]{2,1,0:T(8,128)(2,1)} collective-permute-done((bf16[2,64,2048]{2,1,0:T(8,128)(2,1)}, bf16[2,64,2048]{2,1,0:T(8,128)(2,1)}, u32[]{:S(2)}, u32[]{:S(2)}) %collective-permute-start.59) | collective-permute-done | bytes 524320 | tf_op jit(solution)/shard_map/ppermute | solution.py:128
  (698 shorter events, 412.9 us)
Async XLA Ops:
  0.7 59.3 %collective-permute-start.42 = (bf16[1,1408,64]{1,2,0:T(8,128)(2,1)}, bf16[1,1408,64]{1,2,0:T(8,128)(2,1)}, u32[]{:S(2)}, u32[]{:S(2)}) collective-permute-start(bf16[1,1408,64]{1,2,0:T(8,128)(2,1)} %bitcast.631), channel_id=1, source_target_pairs={{0,12},{4,0},{8,4},{12,8},{16,28},{20,16},{24,20},{28,24},{32,44},... | collective-permute-start | bytes 540680 | tf_op jit(solution)/shard_map/ppermute | solution.py:191
  4.3 56.7 %collective-permute-start.43 = (bf16[1,1408,64]{1,2,0:T(8,128)(2,1)}, bf16[1,1408,64]{1,2,0:T(8,128)(2,1)}, u32[]{:S(2)}, u32[]{:S(2)}) collective-permute-start(bf16[1,1408,64]{1,2,0:T(8,128)(2,1)} %bitcast.632), channel_id=1, source_target_pairs={{0,4},{4,8},{8,12},{12,0},{16,20},{20,24},{24,28},{28,16},{32,36},... | collective-permute-start | bytes 540680 | tf_op jit(solution)/shard_map/ppermute | solution.py:190
  4.3 38.8 %collective-permute-start.22 = (bf16[1,512,64]{1,2,0:T(8,128)(2,1)}, bf16[1,512,64]{1,2,0:T(8,128)(2,1)}, u32[]{:S(2)}, u32[]{:S(2)}) collective-permute-start(bf16[1,512,64]{1,2,0:T(8,128)(2,1)} %bitcast.637), channel_id=1, source_target_pairs={{0,96},{4,100},{8,104},{12,108},{16,112},{20,116},{24,120},{28,124... | collective-permute-start | bytes 196616 | tf_op jit(solution)/shard_map/ppermute | solution.py:191
  6.8 36.4 %collective-permute-start.23 = (bf16[1,512,64]{1,2,0:T(8,128)(2,1)}, bf16[1,512,64]{1,2,0:T(8,128)(2,1)}, u32[]{:S(2)}, u32[]{:S(2)}) collective-permute-start(bf16[1,512,64]{1,2,0:T(8,128)(2,1)} %bitcast.638), channel_id=1, source_target_pairs={{0,32},{4,36},{8,40},{12,44},{16,48},{20,52},{24,56},{28,60},{32,6... | collective-permute-start | bytes 196616 | tf_op jit(solution)/shard_map/ppermute | solution.py:190
  6.8 22.9 %collective-permute-start.12 = (bf16[2,128,16]{1,2,0:T(8,128)(2,1)}, bf16[2,128,16]{1,2,0:T(8,128)(2,1)S(1)}, u32[]{:S(2)}, u32[]{:S(2)}) collective-permute-start(bf16[2,128,16]{1,2,0:T(8,128)(2,1)} %param.35), channel_id=1, source_target_pairs={{0,2},{1,3},{2,0},{3,1},{4,6},{5,7},{6,4},{7,5},{8,10},{9,11},{10,... | collective-permute-start | bytes 24584 | tf_op jit(solution)/shard_map/ppermute | solution.py:106
  39.0 33.1 %collective-permute-start.34 = (bf16[2,1,64,1408]{3,2,1,0:T(8,128)(2,1)}, bf16[2,1,64,1408]{3,2,1,0:T(8,128)(2,1)S(1)}, u32[]{:S(2)}, u32[]{:S(2)}) collective-permute-start(bf16[2,1,64,1408]{3,2,1,0:T(8,128)(2,1)} %bitcast.624), channel_id=1, source_target_pairs={{0,96},{4,100},{8,104},{12,108},{16,112},{20,116},{24,120},{28,124... | collective-permute-start | bytes 1081352 | tf_op jit(solution)/shard_map/ppermute | solution.py:191
  43.1 37.4 %collective-permute-start.35 = (bf16[2,1,64,1408]{3,2,1,0:T(8,128)(2,1)}, bf16[2,1,64,1408]{3,2,1,0:T(8,128)(2,1)S(1)}, u32[]{:S(2)}, u32[]{:S(2)}) collective-permute-start(bf16[2,1,64,1408]{3,2,1,0:T(8,128)(2,1)} %bitcast.625), channel_id=1, source_target_pairs={{0,32},{4,36},{8,40},{12,44},{16,48},{20,52},{24,56},{28,60},{32,6... | collective-permute-start | bytes 1081352 | tf_op jit(solution)/shard_map/ppermute | solution.py:190
  61.0 31.6 %collective-permute-start = (bf16[2,64,2048]{2,1,0:T(8,128)(2,1)S(1)}, bf16[2,64,2048]{2,1,0:T(8,128)(2,1)S(1)}, u32[]{:S(2)}, u32[]{:S(2)}) collective-permute-start(bf16[2,64,2048]{2,1,0:T(8,128)(2,1)S(1)} %copy-done.75), channel_id=1, source_target_pairs={{0,2},{1,3},{2,0},{3,1},{4,6},{5,7},{6,4},{7,5},{8,10},{9,11},{10,... | collective-permute-start | bytes 1572872 | tf_op jit(solution)/shard_map/ppermute | solution.py:106
  67.1 28.5 %collective-permute-start.52 = (bf16[2,64,2048]{2,1,0:T(8,128)(2,1)S(1)}, bf16[2,64,2048]{2,1,0:T(8,128)(2,1)S(1)}, u32[]{:S(2)}, u32[]{:S(2)}) collective-permute-start(bf16[2,64,2048]{2,1,0:T(8,128)(2,1)S(1)} %copy-done.35), channel_id=1, source_target_pairs={{0,2},{1,3},{2,0},{3,1},{4,6},{5,7},{6,4},{7,5},{8,10},{9,11},{10,... | collective-permute-start | bytes 1572872 | tf_op jit(solution)/shard_map/ppermute | solution.py:106
  71.5 17.7 %collective-permute-start.25 = (bf16[4,512,64]{1,2,0:T(8,128)(2,1)S(1)}, bf16[4,512,64]{1,2,0:T(8,128)(2,1)S(1)}, u32[]{:S(2)}, u32[]{:S(2)}) collective-permute-start(bf16[4,512,64]{1,2,0:T(8,128)(2,1)S(1)} %copy-done.68), channel_id=1, source_target_pairs={{0,16},{4,20},{8,24},{12,28},{16,0},{20,4},{24,8},{28,12},{32,48},... | collective-permute-start | bytes 786440 | tf_op jit(solution)/shard_map/ppermute | solution.py:180
  86.8 34.9 %collective-permute-start.45 = (bf16[4,1408,64]{1,2,0:T(8,128)(2,1)S(1)}, bf16[4,1408,64]{1,2,0:T(8,128)(2,1)S(1)}, u32[]{:S(2)}, u32[]{:S(2)}) collective-permute-start(bf16[4,1408,64]{1,2,0:T(8,128)(2,1)S(1)} %constant_dynamic-update-slice_fusion.13), channel_id=1, source_target_pairs={{0,16},{4,20},{8,24},{12,28},{16,0},{20,4},{24,8},{28,12},{32,48},... | collective-permute-start | bytes 2162696 | tf_op jit(solution)/shard_map/ppermute | solution.py:180
  89.5 26.7 %collective-permute-start.17 = (bf16[4,644,128]{2,0,1:T(4,128)(2,1)S(1)}, bf16[4,644,128]{2,0,1:T(4,128)(2,1)S(1)}, u32[]{:S(2)}, u32[]{:S(2)}) collective-permute-start(bf16[4,644,128]{2,0,1:T(4,128)(2,1)S(1)} %copy.252), channel_id=1, source_target_pairs={{0,16},{4,20},{8,24},{12,28},{16,0},{20,4},{24,8},{28,12},{32,48},... | collective-permute-start | bytes 1978376 | tf_op jit(solution)/shard_map/ppermute | solution.py:180
  95.6 14.2 %collective-permute-start.27 = (bf16[8,512,64]{1,2,0:T(8,128)(2,1)S(1)}, bf16[8,512,64]{1,2,0:T(8,128)(2,1)S(1)}, u32[]{:S(2)}, u32[]{:S(2)}) collective-permute-start(bf16[8,512,64]{1,2,0:T(8,128)(2,1)S(1)} %constant_dynamic-update-slice_fusion.33), channel_id=1, source_target_pairs={{0,4},{4,8},{8,12},{12,0},{16,20},{20,24},{24,28},{28,16},{32,36},... | collective-permute-start | bytes 1572872 | tf_op jit(solution)/shard_map/ppermute | solution.py:190
  96.6 36.4 %collective-permute-start.5 = (bf16[3,4,64,512]{3,2,1,0:T(8,128)(2,1)S(1)}, bf16[3,4,64,512]{3,2,1,0:T(8,128)(2,1)S(1)}, u32[]{:S(2)}, u32[]{:S(2)}) collective-permute-start(bf16[3,4,64,512]{3,2,1,0:T(8,128)(2,1)S(1)} %bitcast_dynamic-update-slice_fusion.1), channel_id=1, source_target_pairs={{0,16},{4,20},{8,24},{12,28},{16,0},{20,4},{24,8},{28,12},{32,48},... | collective-permute-start | bytes 2359304 | tf_op jit(solution)/shard_map/ppermute | solution.py:180
  102.7 43.0 %collective-permute-start.1 = (bf16[2,2,64,2048]{3,2,1,0:T(8,128)(2,1)S(1)}, bf16[2,2,64,2048]{3,2,1,0:T(8,128)(2,1)S(1)}, u32[]{:S(2)}, u32[]{:S(2)}) collective-permute-start(bf16[2,2,64,2048]{3,2,1,0:T(8,128)(2,1)S(1)} %maximum_select_fusion.4), channel_id=1, source_target_pairs={{0,1},{1,0},{2,3},{3,2},{4,5},{5,4},{6,7},{7,6},{8,9},{9,8},{10,11... | collective-permute-start | bytes 3145736 | tf_op jit(solution)/shard_map/ppermute | solution.py:110
  109.8 33.4 %collective-permute-start.53 = (bf16[2,2,64,2048]{3,2,0,1:T(8,128)(2,1)S(1)}, bf16[2,2,64,2048]{3,2,0,1:T(8,128)(2,1)S(1)}, u32[]{:S(2)}, u32[]{:S(2)}) collective-permute-start(bf16[2,2,64,2048]{3,2,0,1:T(8,128)(2,1)S(1)} %maximum_select_fusion.7), channel_id=1, source_target_pairs={{0,1},{1,0},{2,3},{3,2},{4,5},{5,4},{6,7},{7,6},{8,9},{9,8},{10,11... | collective-permute-start | bytes 3145736 | tf_op jit(solution)/shard_map/ppermute | solution.py:110
  121.7 42.3 %collective-permute-start.37 = (bf16[2,4,64,1408]{3,2,1,0:T(8,128)(2,1)}, bf16[2,4,64,1408]{3,2,1,0:T(8,128)(2,1)S(1)}, u32[]{:S(2)}, u32[]{:S(2)}) collective-permute-start(bf16[2,4,64,1408]{3,2,1,0:T(8,128)(2,1)} %constant_dynamic-update-slice_fusion.24), channel_id=1, source_target_pairs={{0,16},{4,20},{8,24},{12,28},{16,0},{20,4},{24,8},{28,12},{32,48},... | collective-permute-start | bytes 4325384 | tf_op jit(solution)/shard_map/ppermute | solution.py:180
  133.0 31.0 %collective-permute-start.19 = (bf16[8,644,128]{2,0,1:T(8,128)(2,1)}, bf16[8,644,128]{2,0,1:T(8,128)(2,1)}, u32[]{:S(2)}, u32[]{:S(2)}) collective-permute-start(bf16[8,644,128]{2,0,1:T(8,128)(2,1)} %copy.254), channel_id=1, source_target_pairs={{0,32},{4,36},{8,40},{12,44},{16,48},{20,52},{24,56},{28,60},{32,6... | collective-permute-start | bytes 3956744 | tf_op jit(solution)/shard_map/ppermute | solution.py:190
  136.5 41.1 %collective-permute-start.18 = (bf16[8,644,128]{2,0,1:T(8,128)(2,1)}, bf16[8,644,128]{2,0,1:T(8,128)(2,1)}, u32[]{:S(2)}, u32[]{:S(2)}) collective-permute-start(bf16[8,644,128]{2,0,1:T(8,128)(2,1)} %copy.254), channel_id=1, source_target_pairs={{0,96},{4,100},{8,104},{12,108},{16,112},{20,116},{24,120},{28,124... | collective-permute-start | bytes 3956744 | tf_op jit(solution)/shard_map/ppermute | solution.py:191
  143.1 45.0 %collective-permute-start.46 = (bf16[8,1408,64]{1,2,0:T(8,128)(2,1)}, bf16[8,1408,64]{1,2,0:T(8,128)(2,1)}, u32[]{:S(2)}, u32[]{:S(2)}) collective-permute-start(bf16[8,1408,64]{1,2,0:T(8,128)(2,1)} %constant_dynamic-update-slice_fusion.11), channel_id=1, source_target_pairs={{0,96},{4,100},{8,104},{12,108},{16,112},{20,116},{24,120},{28,124... | collective-permute-start | bytes 4325384 | tf_op jit(solution)/shard_map/ppermute | solution.py:191
  145.7 45.8 %collective-permute-start.47 = (bf16[8,1408,64]{1,2,0:T(8,128)(2,1)}, bf16[8,1408,64]{1,2,0:T(8,128)(2,1)}, u32[]{:S(2)}, u32[]{:S(2)}) collective-permute-start(bf16[8,1408,64]{1,2,0:T(8,128)(2,1)} %constant_dynamic-update-slice_fusion.11), channel_id=1, source_target_pairs={{0,32},{4,36},{8,40},{12,44},{16,48},{20,52},{24,56},{28,60},{32,6... | collective-permute-start | bytes 4325384 | tf_op jit(solution)/shard_map/ppermute | solution.py:190
  164.0 57.8 %collective-permute-start.6 = (bf16[3,8,64,512]{3,2,1,0:T(8,128)(2,1)}, bf16[3,8,64,512]{3,2,1,0:T(8,128)(2,1)}, u32[]{:S(2)}, u32[]{:S(2)}) collective-permute-start(bf16[3,8,64,512]{3,2,1,0:T(8,128)(2,1)} %constant_dynamic-update-slice_fusion.50), channel_id=1, source_target_pairs={{0,96},{4,100},{8,104},{12,108},{16,112},{20,116},{24,120},{28,124... | collective-permute-start | bytes 4718600 | tf_op jit(solution)/shard_map/ppermute | solution.py:191
  164.0 55.4 %collective-permute-start.7 = (bf16[3,8,64,512]{3,2,1,0:T(8,128)(2,1)}, bf16[3,8,64,512]{3,2,1,0:T(8,128)(2,1)}, u32[]{:S(2)}, u32[]{:S(2)}) collective-permute-start(bf16[3,8,64,512]{3,2,1,0:T(8,128)(2,1)} %constant_dynamic-update-slice_fusion.50), channel_id=1, source_target_pairs={{0,32},{4,36},{8,40},{12,44},{16,48},{20,52},{24,56},{28,60},{32,6... | collective-permute-start | bytes 4718600 | tf_op jit(solution)/shard_map/ppermute | solution.py:190
  177.6 205.6 %collective-permute-start.38 = (bf16[2,8,64,1408]{3,2,1,0:T(8,128)(2,1)}, bf16[2,8,64,1408]{3,2,1,0:T(8,128)(2,1)}, u32[]{:S(2)}, u32[]{:S(2)}) collective-permute-start(bf16[2,8,64,1408]{3,2,1,0:T(8,128)(2,1)} %constant_dynamic-update-slice_fusion.22), channel_id=1, source_target_pairs={{0,12},{4,0},{8,4},{12,8},{16,28},{20,16},{24,20},{28,24},{32,44},... | collective-permute-start | bytes 8650760 | tf_op jit(solution)/shard_map/ppermute | solution.py:191
  188.1 45.4 %collective-permute-start.20 = (bf16[4,644,128]{2,0,1:T(4,128)(2,1)S(1)}, bf16[4,644,128]{2,0,1:T(4,128)(2,1)S(1)}, u32[]{:S(2)}, u32[]{:S(2)}) collective-permute-start(bf16[4,644,128]{2,0,1:T(4,128)(2,1)S(1)} %slice.239), channel_id=1, source_target_pairs={{0,32},{4,36},{8,40},{12,44},{16,48},{20,52},{24,56},{28,60},{32,6... | collective-permute-start | bytes 1978376 | tf_op jit(solution)/shard_map/ppermute | solution.py:194
  191.5 44.4 %collective-permute-start.21 = (bf16[4,644,128]{2,0,1:T(4,128)(2,1)S(1)}, bf16[4,644,128]{2,0,1:T(4,128)(2,1)S(1)}, u32[]{:S(2)}, u32[]{:S(2)}) collective-permute-start(bf16[4,644,128]{2,0,1:T(4,128)(2,1)S(1)} %slice.240), channel_id=1, source_target_pairs={{0,96},{4,100},{8,104},{12,108},{16,112},{20,116},{24,120},{28,124... | collective-permute-start | bytes 1978376 | tf_op jit(solution)/shard_map/ppermute | solution.py:195
  219.4 162.2 %collective-permute-start.39 = (bf16[2,8,64,1408]{3,2,1,0:T(8,128)(2,1)}, bf16[2,8,64,1408]{3,2,1,0:T(8,128)(2,1)}, u32[]{:S(2)}, u32[]{:S(2)}) collective-permute-start(bf16[2,8,64,1408]{3,2,1,0:T(8,128)(2,1)} %constant_dynamic-update-slice_fusion.22), channel_id=1, source_target_pairs={{0,4},{4,8},{8,12},{12,0},{16,20},{20,24},{24,28},{28,16},{32,36},... | collective-permute-start | bytes 8650760 | tf_op jit(solution)/shard_map/ppermute | solution.py:190
  221.8 155.7 %collective-permute-start.48 = (bf16[4,1408,64]{1,2,0:T(8,128)(2,1)}, bf16[4,1408,64]{1,2,0:T(8,128)(2,1)}, u32[]{:S(2)}, u32[]{:S(2)}) collective-permute-start(bf16[4,1408,64]{1,2,0:T(8,128)(2,1)} %slice.275), channel_id=1, source_target_pairs={{0,32},{4,36},{8,40},{12,44},{16,48},{20,52},{24,56},{28,60},{32,6... | collective-permute-start | bytes 2162696 | tf_op jit(solution)/shard_map/ppermute | solution.py:194
  233.5 64.6 %collective-permute-start.8 = (bf16[3,4,64,512]{3,2,1,0:T(8,128)(2,1)}, bf16[3,4,64,512]{3,2,1,0:T(8,128)(2,1)}, u32[]{:S(2)}, u32[]{:S(2)}) collective-permute-start(bf16[3,4,64,512]{3,2,1,0:T(8,128)(2,1)} %slice.236), channel_id=1, source_target_pairs={{0,32},{4,36},{8,40},{12,44},{16,48},{20,52},{24,56},{28,60},{32,6... | collective-permute-start | bytes 2359304 | tf_op jit(solution)/shard_map/ppermute | solution.py:194
  235.9 64.5 %collective-permute-start.9 = (bf16[3,4,64,512]{3,2,1,0:T(8,128)(2,1)}, bf16[3,4,64,512]{3,2,1,0:T(8,128)(2,1)}, u32[]{:S(2)}, u32[]{:S(2)}) collective-permute-start(bf16[3,4,64,512]{3,2,1,0:T(8,128)(2,1)} %slice.237), channel_id=1, source_target_pairs={{0,96},{4,100},{8,104},{12,108},{16,112},{20,116},{24,120},{28,124... | collective-permute-start | bytes 2359304 | tf_op jit(solution)/shard_map/ppermute | solution.py:195
  298.1 81.5 %collective-permute-start.49 = (bf16[4,1408,64]{1,2,0:T(8,128)(2,1)}, bf16[4,1408,64]{1,2,0:T(8,128)(2,1)}, u32[]{:S(2)}, u32[]{:S(2)}) collective-permute-start(bf16[4,1408,64]{1,2,0:T(8,128)(2,1)} %slice.276), channel_id=1, source_target_pairs={{0,96},{4,100},{8,104},{12,108},{16,112},{20,116},{24,120},{28,124... | collective-permute-start | bytes 2162696 | tf_op jit(solution)/shard_map/ppermute | solution.py:195
  338.2 49.2 %collective-permute-start.30 = (f32[2,2,64,2048]{3,2,0,1:T(8,128)}, f32[2,2,64,2048]{3,2,0,1:T(8,128)}, u32[]{:S(2)}, u32[]{:S(2)}) collective-permute-start(f32[2,2,64,2048]{3,2,0,1:T(8,128)} %bitcast.504), channel_id=1, source_target_pairs={{0,1},{1,0},{2,3},{3,2},{4,5},{5,4},{6,7},{7,6},{8,9},{9,8},{10,11... | collective-permute-start | bytes 6291464 | tf_op jit(solution)/shard_map/ppermute | solution.py:125
  383.1 34.5 %collective-permute-start.40 = (bf16[2,4,64,1408]{3,2,1,0:T(8,128)(2,1)S(1)}, bf16[2,4,64,1408]{3,2,1,0:T(8,128)(2,1)S(1)}, u32[]{:S(2)}, u32[]{:S(2)}) collective-permute-start(bf16[2,4,64,1408]{3,2,1,0:T(8,128)(2,1)S(1)} %slice.266), channel_id=1, source_target_pairs={{0,4},{4,8},{8,12},{12,0},{16,20},{20,24},{24,28},{28,16},{32,36},... | collective-permute-start | bytes 4325384 | tf_op jit(solution)/shard_map/ppermute | solution.py:194
  384.8 34.0 %collective-permute-start.41 = (bf16[2,4,64,1408]{3,2,1,0:T(8,128)(2,1)S(1)}, bf16[2,4,64,1408]{3,2,1,0:T(8,128)(2,1)S(1)}, u32[]{:S(2)}, u32[]{:S(2)}) collective-permute-start(bf16[2,4,64,1408]{3,2,1,0:T(8,128)(2,1)S(1)} %slice.267), channel_id=1, source_target_pairs={{0,12},{4,0},{8,4},{12,8},{16,28},{20,16},{24,20},{28,24},{32,44},... | collective-permute-start | bytes 4325384 | tf_op jit(solution)/shard_map/ppermute | solution.py:195
  389.4 14.5 %collective-permute-start.31 = (bf16[2,64,2048]{2,1,0:T(8,128)(2,1)S(1)}, bf16[2,64,2048]{2,1,0:T(8,128)(2,1)S(1)}, u32[]{:S(2)}, u32[]{:S(2)}) collective-permute-start(bf16[2,64,2048]{2,1,0:T(8,128)(2,1)S(1)} %fusion.43), channel_id=1, source_target_pairs={{0,2},{1,3},{2,0},{3,1},{4,6},{5,7},{6,4},{7,5},{8,10},{9,11},{10,... | collective-permute-start | bytes 1572872 | tf_op jit(solution)/shard_map/ppermute | solution.py:128
  404.4 15.8 %collective-permute-start.32 = (bf16[2,64,2048]{2,1,0:T(8,128)(2,1)S(1)}, bf16[2,64,2048]{2,1,0:T(8,128)(2,1)S(1)}, u32[]{:S(2)}, u32[]{:S(2)}) collective-permute-start(bf16[2,64,2048]{2,1,0:T(8,128)(2,1)S(1)} %multiply_convert_fusion.3), channel_id=1, source_target_pairs={{0,2},{1,3},{2,0},{3,1},{4,6},{5,7},{6,4},{7,5},{8,10},{9,11},{10,... | collective-permute-start | bytes 1572872 | tf_op jit(solution)/shard_map/ppermute | solution.py:106
  421.3 15.7 %collective-permute-start.33 = (bf16[2,2,64,2048]{3,2,0,1:T(8,128)(2,1)}, bf16[2,2,64,2048]{3,2,0,1:T(8,128)(2,1)S(1)}, u32[]{:S(2)}, u32[]{:S(2)}) collective-permute-start(bf16[2,2,64,2048]{3,2,0,1:T(8,128)(2,1)} %maximum_select_fusion.6), channel_id=1, source_target_pairs={{0,1},{1,0},{2,3},{3,2},{4,5},{5,4},{6,7},{7,6},{8,9},{9,8},{10,11... | collective-permute-start | bytes 3145736 | tf_op jit(solution)/shard_map/ppermute | solution.py:110
  494.2 15.1 %collective-permute-start.55 = (bf16[2,64,2048]{2,1,0:T(8,128)(2,1)S(1)}, bf16[2,64,2048]{2,1,0:T(8,128)(2,1)S(1)}, u32[]{:S(2)}, u32[]{:S(2)}) collective-permute-start(bf16[2,64,2048]{2,1,0:T(8,128)(2,1)S(1)} %fusion.45), channel_id=1, source_target_pairs={{0,2},{1,3},{2,0},{3,1},{4,6},{5,7},{6,4},{7,5},{8,10},{9,11},{10,... | collective-permute-start | bytes 1572872 | tf_op jit(solution)/shard_map/ppermute | solution.py:128
  498.5 22.1 %collective-permute-start.51 = (bf16[2,64,2048]{2,1,0:T(8,128)(2,1)S(1)}, bf16[2,64,2048]{2,1,0:T(8,128)(2,1)S(1)}, u32[]{:S(2)}, u32[]{:S(2)}) collective-permute-start(bf16[2,64,2048]{2,1,0:T(8,128)(2,1)S(1)} %fusion.44), channel_id=1, source_target_pairs={{0,2},{1,3},{2,0},{3,1},{4,6},{5,7},{6,4},{7,5},{8,10},{9,11},{10,... | collective-permute-start | bytes 1572872 | tf_op jit(solution)/shard_map/ppermute | solution.py:128
  522.3 14.2 %collective-permute-start.56 = (bf16[2,64,2048]{2,1,0:T(8,128)(2,1)S(1)}, bf16[2,64,2048]{2,1,0:T(8,128)(2,1)S(1)}, u32[]{:S(2)}, u32[]{:S(2)}) collective-permute-start(bf16[2,64,2048]{2,1,0:T(8,128)(2,1)S(1)} %get-tuple-element.34), channel_id=1, source_target_pairs={{0,2},{1,3},{2,0},{3,1},{4,6},{5,7},{6,4},{7,5},{8,10},{9,11},{10,... | collective-permute-start | bytes 1572872 | tf_op jit(solution)/shard_map/ppermute | solution.py:106
  524.4 25.5 %collective-permute-start.62 = (f32[2,2,256,16]{2,3,1,0:T(8,128)S(1)}, f32[2,2,256,16]{2,3,1,0:T(8,128)S(1)}, u32[]{:S(2)}, u32[]{:S(2)}) collective-permute-start(f32[2,2,256,16]{2,3,1,0:T(8,128)S(1)} %pad_maximum_fusion.11), channel_id=1, source_target_pairs={{0,1},{1,0},{2,3},{3,2},{4,5},{5,4},{6,7},{7,6},{8,9},{9,8},{10,11... | collective-permute-start | bytes 196616 | tf_op jit(solution)/shard_map/ppermute | solution.py:134
  537.6 25.9 %collective-permute-start.57 = (bf16[2,2,64,2048]{3,2,0,1:T(8,128)(2,1)}, bf16[2,2,64,2048]{3,2,0,1:T(8,128)(2,1)}, u32[]{:S(2)}, u32[]{:S(2)}) collective-permute-start(bf16[2,2,64,2048]{3,2,0,1:T(8,128)(2,1)} %maximum_select_fusion.9), channel_id=1, source_target_pairs={{0,1},{1,0},{2,3},{3,2},{4,5},{5,4},{6,7},{7,6},{8,9},{9,8},{10,11... | collective-permute-start | bytes 3145736 | tf_op jit(solution)/shard_map/ppermute | solution.py:110
  554.9 115.9 %all-to-all-start.2 = ((bf16[32,132,128]{2,1,0:T(8,128)(2,1)}), bf16[32,132,128]{2,1,0:T(8,128)(2,1)}, u32[]{:S(2)}, u32[]{:S(2)}) async-start(bf16[32,132,128]{2,1,0:T(8,128)(2,1)} %pad_maximum_fusion.3), calls=%async_computation.2 | async-start | bytes 2228224 | tf_op jit(solution)/shard_map/all_to_all | solution.py:472
  626.4 22.5 %collective-permute-start.60 = (f32[5,2,256,16]{2,3,1,0:T(8,128)}, f32[5,2,256,16]{2,3,1,0:T(8,128)S(1)}, u32[]{:S(2)}, u32[]{:S(2)}) collective-permute-start(f32[5,2,256,16]{2,3,1,0:T(8,128)} %bitcast_dynamic-update-slice_fusion.4), channel_id=1, source_target_pairs={{0,1},{1,0},{2,3},{3,2},{4,5},{5,4},{6,7},{7,6},{8,9},{9,8},{10,11... | collective-permute-start | bytes 491528 | tf_op jit(solution)/shard_map/ppermute | solution.py:134
  647.9 51.5 %collective-permute-start.58 = (f32[2,2,64,2048]{3,2,0,1:T(8,128)}, f32[2,2,64,2048]{3,2,0,1:T(8,128)}, u32[]{:S(2)}, u32[]{:S(2)}) collective-permute-start(f32[2,2,64,2048]{3,2,0,1:T(8,128)} %bitcast.501), channel_id=1, source_target_pairs={{0,1},{1,0},{2,3},{3,2},{4,5},{5,4},{6,7},{7,6},{8,9},{9,8},{10,11... | collective-permute-start | bytes 6291464 | tf_op jit(solution)/shard_map/ppermute | solution.py:125
  670.8 20.7 %all-to-all-start.1 = ((bf16[32,64,128]{2,1,0:T(8,128)(2,1)}), bf16[32,64,128]{2,1,0:T(8,128)(2,1)}, u32[]{:S(2)}, u32[]{:S(2)}) async-start(bf16[32,64,128]{2,1,0:T(8,128)(2,1)} %pad_maximum_fusion.8), calls=%async_computation.1 | async-start | bytes 1048576 | tf_op jit(solution)/shard_map/all_to_all | solution.py:472
  691.6 30.0 %all-to-all-start = ((f32[32,112,128]{2,1,0:T(8,128)}), f32[32,112,128]{2,1,0:T(8,128)}, u32[]{:S(2)}, u32[]{:S(2)}) async-start(f32[32,112,128]{2,1,0:T(8,128)} %pad_maximum_fusion.2), calls=%async_computation | async-start | bytes 3670016 | tf_op jit(solution)/shard_map/all_to_all | solution.py:472
  702.7 32.5 %collective-permute-start.59 = (bf16[2,64,2048]{2,1,0:T(8,128)(2,1)}, bf16[2,64,2048]{2,1,0:T(8,128)(2,1)}, u32[]{:S(2)}, u32[]{:S(2)}) collective-permute-start(bf16[2,64,2048]{2,1,0:T(8,128)(2,1)} %fusion.46), channel_id=1, source_target_pairs={{0,2},{1,3},{2,0},{3,1},{4,6},{5,7},{6,4},{7,5},{8,10},{9,11},{10,... | collective-permute-start | bytes 1572872 | tf_op jit(solution)/shard_map/ppermute | solution.py:128
  (153 other events, 1494.7 us)

commit v15 on v12

--- a/solution.py
+++ b/solution.py
@@ -495,7 +495,7 @@
         jnp.bfloat16,
     )
     a_in_block, b_rows_block = reduce_to_owners(
-        [jnp.moveaxis(a_in_mine, 1, 0), jnp.moveaxis(b_rows_mine, 2, 0)], jnp.float32
+        [jnp.moveaxis(a_in_mine, 1, 0), jnp.moveaxis(b_rows_mine, 2, 0)], jnp.bfloat16
     )
 
     return (

time: 748 us -> 717 us (0.959)
  waiting for transfers between devices: 139 us -> 124 us
  local copies, waits for them, and re-layouts: 271 us -> 261 us
    all_to_all x3, waiting for transfers between devices: 10.3 us -> 2.16 us  [reduce_to_owners(): lax.all_to_all(packed, 'fsdp', 0, 0, tiled=False).astype(jnp.float32).sum(0)]
    unnamed x277 -> x291, local copies, waits for them, and re-layouts: 23 us -> 24.9 us
where the time goes in v15:
time: 717 us; the launch traced here: 704 us
  local copies, waits for them, and re-layouts  261 us (36%)
  waiting for transfers between devices  124 us (17%)
  starting transfers between devices  123 us (17%)
  matrix products  121 us (17%)
  other arithmetic  66.7 us (9%)
  between operations  8.73 us (1%)
    dynamic_update_slice x57, local copies, waits for them, and re-layouts, put(): return lax.dynamic_update_slice(buffer, piece, start)  62.2 us
    dot_general x37, matrix products, hp_dot(): jnp.einsum(spec, left, right, precision=highest, preferred_element_type=j...  58.6 us
    ppermute x4, waiting for transfers between devices, tok_scatter(): got = lax.ppermute(send.astype(jnp.bfloat16), 'tok', xor_pairs(count, 2))  29.9 us
    unnamed x291, local copies, waits for them, and re-layouts  24.9 us
    ppermute x5, waiting for transfers between devices, pair_stage(): other = lax.ppermute(stacks, 'fsdp', fsdp_pairs('z', 1))  24.6 us
    ppermute x10, starting transfers between devices, ring_stage(): from_right = lax.ppermute(stacks, 'fsdp', fsdp_pairs(kind, -1))  24.2 us
    dot_general x5, matrix products, column_backward(): jnp.einsum('ste,de->std', grad_rows, weight, preferred_element_type=jnp.f...  23.2 us
    ppermute x4, starting transfers between devices, tok_scatter(): chip_sum = mine + lax.ppermute(theirs, 'tok', xor_pairs(count, 1))  21.5 us
  transfers between devices with their start and end apart: 67, of which 24 were waited for; matrix products, arithmetic and copies ran while one was open for 55% of the time, Pallas kernels for 0%

profile of v15, /device:TPU:1, one launch (start us, length us, event | category | flops | bytes accessed | tf_op | source)
XLA Modules:
  0.0 703.7 jit_solution(8039726420985079205)
XLA Ops:
  0.7 3.6 collective-permute-start.42
  7.0 3.6 collective-permute-start.12
  47.2 3.1 collective-permute-done.24
  65.6 5.3 collective-permute-done.44
  73.9 5.3 collective-permute-done.16
  96.8 7.1 %collective-permute-start.1 = (bf16[2,2,64,2048]{3,2,1,0:T(8,128)(2,1)S(1)}, bf16[2,2,64,2048]{3,2,1,0:T(8,128)(2,1)S(1)}, u32[]{:S(2)}, u32[]{:S(2)}) collective-permute-start(bf16[2,2,64,2048]{3,2,1,0:T(8,128)(2,1)S(1)} %maximum_select_fusion.4), channel_id=1, source_target_pairs={{0,1},{1,0},{2,3},{3,2},{4,5},{5,4},{6,7},{7,6},{8,9},{9,8},{10,11... | collective-permute-start | bytes 3145736 | tf_op jit(solution)/shard_map/ppermute | solution.py:110
  118.2 6.9 collective-permute-done.5
  139.1 17.0 %collective-permute-done.37 = bf16[2,4,64,1408]{3,2,1,0:T(8,128)(2,1)S(1)} collective-permute-done((bf16[2,4,64,1408]{3,2,1,0:T(8,128)(2,1)}, bf16[2,4,64,1408]{3,2,1,0:T(8,128)(2,1)S(1)}, u32[]{:S(2)}, u32[]{:S(2)}) %collective-permute-start.37) | collective-permute-done | bytes 1441824 | tf_op jit(solution)/shard_map/ppermute | solution.py:180
  159.2 5.7 broadcast_in_dim.134
  164.9 3.6 constant_dynamic-update-slice_fusion.21
  170.0 3.7 collective-permute-start.38
  193.8 17.3 %collective-permute-done.7 = bf16[3,8,64,512]{3,2,1,0:T(8,128)(2,1)} collective-permute-done((bf16[3,8,64,512]{3,2,1,0:T(8,128)(2,1)}, bf16[3,8,64,512]{3,2,1,0:T(8,128)(2,1)}, u32[]{:S(2)}, u32[]{:S(2)}) %collective-permute-start.7) | collective-permute-done | bytes 1572896 | tf_op jit(solution)/shard_map/ppermute | solution.py:190
  221.6 3.7 collective-permute-done.20
  229.0 3.5 collective-permute-start.9
  237.2 3.9 constant_dynamic-slice_fusion.14
  250.9 4.8 copy.279
  255.7 6.4 copy.280
  262.1 3.5 constant_dynamic-slice_fusion.10
  293.6 5.7 fusion.123
  305.5 4.1 convolution_add_fusion.2
  328.4 20.6 %collective-permute-start.30 = (f32[2,2,64,2048]{3,2,0,1:T(8,128)}, f32[2,2,64,2048]{3,2,0,1:T(8,128)}, u32[]{:S(2)}, u32[]{:S(2)}) collective-permute-start(f32[2,2,64,2048]{3,2,0,1:T(8,128)} %bitcast.503), channel_id=1, source_target_pairs={{0,1},{1,0},{2,3},{3,2},{4,5},{5,4},{6,7},{7,6},{8,9},{9,8},{10,11... | collective-permute-start | bytes 6291464 | tf_op jit(solution)/shard_map/ppermute | solution.py:125
  354.1 4.4 constant_dynamic-slice_fusion.7
  383.6 3.6 constant_dynamic-update-slice_fusion.20
  387.2 3.7 constant_dynamic-update-slice_fusion.19
  390.9 5.5 collective-permute-done.31
  399.7 10.4 %collective-permute-done.40 = bf16[2,4,64,1408]{3,2,1,0:T(8,128)(2,1)S(1)} collective-permute-done((bf16[2,4,64,1408]{3,2,1,0:T(8,128)(2,1)S(1)}, bf16[2,4,64,1408]{3,2,1,0:T(8,128)(2,1)S(1)}, u32[]{:S(2)}, u32[]{:S(2)}) %collective-permute-start.40) | collective-permute-done | bytes 1441824 | tf_op jit(solution)/shard_map/ppermute | solution.py:194
  415.5 9.7 %fusion.122 = (bf16[1,4,2,4,64,1408]{5,4,1,2,3,0:T(8,128)(2,1)}, bf16[1,4,2,4,64,1408]{5,4,1,2,3,0:T(8,128)(2,1)}) fusion(bf16[2,4,2,4,64,1408]{5,4,1,2,3,0:T(8,128)(2,1)} %bitcast.80), kind=kLoop, calls=%fused_computation.351 | loop fusion | bytes 23068672 | tf_op jit(solution)/shard_map/slice | solution.py:366
  425.2 3.3 copy.288
  435.4 3.4 fusion.130
  439.5 3.4 fusion.129
  446.1 3.2 fusion.4
  449.3 7.1 %fusion.8 = (bf16[2,256,1408]{2,1,0:T(8,128)(2,1)S(1)}, bf16[2,256,1408]{2,1,0:T(8,128)(2,1)S(1)}, bf16[2,256,1408]{2,1,0:T(8,128)(2,1)S(1)}) fusion(f32[2,256,1408]{2,1,0:T(8,128)} %fusion.4, f32[2,256,1408]{2,1,0:T(8,128)} %fusion.5, f32[2,256,1408]{2,1,0:T(8,128)} %fusion.133, bf16[2,256,2048]{2,1,0:T(8,128)(2,1)S(1)} %bitcast.551, ...), kind=kOutput, calls=%fused_computation.18 | convolution fusion | flops 2965045248 | bytes 20840448 | tf_op jit(solution)/shard_map/ste,de->std/dot_general | solution.py:380
  456.9 5.1 fusion.134
  462.4 3.4 fusion.135
  476.7 3.5 multiply_add_fusion
  496.5 9.1 %collective-permute-done.55 = bf16[2,64,2048]{2,1,0:T(8,128)(2,1)S(1)} collective-permute-done((bf16[2,64,2048]{2,1,0:T(8,128)(2,1)S(1)}, bf16[2,64,2048]{2,1,0:T(8,128)(2,1)S(1)}, u32[]{:S(2)}, u32[]{:S(2)}) %collective-permute-start.55) | collective-permute-done | bytes 524320 | tf_op jit(solution)/shard_map/ppermute | solution.py:128
  506.0 10.9 %collective-permute-done.51 = bf16[2,64,2048]{2,1,0:T(8,128)(2,1)S(1)} collective-permute-done((bf16[2,64,2048]{2,1,0:T(8,128)(2,1)S(1)}, bf16[2,64,2048]{2,1,0:T(8,128)(2,1)S(1)}, u32[]{:S(2)}, u32[]{:S(2)}) %collective-permute-start.51) | collective-permute-done | bytes 524320 | tf_op jit(solution)/shard_map/ppermute | solution.py:128
  523.5 9.3 %collective-permute-done.56 = bf16[2,64,2048]{2,1,0:T(8,128)(2,1)S(1)} collective-permute-done((bf16[2,64,2048]{2,1,0:T(8,128)(2,1)S(1)}, bf16[2,64,2048]{2,1,0:T(8,128)(2,1)S(1)}, u32[]{:S(2)}, u32[]{:S(2)}) %collective-permute-start.56) | collective-permute-done | bytes 524320 | tf_op jit(solution)/shard_map/ppermute | solution.py:106
  550.0 5.6 all-to-all-start.2
  562.2 3.8 convolution_add_fusion.1
  585.2 3.9 multiply_add_fusion.5
  595.9 4.5 fusion.137
  605.4 4.4 fusion.138
  622.5 5.7 add_add_fusion
  647.4 3.7 convolution_bitcast_fusion
  651.1 7.4 %all-to-all-start.1 = ((bf16[32,64,128]{2,1,0:T(8,128)(2,1)}), bf16[32,64,128]{2,1,0:T(8,128)(2,1)S(1)}, u32[]{:S(2)}, u32[]{:S(2)}) async-start(bf16[32,64,128]{2,1,0:T(8,128)(2,1)} %pad_maximum_fusion.8), calls=%async_computation.1 | async-start | bytes 1048576 | tf_op jit(solution)/shard_map/all_to_all | solution.py:470
  668.4 5.6 all-to-all-start
  695.2 4.3 collective-permute-done.59
  (705 shorter events, 408.6 us)
Async XLA Ops:
  0.7 51.4 %collective-permute-start.42 = (bf16[1,1408,64]{1,2,0:T(8,128)(2,1)}, bf16[1,1408,64]{1,2,0:T(8,128)(2,1)}, u32[]{:S(2)}, u32[]{:S(2)}) collective-permute-start(bf16[1,1408,64]{1,2,0:T(8,128)(2,1)} %bitcast.626), channel_id=1, source_target_pairs={{0,12},{4,0},{8,4},{12,8},{16,28},{20,16},{24,20},{28,24},{32,44},... | collective-permute-start | bytes 540680 | tf_op jit(solution)/shard_map/ppermute | solution.py:191
  4.3 48.9 %collective-permute-start.43 = (bf16[1,1408,64]{1,2,0:T(8,128)(2,1)}, bf16[1,1408,64]{1,2,0:T(8,128)(2,1)}, u32[]{:S(2)}, u32[]{:S(2)}) collective-permute-start(bf16[1,1408,64]{1,2,0:T(8,128)(2,1)} %bitcast.627), channel_id=1, source_target_pairs={{0,4},{4,8},{8,12},{12,0},{16,20},{20,24},{24,28},{28,16},{32,36},... | collective-permute-start | bytes 540680 | tf_op jit(solution)/shard_map/ppermute | solution.py:190
  4.3 41.0 %collective-permute-start.22 = (bf16[1,512,64]{1,2,0:T(8,128)(2,1)}, bf16[1,512,64]{1,2,0:T(8,128)(2,1)}, u32[]{:S(2)}, u32[]{:S(2)}) collective-permute-start(bf16[1,512,64]{1,2,0:T(8,128)(2,1)} %bitcast.632), channel_id=1, source_target_pairs={{0,12},{4,0},{8,4},{12,8},{16,28},{20,16},{24,20},{28,24},{32,44},... | collective-permute-start | bytes 196616 | tf_op jit(solution)/shard_map/ppermute | solution.py:191
  7.0 38.4 %collective-permute-start.23 = (bf16[1,512,64]{1,2,0:T(8,128)(2,1)}, bf16[1,512,64]{1,2,0:T(8,128)(2,1)}, u32[]{:S(2)}, u32[]{:S(2)}) collective-permute-start(bf16[1,512,64]{1,2,0:T(8,128)(2,1)} %bitcast.633), channel_id=1, source_target_pairs={{0,4},{4,8},{8,12},{12,0},{16,20},{20,24},{24,28},{28,16},{32,36},... | collective-permute-start | bytes 196616 | tf_op jit(solution)/shard_map/ppermute | solution.py:190
  7.0 24.5 %collective-permute-start.12 = (bf16[2,128,16]{1,2,0:T(8,128)(2,1)}, bf16[2,128,16]{1,2,0:T(8,128)(2,1)}, u32[]{:S(2)}, u32[]{:S(2)}) collective-permute-start(bf16[2,128,16]{1,2,0:T(8,128)(2,1)} %param.35), channel_id=1, source_target_pairs={{0,2},{1,3},{2,0},{3,1},{4,6},{5,7},{6,4},{7,5},{8,10},{9,11},{10,... | collective-permute-start | bytes 24584 | tf_op jit(solution)/shard_map/ppermute | solution.py:106
  40.9 23.8 %collective-permute-start.34 = (bf16[2,1,64,1408]{3,2,1,0:T(8,128)(2,1)}, bf16[2,1,64,1408]{3,2,1,0:T(8,128)(2,1)S(1)}, u32[]{:S(2)}, u32[]{:S(2)}) collective-permute-start(bf16[2,1,64,1408]{3,2,1,0:T(8,128)(2,1)} %bitcast.619), channel_id=1, source_target_pairs={{0,96},{4,100},{8,104},{12,108},{16,112},{20,116},{24,120},{28,124... | collective-permute-start | bytes 1081352 | tf_op jit(solution)/shard_map/ppermute | solution.py:191
  45.3 27.9 %collective-permute-start.35 = (bf16[2,1,64,1408]{3,2,1,0:T(8,128)(2,1)}, bf16[2,1,64,1408]{3,2,1,0:T(8,128)(2,1)S(1)}, u32[]{:S(2)}, u32[]{:S(2)}) collective-permute-start(bf16[2,1,64,1408]{3,2,1,0:T(8,128)(2,1)} %bitcast.620), channel_id=1, source_target_pairs={{0,32},{4,36},{8,40},{12,44},{16,48},{20,52},{24,56},{28,60},{32,6... | collective-permute-start | bytes 1081352 | tf_op jit(solution)/shard_map/ppermute | solution.py:190
  53.2 34.2 %collective-permute-start = (bf16[2,64,2048]{2,1,0:T(8,128)(2,1)S(1)}, bf16[2,64,2048]{2,1,0:T(8,128)(2,1)S(1)}, u32[]{:S(2)}, u32[]{:S(2)}) collective-permute-start(bf16[2,64,2048]{2,1,0:T(8,128)(2,1)S(1)} %copy-done.82), channel_id=1, source_target_pairs={{0,2},{1,3},{2,0},{3,1},{4,6},{5,7},{6,4},{7,5},{8,10},{9,11},{10,... | collective-permute-start | bytes 1572872 | tf_op jit(solution)/shard_map/ppermute | solution.py:106
  60.6 29.4 %collective-permute-start.52 = (bf16[2,64,2048]{2,1,0:T(8,128)(2,1)S(1)}, bf16[2,64,2048]{2,1,0:T(8,128)(2,1)S(1)}, u32[]{:S(2)}, u32[]{:S(2)}) collective-permute-start(bf16[2,64,2048]{2,1,0:T(8,128)(2,1)S(1)} %copy-done.37), channel_id=1, source_target_pairs={{0,2},{1,3},{2,0},{3,1},{4,6},{5,7},{6,4},{7,5},{8,10},{9,11},{10,... | collective-permute-start | bytes 1572872 | tf_op jit(solution)/shard_map/ppermute | solution.py:106
  64.2 17.2 %collective-permute-start.25 = (bf16[4,512,64]{1,2,0:T(8,128)(2,1)S(1)}, bf16[4,512,64]{1,2,0:T(8,128)(2,1)S(1)}, u32[]{:S(2)}, u32[]{:S(2)}) collective-permute-start(bf16[4,512,64]{1,2,0:T(8,128)(2,1)S(1)} %constant_dynamic-update-slice_fusion.35), channel_id=1, source_target_pairs={{0,16},{4,20},{8,24},{12,28},{16,0},{20,4},{24,8},{28,12},{32,48},... | collective-permute-start | bytes 786440 | tf_op jit(solution)/shard_map/ppermute | solution.py:180
  79.2 35.2 %collective-permute-start.45 = (bf16[4,1408,64]{1,2,0:T(8,128)(2,1)S(1)}, bf16[4,1408,64]{1,2,0:T(8,128)(2,1)S(1)}, u32[]{:S(2)}, u32[]{:S(2)}) collective-permute-start(bf16[4,1408,64]{1,2,0:T(8,128)(2,1)S(1)} %constant_dynamic-update-slice_fusion.13), channel_id=1, source_target_pairs={{0,16},{4,20},{8,24},{12,28},{16,0},{20,4},{24,8},{28,12},{32,48},... | collective-permute-start | bytes 2162696 | tf_op jit(solution)/shard_map/ppermute | solution.py:180
  84.3 24.0 %collective-permute-start.17 = (bf16[4,644,128]{2,0,1:T(4,128)(2,1)S(1)}, bf16[4,644,128]{2,0,1:T(4,128)(2,1)S(1)}, u32[]{:S(2)}, u32[]{:S(2)}) collective-permute-start(bf16[4,644,128]{2,0,1:T(4,128)(2,1)S(1)} %copy.256), channel_id=1, source_target_pairs={{0,16},{4,20},{8,24},{12,28},{16,0},{20,4},{24,8},{28,12},{32,48},... | collective-permute-start | bytes 1978376 | tf_op jit(solution)/shard_map/ppermute | solution.py:180
  90.1 14.7 %collective-permute-start.27 = (bf16[8,512,64]{1,2,0:T(8,128)(2,1)S(1)}, bf16[8,512,64]{1,2,0:T(8,128)(2,1)S(1)}, u32[]{:S(2)}, u32[]{:S(2)}) collective-permute-start(bf16[8,512,64]{1,2,0:T(8,128)(2,1)S(1)} %constant_dynamic-update-slice_fusion.33), channel_id=1, source_target_pairs={{0,32},{4,36},{8,40},{12,44},{16,48},{20,52},{24,56},{28,60},{32,6... | collective-permute-start | bytes 1572872 | tf_op jit(solution)/shard_map/ppermute | solution.py:190
  90.5 34.6 %collective-permute-start.5 = (bf16[3,4,64,512]{3,2,1,0:T(8,128)(2,1)S(1)}, bf16[3,4,64,512]{3,2,1,0:T(8,128)(2,1)S(1)}, u32[]{:S(2)}, u32[]{:S(2)}) collective-permute-start(bf16[3,4,64,512]{3,2,1,0:T(8,128)(2,1)S(1)} %bitcast_dynamic-update-slice_fusion.1), channel_id=1, source_target_pairs={{0,16},{4,20},{8,24},{12,28},{16,0},{20,4},{24,8},{28,12},{32,48},... | collective-permute-start | bytes 2359304 | tf_op jit(solution)/shard_map/ppermute | solution.py:180
  96.8 41.2 %collective-permute-start.1 = (bf16[2,2,64,2048]{3,2,1,0:T(8,128)(2,1)S(1)}, bf16[2,2,64,2048]{3,2,1,0:T(8,128)(2,1)S(1)}, u32[]{:S(2)}, u32[]{:S(2)}) collective-permute-start(bf16[2,2,64,2048]{3,2,1,0:T(8,128)(2,1)S(1)} %maximum_select_fusion.4), channel_id=1, source_target_pairs={{0,1},{1,0},{2,3},{3,2},{4,5},{5,4},{6,7},{7,6},{8,9},{9,8},{10,11... | collective-permute-start | bytes 3145736 | tf_op jit(solution)/shard_map/ppermute | solution.py:110
  104.8 30.6 %collective-permute-start.53 = (bf16[2,2,64,2048]{3,2,0,1:T(8,128)(2,1)S(1)}, bf16[2,2,64,2048]{3,2,0,1:T(8,128)(2,1)S(1)}, u32[]{:S(2)}, u32[]{:S(2)}) collective-permute-start(bf16[2,2,64,2048]{3,2,0,1:T(8,128)(2,1)S(1)} %maximum_select_fusion.7), channel_id=1, source_target_pairs={{0,1},{1,0},{2,3},{3,2},{4,5},{5,4},{6,7},{7,6},{8,9},{9,8},{10,11... | collective-permute-start | bytes 3145736 | tf_op jit(solution)/shard_map/ppermute | solution.py:110
  114.4 41.7 %collective-permute-start.37 = (bf16[2,4,64,1408]{3,2,1,0:T(8,128)(2,1)}, bf16[2,4,64,1408]{3,2,1,0:T(8,128)(2,1)S(1)}, u32[]{:S(2)}, u32[]{:S(2)}) collective-permute-start(bf16[2,4,64,1408]{3,2,1,0:T(8,128)(2,1)} %constant_dynamic-update-slice_fusion.24), channel_id=1, source_target_pairs={{0,16},{4,20},{8,24},{12,28},{16,0},{20,4},{24,8},{28,12},{32,48},... | collective-permute-start | bytes 4325384 | tf_op jit(solution)/shard_map/ppermute | solution.py:180
  115.5 14.5 %collective-permute-start.29 = (bf16[4,512,64]{1,2,0:T(8,128)(2,1)S(1)}, bf16[4,512,64]{1,2,0:T(8,128)(2,1)S(1)}, u32[]{:S(2)}, u32[]{:S(2)}) collective-permute-start(bf16[4,512,64]{1,2,0:T(8,128)(2,1)S(1)} %slice.261), channel_id=1, source_target_pairs={{0,96},{4,100},{8,104},{12,108},{16,112},{20,116},{24,120},{28,124... | collective-permute-start | bytes 786440 | tf_op jit(solution)/shard_map/ppermute | solution.py:195
  125.1 32.9 %collective-permute-start.19 = (bf16[8,644,128]{2,0,1:T(8,128)(2,1)}, bf16[8,644,128]{2,0,1:T(8,128)(2,1)}, u32[]{:S(2)}, u32[]{:S(2)}) collective-permute-start(bf16[8,644,128]{2,0,1:T(8,128)(2,1)} %copy.258), channel_id=1, source_target_pairs={{0,32},{4,36},{8,40},{12,44},{16,48},{20,52},{24,56},{28,60},{32,6... | collective-permute-start | bytes 3956744 | tf_op jit(solution)/shard_map/ppermute | solution.py:190
  130.1 39.9 %collective-permute-start.18 = (bf16[8,644,128]{2,0,1:T(8,128)(2,1)}, bf16[8,644,128]{2,0,1:T(8,128)(2,1)}, u32[]{:S(2)}, u32[]{:S(2)}) collective-permute-start(bf16[8,644,128]{2,0,1:T(8,128)(2,1)} %copy.258), channel_id=1, source_target_pairs={{0,96},{4,100},{8,104},{12,108},{16,112},{20,116},{24,120},{28,124... | collective-permute-start | bytes 3956744 | tf_op jit(solution)/shard_map/ppermute | solution.py:191
  135.4 45.8 %collective-permute-start.46 = (bf16[8,1408,64]{1,2,0:T(8,128)(2,1)}, bf16[8,1408,64]{1,2,0:T(8,128)(2,1)}, u32[]{:S(2)}, u32[]{:S(2)}) collective-permute-start(bf16[8,1408,64]{1,2,0:T(8,128)(2,1)} %constant_dynamic-update-slice_fusion.11), channel_id=1, source_target_pairs={{0,96},{4,100},{8,104},{12,108},{16,112},{20,116},{24,120},{28,124... | collective-permute-start | bytes 4325384 | tf_op jit(solution)/shard_map/ppermute | solution.py:191
  137.9 47.3 %collective-permute-start.47 = (bf16[8,1408,64]{1,2,0:T(8,128)(2,1)}, bf16[8,1408,64]{1,2,0:T(8,128)(2,1)}, u32[]{:S(2)}, u32[]{:S(2)}) collective-permute-start(bf16[8,1408,64]{1,2,0:T(8,128)(2,1)} %constant_dynamic-update-slice_fusion.11), channel_id=1, source_target_pairs={{0,32},{4,36},{8,40},{12,44},{16,48},{20,52},{24,56},{28,60},{32,6... | collective-permute-start | bytes 4325384 | tf_op jit(solution)/shard_map/ppermute | solution.py:190
  156.1 58.8 %collective-permute-start.6 = (bf16[3,8,64,512]{3,2,1,0:T(8,128)(2,1)}, bf16[3,8,64,512]{3,2,1,0:T(8,128)(2,1)}, u32[]{:S(2)}, u32[]{:S(2)}) collective-permute-start(bf16[3,8,64,512]{3,2,1,0:T(8,128)(2,1)} %constant_dynamic-update-slice_fusion.50), channel_id=1, source_target_pairs={{0,96},{4,100},{8,104},{12,108},{16,112},{20,116},{24,120},{28,124... | collective-permute-start | bytes 4718600 | tf_op jit(solution)/shard_map/ppermute | solution.py:191
  158.0 53.1 %collective-permute-start.7 = (bf16[3,8,64,512]{3,2,1,0:T(8,128)(2,1)}, bf16[3,8,64,512]{3,2,1,0:T(8,128)(2,1)}, u32[]{:S(2)}, u32[]{:S(2)}) collective-permute-start(bf16[3,8,64,512]{3,2,1,0:T(8,128)(2,1)} %constant_dynamic-update-slice_fusion.50), channel_id=1, source_target_pairs={{0,32},{4,36},{8,40},{12,44},{16,48},{20,52},{24,56},{28,60},{32,6... | collective-permute-start | bytes 4718600 | tf_op jit(solution)/shard_map/ppermute | solution.py:190
  170.0 205.7 %collective-permute-start.38 = (bf16[2,8,64,1408]{3,2,1,0:T(8,128)(2,1)}, bf16[2,8,64,1408]{3,2,1,0:T(8,128)(2,1)}, u32[]{:S(2)}, u32[]{:S(2)}) collective-permute-start(bf16[2,8,64,1408]{3,2,1,0:T(8,128)(2,1)} %constant_dynamic-update-slice_fusion.22), channel_id=1, source_target_pairs={{0,12},{4,0},{8,4},{12,8},{16,28},{20,16},{24,20},{28,24},{32,44},... | collective-permute-start | bytes 8650760 | tf_op jit(solution)/shard_map/ppermute | solution.py:191
  181.2 44.0 %collective-permute-start.20 = (bf16[4,644,128]{2,0,1:T(4,128)(2,1)S(1)}, bf16[4,644,128]{2,0,1:T(4,128)(2,1)S(1)}, u32[]{:S(2)}, u32[]{:S(2)}) collective-permute-start(bf16[4,644,128]{2,0,1:T(4,128)(2,1)S(1)} %slice.239), channel_id=1, source_target_pairs={{0,32},{4,36},{8,40},{12,44},{16,48},{20,52},{24,56},{28,60},{32,6... | collective-permute-start | bytes 1978376 | tf_op jit(solution)/shard_map/ppermute | solution.py:194
  185.2 43.8 %collective-permute-start.21 = (bf16[4,644,128]{2,0,1:T(4,128)(2,1)S(1)}, bf16[4,644,128]{2,0,1:T(4,128)(2,1)S(1)}, u32[]{:S(2)}, u32[]{:S(2)}) collective-permute-start(bf16[4,644,128]{2,0,1:T(4,128)(2,1)S(1)} %slice.240), channel_id=1, source_target_pairs={{0,96},{4,100},{8,104},{12,108},{16,112},{20,116},{24,120},{28,124... | collective-permute-start | bytes 1978376 | tf_op jit(solution)/shard_map/ppermute | solution.py:195
  211.1 163.1 %collective-permute-start.39 = (bf16[2,8,64,1408]{3,2,1,0:T(8,128)(2,1)}, bf16[2,8,64,1408]{3,2,1,0:T(8,128)(2,1)}, u32[]{:S(2)}, u32[]{:S(2)}) collective-permute-start(bf16[2,8,64,1408]{3,2,1,0:T(8,128)(2,1)} %constant_dynamic-update-slice_fusion.22), channel_id=1, source_target_pairs={{0,4},{4,8},{8,12},{12,0},{16,20},{20,24},{24,28},{28,16},{32,36},... | collective-permute-start | bytes 8650760 | tf_op jit(solution)/shard_map/ppermute | solution.py:190
  214.9 155.2 %collective-permute-start.48 = (bf16[4,1408,64]{1,2,0:T(8,128)(2,1)}, bf16[4,1408,64]{1,2,0:T(8,128)(2,1)}, u32[]{:S(2)}, u32[]{:S(2)}) collective-permute-start(bf16[4,1408,64]{1,2,0:T(8,128)(2,1)} %slice.275), channel_id=1, source_target_pairs={{0,32},{4,36},{8,40},{12,44},{16,48},{20,52},{24,56},{28,60},{32,6... | collective-permute-start | bytes 2162696 | tf_op jit(solution)/shard_map/ppermute | solution.py:194
  225.2 63.5 %collective-permute-start.8 = (bf16[3,4,64,512]{3,2,1,0:T(8,128)(2,1)}, bf16[3,4,64,512]{3,2,1,0:T(8,128)(2,1)}, u32[]{:S(2)}, u32[]{:S(2)}) collective-permute-start(bf16[3,4,64,512]{3,2,1,0:T(8,128)(2,1)} %slice.236), channel_id=1, source_target_pairs={{0,32},{4,36},{8,40},{12,44},{16,48},{20,52},{24,56},{28,60},{32,6... | collective-permute-start | bytes 2359304 | tf_op jit(solution)/shard_map/ppermute | solution.py:194
  229.0 62.5 %collective-permute-start.9 = (bf16[3,4,64,512]{3,2,1,0:T(8,128)(2,1)}, bf16[3,4,64,512]{3,2,1,0:T(8,128)(2,1)}, u32[]{:S(2)}, u32[]{:S(2)}) collective-permute-start(bf16[3,4,64,512]{3,2,1,0:T(8,128)(2,1)} %slice.237), channel_id=1, source_target_pairs={{0,96},{4,100},{8,104},{12,108},{16,112},{20,116},{24,120},{28,124... | collective-permute-start | bytes 2359304 | tf_op jit(solution)/shard_map/ppermute | solution.py:195
  288.7 83.4 %collective-permute-start.49 = (bf16[4,1408,64]{1,2,0:T(8,128)(2,1)}, bf16[4,1408,64]{1,2,0:T(8,128)(2,1)}, u32[]{:S(2)}, u32[]{:S(2)}) collective-permute-start(bf16[4,1408,64]{1,2,0:T(8,128)(2,1)} %slice.276), channel_id=1, source_target_pairs={{0,96},{4,100},{8,104},{12,108},{16,112},{20,116},{24,120},{28,124... | collective-permute-start | bytes 2162696 | tf_op jit(solution)/shard_map/ppermute | solution.py:195
  328.4 51.5 %collective-permute-start.30 = (f32[2,2,64,2048]{3,2,0,1:T(8,128)}, f32[2,2,64,2048]{3,2,0,1:T(8,128)}, u32[]{:S(2)}, u32[]{:S(2)}) collective-permute-start(f32[2,2,64,2048]{3,2,0,1:T(8,128)} %bitcast.503), channel_id=1, source_target_pairs={{0,1},{1,0},{2,3},{3,2},{4,5},{5,4},{6,7},{7,6},{8,9},{9,8},{10,11... | collective-permute-start | bytes 6291464 | tf_op jit(solution)/shard_map/ppermute | solution.py:125
  375.6 34.5 %collective-permute-start.40 = (bf16[2,4,64,1408]{3,2,1,0:T(8,128)(2,1)S(1)}, bf16[2,4,64,1408]{3,2,1,0:T(8,128)(2,1)S(1)}, u32[]{:S(2)}, u32[]{:S(2)}) collective-permute-start(bf16[2,4,64,1408]{3,2,1,0:T(8,128)(2,1)S(1)} %slice.266), channel_id=1, source_target_pairs={{0,4},{4,8},{8,12},{12,0},{16,20},{20,24},{24,28},{28,16},{32,36},... | collective-permute-start | bytes 4325384 | tf_op jit(solution)/shard_map/ppermute | solution.py:194
  377.3 34.0 %collective-permute-start.41 = (bf16[2,4,64,1408]{3,2,1,0:T(8,128)(2,1)S(1)}, bf16[2,4,64,1408]{3,2,1,0:T(8,128)(2,1)S(1)}, u32[]{:S(2)}, u32[]{:S(2)}) collective-permute-start(bf16[2,4,64,1408]{3,2,1,0:T(8,128)(2,1)S(1)} %slice.267), channel_id=1, source_target_pairs={{0,12},{4,0},{8,4},{12,8},{16,28},{20,16},{24,20},{28,24},{32,44},... | collective-permute-start | bytes 4325384 | tf_op jit(solution)/shard_map/ppermute | solution.py:195
  381.9 14.5 %collective-permute-start.31 = (bf16[2,64,2048]{2,1,0:T(8,128)(2,1)S(1)}, bf16[2,64,2048]{2,1,0:T(8,128)(2,1)S(1)}, u32[]{:S(2)}, u32[]{:S(2)}) collective-permute-start(bf16[2,64,2048]{2,1,0:T(8,128)(2,1)S(1)} %fusion.44), channel_id=1, source_target_pairs={{0,2},{1,3},{2,0},{3,1},{4,6},{5,7},{6,4},{7,5},{8,10},{9,11},{10,... | collective-permute-start | bytes 1572872 | tf_op jit(solution)/shard_map/ppermute | solution.py:128
  396.9 15.7 %collective-permute-start.32 = (bf16[2,64,2048]{2,1,0:T(8,128)(2,1)S(1)}, bf16[2,64,2048]{2,1,0:T(8,128)(2,1)S(1)}, u32[]{:S(2)}, u32[]{:S(2)}) collective-permute-start(bf16[2,64,2048]{2,1,0:T(8,128)(2,1)S(1)} %multiply_convert_fusion.3), channel_id=1, source_target_pairs={{0,2},{1,3},{2,0},{3,1},{4,6},{5,7},{6,4},{7,5},{8,10},{9,11},{10,... | collective-permute-start | bytes 1572872 | tf_op jit(solution)/shard_map/ppermute | solution.py:106
  414.5 17.4 %collective-permute-start.33 = (bf16[2,2,64,2048]{3,2,0,1:T(8,128)(2,1)}, bf16[2,2,64,2048]{3,2,0,1:T(8,128)(2,1)}, u32[]{:S(2)}, u32[]{:S(2)}) collective-permute-start(bf16[2,2,64,2048]{3,2,0,1:T(8,128)(2,1)} %maximum_select_fusion.6), channel_id=1, source_target_pairs={{0,1},{1,0},{2,3},{3,2},{4,5},{5,4},{6,7},{7,6},{8,9},{9,8},{10,11... | collective-permute-start | bytes 3145736 | tf_op jit(solution)/shard_map/ppermute | solution.py:110
  490.6 15.1 %collective-permute-start.55 = (bf16[2,64,2048]{2,1,0:T(8,128)(2,1)S(1)}, bf16[2,64,2048]{2,1,0:T(8,128)(2,1)S(1)}, u32[]{:S(2)}, u32[]{:S(2)}) collective-permute-start(bf16[2,64,2048]{2,1,0:T(8,128)(2,1)S(1)} %fusion.46), channel_id=1, source_target_pairs={{0,2},{1,3},{2,0},{3,1},{4,6},{5,7},{6,4},{7,5},{8,10},{9,11},{10,... | collective-permute-start | bytes 1572872 | tf_op jit(solution)/shard_map/ppermute | solution.py:128
  494.4 22.5 %collective-permute-start.51 = (bf16[2,64,2048]{2,1,0:T(8,128)(2,1)S(1)}, bf16[2,64,2048]{2,1,0:T(8,128)(2,1)S(1)}, u32[]{:S(2)}, u32[]{:S(2)}) collective-permute-start(bf16[2,64,2048]{2,1,0:T(8,128)(2,1)S(1)} %fusion.45), channel_id=1, source_target_pairs={{0,2},{1,3},{2,0},{3,1},{4,6},{5,7},{6,4},{7,5},{8,10},{9,11},{10,... | collective-permute-start | bytes 1572872 | tf_op jit(solution)/shard_map/ppermute | solution.py:128
  520.9 23.7 %collective-permute-start.62 = (f32[2,2,256,16]{2,3,1,0:T(8,128)}, f32[2,2,256,16]{2,3,1,0:T(8,128)}, u32[]{:S(2)}, u32[]{:S(2)}) collective-permute-start(f32[2,2,256,16]{2,3,1,0:T(8,128)} %pad_maximum_fusion.11), channel_id=1, source_target_pairs={{0,1},{1,0},{2,3},{3,2},{4,5},{5,4},{6,7},{7,6},{8,9},{9,8},{10,11... | collective-permute-start | bytes 196616 | tf_op jit(solution)/shard_map/ppermute | solution.py:134
  533.9 24.0 %collective-permute-start.57 = (bf16[2,2,64,2048]{3,2,0,1:T(8,128)(2,1)}, bf16[2,2,64,2048]{3,2,0,1:T(8,128)(2,1)}, u32[]{:S(2)}, u32[]{:S(2)}) collective-permute-start(bf16[2,2,64,2048]{3,2,0,1:T(8,128)(2,1)} %maximum_select_fusion.9), channel_id=1, source_target_pairs={{0,1},{1,0},{2,3},{3,2},{4,5},{5,4},{6,7},{7,6},{8,9},{9,8},{10,11... | collective-permute-start | bytes 3145736 | tf_op jit(solution)/shard_map/ppermute | solution.py:110
  550.0 101.1 %all-to-all-start.2 = ((bf16[32,132,128]{2,1,0:T(8,128)(2,1)}), bf16[32,132,128]{2,1,0:T(8,128)(2,1)}, u32[]{:S(2)}, u32[]{:S(2)}) async-start(bf16[32,132,128]{2,1,0:T(8,128)(2,1)} %pad_maximum_fusion.2), calls=%async_computation.2 | async-start | bytes 2228224 | tf_op jit(solution)/shard_map/all_to_all | solution.py:470
  613.5 19.5 %collective-permute-start.60 = (f32[5,2,256,16]{2,3,1,0:T(8,128)}, f32[5,2,256,16]{2,3,1,0:T(8,128)}, u32[]{:S(2)}, u32[]{:S(2)}) collective-permute-start(f32[5,2,256,16]{2,3,1,0:T(8,128)} %bitcast_dynamic-update-slice_fusion.4), channel_id=1, source_target_pairs={{0,1},{1,0},{2,3},{3,2},{4,5},{5,4},{6,7},{7,6},{8,9},{9,8},{10,11... | collective-permute-start | bytes 491528 | tf_op jit(solution)/shard_map/ppermute | solution.py:134
  631.5 42.5 %collective-permute-start.58 = (f32[2,2,64,2048]{3,2,0,1:T(8,128)}, f32[2,2,64,2048]{3,2,0,1:T(8,128)}, u32[]{:S(2)}, u32[]{:S(2)}) collective-permute-start(f32[2,2,64,2048]{3,2,0,1:T(8,128)} %bitcast.500), channel_id=1, source_target_pairs={{0,1},{1,0},{2,3},{3,2},{4,5},{5,4},{6,7},{7,6},{8,9},{9,8},{10,11... | collective-permute-start | bytes 6291464 | tf_op jit(solution)/shard_map/ppermute | solution.py:125
  651.1 16.5 %all-to-all-start.1 = ((bf16[32,64,128]{2,1,0:T(8,128)(2,1)}), bf16[32,64,128]{2,1,0:T(8,128)(2,1)S(1)}, u32[]{:S(2)}, u32[]{:S(2)}) async-start(bf16[32,64,128]{2,1,0:T(8,128)(2,1)} %pad_maximum_fusion.8), calls=%async_computation.1 | async-start | bytes 1048576 | tf_op jit(solution)/shard_map/all_to_all | solution.py:470
  668.4 25.3 %all-to-all-start = ((bf16[32,112,128]{2,1,0:T(8,128)(2,1)}), bf16[32,112,128]{2,1,0:T(8,128)(2,1)S(1)}, u32[]{:S(2)}, u32[]{:S(2)}) async-start(bf16[32,112,128]{2,1,0:T(8,128)(2,1)} %pad_maximum_fusion.5), calls=%async_computation | async-start | bytes 1835008 | tf_op jit(solution)/shard_map/all_to_all | solution.py:470
  677.3 22.2 %collective-permute-start.59 = (bf16[2,64,2048]{2,1,0:T(8,128)(2,1)}, bf16[2,64,2048]{2,1,0:T(8,128)(2,1)}, u32[]{:S(2)}, u32[]{:S(2)}) collective-permute-start(bf16[2,64,2048]{2,1,0:T(8,128)(2,1)} %fusion.47), channel_id=1, source_target_pairs={{0,2},{1,3},{2,0},{3,1},{4,6},{5,7},{6,4},{7,5},{8,10},{9,11},{10,... | collective-permute-start | bytes 1572872 | tf_op jit(solution)/shard_map/ppermute | solution.py:128
  (157 other events, 2124.8 us)

commit v16 on v15

--- a/solution.py
+++ b/solution.py
@@ -487,15 +487,14 @@
     )
     dense_b_qkv = hp_dot(onehot, jnp.stack(attn_grads_up, 1), "src,spre->pce")
     dense_a_out = hp_dot(grad_a_out, onehot, "sdr,src->dc")
-    b_qkv_block, a_out_block = reduce_to_owners(
+    b_qkv_block, a_out_block, a_in_block, b_rows_block = reduce_to_owners(
         [
             jnp.moveaxis(dense_b_qkv.reshape(3, fsdp_count, per, qw_here), 1, 0),
             jnp.moveaxis(dense_a_out.reshape(qw_here, fsdp_count, per), 1, 0),
+            jnp.moveaxis(a_in_mine, 1, 0),
+            jnp.moveaxis(b_rows_mine, 2, 0),
         ],
         jnp.bfloat16,
-    )
-    a_in_block, b_rows_block = reduce_to_owners(
-        [jnp.moveaxis(a_in_mine, 1, 0), jnp.moveaxis(b_rows_mine, 2, 0)], jnp.bfloat16
     )
 
     return (

time: 717 us -> 699 us (0.975)
  waiting for transfers between devices: 124 us -> 136 us
  local copies, waits for them, and re-layouts: 261 us -> 250 us
    all_to_all x3 -> x2, waiting for transfers between devices: 2.16 us -> 10.7 us  [reduce_to_owners(): lax.all_to_all(packed, 'fsdp', 0, 0, tiled=False).astype(jnp.float32).sum(0)]
    all_to_all x3 -> x2, starting transfers between devices: 18.5 us -> 13.1 us  [reduce_to_owners(): lax.all_to_all(packed, 'fsdp', 0, 0, tiled=False).astype(jnp.float32).sum(0)]
    unnamed x291 -> x287, local copies, waits for them, and re-layouts: 24.9 us -> 20.4 us
  transfers between devices with their start and end apart: 67 -> 66, of which waited for: 24 -> 25; matrix products, arithmetic and copies ran while one was open for 55% -> 53% of each run, Pallas kernels for 0% -> 0%
where the time goes in v16:
time: 699 us; the launch traced here: 687 us
  local copies, waits for them, and re-layouts  250 us (36%)
  waiting for transfers between devices  136 us (19%)
  starting transfers between devices  116 us (17%)
  matrix products  114 us (16%)
  other arithmetic  62.7 us (9%)
  between operations  8.83 us (1%)
    dynamic_update_slice x57, local copies, waits for them, and re-layouts, put(): return lax.dynamic_update_slice(buffer, piece, start)  62.2 us
    dot_general x37, matrix products, hp_dot(): jnp.einsum(spec, left, right, precision=highest, preferred_element_type=j...  54 us
    ppermute x4, waiting for transfers between devices, tok_scatter(): got = lax.ppermute(send.astype(jnp.bfloat16), 'tok', xor_pairs(count, 2))  32.9 us
    ppermute x5, waiting for transfers between devices, pair_stage(): other = lax.ppermute(stacks, 'fsdp', fsdp_pairs('z', 1))  24.9 us
    ppermute x10, starting transfers between devices, ring_stage(): from_right = lax.ppermute(stacks, 'fsdp', fsdp_pairs(kind, -1))  24.2 us
    ppermute x4, starting transfers between devices, tok_scatter(): chip_sum = mine + lax.ppermute(theirs, 'tok', xor_pairs(count, 1))  21.3 us
    dot_general x5, matrix products, column_backward(): jnp.einsum('ste,de->std', grad_rows, weight, preferred_element_type=jnp.f...  20.7 us
    unnamed x287, local copies, waits for them, and re-layouts  20.4 us
  transfers between devices with their start and end apart: 66, of which 25 were waited for; matrix products, arithmetic and copies ran while one was open for 53% of the time, Pallas kernels for 0%

profile of v16, /device:TPU:1, one launch (start us, length us, event | category | flops | bytes accessed | tf_op | source)
XLA Modules:
  0.0 687.2 jit_solution(9543461746916197757)
XLA Ops:
  0.7 3.6 collective-permute-start.42
  7.0 3.6 collective-permute-start.12
  47.1 3.1 collective-permute-done.24
  65.6 5.3 collective-permute-done.44
  73.8 5.4 collective-permute-done.16
  96.5 7.0 %collective-permute-start.1 = (bf16[2,2,64,2048]{3,2,1,0:T(8,128)(2,1)S(1)}, bf16[2,2,64,2048]{3,2,1,0:T(8,128)(2,1)S(1)}, u32[]{:S(2)}, u32[]{:S(2)}) collective-permute-start(bf16[2,2,64,2048]{3,2,1,0:T(8,128)(2,1)S(1)} %maximum_select_fusion.4), channel_id=1, source_target_pairs={{0,1},{1,0},{2,3},{3,2},{4,5},{5,4},{6,7},{7,6},{8,9},{9,8},{10,11... | collective-permute-start | bytes 3145736 | tf_op jit(solution)/shard_map/ppermute | solution.py:110
  118.1 7.1 %collective-permute-done.5 = bf16[3,4,64,512]{3,2,1,0:T(8,128)(2,1)S(1)} collective-permute-done((bf16[3,4,64,512]{3,2,1,0:T(8,128)(2,1)S(1)}, bf16[3,4,64,512]{3,2,1,0:T(8,128)(2,1)S(1)}, u32[]{:S(2)}, u32[]{:S(2)}) %collective-permute-start.5) | collective-permute-done | bytes 786464 | tf_op jit(solution)/shard_map/ppermute | solution.py:180
  139.2 17.0 %collective-permute-done.37 = bf16[2,4,64,1408]{3,2,1,0:T(8,128)(2,1)S(1)} collective-permute-done((bf16[2,4,64,1408]{3,2,1,0:T(8,128)(2,1)}, bf16[2,4,64,1408]{3,2,1,0:T(8,128)(2,1)S(1)}, u32[]{:S(2)}, u32[]{:S(2)}) %collective-permute-start.37) | collective-permute-done | bytes 1441824 | tf_op jit(solution)/shard_map/ppermute | solution.py:180
  159.3 5.8 broadcast_in_dim.134
  165.1 3.6 constant_dynamic-update-slice_fusion.21
  170.3 3.6 collective-permute-start.38
  193.9 17.5 %collective-permute-done.7 = bf16[3,8,64,512]{3,2,1,0:T(8,128)(2,1)} collective-permute-done((bf16[3,8,64,512]{3,2,1,0:T(8,128)(2,1)}, bf16[3,8,64,512]{3,2,1,0:T(8,128)(2,1)}, u32[]{:S(2)}, u32[]{:S(2)}) %collective-permute-start.7) | collective-permute-done | bytes 1572896 | tf_op jit(solution)/shard_map/ppermute | solution.py:190
  221.8 3.7 collective-permute-done.20
  229.3 3.3 collective-permute-start.9
  237.3 3.7 constant_dynamic-slice_fusion.14
  250.8 4.7 copy.279
  255.5 6.4 copy.280
  261.9 3.5 constant_dynamic-slice_fusion.10
  293.5 5.8 fusion.123
  305.5 4.1 convolution_add_fusion.2
  328.5 20.4 %collective-permute-start.30 = (f32[2,2,64,2048]{3,2,0,1:T(8,128)}, f32[2,2,64,2048]{3,2,0,1:T(8,128)}, u32[]{:S(2)}, u32[]{:S(2)}) collective-permute-start(f32[2,2,64,2048]{3,2,0,1:T(8,128)} %bitcast.503), channel_id=1, source_target_pairs={{0,1},{1,0},{2,3},{3,2},{4,5},{5,4},{6,7},{7,6},{8,9},{9,8},{10,11... | collective-permute-start | bytes 6291464 | tf_op jit(solution)/shard_map/ppermute | solution.py:125
  353.8 4.4 constant_dynamic-slice_fusion.7
  383.2 3.6 constant_dynamic-update-slice_fusion.20
  386.9 3.6 constant_dynamic-update-slice_fusion.19
  390.5 5.5 collective-permute-done.31
  399.3 10.5 %collective-permute-done.40 = bf16[2,4,64,1408]{3,2,1,0:T(8,128)(2,1)S(1)} collective-permute-done((bf16[2,4,64,1408]{3,2,1,0:T(8,128)(2,1)S(1)}, bf16[2,4,64,1408]{3,2,1,0:T(8,128)(2,1)S(1)}, u32[]{:S(2)}, u32[]{:S(2)}) %collective-permute-start.40) | collective-permute-done | bytes 1441824 | tf_op jit(solution)/shard_map/ppermute | solution.py:194
  415.1 9.7 %fusion.122 = (bf16[1,4,2,4,64,1408]{5,4,1,2,3,0:T(8,128)(2,1)}, bf16[1,4,2,4,64,1408]{5,4,1,2,3,0:T(8,128)(2,1)}) fusion(bf16[2,4,2,4,64,1408]{5,4,1,2,3,0:T(8,128)(2,1)} %bitcast.80), kind=kLoop, calls=%fused_computation.349 | loop fusion | bytes 23068672 | tf_op jit(solution)/shard_map/slice | solution.py:366
  424.8 3.3 copy.288
  435.0 3.4 fusion.130
  439.2 3.4 fusion.129
  442.6 3.1 fusion.5
  445.8 3.1 fusion.4
  448.9 7.1 %fusion.8 = (bf16[2,256,1408]{2,1,0:T(8,128)(2,1)S(1)}, bf16[2,256,1408]{2,1,0:T(8,128)(2,1)S(1)}, bf16[2,256,1408]{2,1,0:T(8,128)(2,1)S(1)}) fusion(f32[2,256,1408]{2,1,0:T(8,128)} %fusion.4, f32[2,256,1408]{2,1,0:T(8,128)} %fusion.5, f32[2,256,1408]{2,1,0:T(8,128)} %fusion.133, bf16[2,256,2048]{2,1,0:T(8,128)(2,1)S(1)} %bitcast.551, ...), kind=kOutput, calls=%fused_computation.18 | convolution fusion | flops 2965045248 | bytes 20840448 | tf_op jit(solution)/shard_map/ste,de->std/dot_general | solution.py:380
  456.5 5.0 fusion.134
  462.0 3.4 fusion.135
  476.3 3.5 multiply_add_fusion
  496.2 9.2 %collective-permute-done.55 = bf16[2,64,2048]{2,1,0:T(8,128)(2,1)S(1)} collective-permute-done((bf16[2,64,2048]{2,1,0:T(8,128)(2,1)S(1)}, bf16[2,64,2048]{2,1,0:T(8,128)(2,1)S(1)}, u32[]{:S(2)}, u32[]{:S(2)}) %collective-permute-start.55) | collective-permute-done | bytes 524320 | tf_op jit(solution)/shard_map/ppermute | solution.py:128
  505.7 10.9 %collective-permute-done.51 = bf16[2,64,2048]{2,1,0:T(8,128)(2,1)S(1)} collective-permute-done((bf16[2,64,2048]{2,1,0:T(8,128)(2,1)S(1)}, bf16[2,64,2048]{2,1,0:T(8,128)(2,1)S(1)}, u32[]{:S(2)}, u32[]{:S(2)}) %collective-permute-start.51) | collective-permute-done | bytes 524320 | tf_op jit(solution)/shard_map/ppermute | solution.py:128
  523.2 9.3 %collective-permute-done.56 = bf16[2,64,2048]{2,1,0:T(8,128)(2,1)S(1)} collective-permute-done((bf16[2,64,2048]{2,1,0:T(8,128)(2,1)S(1)}, bf16[2,64,2048]{2,1,0:T(8,128)(2,1)S(1)}, u32[]{:S(2)}, u32[]{:S(2)}) %collective-permute-start.56) | collective-permute-done | bytes 524320 | tf_op jit(solution)/shard_map/ppermute | solution.py:106
  549.7 5.6 all-to-all-start.1
  561.9 3.8 convolution_add_fusion.1
  582.8 4.0 multiply_add_fusion.5
  592.1 3.3 fusion.137
  598.4 3.2 fusion.138
  609.1 5.8 add_add_fusion
  643.8 7.5 %all-to-all-start = ((bf16[32,176,128]{2,1,0:T(8,128)(2,1)}), bf16[32,176,128]{2,1,0:T(8,128)(2,1)}, u32[]{:S(2)}, u32[]{:S(2)}) async-start(bf16[32,176,128]{2,1,0:T(8,128)(2,1)} %pad_maximum_fusion.2), calls=%async_computation | async-start | bytes 2883584 | tf_op jit(solution)/shard_map/all_to_all | solution.py:470
  660.4 10.7 %all-to-all-done = bf16[32,176,128]{2,1,0:T(8,128)(2,1)} async-done(((bf16[32,176,128]{2,1,0:T(8,128)(2,1)}), bf16[32,176,128]{2,1,0:T(8,128)(2,1)}, u32[]{:S(2)}, u32[]{:S(2)}) %all-to-all-start) | async-done | bytes 1441824 | tf_op jit(solution)/shard_map/all_to_all | solution.py:470
  675.7 7.3 %collective-permute-done.59 = bf16[2,64,2048]{2,1,0:T(8,128)(2,1)} collective-permute-done((bf16[2,64,2048]{2,1,0:T(8,128)(2,1)}, bf16[2,64,2048]{2,1,0:T(8,128)(2,1)}, u32[]{:S(2)}, u32[]{:S(2)}) %collective-permute-start.59) | collective-permute-done | bytes 524320 | tf_op jit(solution)/shard_map/ppermute | solution.py:128
  (697 shorter events, 386.8 us)
Async XLA Ops:
  0.7 51.4 %collective-permute-start.42 = (bf16[1,1408,64]{1,2,0:T(8,128)(2,1)}, bf16[1,1408,64]{1,2,0:T(8,128)(2,1)}, u32[]{:S(2)}, u32[]{:S(2)}) collective-permute-start(bf16[1,1408,64]{1,2,0:T(8,128)(2,1)} %bitcast.626), channel_id=1, source_target_pairs={{0,12},{4,0},{8,4},{12,8},{16,28},{20,16},{24,20},{28,24},{32,44},... | collective-permute-start | bytes 540680 | tf_op jit(solution)/shard_map/ppermute | solution.py:191
  4.3 48.9 %collective-permute-start.43 = (bf16[1,1408,64]{1,2,0:T(8,128)(2,1)}, bf16[1,1408,64]{1,2,0:T(8,128)(2,1)}, u32[]{:S(2)}, u32[]{:S(2)}) collective-permute-start(bf16[1,1408,64]{1,2,0:T(8,128)(2,1)} %bitcast.627), channel_id=1, source_target_pairs={{0,4},{4,8},{8,12},{12,0},{16,20},{20,24},{24,28},{28,16},{32,36},... | collective-permute-start | bytes 540680 | tf_op jit(solution)/shard_map/ppermute | solution.py:190
  4.3 41.0 %collective-permute-start.22 = (bf16[1,512,64]{1,2,0:T(8,128)(2,1)}, bf16[1,512,64]{1,2,0:T(8,128)(2,1)}, u32[]{:S(2)}, u32[]{:S(2)}) collective-permute-start(bf16[1,512,64]{1,2,0:T(8,128)(2,1)} %bitcast.632), channel_id=1, source_target_pairs={{0,12},{4,0},{8,4},{12,8},{16,28},{20,16},{24,20},{28,24},{32,44},... | collective-permute-start | bytes 196616 | tf_op jit(solution)/shard_map/ppermute | solution.py:191
  7.0 38.4 %collective-permute-start.23 = (bf16[1,512,64]{1,2,0:T(8,128)(2,1)}, bf16[1,512,64]{1,2,0:T(8,128)(2,1)}, u32[]{:S(2)}, u32[]{:S(2)}) collective-permute-start(bf16[1,512,64]{1,2,0:T(8,128)(2,1)} %bitcast.633), channel_id=1, source_target_pairs={{0,4},{4,8},{8,12},{12,0},{16,20},{20,24},{24,28},{28,16},{32,36},... | collective-permute-start | bytes 196616 | tf_op jit(solution)/shard_map/ppermute | solution.py:190
  7.0 24.5 %collective-permute-start.12 = (bf16[2,128,16]{1,2,0:T(8,128)(2,1)}, bf16[2,128,16]{1,2,0:T(8,128)(2,1)}, u32[]{:S(2)}, u32[]{:S(2)}) collective-permute-start(bf16[2,128,16]{1,2,0:T(8,128)(2,1)} %param.35), channel_id=1, source_target_pairs={{0,2},{1,3},{2,0},{3,1},{4,6},{5,7},{6,4},{7,5},{8,10},{9,11},{10,... | collective-permute-start | bytes 24584 | tf_op jit(solution)/shard_map/ppermute | solution.py:106
  40.9 23.8 %collective-permute-start.34 = (bf16[2,1,64,1408]{3,2,1,0:T(8,128)(2,1)}, bf16[2,1,64,1408]{3,2,1,0:T(8,128)(2,1)S(1)}, u32[]{:S(2)}, u32[]{:S(2)}) collective-permute-start(bf16[2,1,64,1408]{3,2,1,0:T(8,128)(2,1)} %bitcast.619), channel_id=1, source_target_pairs={{0,96},{4,100},{8,104},{12,108},{16,112},{20,116},{24,120},{28,124... | collective-permute-start | bytes 1081352 | tf_op jit(solution)/shard_map/ppermute | solution.py:191
  45.3 27.8 %collective-permute-start.35 = (bf16[2,1,64,1408]{3,2,1,0:T(8,128)(2,1)}, bf16[2,1,64,1408]{3,2,1,0:T(8,128)(2,1)S(1)}, u32[]{:S(2)}, u32[]{:S(2)}) collective-permute-start(bf16[2,1,64,1408]{3,2,1,0:T(8,128)(2,1)} %bitcast.620), channel_id=1, source_target_pairs={{0,32},{4,36},{8,40},{12,44},{16,48},{20,52},{24,56},{28,60},{32,6... | collective-permute-start | bytes 1081352 | tf_op jit(solution)/shard_map/ppermute | solution.py:190
  53.2 34.2 %collective-permute-start = (bf16[2,64,2048]{2,1,0:T(8,128)(2,1)S(1)}, bf16[2,64,2048]{2,1,0:T(8,128)(2,1)S(1)}, u32[]{:S(2)}, u32[]{:S(2)}) collective-permute-start(bf16[2,64,2048]{2,1,0:T(8,128)(2,1)S(1)} %copy-done.79), channel_id=1, source_target_pairs={{0,2},{1,3},{2,0},{3,1},{4,6},{5,7},{6,4},{7,5},{8,10},{9,11},{10,... | collective-permute-start | bytes 1572872 | tf_op jit(solution)/shard_map/ppermute | solution.py:106
  60.6 29.4 %collective-permute-start.52 = (bf16[2,64,2048]{2,1,0:T(8,128)(2,1)S(1)}, bf16[2,64,2048]{2,1,0:T(8,128)(2,1)S(1)}, u32[]{:S(2)}, u32[]{:S(2)}) collective-permute-start(bf16[2,64,2048]{2,1,0:T(8,128)(2,1)S(1)} %copy-done.36), channel_id=1, source_target_pairs={{0,2},{1,3},{2,0},{3,1},{4,6},{5,7},{6,4},{7,5},{8,10},{9,11},{10,... | collective-permute-start | bytes 1572872 | tf_op jit(solution)/shard_map/ppermute | solution.py:106
  64.1 17.2 %collective-permute-start.25 = (bf16[4,512,64]{1,2,0:T(8,128)(2,1)S(1)}, bf16[4,512,64]{1,2,0:T(8,128)(2,1)S(1)}, u32[]{:S(2)}, u32[]{:S(2)}) collective-permute-start(bf16[4,512,64]{1,2,0:T(8,128)(2,1)S(1)} %constant_dynamic-update-slice_fusion.35), channel_id=1, source_target_pairs={{0,16},{4,20},{8,24},{12,28},{16,0},{20,4},{24,8},{28,12},{32,48},... | collective-permute-start | bytes 786440 | tf_op jit(solution)/shard_map/ppermute | solution.py:180
  79.2 35.3 %collective-permute-start.45 = (bf16[4,1408,64]{1,2,0:T(8,128)(2,1)S(1)}, bf16[4,1408,64]{1,2,0:T(8,128)(2,1)S(1)}, u32[]{:S(2)}, u32[]{:S(2)}) collective-permute-start(bf16[4,1408,64]{1,2,0:T(8,128)(2,1)S(1)} %constant_dynamic-update-slice_fusion.13), channel_id=1, source_target_pairs={{0,16},{4,20},{8,24},{12,28},{16,0},{20,4},{24,8},{28,12},{32,48},... | collective-permute-start | bytes 2162696 | tf_op jit(solution)/shard_map/ppermute | solution.py:180
  84.3 24.0 %collective-permute-start.17 = (bf16[4,644,128]{2,0,1:T(4,128)(2,1)S(1)}, bf16[4,644,128]{2,0,1:T(4,128)(2,1)S(1)}, u32[]{:S(2)}, u32[]{:S(2)}) collective-permute-start(bf16[4,644,128]{2,0,1:T(4,128)(2,1)S(1)} %copy.256), channel_id=1, source_target_pairs={{0,16},{4,20},{8,24},{12,28},{16,0},{20,4},{24,8},{28,12},{32,48},... | collective-permute-start | bytes 1978376 | tf_op jit(solution)/shard_map/ppermute | solution.py:180
  90.0 14.5 %collective-permute-start.27 = (bf16[8,512,64]{1,2,0:T(8,128)(2,1)S(1)}, bf16[8,512,64]{1,2,0:T(8,128)(2,1)S(1)}, u32[]{:S(2)}, u32[]{:S(2)}) collective-permute-start(bf16[8,512,64]{1,2,0:T(8,128)(2,1)S(1)} %constant_dynamic-update-slice_fusion.33), channel_id=1, source_target_pairs={{0,32},{4,36},{8,40},{12,44},{16,48},{20,52},{24,56},{28,60},{32,6... | collective-permute-start | bytes 1572872 | tf_op jit(solution)/shard_map/ppermute | solution.py:190
  90.5 34.7 %collective-permute-start.5 = (bf16[3,4,64,512]{3,2,1,0:T(8,128)(2,1)S(1)}, bf16[3,4,64,512]{3,2,1,0:T(8,128)(2,1)S(1)}, u32[]{:S(2)}, u32[]{:S(2)}) collective-permute-start(bf16[3,4,64,512]{3,2,1,0:T(8,128)(2,1)S(1)} %bitcast_dynamic-update-slice_fusion.1), channel_id=1, source_target_pairs={{0,16},{4,20},{8,24},{12,28},{16,0},{20,4},{24,8},{28,12},{32,48},... | collective-permute-start | bytes 2359304 | tf_op jit(solution)/shard_map/ppermute | solution.py:180
  96.5 41.5 %collective-permute-start.1 = (bf16[2,2,64,2048]{3,2,1,0:T(8,128)(2,1)S(1)}, bf16[2,2,64,2048]{3,2,1,0:T(8,128)(2,1)S(1)}, u32[]{:S(2)}, u32[]{:S(2)}) collective-permute-start(bf16[2,2,64,2048]{3,2,1,0:T(8,128)(2,1)S(1)} %maximum_select_fusion.4), channel_id=1, source_target_pairs={{0,1},{1,0},{2,3},{3,2},{4,5},{5,4},{6,7},{7,6},{8,9},{9,8},{10,11... | collective-permute-start | bytes 3145736 | tf_op jit(solution)/shard_map/ppermute | solution.py:110
  104.5 31.0 %collective-permute-start.53 = (bf16[2,2,64,2048]{3,2,0,1:T(8,128)(2,1)S(1)}, bf16[2,2,64,2048]{3,2,0,1:T(8,128)(2,1)S(1)}, u32[]{:S(2)}, u32[]{:S(2)}) collective-permute-start(bf16[2,2,64,2048]{3,2,0,1:T(8,128)(2,1)S(1)} %maximum_select_fusion.7), channel_id=1, source_target_pairs={{0,1},{1,0},{2,3},{3,2},{4,5},{5,4},{6,7},{7,6},{8,9},{9,8},{10,11... | collective-permute-start | bytes 3145736 | tf_op jit(solution)/shard_map/ppermute | solution.py:110
  114.5 41.7 %collective-permute-start.37 = (bf16[2,4,64,1408]{3,2,1,0:T(8,128)(2,1)}, bf16[2,4,64,1408]{3,2,1,0:T(8,128)(2,1)S(1)}, u32[]{:S(2)}, u32[]{:S(2)}) collective-permute-start(bf16[2,4,64,1408]{3,2,1,0:T(8,128)(2,1)} %constant_dynamic-update-slice_fusion.24), channel_id=1, source_target_pairs={{0,16},{4,20},{8,24},{12,28},{16,0},{20,4},{24,8},{28,12},{32,48},... | collective-permute-start | bytes 4325384 | tf_op jit(solution)/shard_map/ppermute | solution.py:180
  115.6 14.6 %collective-permute-start.29 = (bf16[4,512,64]{1,2,0:T(8,128)(2,1)S(1)}, bf16[4,512,64]{1,2,0:T(8,128)(2,1)S(1)}, u32[]{:S(2)}, u32[]{:S(2)}) collective-permute-start(bf16[4,512,64]{1,2,0:T(8,128)(2,1)S(1)} %slice.261), channel_id=1, source_target_pairs={{0,96},{4,100},{8,104},{12,108},{16,112},{20,116},{24,120},{28,124... | collective-permute-start | bytes 786440 | tf_op jit(solution)/shard_map/ppermute | solution.py:195
  125.2 32.9 %collective-permute-start.19 = (bf16[8,644,128]{2,0,1:T(8,128)(2,1)}, bf16[8,644,128]{2,0,1:T(8,128)(2,1)}, u32[]{:S(2)}, u32[]{:S(2)}) collective-permute-start(bf16[8,644,128]{2,0,1:T(8,128)(2,1)} %copy.258), channel_id=1, source_target_pairs={{0,32},{4,36},{8,40},{12,44},{16,48},{20,52},{24,56},{28,60},{32,6... | collective-permute-start | bytes 3956744 | tf_op jit(solution)/shard_map/ppermute | solution.py:190
  130.2 40.1 %collective-permute-start.18 = (bf16[8,644,128]{2,0,1:T(8,128)(2,1)}, bf16[8,644,128]{2,0,1:T(8,128)(2,1)}, u32[]{:S(2)}, u32[]{:S(2)}) collective-permute-start(bf16[8,644,128]{2,0,1:T(8,128)(2,1)} %copy.258), channel_id=1, source_target_pairs={{0,96},{4,100},{8,104},{12,108},{16,112},{20,116},{24,120},{28,124... | collective-permute-start | bytes 3956744 | tf_op jit(solution)/shard_map/ppermute | solution.py:191
  135.5 46.0 %collective-permute-start.46 = (bf16[8,1408,64]{1,2,0:T(8,128)(2,1)}, bf16[8,1408,64]{1,2,0:T(8,128)(2,1)}, u32[]{:S(2)}, u32[]{:S(2)}) collective-permute-start(bf16[8,1408,64]{1,2,0:T(8,128)(2,1)} %constant_dynamic-update-slice_fusion.11), channel_id=1, source_target_pairs={{0,96},{4,100},{8,104},{12,108},{16,112},{20,116},{24,120},{28,124... | collective-permute-start | bytes 4325384 | tf_op jit(solution)/shard_map/ppermute | solution.py:191
  138.1 47.3 %collective-permute-start.47 = (bf16[8,1408,64]{1,2,0:T(8,128)(2,1)}, bf16[8,1408,64]{1,2,0:T(8,128)(2,1)}, u32[]{:S(2)}, u32[]{:S(2)}) collective-permute-start(bf16[8,1408,64]{1,2,0:T(8,128)(2,1)} %constant_dynamic-update-slice_fusion.11), channel_id=1, source_target_pairs={{0,32},{4,36},{8,40},{12,44},{16,48},{20,52},{24,56},{28,60},{32,6... | collective-permute-start | bytes 4325384 | tf_op jit(solution)/shard_map/ppermute | solution.py:190
  156.2 59.0 %collective-permute-start.6 = (bf16[3,8,64,512]{3,2,1,0:T(8,128)(2,1)}, bf16[3,8,64,512]{3,2,1,0:T(8,128)(2,1)}, u32[]{:S(2)}, u32[]{:S(2)}) collective-permute-start(bf16[3,8,64,512]{3,2,1,0:T(8,128)(2,1)} %constant_dynamic-update-slice_fusion.50), channel_id=1, source_target_pairs={{0,96},{4,100},{8,104},{12,108},{16,112},{20,116},{24,120},{28,124... | collective-permute-start | bytes 4718600 | tf_op jit(solution)/shard_map/ppermute | solution.py:191
  158.1 53.3 %collective-permute-start.7 = (bf16[3,8,64,512]{3,2,1,0:T(8,128)(2,1)}, bf16[3,8,64,512]{3,2,1,0:T(8,128)(2,1)}, u32[]{:S(2)}, u32[]{:S(2)}) collective-permute-start(bf16[3,8,64,512]{3,2,1,0:T(8,128)(2,1)} %constant_dynamic-update-slice_fusion.50), channel_id=1, source_target_pairs={{0,32},{4,36},{8,40},{12,44},{16,48},{20,52},{24,56},{28,60},{32,6... | collective-permute-start | bytes 4718600 | tf_op jit(solution)/shard_map/ppermute | solution.py:190
  170.3 205.1 %collective-permute-start.38 = (bf16[2,8,64,1408]{3,2,1,0:T(8,128)(2,1)}, bf16[2,8,64,1408]{3,2,1,0:T(8,128)(2,1)}, u32[]{:S(2)}, u32[]{:S(2)}) collective-permute-start(bf16[2,8,64,1408]{3,2,1,0:T(8,128)(2,1)} %constant_dynamic-update-slice_fusion.22), channel_id=1, source_target_pairs={{0,12},{4,0},{8,4},{12,8},{16,28},{20,16},{24,20},{28,24},{32,44},... | collective-permute-start | bytes 8650760 | tf_op jit(solution)/shard_map/ppermute | solution.py:191
  181.5 44.0 %collective-permute-start.20 = (bf16[4,644,128]{2,0,1:T(4,128)(2,1)S(1)}, bf16[4,644,128]{2,0,1:T(4,128)(2,1)S(1)}, u32[]{:S(2)}, u32[]{:S(2)}) collective-permute-start(bf16[4,644,128]{2,0,1:T(4,128)(2,1)S(1)} %slice.239), channel_id=1, source_target_pairs={{0,32},{4,36},{8,40},{12,44},{16,48},{20,52},{24,56},{28,60},{32,6... | collective-permute-start | bytes 1978376 | tf_op jit(solution)/shard_map/ppermute | solution.py:194
  185.4 43.9 %collective-permute-start.21 = (bf16[4,644,128]{2,0,1:T(4,128)(2,1)S(1)}, bf16[4,644,128]{2,0,1:T(4,128)(2,1)S(1)}, u32[]{:S(2)}, u32[]{:S(2)}) collective-permute-start(bf16[4,644,128]{2,0,1:T(4,128)(2,1)S(1)} %slice.240), channel_id=1, source_target_pairs={{0,96},{4,100},{8,104},{12,108},{16,112},{20,116},{24,120},{28,124... | collective-permute-start | bytes 1978376 | tf_op jit(solution)/shard_map/ppermute | solution.py:195
  211.4 162.5 %collective-permute-start.39 = (bf16[2,8,64,1408]{3,2,1,0:T(8,128)(2,1)}, bf16[2,8,64,1408]{3,2,1,0:T(8,128)(2,1)}, u32[]{:S(2)}, u32[]{:S(2)}) collective-permute-start(bf16[2,8,64,1408]{3,2,1,0:T(8,128)(2,1)} %constant_dynamic-update-slice_fusion.22), channel_id=1, source_target_pairs={{0,4},{4,8},{8,12},{12,0},{16,20},{20,24},{24,28},{28,16},{32,36},... | collective-permute-start | bytes 8650760 | tf_op jit(solution)/shard_map/ppermute | solution.py:190
  215.2 154.6 %collective-permute-start.48 = (bf16[4,1408,64]{1,2,0:T(8,128)(2,1)}, bf16[4,1408,64]{1,2,0:T(8,128)(2,1)}, u32[]{:S(2)}, u32[]{:S(2)}) collective-permute-start(bf16[4,1408,64]{1,2,0:T(8,128)(2,1)} %slice.275), channel_id=1, source_target_pairs={{0,32},{4,36},{8,40},{12,44},{16,48},{20,52},{24,56},{28,60},{32,6... | collective-permute-start | bytes 2162696 | tf_op jit(solution)/shard_map/ppermute | solution.py:194
  225.5 63.1 %collective-permute-start.8 = (bf16[3,4,64,512]{3,2,1,0:T(8,128)(2,1)}, bf16[3,4,64,512]{3,2,1,0:T(8,128)(2,1)}, u32[]{:S(2)}, u32[]{:S(2)}) collective-permute-start(bf16[3,4,64,512]{3,2,1,0:T(8,128)(2,1)} %slice.236), channel_id=1, source_target_pairs={{0,32},{4,36},{8,40},{12,44},{16,48},{20,52},{24,56},{28,60},{32,6... | collective-permute-start | bytes 2359304 | tf_op jit(solution)/shard_map/ppermute | solution.py:194
  229.3 62.1 %collective-permute-start.9 = (bf16[3,4,64,512]{3,2,1,0:T(8,128)(2,1)}, bf16[3,4,64,512]{3,2,1,0:T(8,128)(2,1)}, u32[]{:S(2)}, u32[]{:S(2)}) collective-permute-start(bf16[3,4,64,512]{3,2,1,0:T(8,128)(2,1)} %slice.237), channel_id=1, source_target_pairs={{0,96},{4,100},{8,104},{12,108},{16,112},{20,116},{24,120},{28,124... | collective-permute-start | bytes 2359304 | tf_op jit(solution)/shard_map/ppermute | solution.py:195
  288.6 83.2 %collective-permute-start.49 = (bf16[4,1408,64]{1,2,0:T(8,128)(2,1)}, bf16[4,1408,64]{1,2,0:T(8,128)(2,1)}, u32[]{:S(2)}, u32[]{:S(2)}) collective-permute-start(bf16[4,1408,64]{1,2,0:T(8,128)(2,1)} %slice.276), channel_id=1, source_target_pairs={{0,96},{4,100},{8,104},{12,108},{16,112},{20,116},{24,120},{28,124... | collective-permute-start | bytes 2162696 | tf_op jit(solution)/shard_map/ppermute | solution.py:195
  328.5 51.2 %collective-permute-start.30 = (f32[2,2,64,2048]{3,2,0,1:T(8,128)}, f32[2,2,64,2048]{3,2,0,1:T(8,128)}, u32[]{:S(2)}, u32[]{:S(2)}) collective-permute-start(f32[2,2,64,2048]{3,2,0,1:T(8,128)} %bitcast.503), channel_id=1, source_target_pairs={{0,1},{1,0},{2,3},{3,2},{4,5},{5,4},{6,7},{7,6},{8,9},{9,8},{10,11... | collective-permute-start | bytes 6291464 | tf_op jit(solution)/shard_map/ppermute | solution.py:125
  375.3 34.5 %collective-permute-start.40 = (bf16[2,4,64,1408]{3,2,1,0:T(8,128)(2,1)S(1)}, bf16[2,4,64,1408]{3,2,1,0:T(8,128)(2,1)S(1)}, u32[]{:S(2)}, u32[]{:S(2)}) collective-permute-start(bf16[2,4,64,1408]{3,2,1,0:T(8,128)(2,1)S(1)} %slice.266), channel_id=1, source_target_pairs={{0,4},{4,8},{8,12},{12,0},{16,20},{20,24},{24,28},{28,16},{32,36},... | collective-permute-start | bytes 4325384 | tf_op jit(solution)/shard_map/ppermute | solution.py:194
  377.0 34.0 %collective-permute-start.41 = (bf16[2,4,64,1408]{3,2,1,0:T(8,128)(2,1)S(1)}, bf16[2,4,64,1408]{3,2,1,0:T(8,128)(2,1)S(1)}, u32[]{:S(2)}, u32[]{:S(2)}) collective-permute-start(bf16[2,4,64,1408]{3,2,1,0:T(8,128)(2,1)S(1)} %slice.267), channel_id=1, source_target_pairs={{0,12},{4,0},{8,4},{12,8},{16,28},{20,16},{24,20},{28,24},{32,44},... | collective-permute-start | bytes 4325384 | tf_op jit(solution)/shard_map/ppermute | solution.py:195
  381.6 14.5 %collective-permute-start.31 = (bf16[2,64,2048]{2,1,0:T(8,128)(2,1)S(1)}, bf16[2,64,2048]{2,1,0:T(8,128)(2,1)S(1)}, u32[]{:S(2)}, u32[]{:S(2)}) collective-permute-start(bf16[2,64,2048]{2,1,0:T(8,128)(2,1)S(1)} %fusion.44), channel_id=1, source_target_pairs={{0,2},{1,3},{2,0},{3,1},{4,6},{5,7},{6,4},{7,5},{8,10},{9,11},{10,... | collective-permute-start | bytes 1572872 | tf_op jit(solution)/shard_map/ppermute | solution.py:128
  396.6 15.7 %collective-permute-start.32 = (bf16[2,64,2048]{2,1,0:T(8,128)(2,1)S(1)}, bf16[2,64,2048]{2,1,0:T(8,128)(2,1)S(1)}, u32[]{:S(2)}, u32[]{:S(2)}) collective-permute-start(bf16[2,64,2048]{2,1,0:T(8,128)(2,1)S(1)} %multiply_convert_fusion.3), channel_id=1, source_target_pairs={{0,2},{1,3},{2,0},{3,1},{4,6},{5,7},{6,4},{7,5},{8,10},{9,11},{10,... | collective-permute-start | bytes 1572872 | tf_op jit(solution)/shard_map/ppermute | solution.py:106
  414.1 17.4 %collective-permute-start.33 = (bf16[2,2,64,2048]{3,2,0,1:T(8,128)(2,1)}, bf16[2,2,64,2048]{3,2,0,1:T(8,128)(2,1)}, u32[]{:S(2)}, u32[]{:S(2)}) collective-permute-start(bf16[2,2,64,2048]{3,2,0,1:T(8,128)(2,1)} %maximum_select_fusion.6), channel_id=1, source_target_pairs={{0,1},{1,0},{2,3},{3,2},{4,5},{5,4},{6,7},{7,6},{8,9},{9,8},{10,11... | collective-permute-start | bytes 3145736 | tf_op jit(solution)/shard_map/ppermute | solution.py:110
  490.2 15.1 %collective-permute-start.55 = (bf16[2,64,2048]{2,1,0:T(8,128)(2,1)S(1)}, bf16[2,64,2048]{2,1,0:T(8,128)(2,1)S(1)}, u32[]{:S(2)}, u32[]{:S(2)}) collective-permute-start(bf16[2,64,2048]{2,1,0:T(8,128)(2,1)S(1)} %fusion.46), channel_id=1, source_target_pairs={{0,2},{1,3},{2,0},{3,1},{4,6},{5,7},{6,4},{7,5},{8,10},{9,11},{10,... | collective-permute-start | bytes 1572872 | tf_op jit(solution)/shard_map/ppermute | solution.py:128
  494.0 22.5 %collective-permute-start.51 = (bf16[2,64,2048]{2,1,0:T(8,128)(2,1)S(1)}, bf16[2,64,2048]{2,1,0:T(8,128)(2,1)S(1)}, u32[]{:S(2)}, u32[]{:S(2)}) collective-permute-start(bf16[2,64,2048]{2,1,0:T(8,128)(2,1)S(1)} %fusion.45), channel_id=1, source_target_pairs={{0,2},{1,3},{2,0},{3,1},{4,6},{5,7},{6,4},{7,5},{8,10},{9,11},{10,... | collective-permute-start | bytes 1572872 | tf_op jit(solution)/shard_map/ppermute | solution.py:128
  518.3 14.2 %collective-permute-start.56 = (bf16[2,64,2048]{2,1,0:T(8,128)(2,1)S(1)}, bf16[2,64,2048]{2,1,0:T(8,128)(2,1)S(1)}, u32[]{:S(2)}, u32[]{:S(2)}) collective-permute-start(bf16[2,64,2048]{2,1,0:T(8,128)(2,1)S(1)} %get-tuple-element.34), channel_id=1, source_target_pairs={{0,2},{1,3},{2,0},{3,1},{4,6},{5,7},{6,4},{7,5},{8,10},{9,11},{10,... | collective-permute-start | bytes 1572872 | tf_op jit(solution)/shard_map/ppermute | solution.py:106
  520.5 23.8 %collective-permute-start.62 = (f32[2,2,256,16]{2,3,1,0:T(8,128)}, f32[2,2,256,16]{2,3,1,0:T(8,128)}, u32[]{:S(2)}, u32[]{:S(2)}) collective-permute-start(f32[2,2,256,16]{2,3,1,0:T(8,128)} %pad_maximum_fusion.10), channel_id=1, source_target_pairs={{0,1},{1,0},{2,3},{3,2},{4,5},{5,4},{6,7},{7,6},{8,9},{9,8},{10,11... | collective-permute-start | bytes 196616 | tf_op jit(solution)/shard_map/ppermute | solution.py:134
  533.6 24.1 %collective-permute-start.57 = (bf16[2,2,64,2048]{3,2,0,1:T(8,128)(2,1)}, bf16[2,2,64,2048]{3,2,0,1:T(8,128)(2,1)}, u32[]{:S(2)}, u32[]{:S(2)}) collective-permute-start(bf16[2,2,64,2048]{3,2,0,1:T(8,128)(2,1)} %maximum_select_fusion.9), channel_id=1, source_target_pairs={{0,1},{1,0},{2,3},{3,2},{4,5},{5,4},{6,7},{7,6},{8,9},{9,8},{10,11... | collective-permute-start | bytes 3145736 | tf_op jit(solution)/shard_map/ppermute | solution.py:110
  549.7 94.1 %all-to-all-start.1 = ((bf16[32,132,128]{2,1,0:T(8,128)(2,1)}), bf16[32,132,128]{2,1,0:T(8,128)(2,1)}, u32[]{:S(2)}, u32[]{:S(2)}) async-start(bf16[32,132,128]{2,1,0:T(8,128)(2,1)} %pad_maximum_fusion.3), calls=%async_computation.1 | async-start | bytes 2228224 | tf_op jit(solution)/shard_map/all_to_all | solution.py:470
  602.9 19.2 %collective-permute-start.60 = (f32[5,2,256,16]{2,3,1,0:T(8,128)S(1)}, f32[5,2,256,16]{2,3,1,0:T(8,128)S(1)}, u32[]{:S(2)}, u32[]{:S(2)}) collective-permute-start(f32[5,2,256,16]{2,3,1,0:T(8,128)S(1)} %bitcast_dynamic-update-slice_fusion.4), channel_id=1, source_target_pairs={{0,1},{1,0},{2,3},{3,2},{4,5},{5,4},{6,7},{7,6},{8,9},{9,8},{10,11... | collective-permute-start | bytes 491528 | tf_op jit(solution)/shard_map/ppermute | solution.py:134
  618.2 33.1 %collective-permute-start.58 = (f32[2,2,64,2048]{3,2,0,1:T(8,128)}, f32[2,2,64,2048]{3,2,0,1:T(8,128)}, u32[]{:S(2)}, u32[]{:S(2)}) collective-permute-start(f32[2,2,64,2048]{3,2,0,1:T(8,128)} %bitcast.500), channel_id=1, source_target_pairs={{0,1},{1,0},{2,3},{3,2},{4,5},{5,4},{6,7},{7,6},{8,9},{9,8},{10,11... | collective-permute-start | bytes 6291464 | tf_op jit(solution)/shard_map/ppermute | solution.py:125
  643.8 27.3 %all-to-all-start = ((bf16[32,176,128]{2,1,0:T(8,128)(2,1)}), bf16[32,176,128]{2,1,0:T(8,128)(2,1)}, u32[]{:S(2)}, u32[]{:S(2)}) async-start(bf16[32,176,128]{2,1,0:T(8,128)(2,1)} %pad_maximum_fusion.2), calls=%async_computation | async-start | bytes 2883584 | tf_op jit(solution)/shard_map/all_to_all | solution.py:470
  654.6 28.4 %collective-permute-start.59 = (bf16[2,64,2048]{2,1,0:T(8,128)(2,1)}, bf16[2,64,2048]{2,1,0:T(8,128)(2,1)}, u32[]{:S(2)}, u32[]{:S(2)}) collective-permute-start(bf16[2,64,2048]{2,1,0:T(8,128)(2,1)} %fusion.47), channel_id=1, source_target_pairs={{0,2},{1,3},{2,0},{3,1},{4,6},{5,7},{6,4},{7,5},{8,10},{9,11},{10,... | collective-permute-start | bytes 1572872 | tf_op jit(solution)/shard_map/ppermute | solution.py:128
  (154 other events, 2116.4 us)
